TPU v7x, 256 devices: a whole 4x4x8 slice. The times are simulated.
256 devices in a mesh: pipe: 8 (over z_lo, y), dp: 32 (over x, z_hi, core).
Axes of the slice: x: 4, y: 4, z: 8 (z_hi: 4, z_lo: 2; z = z_hi * 2 + z_lo), core: 2. Of those that a mesh axis runs over, the one named last changes fastest.
Arguments:
- inputs: bfloat16 [2, 4096, 2048], P(None, 'dp'), may hold values from -6 to 6
- cotangent: bfloat16 [2, 4096, 2048], P(None, 'dp'), may hold values from -0.125 to 0.125
- joined: int32 [2, 16], replicated, may hold values 0 or 1
- w_qkv: bfloat16 [8, 2048, 1536], P('pipe', 'dp'), may hold values from -0.125 to 0.125
- w_out: bfloat16 [8, 1024, 2048], P('pipe', 'dp'), may hold values from -0.1875 to 0.1875
Outputs:
- grad_qkv: float32 [8, 2048, 1536], P('pipe', 'dp')
- grad_out: float32 [8, 1024, 2048], P('pipe', 'dp')
Inputs may be any that keep to these rules, and one draw needn't show every extreme that they name: joined[m, j] is 1 where bin j of micro-batch m holds one molecule covering both of its blocks, 0 where each block holds its own molecule.
All inputs are finite; a program needn't handle non-finite values.
Results may differ from a plain program's by a relative error of at most 0.028.
Values may be sent and summed in bfloat16 or wider, within the bound.
No kernel may reach another device: no remote copies, remote signals or barrier semaphores. Data moves between devices by JAX's collectives and lax.ppermute only.
A program may use at most 192 MiB of HBM per device.

v0:
```python
import math

import jax
import jax.numpy as jnp
from jax import lax
from jax.sharding import PartitionSpec as P

HEADS = 16
HEAD = 64
KVH = 4


norm_eps = 1e-05


def from_partner(block, axis, apart):
    count = lax.axis_size(axis)
    route = []
    for low in range(count):
        high = low | 1 << apart
        if high != low and high < count:
            route += [(low, high), (high, low)]
    return lax.ppermute(block, axis, route)


def from_behind(value, axis, steps):
    count = lax.axis_size(axis)
    leading, last = (max(0, -steps), min(count, count - steps))
    return lax.ppermute(value, axis, [(source, source + steps) for source in range(leading, last)])


def normalize(hidden):
    widened = hidden.astype(jnp.float32)
    inv_rms = lax.rsqrt(jnp.mean(widened * widened, axis=-1, keepdims=True) + norm_eps)
    return (widened * inv_rms).astype(jnp.bfloat16)


def project(hidden, w_qkv):
    normed = normalize(hidden)
    projected = jnp.dot(normed, w_qkv, preferred_element_type=jnp.float32)
    inner_width = HEADS * HEAD
    kv_width = KVH * HEAD
    queries = projected[:, :inner_width].astype(jnp.bfloat16)
    own_kv = jnp.stack(
        [projected[:, inner_width : inner_width + kv_width], projected[:, inner_width + kv_width :]]
    ).astype(jnp.bfloat16)
    return (normed, queries, own_kv)


def attend(queries, key_rows, value_rows, visible):
    row_count = queries.shape[0]
    key_count = key_rows.shape[0]
    grouped = queries.astype(jnp.float32).reshape(row_count, KVH, HEADS // KVH, HEAD)
    key_heads = key_rows.astype(jnp.float32).reshape(key_count, KVH, HEAD)
    value_heads = value_rows.astype(jnp.float32).reshape(key_count, KVH, HEAD)
    scores = jnp.einsum("tkgd,ukd->kgtu", grouped, key_heads) * (1.0 / math.sqrt(HEAD))
    raised = jnp.exp(scores) * visible
    prob_rows = (raised / jnp.sum(raised, axis=-1, keepdims=True)).astype(jnp.bfloat16)
    prob_rows = lax.optimization_barrier(prob_rows)
    context = jnp.einsum("kgtu,ukd->tkgd", prob_rows.astype(jnp.float32), value_heads)
    return context.reshape(row_count, HEADS * HEAD).astype(jnp.bfloat16)


def attend_pair(queries, own_kv, pair_kv, joined_flag):
    row_count = own_kv.shape[1]
    pair_mask = jnp.where(joined_flag > 0, 1.0, 0.0).astype(jnp.float32) * jnp.ones(
        (row_count,), jnp.float32
    )
    visible = jnp.concatenate([jnp.ones((row_count,), jnp.float32), pair_mask])
    key_rows = jnp.concatenate([own_kv[0], pair_kv[0]])
    value_rows = jnp.concatenate([own_kv[1], pair_kv[1]])
    return attend(queries, key_rows, value_rows, visible)


def attention_choice(queries, own_kv, pair_kv, joined_flag):
    return attend_pair(queries, own_kv, pair_kv, joined_flag)


def finish(hidden, context, w_out):
    return (
        hidden.astype(jnp.float32) + jnp.dot(context, w_out, preferred_element_type=jnp.float32)
    ).astype(jnp.bfloat16)


def attention_grads(upstream, queries, own_kv, pair_kv, joined_flag, w_out):
    d_context = jnp.dot(upstream, w_out.T, preferred_element_type=jnp.float32).astype(jnp.bfloat16)

    def forward_part(query_rows, own_rows, pair_rows):
        return attention_choice(query_rows, own_rows, pair_rows, joined_flag)

    unused, pull = jax.vjp(forward_part, queries, own_kv, pair_kv)
    return pull(d_context)


def input_grads(upstream, hidden, d_query, d_own, back_kv, w_qkv):
    combined = (d_own.astype(jnp.float32) + back_kv.astype(jnp.float32)).astype(jnp.bfloat16)
    d_proj = jnp.concatenate([d_query, combined[0], combined[1]], axis=-1)
    d_normed = jnp.dot(d_proj, w_qkv.T, preferred_element_type=jnp.float32)
    widened = hidden.astype(jnp.float32)
    inv_rms = lax.rsqrt(jnp.mean(widened * widened, axis=-1, keepdims=True) + norm_eps)
    cubed = inv_rms * inv_rms * inv_rms
    d_widened = inv_rms * d_normed - widened * cubed * jnp.mean(
        d_normed * widened, axis=-1, keepdims=True
    )
    previous = (upstream.astype(jnp.float32) + d_widened).astype(jnp.bfloat16)
    return (d_proj, previous)


def keep_slot(store, value, slot_index, active):
    current = lax.dynamic_index_in_dim(store, slot_index, 0, keepdims=False)
    return lax.dynamic_update_index_in_dim(store, jnp.where(active, value, current), slot_index, 0)


def on_device(inputs, cotangent, joined, w_qkv, w_out):
    segments = lax.axis_size("pipe")
    segment_index = lax.axis_index("pipe")
    member = lax.axis_index("dp")
    micro_count = inputs.shape[0]
    row_count = inputs.shape[1]
    model_width = inputs.shape[2]
    full_qkv, full_out = (
        lax.all_gather(w_qkv[0], "dp", axis=0, tiled=True),
        lax.all_gather(w_out[0], "dp", axis=0, tiled=True),
    )
    inner_width = full_out.shape[0]
    proj_width = full_qkv.shape[1]
    kv_width = (proj_width - inner_width) // 2
    bin_flags = lax.dynamic_index_in_dim(joined, member // 2, 1, keepdims=False)
    turn_count = micro_count + segments - 1
    blank_rows = jnp.zeros((row_count, model_width), jnp.bfloat16)
    blank_query = jnp.zeros((row_count, inner_width), jnp.bfloat16)
    blank_kv = jnp.zeros((2, row_count, kv_width), jnp.bfloat16)
    blank_proj = jnp.zeros((row_count, proj_width), jnp.bfloat16)
    stores = tuple(
        (
            jnp.zeros((micro_count,) + shaped.shape, jnp.bfloat16)
            for shaped in (blank_rows, blank_rows, blank_query, blank_kv, blank_kv, blank_query)
        )
    )

    def forward_step(turn, incoming, saved):
        position = turn - segment_index
        active = (position >= 0) & (position < micro_count)
        slot_index = jnp.clip(position, 0, micro_count - 1)
        fresh_rows = lax.dynamic_index_in_dim(
            inputs, jnp.clip(turn, 0, micro_count - 1), 0, keepdims=False
        )
        hidden = jnp.where(segment_index == 0, fresh_rows, incoming)
        joined_flag = bin_flags[slot_index]

        def run_project(state):
            return project(state, full_qkv)

        def skip_project(state):
            return (blank_rows, blank_query, blank_kv)

        normed, queries, own_kv = lax.cond(active, run_project, skip_project, hidden)
        pair_kv = from_partner(own_kv, "dp", 0)

        def run_attend(operands):
            context = attention_choice(operands[0], operands[1], operands[2], joined_flag)
            return (context, finish(operands[3], context, full_out))

        def skip_attend(operands):
            return (blank_query, blank_rows)

        context, result = lax.cond(
            active, run_attend, skip_attend, (queries, own_kv, pair_kv, hidden)
        )
        fresh_values = (hidden, normed, queries, own_kv, pair_kv, context)
        saved = tuple(
            (
                keep_slot(store, value, slot_index, active)
                for store, value in zip(saved, fresh_values)
            )
        )
        return (result, saved)

    def forward_turn(turn, carry):
        result, new_stores = forward_step(turn, carry[0], carry[1])
        return (from_behind(result, "pipe", 1), new_stores)

    carry = lax.fori_loop(0, turn_count - 1, forward_turn, (blank_rows, stores))
    unused, stores = forward_step(turn_count - 1, carry[0], carry[1])
    ledger = (jnp.zeros(full_qkv.shape, jnp.float32), jnp.zeros(full_out.shape, jnp.float32))

    def backward_step(turn, incoming, tally):
        position = turn - (segments - 1 - segment_index)
        active = (position >= 0) & (position < micro_count)
        slot_index = jnp.clip(position, 0, micro_count - 1)
        fresh_rows = lax.dynamic_index_in_dim(
            cotangent, jnp.clip(turn, 0, micro_count - 1), 0, keepdims=False
        )
        upstream = jnp.where(segment_index == segments - 1, fresh_rows, incoming)
        hidden, normed, queries, own_kv, pair_kv, context = tuple(
            (lax.dynamic_index_in_dim(store, slot_index, 0, keepdims=False) for store in stores)
        )
        joined_flag = bin_flags[slot_index]

        def run_first(state):
            return attention_grads(state, queries, own_kv, pair_kv, joined_flag, full_out)

        def skip_first(state):
            return (blank_query, blank_kv, blank_kv)

        d_query, d_own, d_pair = lax.cond(active, run_first, skip_first, upstream)
        back_kv = from_partner(d_pair, "dp", 0)

        def run_second(operands):
            return input_grads(operands[0], hidden, operands[1], operands[2], operands[3], full_qkv)

        def skip_second(operands):
            return (blank_proj, blank_rows)

        d_proj, previous = lax.cond(
            active, run_second, skip_second, (upstream, d_query, d_own, back_kv)
        )

        def run_terms(totals):
            qkv_total = totals[0] + jnp.dot(normed.T, d_proj, preferred_element_type=jnp.float32)
            out_total = totals[1] + jnp.dot(context.T, upstream, preferred_element_type=jnp.float32)
            return (qkv_total, out_total)

        def skip_terms(totals):
            return totals

        tally = lax.cond(active, run_terms, skip_terms, tally)
        return (previous, tally)

    def backward_turn(turn, carry):
        previous, new_tally = backward_step(turn, carry[0], carry[1])
        return (from_behind(previous, "pipe", -1), new_tally)

    carry = lax.fori_loop(0, turn_count - 1, backward_turn, (blank_rows, ledger))
    unused, ledger = backward_step(turn_count - 1, carry[0], carry[1])
    grad_qkv, grad_out = (
        lax.psum_scatter(
            ledger[0].astype(jnp.bfloat16), "dp", scatter_dimension=0, tiled=True
        ).astype(jnp.float32),
        lax.psum_scatter(
            ledger[1].astype(jnp.bfloat16), "dp", scatter_dimension=0, tiled=True
        ).astype(jnp.float32),
    )
    return (grad_qkv[None], grad_out[None])


def solution(mesh):
    return jax.shard_map(
        on_device,
        mesh=mesh,
        in_specs=(
            P(None, "dp", None),
            P(None, "dp", None),
            P(),
            P("pipe", "dp", None),
            P("pipe", "dp", None),
        ),
        out_specs=(P("pipe", "dp", None), P("pipe", "dp", None)),
        check_vma=False,
    )
```

profile of v0, /device:TPU:32, one launch (start us, length us, event | category | flops | bytes accessed | tf_op | source)
XLA Modules:
  0.0 1103.6 jit_solution(1348793310206374245)
XLA Ops:
  10.2 62.3 %all-gather.5.cloned.1.call-done = bf16[1,1024,2048]{2,1,0:T(8,128)(2,1)} async-done(((bf16[1,32,2048]{2,1,0:T(8,128)(2,1)}), bf16[1,1024,2048]{2,1,0:T(8,128)(2,1)}) %all-gather.5.cloned.1.call-update) | async-done | bytes 4194320 | tf_op jit(solution)/shard_map/all_gather | solution.py:123
  72.5 66.8 %all-gather.7.cloned.1.call-done = bf16[1,2048,1536]{2,1,0:T(8,128)(2,1)} async-done(((bf16[1,64,1536]{2,1,0:T(8,128)(2,1)}), bf16[1,2048,1536]{2,1,0:T(8,128)(2,1)}) %all-gather.7.cloned.1.call-update) | async-done | bytes 6291472 | tf_op jit(solution)/shard_map/all_gather | solution.py:122
  143.2 303.1 %while.45 = (s32[]{:T(128)}, bf16[128,2048]{1,0:T(8,128)(2,1)S(1)}, bf16[2,128,2048]{2,1,0:T(8,128)(2,1)}, bf16[2,128,2048]{2,1,0:T(8,128)(2,1)}, bf16[2,128,102...) while((s32[]{:T(128)}, bf16[128,2048]{1,0:T(8,128)(2,1)S(1)}, ...), condition=%wide.region_7.8_spmd, body=%wide.region_0.7_spmd.sunk | while | flops 1484519552 | bytes 54158364 | solution.py:183
  153.2 4.1 collective-permute-start.1
  159.1 14.3 %collective-permute-done.1 = bf16[128,2048]{1,0:T(8,128)(2,1)S(1)} collective-permute-done((bf16[128,2048]{1,0:T(8,128)(2,1)S(1)}, bf16[128,2048]{1,0:T(8,128)(2,1)S(1)}, u32[]{:S(2)}, u32[]{:S(2)}) %collective-permute-start.1) | collective-permute-done | bytes 524320 | tf_op jit(solution)/shard_map/while/body/eval_jaxpr/ppermute | solution.py:29
  186.8 14.6 %collective-permute-done.1 = bf16[128,2048]{1,0:T(8,128)(2,1)S(1)} collective-permute-done((bf16[128,2048]{1,0:T(8,128)(2,1)S(1)}, bf16[128,2048]{1,0:T(8,128)(2,1)S(1)}, u32[]{:S(2)}, u32[]{:S(2)}) %collective-permute-start.1) | collective-permute-done | bytes 524320 | tf_op jit(solution)/shard_map/while/body/eval_jaxpr/ppermute | solution.py:29
  214.8 14.6 %collective-permute-done.1 = bf16[128,2048]{1,0:T(8,128)(2,1)S(1)} collective-permute-done((bf16[128,2048]{1,0:T(8,128)(2,1)S(1)}, bf16[128,2048]{1,0:T(8,128)(2,1)S(1)}, u32[]{:S(2)}, u32[]{:S(2)}) %collective-permute-start.1) | collective-permute-done | bytes 524320 | tf_op jit(solution)/shard_map/while/body/eval_jaxpr/ppermute | solution.py:29
  242.9 57.7 %collective-permute-done.1 = bf16[128,2048]{1,0:T(8,128)(2,1)S(1)} collective-permute-done((bf16[128,2048]{1,0:T(8,128)(2,1)S(1)}, bf16[128,2048]{1,0:T(8,128)(2,1)S(1)}, u32[]{:S(2)}, u32[]{:S(2)}) %collective-permute-start.1) | collective-permute-done | bytes 524320 | tf_op jit(solution)/shard_map/while/body/eval_jaxpr/ppermute | solution.py:29
  303.9 6.9 conditional.20
  305.0 4.0 convolution_convert_fusion
  315.9 7.8 conditional.21
  328.3 13.7 %collective-permute-done.1 = bf16[128,2048]{1,0:T(8,128)(2,1)S(1)} collective-permute-done((bf16[128,2048]{1,0:T(8,128)(2,1)S(1)}, bf16[128,2048]{1,0:T(8,128)(2,1)S(1)}, u32[]{:S(2)}, u32[]{:S(2)}) %collective-permute-start.1) | collective-permute-done | bytes 524320 | tf_op jit(solution)/shard_map/while/body/eval_jaxpr/ppermute | solution.py:29
  345.2 6.9 conditional.20
  346.4 4.0 convolution_convert_fusion
  357.2 7.8 conditional.21
  369.7 13.7 %collective-permute-done.1 = bf16[128,2048]{1,0:T(8,128)(2,1)S(1)} collective-permute-done((bf16[128,2048]{1,0:T(8,128)(2,1)S(1)}, bf16[128,2048]{1,0:T(8,128)(2,1)S(1)}, u32[]{:S(2)}, u32[]{:S(2)}) %collective-permute-start.1) | collective-permute-done | bytes 524320 | tf_op jit(solution)/shard_map/while/body/eval_jaxpr/ppermute | solution.py:29
  393.1 13.4 %collective-permute-start.1 = (bf16[128,2048]{1,0:T(8,128)(2,1)S(1)}, bf16[128,2048]{1,0:T(8,128)(2,1)S(1)}, u32[]{:S(2)}, u32[]{:S(2)}) collective-permute-start(bf16[128,2048]{1,0:T(8,128)(2,1)S(1)} %get-tuple-element.1417), channel_id=1, source_target_pairs={{0,32},{32,64},{64,96},{96,128},{128,160},{160,192},{192,224},{1,3... | collective-permute-start | bytes 1572872 | tf_op jit(solution)/shard_map/while/body/eval_jaxpr/ppermute | solution.py:29
  408.3 10.1 collective-permute-done.1
  428.0 4.4 collective-permute-start.1
  434.2 12.2 %collective-permute-done.1 = bf16[128,2048]{1,0:T(8,128)(2,1)S(1)} collective-permute-done((bf16[128,2048]{1,0:T(8,128)(2,1)S(1)}, bf16[128,2048]{1,0:T(8,128)(2,1)S(1)}, u32[]{:S(2)}, u32[]{:S(2)}) %collective-permute-start.1) | collective-permute-done | bytes 524320 | tf_op jit(solution)/shard_map/while/body/eval_jaxpr/ppermute | solution.py:29
  459.3 6.2 broadcast_in_dim.196
  465.4 4.3 broadcast_in_dim.197
  470.5 348.2 %while.46 = (s32[]{:T(128)}, bf16[128,2048]{1,0:T(8,128)(2,1)}, f32[2048,1536]{1,0:T(8,128)}, f32[1024,2048]{1,0:T(8,128)}, s32[]{:T(128)}, /*index=5*/pred[]{:T...) while((s32[]{:T(128)}, bf16[128,2048]{1,0:T(8,128)(2,1)}, ...), condition=%wide.region_25.26_spmd, body=%wide.region_14.25_spmd.sunk | while | flops 3045198336 | bytes 92394472 | solution.py:234
  478.0 24.0 %collective-permute-done.3 = bf16[128,2048]{1,0:T(8,128)(2,1)} collective-permute-done((bf16[128,2048]{1,0:T(8,128)(2,1)S(1)}, bf16[128,2048]{1,0:T(8,128)(2,1)}, u32[]{:S(2)}, u32[]{:S(2)}) %collective-permute-start.3) | collective-permute-done | bytes 524320 | tf_op jit(solution)/shard_map/while/body/eval_jaxpr/ppermute | solution.py:29
  509.3 14.8 %collective-permute-done.3 = bf16[128,2048]{1,0:T(8,128)(2,1)} collective-permute-done((bf16[128,2048]{1,0:T(8,128)(2,1)S(1)}, bf16[128,2048]{1,0:T(8,128)(2,1)}, u32[]{:S(2)}, u32[]{:S(2)}) %collective-permute-start.3) | collective-permute-done | bytes 524320 | tf_op jit(solution)/shard_map/while/body/eval_jaxpr/ppermute | solution.py:29
  533.1 87.2 %collective-permute-done.3 = bf16[128,2048]{1,0:T(8,128)(2,1)} collective-permute-done((bf16[128,2048]{1,0:T(8,128)(2,1)S(1)}, bf16[128,2048]{1,0:T(8,128)(2,1)}, u32[]{:S(2)}, u32[]{:S(2)}) %collective-permute-start.3) | collective-permute-done | bytes 524320 | tf_op jit(solution)/shard_map/while/body/eval_jaxpr/ppermute | solution.py:29
  621.7 15.6 %conditional.22 = (bf16[128,1024]{0,1:T(8,128)(2,1)}, bf16[2,128,256]{1,2,0:T(8,128)(2,1)S(1)}, bf16[2,128,256]{1,2,0:T(8,128)(2,1)}) conditional(s32[]{:T(128)} %convert_element_type.320, () %tuple.239, (bf16[128,2048]{1,0:T(8,128)(2,1)S(1)}, bf16[1024,2048]{1,0:T(8,128)(2,1)}, bf16[2,2,128,256]{2,3,1,0:T(8,128)(2,1)S(1)}, s32[]{:T(128)}, ...), branch_computations={%region_15.15_spmd, %region_16.18_spmd} | conditional | flops 887359488 | bytes 25934138 | solution.py:206
  639.7 8.2 conditional.23
  641.0 5.2 fusion.41
  649.9 19.2 %conditional.24 = ((f32[2048,1536]{1,0:T(8,128)}, f32[1024,2048]{1,0:T(8,128)})) conditional(s32[]{:T(128)} %convert_element_type.320, (f32[2048,1536]{1,0:T(8,128)}, f32[1024,2048]{1,0:T(8,128)}) %tuple.242, (bf16[2,128,2048]{2,1,0:T(8,128)(2,1)}, s32[]{:T(128)}, bf16[128,1536]{1,0:T(8,128)(2,1)S(1)}, f32[2048,1536]{1,0:T(8,128)}, ...), branch_computations={%region_23.23_spmd, %region_24.24_spmd} | conditional | flops 1347420160 | bytes 43648024 | solution.py:227
  649.9 11.2 %convolution_add_fusion.1 = f32[2048,1536]{1,0:T(8,128)} fusion(f32[2048,1536]{1,0:T(8,128)} %get-tuple-element.966, bf16[128,1536]{1,0:T(8,128)(2,1)S(1)} %get-tuple-element.969, bf16[2,128,2048]{2,1,0:T(8,128)(2,1)} %get-tuple-element.967, s32[]{:T(128)} %get-tuple-element.968), kind=kOutput, calls=%fused_computation.121 | convolution fusion | flops 808452096 | bytes 26083840 | tf_op jit(solution)/shard_map/while/body/eval_jaxpr/cond/branch_1_fun/dot_general | solution.py:220
  661.1 8.0 convolution_add_fusion.2
  670.4 15.6 %conditional.22 = (bf16[128,1024]{0,1:T(8,128)(2,1)}, bf16[2,128,256]{1,2,0:T(8,128)(2,1)S(1)}, bf16[2,128,256]{1,2,0:T(8,128)(2,1)}) conditional(s32[]{:T(128)} %convert_element_type.320, () %tuple.239, (bf16[128,2048]{1,0:T(8,128)(2,1)S(1)}, bf16[1024,2048]{1,0:T(8,128)(2,1)}, bf16[2,2,128,256]{2,3,1,0:T(8,128)(2,1)S(1)}, s32[]{:T(128)}, ...), branch_computations={%region_15.15_spmd, %region_16.18_spmd} | conditional | flops 887359488 | bytes 25934138 | solution.py:206
  688.5 8.2 conditional.23
  689.8 5.2 fusion.41
  698.6 19.2 %conditional.24 = ((f32[2048,1536]{1,0:T(8,128)}, f32[1024,2048]{1,0:T(8,128)})) conditional(s32[]{:T(128)} %convert_element_type.320, (f32[2048,1536]{1,0:T(8,128)}, f32[1024,2048]{1,0:T(8,128)}) %tuple.242, (bf16[2,128,2048]{2,1,0:T(8,128)(2,1)}, s32[]{:T(128)}, bf16[128,1536]{1,0:T(8,128)(2,1)S(1)}, f32[2048,1536]{1,0:T(8,128)}, ...), branch_computations={%region_23.23_spmd, %region_24.24_spmd} | conditional | flops 1347420160 | bytes 43648024 | solution.py:227
  698.7 11.2 %convolution_add_fusion.1 = f32[2048,1536]{1,0:T(8,128)} fusion(f32[2048,1536]{1,0:T(8,128)} %get-tuple-element.966, bf16[128,1536]{1,0:T(8,128)(2,1)S(1)} %get-tuple-element.969, bf16[2,128,2048]{2,1,0:T(8,128)(2,1)} %get-tuple-element.967, s32[]{:T(128)} %get-tuple-element.968), kind=kOutput, calls=%fused_computation.121 | convolution fusion | flops 808452096 | bytes 26083840 | tf_op jit(solution)/shard_map/while/body/eval_jaxpr/cond/branch_1_fun/dot_general | solution.py:220
  709.9 8.0 convolution_add_fusion.2
  723.2 21.4 %collective-permute-start.3 = (bf16[128,2048]{1,0:T(8,128)(2,1)S(1)}, bf16[128,2048]{1,0:T(8,128)(2,1)}, u32[]{:S(2)}, u32[]{:S(2)}) collective-permute-start(bf16[128,2048]{1,0:T(8,128)(2,1)S(1)} %get-tuple-element.1444), channel_id=1, source_target_pairs={{32,0},{64,32},{96,64},{128,96},{160,128},{192,160},{224,192},{33,... | collective-permute-start | bytes 1572872 | tf_op jit(solution)/shard_map/while/body/eval_jaxpr/ppermute | solution.py:29
  744.7 11.4 %collective-permute-done.3 = bf16[128,2048]{1,0:T(8,128)(2,1)} collective-permute-done((bf16[128,2048]{1,0:T(8,128)(2,1)S(1)}, bf16[128,2048]{1,0:T(8,128)(2,1)}, u32[]{:S(2)}, u32[]{:S(2)}) %collective-permute-start.3) | collective-permute-done | bytes 524320 | tf_op jit(solution)/shard_map/while/body/eval_jaxpr/ppermute | solution.py:29
  761.5 9.7 collective-permute-start.3
  771.2 11.4 %collective-permute-done.3 = bf16[128,2048]{1,0:T(8,128)(2,1)} collective-permute-done((bf16[128,2048]{1,0:T(8,128)(2,1)S(1)}, bf16[128,2048]{1,0:T(8,128)(2,1)}, u32[]{:S(2)}, u32[]{:S(2)}) %collective-permute-start.3) | collective-permute-done | bytes 524320 | tf_op jit(solution)/shard_map/while/body/eval_jaxpr/ppermute | solution.py:29
  788.0 19.3 %collective-permute-start.3 = (bf16[128,2048]{1,0:T(8,128)(2,1)S(1)}, bf16[128,2048]{1,0:T(8,128)(2,1)}, u32[]{:S(2)}, u32[]{:S(2)}) collective-permute-start(bf16[128,2048]{1,0:T(8,128)(2,1)S(1)} %get-tuple-element.1444), channel_id=1, source_target_pairs={{32,0},{64,32},{96,64},{128,96},{160,128},{192,160},{224,192},{33,... | collective-permute-start | bytes 1572872 | tf_op jit(solution)/shard_map/while/body/eval_jaxpr/ppermute | solution.py:29
  807.3 11.4 %collective-permute-done.3 = bf16[128,2048]{1,0:T(8,128)(2,1)} collective-permute-done((bf16[128,2048]{1,0:T(8,128)(2,1)S(1)}, bf16[128,2048]{1,0:T(8,128)(2,1)}, u32[]{:S(2)}, u32[]{:S(2)}) %collective-permute-start.3) | collective-permute-done | bytes 524320 | tf_op jit(solution)/shard_map/while/body/eval_jaxpr/ppermute | solution.py:29
  824.6 6.1 convert_element_type.231
  830.8 8.0 convert_element_type.230
  838.7 145.3 %reduce-scatter.5.cloned.1.call-done = bf16[32,2048]{1,0:T(8,128)(2,1)} async-done(((bf16[1024,2048]{1,0:T(8,128)(2,1)}), bf16[32,2048]{1,0:T(8,128)(2,1)}) %reduce-scatter.5.cloned.1.call-update) | async-done | bytes 131088 | tf_op jit(solution)/shard_map/reduce_scatter | solution.py:240
  985.6 109.7 %reduce-scatter.3.cloned.1.call-done = bf16[64,1536]{1,0:T(8,128)(2,1)} async-done(((bf16[2048,1536]{1,0:T(8,128)(2,1)}), bf16[64,1536]{1,0:T(8,128)(2,1)}) %reduce-scatter.3.cloned.1.call-update) | async-done | bytes 196624 | tf_op jit(solution)/shard_map/reduce_scatter | solution.py:237
  (464 shorter events, 263.2 us)
Async XLA Ops:
  7.2 65.3 %all-gather.5.cloned.1.call-start = ((), (), s32[]{:S(2)}) async-start(), calls=%async_computation.4 | async-start | bytes 4325376 | tf_op jit(solution)/shard_map/all_gather | solution.py:123
  7.9 131.4 %all-gather.7.cloned.1.call-start = ((), (), s32[]{:S(2)}) async-start(), calls=%async_computation.5 | async-start | bytes 6488064 | tf_op jit(solution)/shard_map/all_gather | solution.py:122
  8.6 975.4 %reduce-scatter.5.cloned.1.call-start = ((), (), s32[]{:S(2)}) async-start(), calls=%async_computation.3 | async-start | bytes 4325376 | tf_op jit(solution)/shard_map/reduce_scatter | solution.py:240
  148.1 4.3 collective-permute-start
  153.2 20.2 %collective-permute-start.1 = (bf16[128,2048]{1,0:T(8,128)(2,1)S(1)}, bf16[128,2048]{1,0:T(8,128)(2,1)S(1)}, u32[]{:S(2)}, u32[]{:S(2)}) collective-permute-start(bf16[128,2048]{1,0:T(8,128)(2,1)S(1)} %get-tuple-element.1417), channel_id=1, source_target_pairs={{0,32},{32,64},{64,96},{96,128},{128,160},{160,192},{192,224},{1,3... | collective-permute-start | bytes 1572872 | tf_op jit(solution)/shard_map/while/body/eval_jaxpr/ppermute | solution.py:29
  178.2 4.1 collective-permute-start
  183.1 18.3 %collective-permute-start.1 = (bf16[128,2048]{1,0:T(8,128)(2,1)S(1)}, bf16[128,2048]{1,0:T(8,128)(2,1)S(1)}, u32[]{:S(2)}, u32[]{:S(2)}) collective-permute-start(bf16[128,2048]{1,0:T(8,128)(2,1)S(1)} %get-tuple-element.1417), channel_id=1, source_target_pairs={{0,32},{32,64},{64,96},{96,128},{128,160},{160,192},{192,224},{1,3... | collective-permute-start | bytes 1572872 | tf_op jit(solution)/shard_map/while/body/eval_jaxpr/ppermute | solution.py:29
  206.3 4.1 collective-permute-start
  211.2 18.3 %collective-permute-start.1 = (bf16[128,2048]{1,0:T(8,128)(2,1)S(1)}, bf16[128,2048]{1,0:T(8,128)(2,1)S(1)}, u32[]{:S(2)}, u32[]{:S(2)}) collective-permute-start(bf16[128,2048]{1,0:T(8,128)(2,1)S(1)} %get-tuple-element.1417), channel_id=1, source_target_pairs={{0,32},{32,64},{64,96},{96,128},{128,160},{160,192},{192,224},{1,3... | collective-permute-start | bytes 1572872 | tf_op jit(solution)/shard_map/while/body/eval_jaxpr/ppermute | solution.py:29
  234.3 4.1 collective-permute-start
  239.2 61.4 %collective-permute-start.1 = (bf16[128,2048]{1,0:T(8,128)(2,1)S(1)}, bf16[128,2048]{1,0:T(8,128)(2,1)S(1)}, u32[]{:S(2)}, u32[]{:S(2)}) collective-permute-start(bf16[128,2048]{1,0:T(8,128)(2,1)S(1)} %get-tuple-element.1417), channel_id=1, source_target_pairs={{0,32},{32,64},{64,96},{96,128},{128,160},{160,192},{192,224},{1,3... | collective-permute-start | bytes 1572872 | tf_op jit(solution)/shard_map/while/body/eval_jaxpr/ppermute | solution.py:29
  310.8 5.1 collective-permute-start
  323.7 18.3 %collective-permute-start.1 = (bf16[128,2048]{1,0:T(8,128)(2,1)S(1)}, bf16[128,2048]{1,0:T(8,128)(2,1)S(1)}, u32[]{:S(2)}, u32[]{:S(2)}) collective-permute-start(bf16[128,2048]{1,0:T(8,128)(2,1)S(1)} %get-tuple-element.1417), channel_id=1, source_target_pairs={{0,32},{32,64},{64,96},{96,128},{128,160},{160,192},{192,224},{1,3... | collective-permute-start | bytes 1572872 | tf_op jit(solution)/shard_map/while/body/eval_jaxpr/ppermute | solution.py:29
  352.1 5.1 collective-permute-start
  365.0 18.3 %collective-permute-start.1 = (bf16[128,2048]{1,0:T(8,128)(2,1)S(1)}, bf16[128,2048]{1,0:T(8,128)(2,1)S(1)}, u32[]{:S(2)}, u32[]{:S(2)}) collective-permute-start(bf16[128,2048]{1,0:T(8,128)(2,1)S(1)} %get-tuple-element.1417), channel_id=1, source_target_pairs={{0,32},{32,64},{64,96},{96,128},{128,160},{160,192},{192,224},{1,3... | collective-permute-start | bytes 1572872 | tf_op jit(solution)/shard_map/while/body/eval_jaxpr/ppermute | solution.py:29
  388.2 4.1 collective-permute-start
  393.1 25.2 %collective-permute-start.1 = (bf16[128,2048]{1,0:T(8,128)(2,1)S(1)}, bf16[128,2048]{1,0:T(8,128)(2,1)S(1)}, u32[]{:S(2)}, u32[]{:S(2)}) collective-permute-start(bf16[128,2048]{1,0:T(8,128)(2,1)S(1)} %get-tuple-element.1417), channel_id=1, source_target_pairs={{0,32},{32,64},{64,96},{96,128},{128,160},{160,192},{192,224},{1,3... | collective-permute-start | bytes 1572872 | tf_op jit(solution)/shard_map/while/body/eval_jaxpr/ppermute | solution.py:29
  423.2 4.1 collective-permute-start
  428.0 18.3 %collective-permute-start.1 = (bf16[128,2048]{1,0:T(8,128)(2,1)S(1)}, bf16[128,2048]{1,0:T(8,128)(2,1)S(1)}, u32[]{:S(2)}, u32[]{:S(2)}) collective-permute-start(bf16[128,2048]{1,0:T(8,128)(2,1)S(1)} %get-tuple-element.1417), channel_id=1, source_target_pairs={{0,32},{32,64},{64,96},{96,128},{128,160},{160,192},{192,224},{1,3... | collective-permute-start | bytes 1572872 | tf_op jit(solution)/shard_map/while/body/eval_jaxpr/ppermute | solution.py:29
  451.2 6.4 collective-permute-start.4
  474.4 1.6 collective-permute-start.2
  476.0 26.0 %collective-permute-start.3 = (bf16[128,2048]{1,0:T(8,128)(2,1)S(1)}, bf16[128,2048]{1,0:T(8,128)(2,1)}, u32[]{:S(2)}, u32[]{:S(2)}) collective-permute-start(bf16[128,2048]{1,0:T(8,128)(2,1)S(1)} %get-tuple-element.1444), channel_id=1, source_target_pairs={{32,0},{64,32},{96,64},{128,96},{160,128},{192,160},{224,192},{33,... | collective-permute-start | bytes 1572872 | tf_op jit(solution)/shard_map/while/body/eval_jaxpr/ppermute | solution.py:29
  478.0 24.0 %copy-start.4 = (bf16[2,2,128,256]{2,3,1,0:T(8,128)(2,1)S(1)}, bf16[2,2,128,256]{2,3,1,0:T(8,128)(2,1)}, u32[]{:S(2)}) copy-start(bf16[2,2,128,256]{2,3,1,0:T(8,128)(2,1)} %copy-done.3) | copy-start | bytes 786436 | tf_op jit(solution)/shard_map/while
  505.8 1.4 collective-permute-start.2
  507.4 16.7 %collective-permute-start.3 = (bf16[128,2048]{1,0:T(8,128)(2,1)S(1)}, bf16[128,2048]{1,0:T(8,128)(2,1)}, u32[]{:S(2)}, u32[]{:S(2)}) collective-permute-start(bf16[128,2048]{1,0:T(8,128)(2,1)S(1)} %get-tuple-element.1444), channel_id=1, source_target_pairs={{32,0},{64,32},{96,64},{128,96},{160,128},{192,160},{224,192},{33,... | collective-permute-start | bytes 1572872 | tf_op jit(solution)/shard_map/while/body/eval_jaxpr/ppermute | solution.py:29
  509.3 14.8 %copy-start.4 = (bf16[2,2,128,256]{2,3,1,0:T(8,128)(2,1)S(1)}, bf16[2,2,128,256]{2,3,1,0:T(8,128)(2,1)}, u32[]{:S(2)}) copy-start(bf16[2,2,128,256]{2,3,1,0:T(8,128)(2,1)} %copy-done.3) | copy-start | bytes 786436 | tf_op jit(solution)/shard_map/while
  527.9 1.4 collective-permute-start.2
  529.5 90.8 %collective-permute-start.3 = (bf16[128,2048]{1,0:T(8,128)(2,1)S(1)}, bf16[128,2048]{1,0:T(8,128)(2,1)}, u32[]{:S(2)}, u32[]{:S(2)}) collective-permute-start(bf16[128,2048]{1,0:T(8,128)(2,1)S(1)} %get-tuple-element.1444), channel_id=1, source_target_pairs={{32,0},{64,32},{96,64},{128,96},{160,128},{192,160},{224,192},{33,... | collective-permute-start | bytes 1572872 | tf_op jit(solution)/shard_map/while/body/eval_jaxpr/ppermute | solution.py:29
  533.0 87.2 %copy-start.4 = (bf16[2,2,128,256]{2,3,1,0:T(8,128)(2,1)S(1)}, bf16[2,2,128,256]{2,3,1,0:T(8,128)(2,1)}, u32[]{:S(2)}) copy-start(bf16[2,2,128,256]{2,3,1,0:T(8,128)(2,1)} %copy-done.3) | copy-start | bytes 786436 | tf_op jit(solution)/shard_map/while
  638.3 1.4 collective-permute-start.2
  641.0 5.3 copy-start.1
  647.9 21.2 %collective-permute-start.3 = (bf16[128,2048]{1,0:T(8,128)(2,1)S(1)}, bf16[128,2048]{1,0:T(8,128)(2,1)}, u32[]{:S(2)}, u32[]{:S(2)}) collective-permute-start(bf16[128,2048]{1,0:T(8,128)(2,1)S(1)} %get-tuple-element.1444), channel_id=1, source_target_pairs={{32,0},{64,32},{96,64},{128,96},{160,128},{192,160},{224,192},{33,... | collective-permute-start | bytes 1572872 | tf_op jit(solution)/shard_map/while/body/eval_jaxpr/ppermute | solution.py:29
  649.8 19.2 %copy-start.4 = (bf16[2,2,128,256]{2,3,1,0:T(8,128)(2,1)S(1)}, bf16[2,2,128,256]{2,3,1,0:T(8,128)(2,1)}, u32[]{:S(2)}) copy-start(bf16[2,2,128,256]{2,3,1,0:T(8,128)(2,1)} %copy-done.3) | copy-start | bytes 786436 | tf_op jit(solution)/shard_map/while
  687.1 1.4 collective-permute-start.2
  689.8 5.3 copy-start.1
  696.7 21.1 %collective-permute-start.3 = (bf16[128,2048]{1,0:T(8,128)(2,1)S(1)}, bf16[128,2048]{1,0:T(8,128)(2,1)}, u32[]{:S(2)}, u32[]{:S(2)}) collective-permute-start(bf16[128,2048]{1,0:T(8,128)(2,1)S(1)} %get-tuple-element.1444), channel_id=1, source_target_pairs={{32,0},{64,32},{96,64},{128,96},{160,128},{192,160},{224,192},{33,... | collective-permute-start | bytes 1572872 | tf_op jit(solution)/shard_map/while/body/eval_jaxpr/ppermute | solution.py:29
  698.6 19.2 %copy-start.4 = (bf16[2,2,128,256]{2,3,1,0:T(8,128)(2,1)S(1)}, bf16[2,2,128,256]{2,3,1,0:T(8,128)(2,1)}, u32[]{:S(2)}) copy-start(bf16[2,2,128,256]{2,3,1,0:T(8,128)(2,1)} %copy-done.3) | copy-start | bytes 786436 | tf_op jit(solution)/shard_map/while
  721.7 1.4 collective-permute-start.2
  723.2 32.9 %collective-permute-start.3 = (bf16[128,2048]{1,0:T(8,128)(2,1)S(1)}, bf16[128,2048]{1,0:T(8,128)(2,1)}, u32[]{:S(2)}, u32[]{:S(2)}) collective-permute-start(bf16[128,2048]{1,0:T(8,128)(2,1)S(1)} %get-tuple-element.1444), channel_id=1, source_target_pairs={{32,0},{64,32},{96,64},{128,96},{160,128},{192,160},{224,192},{33,... | collective-permute-start | bytes 1572872 | tf_op jit(solution)/shard_map/while/body/eval_jaxpr/ppermute | solution.py:29
  744.6 11.5 %copy-start.4 = (bf16[2,2,128,256]{2,3,1,0:T(8,128)(2,1)S(1)}, bf16[2,2,128,256]{2,3,1,0:T(8,128)(2,1)}, u32[]{:S(2)}) copy-start(bf16[2,2,128,256]{2,3,1,0:T(8,128)(2,1)} %copy-done.3) | copy-start | bytes 786436 | tf_op jit(solution)/shard_map/while
  759.9 1.4 collective-permute-start.2
  761.5 21.1 %collective-permute-start.3 = (bf16[128,2048]{1,0:T(8,128)(2,1)S(1)}, bf16[128,2048]{1,0:T(8,128)(2,1)}, u32[]{:S(2)}, u32[]{:S(2)}) collective-permute-start(bf16[128,2048]{1,0:T(8,128)(2,1)S(1)} %get-tuple-element.1444), channel_id=1, source_target_pairs={{32,0},{64,32},{96,64},{128,96},{160,128},{192,160},{224,192},{33,... | collective-permute-start | bytes 1572872 | tf_op jit(solution)/shard_map/while/body/eval_jaxpr/ppermute | solution.py:29
  771.1 11.5 %copy-start.4 = (bf16[2,2,128,256]{2,3,1,0:T(8,128)(2,1)S(1)}, bf16[2,2,128,256]{2,3,1,0:T(8,128)(2,1)}, u32[]{:S(2)}) copy-start(bf16[2,2,128,256]{2,3,1,0:T(8,128)(2,1)} %copy-done.3) | copy-start | bytes 786436 | tf_op jit(solution)/shard_map/while
  786.4 1.4 collective-permute-start.2
  788.0 30.8 %collective-permute-start.3 = (bf16[128,2048]{1,0:T(8,128)(2,1)S(1)}, bf16[128,2048]{1,0:T(8,128)(2,1)}, u32[]{:S(2)}, u32[]{:S(2)}) collective-permute-start(bf16[128,2048]{1,0:T(8,128)(2,1)S(1)} %get-tuple-element.1444), channel_id=1, source_target_pairs={{32,0},{64,32},{96,64},{128,96},{160,128},{192,160},{224,192},{33,... | collective-permute-start | bytes 1572872 | tf_op jit(solution)/shard_map/while/body/eval_jaxpr/ppermute | solution.py:29
  807.3 11.5 %copy-start.4 = (bf16[2,2,128,256]{2,3,1,0:T(8,128)(2,1)S(1)}, bf16[2,2,128,256]{2,3,1,0:T(8,128)(2,1)}, u32[]{:S(2)}) copy-start(bf16[2,2,128,256]{2,3,1,0:T(8,128)(2,1)} %copy-done.3) | copy-start | bytes 786436 | tf_op jit(solution)/shard_map/while
  823.1 1.4 collective-permute-start.5
  830.7 264.7 %reduce-scatter.3.cloned.1.call-start = ((), (), s32[]{:S(2)}) async-start(), calls=%async_computation.2 | async-start | bytes 6488064 | tf_op jit(solution)/shard_map/reduce_scatter | solution.py:237
  (29 other events, 67.5 us)
Sparse Core Ops, SparseCore 0:
  10.6 61.8 all-gather.4
  75.0 64.1 all-gather.6
  830.8 153.1 reduce-scatter.4
  988.4 106.8 reduce-scatter.2
where the time goes:
time: 1110 us; the launch traced here: 1100 us
  waiting for transfers between devices  708 us (64%)
  local copies, waits for them, and re-layouts  104 us (9%)
  other arithmetic  97 us (9%)
  starting transfers between devices  95.9 us (9%)
  matrix products  79.5 us (7%)
  between operations  13.9 us (1%)
    ppermute x16, waiting for transfers between devices, from_behind(): lax.ppermute(value, axis, [(source, source + steps) for source in range(l...  311 us
    reduce_scatter x1, waiting for transfers between devices, on_device(): lax.psum_scatter(ledger[1].astype(jnp.bfloat16), 'dp', scatter_dimension=...  145 us
    reduce_scatter x1, waiting for transfers between devices, on_device(): lax.psum_scatter(ledger[0].astype(jnp.bfloat16), 'dp', scatter_dimension=...  110 us
    ppermute x16, starting transfers between devices, from_behind(): lax.ppermute(value, axis, [(source, source + steps) for source in range(l...  93.1 us
    all_gather x1, waiting for transfers between devices, on_device(): lax.all_gather(w_qkv[0], 'dp', axis=0, tiled=True)  66.8 us
    all_gather x1, waiting for transfers between devices, on_device(): lax.all_gather(w_out[0], 'dp', axis=0, tiled=True)  62.3 us
    dynamic_update_slice x53, other arithmetic, keep_slot(): lax.dynamic_update_index_in_dim(store, jnp.where(active, value, current),...  54.4 us
    dynamic_slice x39, local copies, waits for them, and re-layouts, keep_slot(): current = lax.dynamic_index_in_dim(store, slot_index, 0, keepdims=False)  29.4 us
  transfers between devices with their start and end apart: 38, of which 27 were waited for; matrix products, arithmetic and copies ran while one was open for 10% of the time, Pallas kernels for 0%

commit v1 on v0

v1 whole, which is shorter than its diff:
```python
import functools
import math

import jax
import jax.numpy as jnp
import numpy as np
from jax import lax
from jax.experimental import pallas as pl
from jax.experimental.pallas import tpu as pltpu
from jax.sharding import PartitionSpec as P

HEADS = 16
HEAD = 64
KVH = 4
GROUP = HEADS // KVH
ROWS = 256
HALF = 128
D = 2048
HQ = HEADS * HEAD
KV = KVH * HEAD
WCOLS = HQ + 2 * KV
CHUNK = 256
EPS = 1e-5
SCALE = 1.0 / math.sqrt(HEAD)
TO_EXP2 = SCALE * math.log2(math.e)
NT = (((1,), (1,)), ((), ()))
VMEM_LIMIT = 48 * 1024 * 1024
ANY = pl.BlockSpec(memory_space=pl.ANY)
SMEM = pl.BlockSpec(memory_space=pltpu.SMEM)


def dot_nt(left, right):
    return lax.dot_general(left, right, NT, preferred_element_type=jnp.float32)


def dot_nn(left, right):
    return jnp.dot(left, right, preferred_element_type=jnp.float32)


def cols(start, size):
    return pl.ds(pl.multiple_of(start, size), size)


def bias_matrix(joined):
    row = lax.broadcasted_iota(jnp.int32, (ROWS, ROWS), 0)
    col = lax.broadcasted_iota(jnp.int32, (ROWS, ROWS), 1)
    same = (row >= HALF) == (col >= HALF)
    return jnp.where(jnp.logical_or(same, joined > 0), 0.0, -1e30).astype(jnp.float32)


def probs_t(keys, query, bias):
    logits = dot_nt(keys, query) * TO_EXP2 + bias
    total = jnp.sum(jnp.exp2(logits), axis=0, keepdims=True)
    return jnp.exp2(logits - jnp.log2(total))


def forward_kernel(
    final, info, h_in, wq_in, wo_in, a0, a1, a2, a3,
    h_out, normed_out, proj_out, ctx_out, keep_out,
    h_v, normed_v, wq_v, wo_v, proj_v, ctx_v, out_v, bias_v, key_s, vt_s, in_sem, q_sem, o_sem, w_sem,
):
    del a0, a1, a2, a3

    @pl.when(info[0] == 1)
    def _():
        h_copy = pltpu.make_async_copy(h_in, h_v, in_sem)
        h_copy.start()

        def q_copy(i):
            c = cols(i * CHUNK, CHUNK)
            return pltpu.make_async_copy(wq_in.at[:, c], wq_v.at[:, c], q_sem.at[i])

        def o_copy(i):
            c = cols(i * CHUNK, CHUNK)
            return pltpu.make_async_copy(wo_in.at[:, c], wo_v.at[:, c], o_sem.at[i])

        for i in (4, 5, 0, 1, 2, 3):
            q_copy(i).start()
        if not final:
            for i in range(8):
                o_copy(i).start()
        bias_v[...] = bias_matrix(info[1])
        h_copy.wait()
        keep = pltpu.make_async_copy(h_v, keep_out, w_sem.at[0])
        keep.start()
        wide = h_v[...].astype(jnp.float32)
        scale = lax.rsqrt(jnp.mean(wide * wide, axis=-1, keepdims=True) + EPS)
        normed_v[...] = (wide * scale).astype(jnp.bfloat16)
        normed_copy = pltpu.make_async_copy(normed_v, normed_out, w_sem.at[1])
        normed_copy.start()
        q_copy(4).wait()
        q_copy(5).wait()
        keys = dot_nn(normed_v[...], wq_v[:, HQ : HQ + KV]).astype(jnp.bfloat16)
        proj_v[:, HQ : HQ + KV] = keys
        values = dot_nn(normed_v[...], wq_v[:, HQ + KV :])
        proj_v[:, HQ + KV :] = values.astype(jnp.bfloat16)
        values_t = values.T.astype(jnp.bfloat16)
        for g in range(KVH):
            key_s[g] = keys[:, g * HEAD : (g + 1) * HEAD]
            vt_s[g] = values_t[g * HEAD : (g + 1) * HEAD, :]

        def group(g, carry):
            c = cols(g * CHUNK, CHUNK)
            q_copy(g).wait()
            queries = dot_nn(normed_v[...], wq_v[:, c]).astype(jnp.bfloat16)
            proj_v[:, c] = queries
            pieces = []
            for i in range(GROUP):
                part = queries[:, i * HEAD : (i + 1) * HEAD]
                weights = probs_t(key_s[g], part, bias_v[...]).astype(jnp.bfloat16)
                pieces.append(dot_nn(vt_s[g], weights))
            ctx_v[:, c] = jnp.concatenate(pieces, axis=0).T.astype(jnp.bfloat16)
            return carry

        lax.fori_loop(0, KVH, group, 0)
        proj_copy = pltpu.make_async_copy(proj_v, proj_out, w_sem.at[2])
        proj_copy.start()
        ctx_copy = pltpu.make_async_copy(ctx_v, ctx_out, w_sem.at[3])
        ctx_copy.start()

        def finish(i, carry):
            c = cols(i * CHUNK, CHUNK)
            o_copy(i).wait()
            out = h_v[:, c].astype(jnp.float32) + dot_nn(ctx_v[...], wo_v[:, c])
            out_v[:, c] = out.astype(jnp.bfloat16)
            return carry

        if not final:
            lax.fori_loop(0, 8, finish, 0)
            out_copy = pltpu.make_async_copy(out_v, h_out, w_sem.at[4])
            out_copy.start()
            out_copy.wait()
        keep.wait()
        normed_copy.wait()
        proj_copy.wait()
        ctx_copy.wait()


def bf16(*shape):
    return jax.ShapeDtypeStruct(shape, jnp.bfloat16)


def v16(*shape):
    return pltpu.VMEM(shape, jnp.bfloat16)


def v32(*shape):
    return pltpu.VMEM(shape, jnp.float32)


def forward_layer(final, info, hidden, w_qkv, w_out, normed, proj, ctx, kept):
    return pl.pallas_call(
        functools.partial(forward_kernel, final),
        out_shape=(bf16(ROWS, D), bf16(ROWS, D), bf16(ROWS, WCOLS), bf16(ROWS, HQ), bf16(ROWS, D)),
        in_specs=[SMEM] + [ANY] * 7,
        out_specs=(ANY,) * 5,
        input_output_aliases={4: 1, 5: 2, 6: 3, 7: 4},
        scratch_shapes=[
            v16(ROWS, D), v16(ROWS, D), v16(D, WCOLS), v16(HQ, D), v16(ROWS, WCOLS), v16(ROWS, HQ), v16(ROWS, D),
            v32(ROWS, ROWS), v16(KVH, ROWS, HEAD), v16(KVH, HEAD, ROWS),
            pltpu.SemaphoreType.DMA, pltpu.SemaphoreType.DMA((6,)), pltpu.SemaphoreType.DMA((8,)),
            pltpu.SemaphoreType.DMA((5,)),
        ],
        compiler_params=pltpu.CompilerParams(vmem_limit_bytes=VMEM_LIMIT),
        cost_estimate=pl.CostEstimate(flops=3_000_000_000, bytes_accessed=14_000_000, transcendentals=2_000_000),
        name="forward_last" if final else "forward_layer",
    )(info, hidden, w_qkv, w_out, normed, proj, ctx, kept)


def backward_kernel(
    last, info, u_in, h_in, proj_in, wq_in, wo_in, a0, a1,
    up_out, dproj_out, keep_out,
    u_v, h_v, proj_v, wq_v, wo_v, dproj_v, dn_v, bias_v, key_s, kt_s, value_s, dk_s, dv_s,
    in_sem, q_sem, o_sem, w_sem,
):
    del a0, a1

    @pl.when(info[0] == 1)
    def _():
        u_copy = pltpu.make_async_copy(u_in, u_v, in_sem.at[0])
        u_copy.start()
        proj_copy = pltpu.make_async_copy(proj_in, proj_v, in_sem.at[1])
        h_copy = pltpu.make_async_copy(h_in, h_v, in_sem.at[2])

        def o_copy(i):
            r = cols(i * CHUNK, CHUNK)
            return pltpu.make_async_copy(wo_in.at[r, :], wo_v.at[r, :], o_sem.at[i])

        def q_copy(i):
            r = cols(i * CHUNK, CHUNK)
            return pltpu.make_async_copy(wq_in.at[r, :], wq_v.at[r, :], q_sem.at[i])

        o_copy(0).start()
        proj_copy.start()
        for i in range(1, 4):
            o_copy(i).start()
        if not last:
            h_copy.start()
            for i in range(8):
                q_copy(i).start()
        bias_v[...] = bias_matrix(info[1])
        proj_copy.wait()
        keys_t = proj_v[:, HQ : HQ + KV].astype(jnp.float32).T.astype(jnp.bfloat16)
        for g in range(KVH):
            key_s[g] = proj_v[:, HQ + g * HEAD : HQ + (g + 1) * HEAD]
            value_s[g] = proj_v[:, HQ + KV + g * HEAD : HQ + KV + (g + 1) * HEAD]
            kt_s[g] = keys_t[g * HEAD : (g + 1) * HEAD, :]
        u_copy.wait()
        keep = pltpu.make_async_copy(u_v, keep_out, w_sem.at[0])
        keep.start()

        def group(g, carry):
            c = cols(g * CHUNK, CHUNK)
            o_copy(g).wait()
            d_ctx = dot_nt(u_v[...], wo_v[c, :]).astype(jnp.bfloat16)
            queries = proj_v[:, c]
            pieces = []
            d_key = jnp.zeros((ROWS, HEAD), jnp.float32)
            d_value = jnp.zeros((ROWS, HEAD), jnp.float32)
            for i in range(GROUP):
                part = queries[:, i * HEAD : (i + 1) * HEAD]
                d_part = d_ctx[:, i * HEAD : (i + 1) * HEAD]
                weights = probs_t(key_s[g], part, bias_v[...])
                d_weights = dot_nt(value_s[g], d_part)
                inner = jnp.sum(d_weights * weights, axis=0, keepdims=True)
                d_scores = (weights * (d_weights - inner) * SCALE).astype(jnp.bfloat16)
                pieces.append(dot_nn(kt_s[g], d_scores))
                d_key += dot_nn(d_scores, part)
                d_value += dot_nn(weights.astype(jnp.bfloat16), d_part)
            dproj_v[:, c] = jnp.concatenate(pieces, axis=0).T.astype(jnp.bfloat16)
            dk_s[g] = d_key.astype(jnp.bfloat16)
            dv_s[g] = d_value.astype(jnp.bfloat16)
            return carry

        lax.fori_loop(0, KVH, group, 0)
        dproj_v[:, HQ : HQ + KV] = jnp.concatenate([dk_s[g] for g in range(KVH)], axis=1)
        dproj_v[:, HQ + KV :] = jnp.concatenate([dv_s[g] for g in range(KVH)], axis=1)
        dproj_copy = pltpu.make_async_copy(dproj_v, dproj_out, w_sem.at[1])
        dproj_copy.start()
        if not last:
            h_copy.wait()

            def widen(i, partial):
                c = cols(i * CHUNK, CHUNK)
                q_copy(i).wait()
                d_normed = dot_nt(dproj_v[...], wq_v[c, :])
                dn_v[:, c] = d_normed
                product = d_normed * h_v[:, c].astype(jnp.float32)
                return partial + product[:, :HALF] + product[:, HALF:]

            partial = lax.fori_loop(0, 8, widen, jnp.zeros((ROWS, HALF), jnp.float32))
            mean = jnp.sum(partial, axis=-1, keepdims=True) * (1.0 / D)
            wide = h_v[...].astype(jnp.float32)
            scale = lax.rsqrt(jnp.mean(wide * wide, axis=-1, keepdims=True) + EPS)
            pull = scale * scale * scale * mean

            def previous(i, carry):
                c = cols(i * CHUNK, CHUNK)
                out = u_v[:, c].astype(jnp.float32) + (scale * dn_v[:, c] - h_v[:, c].astype(jnp.float32) * pull)
                h_v[:, c] = out.astype(jnp.bfloat16)
                return carry

            lax.fori_loop(0, 8, previous, 0)
            up_copy = pltpu.make_async_copy(h_v, up_out, w_sem.at[2])
            up_copy.start()
            up_copy.wait()
        keep.wait()
        dproj_copy.wait()


def backward_layer(last, info, upstream, kept, proj, w_qkv, w_out, dproj, ups):
    return pl.pallas_call(
        functools.partial(backward_kernel, last),
        out_shape=(bf16(ROWS, D), bf16(ROWS, WCOLS), bf16(ROWS, D)),
        in_specs=[SMEM] + [ANY] * 7,
        out_specs=(ANY,) * 3,
        input_output_aliases={6: 1, 7: 2},
        scratch_shapes=[
            v16(ROWS, D), v16(ROWS, D), v16(ROWS, WCOLS), v16(D, WCOLS), v16(HQ, D), v16(ROWS, WCOLS), v32(ROWS, D),
            v32(ROWS, ROWS), v16(KVH, ROWS, HEAD), v16(KVH, HEAD, ROWS), v16(KVH, ROWS, HEAD),
            v16(KVH, ROWS, HEAD), v16(KVH, ROWS, HEAD),
            pltpu.SemaphoreType.DMA((3,)), pltpu.SemaphoreType.DMA((8,)), pltpu.SemaphoreType.DMA((4,)),
            pltpu.SemaphoreType.DMA((3,)),
        ],
        compiler_params=pltpu.CompilerParams(vmem_limit_bytes=VMEM_LIMIT),
        cost_estimate=pl.CostEstimate(flops=4_000_000_000, bytes_accessed=15_000_000, transcendentals=2_000_000),
        name="backward_last" if last else "backward_layer",
    )(info, upstream, kept, proj, w_qkv, w_out, dproj, ups)


LAYERS = 8
FINE = (("zlo", 2), ("y", 4), ("x", 4), ("zhi", 4), ("core", 2))
NAMES = tuple(name for name, size in FINE)
SIZES = tuple(size for name, size in FINE)
RING = ("x", "zhi", "zlo")
STAGE = ("y", "core")


def regroup(back):
    pairs = []
    for zlo, y, x, zhi, core in np.ndindex(*SIZES):
        source = np.ravel_multi_index((zlo, y, x, zhi, core), SIZES)
        target = np.ravel_multi_index((core, zlo * 2 + y // 2, x, zhi, y % 2), SIZES)
        pairs.append((int(target), int(source)) if back else (int(source), int(target)))
    return pairs


def on_device(inputs, cotangent, joined, w_qkv, w_out):
    micro = lax.axis_index("zlo")
    stage = 2 * lax.axis_index("y") + lax.axis_index("core")
    bin_index = 4 * lax.axis_index("x") + lax.axis_index("zhi")
    flag = joined[micro, bin_index]
    near, far = w_qkv[0], w_out[0]
    near = lax.ppermute(near, NAMES, regroup(False))
    far = lax.ppermute(far, NAMES, regroup(False))
    full_qkv = lax.all_gather(near, RING, axis=0, tiled=True)
    full_out = lax.all_gather(far, RING, axis=0, tiled=True)
    block = lax.dynamic_index_in_dim(inputs, micro, 0, keepdims=False)
    hidden = jnp.concatenate([block, lax.ppermute(block, "core", [(1, 0)])])
    block = lax.dynamic_index_in_dim(cotangent, micro, 0, keepdims=False)
    upstream = jnp.concatenate([lax.ppermute(block, "core", [(0, 1)]), block])

    def info(layer):
        return jnp.stack([(stage == layer).astype(jnp.int32), flag])

    normed = jnp.zeros((ROWS, D), jnp.bfloat16)
    kept = jnp.zeros((ROWS, D), jnp.bfloat16)
    proj = jnp.zeros((ROWS, WCOLS), jnp.bfloat16)
    ctx = jnp.zeros((ROWS, HQ), jnp.bfloat16)
    for layer in range(LAYERS):
        final = layer == LAYERS - 1
        result, normed, proj, ctx, kept = forward_layer(
            final, info(layer), hidden, full_qkv, full_out, normed, proj, ctx, kept
        )
        if not final:
            hidden = lax.ppermute(result, STAGE, [(layer, layer + 1)])
    dproj = jnp.zeros((ROWS, WCOLS), jnp.bfloat16)
    ups = jnp.zeros((ROWS, D), jnp.bfloat16)
    for layer in reversed(range(LAYERS)):
        result, dproj, ups = backward_layer(
            layer == 0, info(layer), upstream, kept, proj, full_qkv, full_out, dproj, ups
        )
        if layer:
            upstream = lax.ppermute(result, STAGE, [(layer, layer - 1)])
    contract = (((0,), (0,)), ((), ()))
    part_out = lax.dot_general(ctx, ups, contract, preferred_element_type=jnp.float32).astype(jnp.bfloat16)
    part_qkv = lax.dot_general(normed, dproj, contract, preferred_element_type=jnp.float32).astype(jnp.bfloat16)
    grad_out = lax.psum_scatter(part_out, RING, scatter_dimension=0, tiled=True)
    grad_qkv = lax.psum_scatter(part_qkv, RING, scatter_dimension=0, tiled=True)
    grad_out = lax.ppermute(grad_out, NAMES, regroup(True)).astype(jnp.float32)
    grad_qkv = lax.ppermute(grad_qkv, NAMES, regroup(True)).astype(jnp.float32)
    return (grad_qkv[None], grad_out[None])


def solution(mesh):
    fine = jax.sharding.Mesh(mesh.devices.reshape(SIZES), NAMES)
    token = P(None, ("x", "zhi", "core"), None)
    weight = P(("zlo", "y"), ("x", "zhi", "core"), None)
    return jax.shard_map(
        on_device,
        mesh=fine,
        in_specs=(token, token, P(), weight, weight),
        out_specs=(weight, weight),
        check_vma=False,
    )
```

time: 1110 us -> 1070 us (0.964)
  waiting for transfers between devices: 708 us -> 898 us
  other arithmetic: 97 us -> 8.96 us
  local copies, waits for them, and re-layouts: 104 us -> 22.4 us
  matrix products: 79.5 us -> 7.89 us
  Pallas kernels: 0 us -> 38.3 us
  starting transfers between devices: 95.9 us -> 68.4 us
    reduce_scatter x2, waiting for transfers between devices: 255 us -> 436 us  [the longest x1 225 us: on_device(): grad_qkv = lax.psum_scatter(part_qkv, RING, scatter_dimension=0, tiled=True)]
    dot_general x26 -> x2, matrix products: 79.5 us -> 7.89 us  [the longest x1 4.48 us: on_device(): lax.dot_general(normed, dproj, contract, preferred_element_type=jnp.float32)]
    dynamic_update_slice x53 -> x0, other arithmetic: 54.4 us -> none  [keep_slot(): lax.dynamic_update_index_in_dim(store, jnp.where(active, value, current),...]
    broadcast_in_dim x80 -> x1, local copies, waits for them, and re-layouts: 38.4 us -> 0.05 us  [on_device(): ctx = jnp.zeros((ROWS, HQ), jnp.bfloat16)]
    pallas_call x0 -> x16, Pallas kernels: none -> 38.3 us  [the longest x8 20.7 us: forward_layer(): pl.pallas_call(functools.partial(forward_kernel, final), out_shape=(bf16(...]
    dynamic_slice x46 -> x1, local copies, waits for them, and re-layouts: 37.8 us -> 1.24 us  [on_device(): flag = joined[micro, bin_index]]
    all_gather x2, waiting for transfers between devices: 129 us -> 159 us  [the longest x1 88.5 us: on_device(): full_qkv = lax.all_gather(near, RING, axis=0, tiled=True)]
    ppermute x34 -> x20, starting transfers between devices: 95.8 us -> 68.2 us  [the longest x1 31 us: on_device(): upstream = jnp.concatenate([lax.ppermute(block, 'core', [(0, 1)]), block])]
  transfers between devices with their start and end apart: 38 -> 24, of which waited for: 27 -> 11; matrix products, arithmetic and copies ran while one was open for 10% -> 1% of each run, Pallas kernels for 0% -> 0%
where the time goes in v1:
time: 1070 us; the launch traced here: 1060 us
  waiting for transfers between devices  898 us (84%)
  starting transfers between devices  68.4 us (6%)
  Pallas kernels  38.3 us (4%)
  local copies, waits for them, and re-layouts  22.4 us (2%)
  between operations  14.7 us (1%)
    ppermute x7, waiting for transfers between devices, on_device(): upstream = lax.ppermute(result, STAGE, [(layer, layer - 1)])  285 us
    reduce_scatter x1, waiting for transfers between devices, on_device(): grad_qkv = lax.psum_scatter(part_qkv, RING, scatter_dimension=0, tiled=True)  225 us
    reduce_scatter x1, waiting for transfers between devices, on_device(): grad_out = lax.psum_scatter(part_out, RING, scatter_dimension=0, tiled=True)  211 us
    all_gather x1, waiting for transfers between devices, on_device(): full_qkv = lax.all_gather(near, RING, axis=0, tiled=True)  88.5 us
    all_gather x1, waiting for transfers between devices, on_device(): full_out = lax.all_gather(far, RING, axis=0, tiled=True)  70.8 us
    ppermute x1, starting transfers between devices, on_device(): upstream = jnp.concatenate([lax.ppermute(block, 'core', [(0, 1)]), block])  31 us
  transfers between devices with their start and end apart: 24, of which 11 were waited for; matrix products, arithmetic and copies ran while one was open for 1% of the time, Pallas kernels for 0%

profile of v1, /device:TPU:32, one launch (start us, length us, event | category | flops | bytes accessed | tf_op | source)
XLA Modules:
  0.0 1058.8 jit_solution(8964904928872649839)
XLA Ops:
  7.2 4.8 collective-permute-start.2
  12.0 2.8 collective-permute-done.2
  15.6 6.7 collective-permute-start.1
  22.2 3.5 collective-permute-done.1
  26.5 1.3 collective-permute-start
  27.8 1.2 dynamic_slice.10
  30.3 1.0 pad_maximum_fusion.h_in
  31.4 70.8 %all-gather.5.cloned.1.call-done.wo_in = bf16[1024,2048]{1,0:T(8,128)(2,1)} async-done(((bf16[32,2048]{1,0:T(8,128)(2,1)}), bf16[1024,2048]{1,0:T(8,128)(2,1)}) %all-gather.5.cloned.1.call-update) | async-done | bytes 4194320 | tf_op jit(solution)/shard_map/all_gather | solution.py:317
  102.2 88.5 %all-gather.3.cloned.1.call-done.wq_in = bf16[2048,1536]{1,0:T(8,128)(2,1)} async-done(((bf16[64,1536]{1,0:T(8,128)(2,1)}), bf16[2048,1536]{1,0:T(8,128)(2,1)}) %all-gather.3.cloned.1.call-update) | async-done | bytes 6291472 | tf_op jit(solution)/shard_map/all_gather | solution.py:316
  191.1 1.2 copy-done.19
  192.3 15.2 %forward_layer.7 = (bf16[256,2048]{1,0:T(8,128)(2,1)}, bf16[256,2048]{1,0:T(8,128)(2,1)S(1)}, bf16[256,1536]{1,0:T(8,128)(2,1)S(1)}, bf16[256,1024]{1,0:T(8,128)(2,1)S(1)}, bf16[256,2048]{1,0:T(8,128)(2,1)S(1)}) custom-call(s32[2]{0:T(128)S(1)} %pad_add_fusion.7.info, ...), custom_call_target="tpu_custom_call", output_to_operand_aliasing={{1}: (4, {}), {2}: (5, {}), {3}: (6, {}), {4}: (7, {})} | custom-call | flops 3000000000 | bytes 14000000 | tf_op jit(solution)/shard_map/forward_layer/pallas_call | solution.py:152
  207.5 1.0 copy-done.1
  208.5 2.3 collective-permute-start.3
  211.4 1.0 collective-permute-done.3.h_in
  212.4 1.2 copy-done.2
  214.3 1.0 copy-done.3
  215.3 1.6 collective-permute-start.4
  217.6 1.2 copy-done.4
  219.5 1.0 copy-done.5
  220.5 1.6 collective-permute-start.5
  222.8 1.2 copy-done.6
  224.8 1.0 copy-done.7
  225.7 1.6 collective-permute-start.6
  228.0 1.2 copy-done.8
  229.2 1.2 forward_layer.11
  230.4 1.0 copy-done.9
  231.4 1.6 collective-permute-start.7
  233.7 1.2 copy-done.10
  235.6 1.0 copy-done.11
  236.6 1.6 collective-permute-start.8
  238.9 1.2 copy-done.12
  240.8 1.0 copy-done.13
  241.8 1.7 collective-permute-start.9
  244.3 31.0 %collective-permute-start.10 = (bf16[128,2048]{1,0:T(8,128)(2,1)}, bf16[128,2048]{1,0:T(8,128)(2,1)}, u32[]{:S(2)}, u32[]{:S(2)}) collective-permute-start(bf16[128,2048]{1,0:T(8,128)(2,1)} %dynamic-slice_bitcast_fusion), channel_id=1, source_target_pairs={{0,1},{2,3},{4,5},{6,7},{8,9},{10,11},{12,13},{14,15},{16,17},{18,... | collective-permute-start | bytes 1572872 | tf_op jit(solution)/shard_map/ppermute | solution.py:321
  276.3 1.3 pad_maximum_fusion.1.u_in
  277.7 1.2 copy-done.14
  279.6 1.0 copy-done.15
  286.1 3.7 collective-permute-start.14
  293.5 1.3 collective-permute-start.17
  294.8 285.4 %collective-permute-done.17.u_in = bf16[256,2048]{1,0:T(8,128)(2,1)S(1)} collective-permute-done((bf16[256,2048]{1,0:T(8,128)(2,1)S(1)}, bf16[256,2048]{1,0:T(8,128)(2,1)S(1)}, u32[]{:S(2)}, u32[]{:S(2)}) %collective-permute-start.17) | collective-permute-done | bytes 1048608 | tf_op jit(solution)/shard_map/ppermute | solution.py:344
  580.1 12.4 %backward_last.1 = (bf16[256,2048]{1,0:T(8,128)(2,1)}, bf16[256,1536]{1,0:T(8,128)(2,1)S(1)}, bf16[256,2048]{1,0:T(8,128)(2,1)S(1)}) custom-call(s32[2]{0:T(128)S(1)} %pad_add_fusion.7.info, bf16[256,2048]{1,0:T(8,128)(2,1)S(1)} %collective-permute-done.17.u_in, ...), custom_call_target="tpu_custom_call", output_to_operand_aliasing={{1}: (6, {}), {2}: (7, {})} | custom-call | flops 4000000000 | bytes 15000000 | tf_op jit(solution)/shard_map/backward_last/pallas_call | solution.py:272
  593.4 3.4 convolution_convert_fusion.1
  596.9 4.5 convolution_convert_fusion
  601.4 210.8 %reduce-scatter.5.cloned.1.call-done = bf16[32,2048]{1,0:T(8,128)(2,1)} async-done(((bf16[1024,2048]{1,0:T(8,128)(2,1)}), bf16[32,2048]{1,0:T(8,128)(2,1)}) %reduce-scatter.5.cloned.1.call-update) | async-done | bytes 131088 | tf_op jit(solution)/shard_map/reduce_scatter | solution.py:348
  812.3 1.9 collective-permute-start.19
  814.2 225.1 %reduce-scatter.3.cloned.1.call-done = bf16[64,1536]{1,0:T(8,128)(2,1)} async-done(((bf16[2048,1536]{1,0:T(8,128)(2,1)}), bf16[64,1536]{1,0:T(8,128)(2,1)}) %reduce-scatter.3.cloned.1.call-update) | async-done | bytes 196624 | tf_op jit(solution)/shard_map/reduce_scatter | solution.py:349
  1039.3 1.9 collective-permute-start.18
  1042.0 9.1 collective-permute-done.18
  (89 shorter events, 24.7 us)
Async XLA Ops:
  7.2 19.3 %copy-start = (bf16[2,128,2048]{2,1,0:T(8,128)(2,1)S(1)}, bf16[2,128,2048]{2,1,0:T(8,128)(2,1)}, u32[]{:S(2)}) copy-start(bf16[2,128,2048]{2,1,0:T(8,128)(2,1)} %param.5) | copy-start | bytes 3145732
  7.2 95.0 %all-gather.5.cloned.1.call-start = ((), (), s32[]{:S(2)}) async-start(), calls=%async_computation.3 | async-start | bytes 4325376 | tf_op jit(solution)/shard_map/all_gather | solution.py:317
  7.2 7.6 collective-permute-start.2
  14.8 0.7 copy-start.22
  15.5 175.2 %all-gather.3.cloned.1.call-start = ((), (), s32[]{:S(2)}) async-start(), calls=%async_computation.2 | async-start | bytes 6488064 | tf_op jit(solution)/shard_map/all_gather | solution.py:316
  15.6 10.1 collective-permute-start.1
  25.7 0.7 copy-start.21
  26.4 785.9 %reduce-scatter.5.cloned.1.call-start = ((), (), s32[]{:S(2)}) async-start(), calls=%async_computation.5 | async-start | bytes 4325376 | tf_op jit(solution)/shard_map/reduce_scatter | solution.py:348
  26.5 3.8 collective-permute-start
  191.1 1.2 copy-start.19
  207.5 1.0 copy-start.1
  208.5 3.9 collective-permute-start.3
  212.4 1.2 copy-start.2
  214.3 1.0 copy-start.3
  215.3 2.3 collective-permute-start.4
  217.6 1.2 copy-start.4
  219.5 1.0 copy-start.5
  220.5 2.3 collective-permute-start.5
  222.8 1.2 copy-start.6
  224.7 1.0 copy-start.7
  225.7 2.3 collective-permute-start.6
  228.0 1.2 copy-start.8
  230.4 1.0 copy-start.9
  231.4 2.3 collective-permute-start.7
  233.7 1.2 copy-start.10
  235.6 1.0 copy-start.11
  236.6 2.3 collective-permute-start.8
  238.9 1.2 copy-start.12
  240.1 3.4 copy-start.20
  240.8 1.0 copy-start.13
  241.8 35.9 %collective-permute-start.9 = (bf16[256,2048]{1,0:T(8,128)(2,1)}, bf16[256,2048]{1,0:T(8,128)(2,1)}, u32[]{:S(2)}, u32[]{:S(2)}) collective-permute-start(bf16[256,2048]{1,0:T(8,128)(2,1)} %get-tuple-element.94), channel_id=1, source_target_pairs={{96,97},{98,99},{100,101},{102,103},{104,105},{106,107},{108,109},... | collective-permute-start | bytes 3145736 | tf_op jit(solution)/shard_map/ppermute | solution.py:336
  244.3 32.0 %collective-permute-start.10 = (bf16[128,2048]{1,0:T(8,128)(2,1)}, bf16[128,2048]{1,0:T(8,128)(2,1)}, u32[]{:S(2)}, u32[]{:S(2)}) collective-permute-start(bf16[128,2048]{1,0:T(8,128)(2,1)} %dynamic-slice_bitcast_fusion), channel_id=1, source_target_pairs={{0,1},{2,3},{4,5},{6,7},{8,9},{10,11},{12,13},{14,15},{16,17},{18,... | collective-permute-start | bytes 1572872 | tf_op jit(solution)/shard_map/ppermute | solution.py:321
  277.7 1.2 copy-start.14
  279.6 1.0 copy-start.15
  281.7 0.7 collective-permute-start.11
  283.1 0.7 collective-permute-start.12
  284.6 0.7 collective-permute-start.13
  286.1 3.7 collective-permute-start.14
  290.5 0.7 collective-permute-start.15
  292.0 0.7 collective-permute-start.16
  293.5 286.7 %collective-permute-start.17 = (bf16[256,2048]{1,0:T(8,128)(2,1)S(1)}, bf16[256,2048]{1,0:T(8,128)(2,1)S(1)}, u32[]{:S(2)}, u32[]{:S(2)}) collective-permute-start(bf16[256,2048]{1,0:T(8,128)(2,1)S(1)} %get-tuple-element.120), channel_id=1, source_target_pairs={{1,0},{3,2},{5,4},{7,6},{9,8},{11,10},{13,12},{15,14},{17,16},{19,... | collective-permute-start | bytes 3145736 | tf_op jit(solution)/shard_map/ppermute | solution.py:344
  592.5 0.9 copy-start.17
  593.4 3.5 copy-start.16
  593.4 3.5 copy-start.18
  596.9 442.5 %reduce-scatter.3.cloned.1.call-start = ((), (), s32[]{:S(2)}) async-start(), calls=%async_computation.4 | async-start | bytes 6488064 | tf_op jit(solution)/shard_map/reduce_scatter | solution.py:349
  812.3 229.0 %collective-permute-start.19 = (bf16[32,2048]{1,0:T(8,128)(2,1)}, bf16[32,2048]{1,0:T(8,128)(2,1)S(1)}, u32[]{:S(2)}, u32[]{:S(2)}) collective-permute-start(bf16[32,2048]{1,0:T(8,128)(2,1)} %reduce-scatter.5.cloned.1.call-done), channel_id=1, source_target_pairs={{0,0},{128,1},{2,2},{130,3},{4,4},{132,5},{6,6},{134,7},{8,8},{136... | collective-permute-start | bytes 393224 | tf_op jit(solution)/shard_map/ppermute | solution.py:350
  1039.3 11.7 %collective-permute-start.18 = (bf16[64,1536]{1,0:T(8,128)(2,1)}, bf16[64,1536]{1,0:T(8,128)(2,1)S(1)}, u32[]{:S(2)}, u32[]{:S(2)}) collective-permute-start(bf16[64,1536]{1,0:T(8,128)(2,1)} %reduce-scatter.3.cloned.1.call-done), channel_id=1, source_target_pairs={{0,0},{128,1},{2,2},{130,3},{4,4},{132,5},{6,6},{134,7},{8,8},{136... | collective-permute-start | bytes 589832 | tf_op jit(solution)/shard_map/ppermute | solution.py:351
Sparse Core Ops, SparseCore 0:
  15.6 86.5 all-gather.4
  105.4 85.3 all-gather.2
  597.0 215.2 reduce-scatter.4
  816.6 222.6 reduce-scatter.2

commit v2 on v1

--- a/solution.py
+++ b/solution.py
@@ -292,7 +292,6 @@
 FINE = (("zlo", 2), ("y", 4), ("x", 4), ("zhi", 4), ("core", 2))
 NAMES = tuple(name for name, size in FINE)
 SIZES = tuple(size for name, size in FINE)
-RING = ("x", "zhi", "zlo")
 STAGE = ("y", "core")
 
 
@@ -305,16 +304,113 @@
     return pairs
 
 
+def z_index(z):
+    return (z % 2) * 4 + z // 2
+
+
+def send_x(value, step):
+    return lax.ppermute(value, "x", [(i, (i + step) % 4) for i in range(4)])
+
+
+def send_z(value, step):
+    return lax.ppermute(value, ("zlo", "zhi"), [(z_index(i), z_index((i + step) % 8)) for i in range(8)])
+
+
+def gather_ring(own, count, send):
+    below, above = [own], [own]
+    for step in range(count // 2 - 1):
+        below.append(send(below[-1], 1))
+        above.append(send(above[-1], -1))
+    half = own.shape[0] // 2
+    far = [send(below[-1][:half], 1), send(above[-1][half:], -1)]
+    return above + far + below[:0:-1]
+
+
+def scatter_ring(take, count, send, axis):
+    far = count // 2
+
+    def halves(value):
+        return jnp.split(value, 2, axis=axis)
+
+    def add(own, came):
+        return (own.astype(jnp.float32) + came.astype(jnp.float32)).astype(jnp.bfloat16)
+
+    low, high = halves(take(far))
+    up, down = send(low, 1), send(high, -1)
+    for step in range(far - 1, 0, -1):
+        if step == far - 1:
+            low, high = halves(take(step))
+            next_up = jnp.concatenate([add(low, up), high], axis=axis)
+            low, high = halves(take(-step))
+            next_down = jnp.concatenate([low, add(high, down)], axis=axis)
+        else:
+            next_up, next_down = add(take(step), up), add(take(-step), down)
+        up, down = send(next_up, 1), send(next_down, -1)
+    total = take(0).astype(jnp.float32) + up.astype(jnp.float32) + down.astype(jnp.float32)
+    return total.astype(jnp.bfloat16)
+
+
+def assemble_kernel(place, *refs):
+    qkv_parts, out_parts, (full_qkv, full_out, sems) = refs[:5], refs[5:14], refs[14:]
+    x, z = place[0], place[1]
+    copies = []
+    for ref, dx, first, pieces in zip(qkv_parts, (0, 1, 2, 2, 3), (0, 0, 0, 4, 0), (8, 8, 4, 4, 8)):
+        for i in range(pieces):
+            row = (lax.rem(x + dx, 4) * 8 + lax.rem(z + first + i, 8)) * 64
+            target = full_qkv.at[pl.ds(pl.multiple_of(row, 64), 64), :]
+            copies.append(pltpu.make_async_copy(ref.at[pl.ds(i * 64, 64), :], target, sems.at[len(copies)]))
+    for ref, dz, first, pieces in zip(
+        out_parts, (0, 1, 2, 3, 4, 4, 5, 6, 7), (0, 0, 0, 0, 0, 2, 0, 0, 0), (4, 4, 4, 4, 2, 2, 4, 4, 4)
+    ):
+        for i in range(pieces):
+            row = (lax.rem(x + first + i, 4) * 8 + lax.rem(z + dz, 8)) * 32
+            target = full_out.at[pl.ds(pl.multiple_of(row, 32), 32), :]
+            copies.append(pltpu.make_async_copy(ref.at[pl.ds(i * 32, 32), :], target, sems.at[len(copies)]))
+    for copy in copies:
+        copy.start()
+    for copy in copies:
+        copy.wait()
+
+
+def gather_weights(near, far, x, z):
+    column = jnp.concatenate(gather_ring(near, 8, send_z))
+    row = jnp.concatenate(gather_ring(far, 4, send_x))
+    qkv_parts = gather_ring(column, 4, send_x)
+    out_parts = gather_ring(row, 8, send_z)
+    return pl.pallas_call(
+        assemble_kernel,
+        out_shape=(bf16(D, WCOLS), bf16(HQ, D)),
+        in_specs=[SMEM] + [ANY] * 14,
+        out_specs=(ANY, ANY),
+        scratch_shapes=[pltpu.SemaphoreType.DMA((64,))],
+        cost_estimate=pl.CostEstimate(flops=0, bytes_accessed=21_000_000, transcendentals=0),
+        name="assemble",
+    )(jnp.stack([x, z]), *qkv_parts, *out_parts)
+
+
+def scatter_qkv(part, x, z):
+    part = part.reshape(4, 512, WCOLS)
+    mine = scatter_ring(lambda d: lax.dynamic_index_in_dim(part, (x + d) % 4, 0, keepdims=False), 4, send_x, 0)
+    mine = mine.reshape(8, 64, WCOLS)
+    return scatter_ring(lambda d: lax.dynamic_index_in_dim(mine, (z + d) % 8, 0, keepdims=False), 8, send_z, 0)
+
+
+def scatter_out(part, x, z):
+    part = part.reshape(4, 8, 32, D)
+    mine = scatter_ring(lambda d: lax.dynamic_index_in_dim(part, (z + d) % 8, 1, keepdims=False), 8, send_z, 0)
+    return scatter_ring(lambda d: lax.dynamic_index_in_dim(mine, (x + d) % 4, 0, keepdims=False), 4, send_x, 0)
+
+
 def on_device(inputs, cotangent, joined, w_qkv, w_out):
     micro = lax.axis_index("zlo")
     stage = 2 * lax.axis_index("y") + lax.axis_index("core")
-    bin_index = 4 * lax.axis_index("x") + lax.axis_index("zhi")
+    x_index = lax.axis_index("x")
+    z_place = 2 * lax.axis_index("zhi") + micro
+    bin_index = 4 * x_index + lax.axis_index("zhi")
     flag = joined[micro, bin_index]
-    near, far = w_qkv[0], w_out[0]
-    near = lax.ppermute(near, NAMES, regroup(False))
-    far = lax.ppermute(far, NAMES, regroup(False))
-    full_qkv = lax.all_gather(near, RING, axis=0, tiled=True)
-    full_out = lax.all_gather(far, RING, axis=0, tiled=True)
+    near = lax.ppermute(w_qkv[0], NAMES, regroup(False))
+    far = lax.ppermute(w_out[0], NAMES, regroup(False))
+    full_qkv, full_out = gather_weights(near, far, x_index, z_place)
     block = lax.dynamic_index_in_dim(inputs, micro, 0, keepdims=False)
     hidden = jnp.concatenate([block, lax.ppermute(block, "core", [(1, 0)])])
     block = lax.dynamic_index_in_dim(cotangent, micro, 0, keepdims=False)
@@ -345,8 +441,8 @@
     contract = (((0,), (0,)), ((), ()))
     part_out = lax.dot_general(ctx, ups, contract, preferred_element_type=jnp.float32).astype(jnp.bfloat16)
     part_qkv = lax.dot_general(normed, dproj, contract, preferred_element_type=jnp.float32).astype(jnp.bfloat16)
-    grad_out = lax.psum_scatter(part_out, RING, scatter_dimension=0, tiled=True)
-    grad_qkv = lax.psum_scatter(part_qkv, RING, scatter_dimension=0, tiled=True)
+    grad_out = scatter_out(part_out, x_index, z_place)
+    grad_qkv = scatter_qkv(part_qkv, x_index, z_place)
     grad_out = lax.ppermute(grad_out, NAMES, regroup(True)).astype(jnp.float32)
     grad_qkv = lax.ppermute(grad_qkv, NAMES, regroup(True)).astype(jnp.float32)
     return (grad_qkv[None], grad_out[None])

time: 1070 us -> 941 us (0.88)
  waiting for transfers between devices: 898 us -> 380 us
  Pallas kernels: 38.3 us -> 358 us
  starting transfers between devices: 68.4 us -> 143 us
  other arithmetic: 8.96 us -> 23.2 us
  between operations: 14.7 us -> 1.96 us
    reduce_scatter x2 -> x0, waiting for transfers between devices: 436 us -> none  [the longest x1 225 us: on_device(): grad_qkv = lax.psum_scatter(part_qkv, RING, scatter_dimension=0, tiled=True)]
    pallas_call x0 -> x1, Pallas kernels: none -> 320 us  [gather_weights(): pl.pallas_call(assemble_kernel, out_shape=(bf16(D, WCOLS), bf16(HQ, D)),...]
    all_gather x2 -> x0, waiting for transfers between devices: 159 us -> none  [the longest x1 88.5 us: on_device(): full_qkv = lax.all_gather(near, RING, axis=0, tiled=True)]
    ppermute x2 -> x50, waiting for transfers between devices: 6.3 us -> 84.9 us  [the longest x32 71.9 us: send_z(): lax.ppermute(value, ('zlo', 'zhi'), [(z_index(i), z_index((i + step) % 8)...]
    ppermute x2 -> x50, starting transfers between devices: 11.4 us -> 86.1 us  [the longest x32 53.8 us: send_z(): lax.ppermute(value, ('zlo', 'zhi'), [(z_index(i), z_index((i + step) % 8)...]
    convert_element_type x0 -> x14, other arithmetic: none -> 11.6 us  [the longest x10 7.23 us: add(): (own.astype(jnp.float32) + came.astype(jnp.float32)).astype(jnp.bfloat16)]
  transfers between devices with their start and end apart: 24 -> 68, of which waited for: 11 -> 36; matrix products, arithmetic and copies ran while one was open for 1% -> 4% of each run, Pallas kernels for 0% -> 0%
where the time goes in v2:
time: 941 us; the launch traced here: 929 us
  waiting for transfers between devices  380 us (40%)
  Pallas kernels  358 us (38%)
  starting transfers between devices  143 us (15%)
  other arithmetic  23.2 us (2%)
  local copies, waits for them, and re-layouts  19.6 us (2%)
    pallas_call x1, Pallas kernels, gather_weights(): pl.pallas_call(assemble_kernel, out_shape=(bf16(D, WCOLS), bf16(HQ, D)),...  320 us
    ppermute x7, waiting for transfers between devices, on_device(): upstream = lax.ppermute(result, STAGE, [(layer, layer - 1)])  286 us
    ppermute x32, waiting for transfers between devices, send_z(): lax.ppermute(value, ('zlo', 'zhi'), [(z_index(i), z_index((i + step) % 8)...  71.9 us
    ppermute x32, starting transfers between devices, send_z(): lax.ppermute(value, ('zlo', 'zhi'), [(z_index(i), z_index((i + step) % 8)...  53.8 us
    ppermute x1, starting transfers between devices, on_device(): upstream = jnp.concatenate([lax.ppermute(block, 'core', [(0, 1)]), block])  30.8 us
    ppermute x16, starting transfers between devices, send_x(): return lax.ppermute(value, 'x', [(i, (i + step) % 4) for i in range(4)])  25.2 us
    pallas_call x8, Pallas kernels, forward_layer(): pl.pallas_call(functools.partial(forward_kernel, final), out_shape=(bf16(...  20.6 us
  transfers between devices with their start and end apart: 68, of which 36 were waited for; matrix products, arithmetic and copies ran while one was open for 4% of the time, Pallas kernels for 0%

profile of v2, /device:TPU:32, one launch (start us, length us, event | category | flops | bytes accessed | tf_op | source)
XLA Modules:
  0.0 928.7 jit_solution(3799356482768990431)
XLA Ops:
  0.6 4.8 collective-permute-start.14
  5.4 2.4 collective-permute-start.1
  8.2 2.8 collective-permute-start.15
  15.4 2.6 collective-permute-done.16
  18.0 3.3 collective-permute-start.18
  21.3 2.5 collective-permute-start.3
  25.0 2.4 collective-permute-done.3
  27.4 4.1 collective-permute-start.4
  32.6 6.2 collective-permute-done.7
  39.0 3.3 collective-permute-start.9
  52.5 3.4 collective-permute-start.19
  55.9 7.8 collective-permute-done.22.refs_13_
  67.5 9.4 %collective-permute-done.23.refs_12_ = bf16[128,2048]{1,0:T(8,128)(2,1)} collective-permute-done((bf16[128,2048]{1,0:T(8,128)(2,1)S(1)}, bf16[128,2048]{1,0:T(8,128)(2,1)}, u32[]{:S(2)}, u32[]{:S(2)}) %collective-permute-start.23) | collective-permute-done | bytes 524320 | tf_op jit(solution)/shard_map/ppermute | solution.py:316
  78.1 3.3 collective-permute-start.21
  85.6 2.4 collective-permute-start.13
  90.6 2.5 collective-permute-start.25
  97.0 3.8 collective-permute-done.25.refs_9_
  100.8 3.2 collective-permute-done.26.refs_10_
  104.7 320.0 %assemble.1 = (bf16[2048,1536]{1,0:T(8,128)(2,1)}, bf16[1024,2048]{1,0:T(8,128)(2,1)}) custom-call(s32[2]{0:T(128)} %pad_add_fusion.8.place, bf16[512,1536]{1,0:T(8,128)(2,1)} %constant_dynamic-update-slice_fusion.refs_0_, bf16[512,1536]{1,0:T(8,128)(2,1)} %collective-permute-done.10.refs_1_, bf16[256,1536]{1,0:T(8,128)(2,1)} %collective-permute-done.12.refs_2_, ...), custom_call_target="tpu_custom_call" | custom-call | bytes 21000000 | tf_op jit(solution)/shard_map/assemble/pallas_call | solution.py:380
  426.0 15.1 %forward_layer.7 = (bf16[256,2048]{1,0:T(8,128)(2,1)}, bf16[256,2048]{1,0:T(8,128)(2,1)S(1)}, bf16[256,1536]{1,0:T(8,128)(2,1)S(1)}, bf16[256,1024]{1,0:T(8,128)(2,1)S(1)}, bf16[256,2048]{1,0:T(8,128)(2,1)S(1)}) custom-call(s32[2]{0:T(128)S(1)} %pad_add_fusion.7.info, ...), custom_call_target="tpu_custom_call", output_to_operand_aliasing={{1}: (4, {}), {2}: (5, {}), {3}: (6, {}), {4}: (7, {})} | custom-call | flops 3000000000 | bytes 14000000 | tf_op jit(solution)/shard_map/forward_layer/pallas_call | solution.py:152
  441.1 2.3 collective-permute-start.27
  464.2 30.8 %collective-permute-start.34 = (bf16[128,2048]{1,0:T(8,128)(2,1)}, bf16[128,2048]{1,0:T(8,128)(2,1)}, u32[]{:S(2)}, u32[]{:S(2)}) collective-permute-start(bf16[128,2048]{1,0:T(8,128)(2,1)} %dynamic-slice_bitcast_fusion.6), channel_id=1, source_target_pairs={{0,1},{2,3},{4,5},{6,7},{8,9},{10,11},{12,13},{14,15},{16,17},{18,... | collective-permute-start | bytes 1572872 | tf_op jit(solution)/shard_map/ppermute | solution.py:417
  505.3 3.5 collective-permute-start.39
  514.2 286.1 %collective-permute-done.41.u_in = bf16[256,2048]{1,0:T(8,128)(2,1)} collective-permute-done((bf16[256,2048]{1,0:T(8,128)(2,1)}, bf16[256,2048]{1,0:T(8,128)(2,1)}, u32[]{:S(2)}, u32[]{:S(2)}) %collective-permute-start.41) | collective-permute-done | bytes 1048608 | tf_op jit(solution)/shard_map/ppermute | solution.py:440
  802.7 12.4 %backward_last.1 = (bf16[256,2048]{1,0:T(8,128)(2,1)}, bf16[256,1536]{1,0:T(8,128)(2,1)S(1)}, bf16[256,2048]{1,0:T(8,128)(2,1)S(1)}) custom-call(s32[2]{0:T(128)S(1)} %pad_add_fusion.7.info, bf16[256,2048]{1,0:T(8,128)(2,1)} %collective-permute-done.41.u_in, ...), custom_call_target="tpu_custom_call", output_to_operand_aliasing={{1}: (6, {}), {2}: (7, {})} | custom-call | flops 4000000000 | bytes 15000000 | tf_op jit(solution)/shard_map/backward_last/pallas_call | solution.py:272
  820.8 3.1 collective-permute-done.55
  823.9 4.2 collective-permute-done.59
  831.9 3.2 collective-permute-start.44
  835.3 2.4 collective-permute-done.56
  841.2 8.1 collective-permute-done.42
  853.3 2.3 fusion.7
  855.7 3.7 collective-permute-start.61
  860.8 3.2 collective-permute-start.45
  867.2 2.6 collective-permute-start.62
  869.8 4.7 collective-permute-done.58
  874.5 3.1 collective-permute-done.62
  879.0 3.5 collective-permute-start.65
  882.4 2.9 fusion.1
  888.1 3.5 collective-permute-done.46
  892.4 2.3 collective-permute-start.47
  894.8 3.3 collective-permute-done.47
  898.2 3.2 collective-permute-start.48
  901.8 3.2 collective-permute-done.48
  905.1 3.3 collective-permute-start.52
  908.5 2.5 collective-permute-start.66
  911.7 2.6 collective-permute-start.53
  919.4 4.1 collective-permute-done.67
  924.3 3.2 collective-permute-done.54
  (211 shorter events, 108.2 us)
Async XLA Ops:
  0.6 7.6 collective-permute-start.14
  5.4 7.2 collective-permute-start.1
  8.2 9.7 %collective-permute-start.15 = (bf16[32,2048]{1,0:T(8,128)(2,1)S(1)}, bf16[32,2048]{1,0:T(8,128)(2,1)S(1)}, u32[]{:S(2)}, u32[]{:S(2)}) collective-permute-start(bf16[32,2048]{1,0:T(8,128)(2,1)S(1)} %collective-permute-done.14), channel_id=1, source_target_pairs={{0,24},{8,0},{16,8},{24,16},{1,25},{9,1},{17,9},{25,17},{2,26},{10... | collective-permute-start | bytes 393224 | tf_op jit(solution)/shard_map/ppermute | solution.py:312
  11.0 6.9 collective-permute-start.16
  12.6 8.6 collective-permute-start.2
  12.6 11.6 %collective-permute-start.5 = (bf16[64,1536]{1,0:T(8,128)(2,1)S(1)}, bf16[64,1536]{1,0:T(8,128)(2,1)S(1)}, u32[]{:S(2)}, u32[]{:S(2)}) collective-permute-start(bf16[64,1536]{1,0:T(8,128)(2,1)S(1)} %collective-permute-done.1), channel_id=1, source_target_pairs={{0,128},{128,2},{2,130},{130,4},{4,132},{132,6},{6,134},{134,0},{1... | collective-permute-start | bytes 589832 | tf_op jit(solution)/shard_map/ppermute | solution.py:316
  17.9 33.4 %collective-permute-start.17 = (bf16[16,2048]{1,0:T(8,128)(2,1)S(1)}, bf16[16,2048]{1,0:T(8,128)(2,1)S(1)}, u32[]{:S(2)}, u32[]{:S(2)}) collective-permute-start(bf16[16,2048]{1,0:T(8,128)(2,1)S(1)} %slice.60), channel_id=1, source_target_pairs={{0,8},{8,16},{16,24},{24,0},{1,9},{9,17},{17,25},{25,1},{2,10},{10... | collective-permute-start | bytes 196616 | tf_op jit(solution)/shard_map/ppermute | solution.py:312
  18.0 33.4 %collective-permute-start.18 = (bf16[16,2048]{1,0:T(8,128)(2,1)S(1)}, bf16[16,2048]{1,0:T(8,128)(2,1)S(1)}, u32[]{:S(2)}, u32[]{:S(2)}) collective-permute-start(bf16[16,2048]{1,0:T(8,128)(2,1)S(1)} %slice.61), channel_id=1, source_target_pairs={{0,24},{8,0},{16,8},{24,16},{1,25},{9,1},{17,9},{25,17},{2,26},{10... | collective-permute-start | bytes 196616 | tf_op jit(solution)/shard_map/ppermute | solution.py:312
  24.3 7.7 collective-permute-start.6
  27.4 11.5 %collective-permute-start.4 = (bf16[64,1536]{1,0:T(8,128)(2,1)S(1)}, bf16[64,1536]{1,0:T(8,128)(2,1)S(1)}, u32[]{:S(2)}, u32[]{:S(2)}) collective-permute-start(bf16[64,1536]{1,0:T(8,128)(2,1)S(1)} %collective-permute-done.3), channel_id=1, source_target_pairs={{0,134},{128,0},{2,128},{130,2},{4,130},{132,4},{6,132},{134,6},{1... | collective-permute-start | bytes 589832 | tf_op jit(solution)/shard_map/ppermute | solution.py:316
  31.9 6.9 collective-permute-start.7
  39.0 6.4 collective-permute-start.9
  48.1 33.6 %collective-permute-start.11 = (bf16[512,1536]{1,0:T(8,128)(2,1)}, bf16[512,1536]{1,0:T(8,128)(2,1)S(1)}, u32[]{:S(2)}, u32[]{:S(2)}) collective-permute-start(bf16[512,1536]{1,0:T(8,128)(2,1)} %constant_dynamic-update-slice_fusion.refs_0_), channel_id=1, source_target_pairs={{0,8},{8,16},{16,24},{24,0},{1,9},{9,17},{17,25},{25,1},{2,10},{10... | collective-permute-start | bytes 4718600 | tf_op jit(solution)/shard_map/ppermute | solution.py:312
  49.1 34.5 %collective-permute-start.10 = (bf16[512,1536]{1,0:T(8,128)(2,1)}, bf16[512,1536]{1,0:T(8,128)(2,1)}, u32[]{:S(2)}, u32[]{:S(2)}) collective-permute-start(bf16[512,1536]{1,0:T(8,128)(2,1)} %constant_dynamic-update-slice_fusion.refs_0_), channel_id=1, source_target_pairs={{0,24},{8,0},{16,8},{24,16},{1,25},{9,1},{17,9},{25,17},{2,26},{10... | collective-permute-start | bytes 4718600 | tf_op jit(solution)/shard_map/ppermute | solution.py:312
  51.4 12.3 %collective-permute-start.22 = (bf16[128,2048]{1,0:T(8,128)(2,1)S(1)}, bf16[128,2048]{1,0:T(8,128)(2,1)S(1)}, u32[]{:S(2)}, u32[]{:S(2)}) collective-permute-start(bf16[128,2048]{1,0:T(8,128)(2,1)S(1)} %constant_dynamic-update-slice_fusion.9.refs_5_), channel_id=1, source_target_pairs={{0,128},{128,2},{2,130},{130,4},{4,132},{132,6},{6,134},{134,0},{1... | collective-permute-start | bytes 1572872 | tf_op jit(solution)/shard_map/ppermute | solution.py:316
  52.5 13.5 %collective-permute-start.19 = (bf16[128,2048]{1,0:T(8,128)(2,1)S(1)}, bf16[128,2048]{1,0:T(8,128)(2,1)}, u32[]{:S(2)}, u32[]{:S(2)}) collective-permute-start(bf16[128,2048]{1,0:T(8,128)(2,1)S(1)} %constant_dynamic-update-slice_fusion.9.refs_5_), channel_id=1, source_target_pairs={{0,134},{128,0},{2,128},{130,2},{4,130},{132,4},{6,132},{134,6},{1... | collective-permute-start | bytes 1572872 | tf_op jit(solution)/shard_map/ppermute | solution.py:316
  63.7 13.2 %collective-permute-start.23 = (bf16[128,2048]{1,0:T(8,128)(2,1)S(1)}, bf16[128,2048]{1,0:T(8,128)(2,1)}, u32[]{:S(2)}, u32[]{:S(2)}) collective-permute-start(bf16[128,2048]{1,0:T(8,128)(2,1)S(1)} %collective-permute-done.22.refs_13_), channel_id=1, source_target_pairs={{0,128},{128,2},{2,130},{130,4},{4,132},{132,6},{6,134},{134,0},{1... | collective-permute-start | bytes 1572872 | tf_op jit(solution)/shard_map/ppermute | solution.py:316
  66.0 12.0 %collective-permute-start.20 = (bf16[128,2048]{1,0:T(8,128)(2,1)}, bf16[128,2048]{1,0:T(8,128)(2,1)}, u32[]{:S(2)}, u32[]{:S(2)}) collective-permute-start(bf16[128,2048]{1,0:T(8,128)(2,1)} %collective-permute-done.19.refs_6_), channel_id=1, source_target_pairs={{0,134},{128,0},{2,128},{130,2},{4,130},{132,4},{6,132},{134,6},{1... | collective-permute-start | bytes 1572872 | tf_op jit(solution)/shard_map/ppermute | solution.py:316
  76.9 13.7 %collective-permute-start.24 = (bf16[128,2048]{1,0:T(8,128)(2,1)}, bf16[128,2048]{1,0:T(8,128)(2,1)S(1)}, u32[]{:S(2)}, u32[]{:S(2)}) collective-permute-start(bf16[128,2048]{1,0:T(8,128)(2,1)} %collective-permute-done.23.refs_12_), channel_id=1, source_target_pairs={{0,128},{128,2},{2,130},{130,4},{4,132},{132,6},{6,134},{134,0},{1... | collective-permute-start | bytes 1572872 | tf_op jit(solution)/shard_map/ppermute | solution.py:316
  78.1 15.0 %collective-permute-start.21 = (bf16[128,2048]{1,0:T(8,128)(2,1)}, bf16[128,2048]{1,0:T(8,128)(2,1)}, u32[]{:S(2)}, u32[]{:S(2)}) collective-permute-start(bf16[128,2048]{1,0:T(8,128)(2,1)} %collective-permute-done.20.refs_7_), channel_id=1, source_target_pairs={{0,134},{128,0},{2,128},{130,2},{4,130},{132,4},{6,132},{134,6},{1... | collective-permute-start | bytes 1572872 | tf_op jit(solution)/shard_map/ppermute | solution.py:316
  82.7 21.4 %collective-permute-start.12 = (bf16[256,1536]{1,0:T(8,128)(2,1)}, bf16[256,1536]{1,0:T(8,128)(2,1)}, u32[]{:S(2)}, u32[]{:S(2)}) collective-permute-start(bf16[256,1536]{1,0:T(8,128)(2,1)} %slice.58), channel_id=1, source_target_pairs={{0,8},{8,16},{16,24},{24,0},{1,9},{9,17},{17,25},{25,1},{2,10},{10... | collective-permute-start | bytes 2359304 | tf_op jit(solution)/shard_map/ppermute | solution.py:312
  85.6 18.4 %collective-permute-start.13 = (bf16[256,1536]{1,0:T(8,128)(2,1)}, bf16[256,1536]{1,0:T(8,128)(2,1)}, u32[]{:S(2)}, u32[]{:S(2)}) collective-permute-start(bf16[256,1536]{1,0:T(8,128)(2,1)} %slice.59), channel_id=1, source_target_pairs={{0,24},{8,0},{16,8},{24,16},{1,25},{9,1},{17,9},{25,17},{2,26},{10... | collective-permute-start | bytes 2359304 | tf_op jit(solution)/shard_map/ppermute | solution.py:312
  88.0 7.9 collective-permute-start
  90.6 10.3 %collective-permute-start.25 = (bf16[64,2048]{1,0:T(8,128)(2,1)S(1)}, bf16[64,2048]{1,0:T(8,128)(2,1)S(1)}, u32[]{:S(2)}, u32[]{:S(2)}) collective-permute-start(bf16[64,2048]{1,0:T(8,128)(2,1)S(1)} %slice.62), channel_id=1, source_target_pairs={{0,128},{128,2},{2,130},{130,4},{4,132},{132,6},{6,134},{134,0},{1... | collective-permute-start | bytes 786440 | tf_op jit(solution)/shard_map/ppermute | solution.py:316
  94.0 10.0 %collective-permute-start.26 = (bf16[64,2048]{1,0:T(8,128)(2,1)S(1)}, bf16[64,2048]{1,0:T(8,128)(2,1)S(1)}, u32[]{:S(2)}, u32[]{:S(2)}) collective-permute-start(bf16[64,2048]{1,0:T(8,128)(2,1)S(1)} %slice.63), channel_id=1, source_target_pairs={{0,134},{128,0},{2,128},{130,2},{4,130},{132,4},{6,132},{134,6},{1... | collective-permute-start | bytes 786440 | tf_op jit(solution)/shard_map/ppermute | solution.py:316
  461.8 35.6 %collective-permute-start.33 = (bf16[256,2048]{1,0:T(8,128)(2,1)}, bf16[256,2048]{1,0:T(8,128)(2,1)}, u32[]{:S(2)}, u32[]{:S(2)}) collective-permute-start(bf16[256,2048]{1,0:T(8,128)(2,1)} %get-tuple-element.98), channel_id=1, source_target_pairs={{96,97},{98,99},{100,101},{102,103},{104,105},{106,107},{108,109},... | collective-permute-start | bytes 3145736 | tf_op jit(solution)/shard_map/ppermute | solution.py:432
  464.2 31.8 %collective-permute-start.34 = (bf16[128,2048]{1,0:T(8,128)(2,1)}, bf16[128,2048]{1,0:T(8,128)(2,1)}, u32[]{:S(2)}, u32[]{:S(2)}) collective-permute-start(bf16[128,2048]{1,0:T(8,128)(2,1)} %dynamic-slice_bitcast_fusion.6), channel_id=1, source_target_pairs={{0,1},{2,3},{4,5},{6,7},{8,9},{10,11},{12,13},{14,15},{16,17},{18,... | collective-permute-start | bytes 1572872 | tf_op jit(solution)/shard_map/ppermute | solution.py:417
  512.8 287.5 %collective-permute-start.41 = (bf16[256,2048]{1,0:T(8,128)(2,1)}, bf16[256,2048]{1,0:T(8,128)(2,1)}, u32[]{:S(2)}, u32[]{:S(2)}) collective-permute-start(bf16[256,2048]{1,0:T(8,128)(2,1)} %get-tuple-element.124), channel_id=1, source_target_pairs={{1,0},{3,2},{5,4},{7,6},{9,8},{11,10},{13,12},{15,14},{17,16},{19,... | collective-permute-start | bytes 3145736 | tf_op jit(solution)/shard_map/ppermute | solution.py:440
  816.5 7.4 collective-permute-start.55
  818.7 9.4 %collective-permute-start.59 = (bf16[2,32,2048]{2,1,0:T(8,128)(2,1)S(1)}, bf16[2,32,2048]{2,1,0:T(8,128)(2,1)S(1)}, u32[]{:S(2)}, u32[]{:S(2)}) collective-permute-start(bf16[2,32,2048]{2,1,0:T(8,128)(2,1)S(1)} %get-tuple-element.142), channel_id=1, source_target_pairs={{0,134},{128,0},{2,128},{130,2},{4,130},{132,4},{6,132},{134,6},{1... | collective-permute-start | bytes 786440 | tf_op jit(solution)/shard_map/ppermute | solution.py:316
  828.4 9.4 %collective-permute-start.56 = (bf16[4,32,2048]{2,1,0:T(8,128)(2,1)S(1)}, bf16[4,32,2048]{2,1,0:T(8,128)(2,1)}, u32[]{:S(2)}, u32[]{:S(2)}) collective-permute-start(bf16[4,32,2048]{2,1,0:T(8,128)(2,1)S(1)} %pad_maximum_fusion.4), channel_id=1, source_target_pairs={{0,128},{128,2},{2,130},{130,4},{4,132},{132,6},{6,134},{134,0},{1... | collective-permute-start | bytes 1572872 | tf_op jit(solution)/shard_map/ppermute | solution.py:316
  831.9 17.3 %collective-permute-start.42 = (bf16[256,1536]{1,0:T(8,128)(2,1)}, bf16[256,1536]{1,0:T(8,128)(2,1)S(1)}, u32[]{:S(2)}, u32[]{:S(2)}) collective-permute-start(bf16[256,1536]{1,0:T(8,128)(2,1)} %get-tuple-element.132), channel_id=1, source_target_pairs={{0,8},{8,16},{16,24},{24,0},{1,9},{9,17},{17,25},{25,1},{2,10},{10... | collective-permute-start | bytes 2359304 | tf_op jit(solution)/shard_map/ppermute | solution.py:312
  831.9 17.3 %collective-permute-start.44 = (bf16[256,1536]{1,0:T(8,128)(2,1)}, bf16[256,1536]{1,0:T(8,128)(2,1)}, u32[]{:S(2)}, u32[]{:S(2)}) collective-permute-start(bf16[256,1536]{1,0:T(8,128)(2,1)} %get-tuple-element.134), channel_id=1, source_target_pairs={{0,24},{8,0},{16,8},{24,16},{1,25},{9,1},{17,9},{25,17},{2,26},{10... | collective-permute-start | bytes 2359304 | tf_op jit(solution)/shard_map/ppermute | solution.py:312
  835.2 16.0 %collective-permute-start.60 = (bf16[4,32,2048]{2,1,0:T(8,128)(2,1)S(1)}, bf16[4,32,2048]{2,1,0:T(8,128)(2,1)S(1)}, u32[]{:S(2)}, u32[]{:S(2)}) collective-permute-start(bf16[4,32,2048]{2,1,0:T(8,128)(2,1)S(1)} %pad_maximum_fusion.5), channel_id=1, source_target_pairs={{0,134},{128,0},{2,128},{130,2},{4,130},{132,4},{6,132},{134,6},{1... | collective-permute-start | bytes 1572872 | tf_op jit(solution)/shard_map/ppermute | solution.py:316
  839.0 14.3 %collective-permute-start.57 = (bf16[4,32,2048]{2,1,0:T(8,128)(2,1)S(1)}, bf16[4,32,2048]{2,1,0:T(8,128)(2,1)S(1)}, u32[]{:S(2)}, u32[]{:S(2)}) collective-permute-start(bf16[4,32,2048]{2,1,0:T(8,128)(2,1)S(1)} %fusion.6), channel_id=1, source_target_pairs={{0,128},{128,2},{2,130},{130,4},{4,132},{132,6},{6,134},{134,0},{1... | collective-permute-start | bytes 1572872 | tf_op jit(solution)/shard_map/ppermute | solution.py:316
  855.7 10.4 %collective-permute-start.61 = (bf16[4,32,2048]{2,1,0:T(8,128)(2,1)S(1)}, bf16[4,32,2048]{2,1,0:T(8,128)(2,1)S(1)}, u32[]{:S(2)}, u32[]{:S(2)}) collective-permute-start(bf16[4,32,2048]{2,1,0:T(8,128)(2,1)S(1)} %get-tuple-element.137), channel_id=1, source_target_pairs={{0,134},{128,0},{2,128},{130,2},{4,130},{132,4},{6,132},{134,6},{1... | collective-permute-start | bytes 1572872 | tf_op jit(solution)/shard_map/ppermute | solution.py:316
  859.5 23.0 %collective-permute-start.43 = (bf16[512,1536]{1,0:T(8,128)(2,1)S(1)}, bf16[512,1536]{1,0:T(8,128)(2,1)}, u32[]{:S(2)}, u32[]{:S(2)}) collective-permute-start(bf16[512,1536]{1,0:T(8,128)(2,1)S(1)} %pad_maximum_fusion), channel_id=1, source_target_pairs={{0,8},{8,16},{16,24},{24,0},{1,9},{9,17},{17,25},{25,1},{2,10},{10... | collective-permute-start | bytes 4718600 | tf_op jit(solution)/shard_map/ppermute | solution.py:312
  860.8 21.6 %collective-permute-start.45 = (bf16[512,1536]{1,0:T(8,128)(2,1)}, bf16[512,1536]{1,0:T(8,128)(2,1)}, u32[]{:S(2)}, u32[]{:S(2)}) collective-permute-start(bf16[512,1536]{1,0:T(8,128)(2,1)} %pad_maximum_fusion.1), channel_id=1, source_target_pairs={{0,24},{8,0},{16,8},{24,16},{1,25},{9,1},{17,9},{25,17},{2,26},{10... | collective-permute-start | bytes 4718600 | tf_op jit(solution)/shard_map/ppermute | solution.py:312
  864.0 10.4 %collective-permute-start.58 = (bf16[4,32,2048]{2,1,0:T(8,128)(2,1)}, bf16[4,32,2048]{2,1,0:T(8,128)(2,1)S(1)}, u32[]{:S(2)}, u32[]{:S(2)}) collective-permute-start(bf16[4,32,2048]{2,1,0:T(8,128)(2,1)} %get-tuple-element.136), channel_id=1, source_target_pairs={{0,128},{128,2},{2,130},{130,4},{4,132},{132,6},{6,134},{134,0},{1... | collective-permute-start | bytes 1572872 | tf_op jit(solution)/shard_map/ppermute | solution.py:316
  867.2 10.3 %collective-permute-start.62 = (bf16[4,32,2048]{2,1,0:T(8,128)(2,1)S(1)}, bf16[4,32,2048]{2,1,0:T(8,128)(2,1)S(1)}, u32[]{:S(2)}, u32[]{:S(2)}) collective-permute-start(bf16[4,32,2048]{2,1,0:T(8,128)(2,1)S(1)} %fusion.5), channel_id=1, source_target_pairs={{0,134},{128,0},{2,128},{130,2},{4,130},{132,4},{6,132},{134,6},{1... | collective-permute-start | bytes 1572872 | tf_op jit(solution)/shard_map/ppermute | solution.py:316
  878.9 9.2 collective-permute-start.63
  879.0 9.1 collective-permute-start.65
  894.7 7.1 collective-permute-start.51
  898.2 6.9 collective-permute-start.48
  901.4 12.8 %collective-permute-start.64 = (bf16[32,2048]{1,0:T(8,128)(2,1)S(1)}, bf16[32,2048]{1,0:T(8,128)(2,1)S(1)}, u32[]{:S(2)}, u32[]{:S(2)}) collective-permute-start(bf16[32,2048]{1,0:T(8,128)(2,1)S(1)} %pad_maximum_fusion.8), channel_id=1, source_target_pairs={{0,8},{8,16},{16,24},{24,0},{1,9},{9,17},{17,25},{25,1},{2,10},{10... | collective-permute-start | bytes 393224 | tf_op jit(solution)/shard_map/ppermute | solution.py:312
  905.1 6.5 collective-permute-start.52
  914.3 9.3 collective-permute-start.67
  917.5 10.0 %collective-permute-start.54 = (bf16[64,1536]{1,0:T(8,128)(2,1)S(1)}, bf16[64,1536]{1,0:T(8,128)(2,1)S(1)}, u32[]{:S(2)}, u32[]{:S(2)}) collective-permute-start(bf16[64,1536]{1,0:T(8,128)(2,1)S(1)} %fusion.17), channel_id=1, source_target_pairs={{0,0},{128,1},{2,2},{130,3},{4,4},{132,5},{6,6},{134,7},{8,8},{136... | collective-permute-start | bytes 589832 | tf_op jit(solution)/shard_map/ppermute | solution.py:447
  (37 other events, 232.9 us)

commit v3 on v2

--- a/solution.py
+++ b/solution.py
@@ -24,9 +24,10 @@
 SCALE = 1.0 / math.sqrt(HEAD)
 TO_EXP2 = SCALE * math.log2(math.e)
 NT = (((1,), (1,)), ((), ()))
-VMEM_LIMIT = 48 * 1024 * 1024
+VMEM_LIMIT = 40 * 1024 * 1024
 ANY = pl.BlockSpec(memory_space=pl.ANY)
 SMEM = pl.BlockSpec(memory_space=pltpu.SMEM)
+INSIDE = pl.BlockSpec(memory_space=pltpu.VMEM)
 
 
 def dot_nt(left, right):
@@ -41,45 +42,64 @@
     return pl.ds(pl.multiple_of(start, size), size)
 
 
-def bias_matrix(joined):
-    row = lax.broadcasted_iota(jnp.int32, (ROWS, ROWS), 0)
-    col = lax.broadcasted_iota(jnp.int32, (ROWS, ROWS), 1)
-    same = (row >= HALF) == (col >= HALF)
-    return jnp.where(jnp.logical_or(same, joined > 0), 0.0, -1e30).astype(jnp.float32)
-
-
-def probs_t(keys, query, bias):
-    logits = dot_nt(keys, query) * TO_EXP2 + bias
-    total = jnp.sum(jnp.exp2(logits), axis=0, keepdims=True)
-    return jnp.exp2(logits - jnp.log2(total))
+def packed_halves(tile, upper):
+    lane = lax.broadcasted_iota(jnp.int32, tile.shape, 1)
+    wide = tile.astype(jnp.float32)
+    kept = jnp.where((lane >= HEAD) == upper, wide, 0.0)
+    turned = pltpu.roll(kept, HEAD, 1)
+    low, high = (turned, kept) if upper else (kept, turned)
+    return low.astype(jnp.bfloat16), high.astype(jnp.bfloat16)
+
+
+def fill_keys(keys, key_s, joined):
+    row = lax.broadcasted_iota(jnp.int32, (ROWS, 2 * HEAD), 0)
+    lane = lax.broadcasted_iota(jnp.int32, (ROWS, 2 * HEAD), 1)
+    hidden = jnp.where(joined > 0, 0.0, -1e30)
+    other = jnp.logical_or(
+        jnp.logical_and(lane == 3, row >= HALF), jnp.logical_and(lane == 4, row < HALF)
+    )
+    apart = jnp.where(other, hidden, 0.0)
+    low_marks = jnp.where(lane < 3, -1.0, apart).astype(jnp.bfloat16)
+    high_marks = jnp.where(jnp.logical_and(lane >= HEAD, lane < HEAD + 3), -1.0, apart).astype(jnp.bfloat16)
+    for g in range(KVH):
+        low, high = packed_halves(keys[:, g // 2 * 128 : g // 2 * 128 + 128], g % 2 == 1)
+        key_s[g, :ROWS, :128] = low
+        key_s[g, ROWS:, :128] = high
+        key_s[g, :ROWS, 128:] = low_marks
+        key_s[g, ROWS:, 128:] = high_marks
+
+
+def fill_values(values, value_s, mark):
+    lane = lax.broadcasted_iota(jnp.int32, (ROWS, 2 * HEAD), 1)
+    low_marks = jnp.where(lane < HEAD, mark, 0.0).astype(jnp.bfloat16)
+    high_marks = jnp.where(lane >= HEAD, mark, 0.0).astype(jnp.bfloat16)
+    for g in range(KVH):
+        low, high = packed_halves(values[:, g // 2 * 128 : g // 2 * 128 + 128], g % 2 == 1)
+        value_s[g, :ROWS, :128] = low
+        value_s[g, ROWS:, :128] = high
+        value_s[g, :ROWS, 128:] = low_marks
+        value_s[g, ROWS:, 128:] = high_marks
+
+
+def stack_pairs(value):
+    return jnp.concatenate([value[:, :128], value[:, 128:]], axis=0)
 
 
 def forward_kernel(
-    final, info, h_in, wq_in, wo_in, a0, a1, a2, a3,
-    h_out, normed_out, proj_out, ctx_out, keep_out,
-    h_v, normed_v, wq_v, wo_v, proj_v, ctx_v, out_v, bias_v, key_s, vt_s, in_sem, q_sem, o_sem, w_sem,
+    final, layer, place, h_in, wq_v, wo_v, a0, a1, a2, a3, a4,
+    h_out, normed_out, proj_out, ctx_out, keep_out, marks_out,
+    h_v, normed_v, proj_v, ctx_v, out_v, marks_v, key_s, value_s, in_sem, w_sem,
 ):
-    del a0, a1, a2, a3
-
-    @pl.when(info[0] == 1)
+    del a0, a1, a2, a3, a4
+
+    @pl.when(place[0] == layer)
     def _():
         h_copy = pltpu.make_async_copy(h_in, h_v, in_sem)
         h_copy.start()
-
-        def q_copy(i):
-            c = cols(i * CHUNK, CHUNK)
-            return pltpu.make_async_copy(wq_in.at[:, c], wq_v.at[:, c], q_sem.at[i])
-
-        def o_copy(i):
-            c = cols(i * CHUNK, CHUNK)
-            return pltpu.make_async_copy(wo_in.at[:, c], wo_v.at[:, c], o_sem.at[i])
-
-        for i in (4, 5, 0, 1, 2, 3):
-            q_copy(i).start()
-        if not final:
-            for i in range(8):
-                o_copy(i).start()
-        bias_v[...] = bias_matrix(info[1])
+        block = (lax.broadcasted_iota(jnp.int32, (2 * ROWS, 128), 0) // HALF) % 2
+        lane = lax.broadcasted_iota(jnp.int32, (2 * ROWS, 128), 1)
+        spot = lane % HEAD
+        seen = jnp.where(jnp.logical_or(jnp.logical_and(lane == 3, block == 0), jnp.logical_and(lane == 4, block == 1)), 1.0, 0.0)
         h_copy.wait()
         keep = pltpu.make_async_copy(h_v, keep_out, w_sem.at[0])
         keep.start()
@@ -88,39 +108,47 @@
         normed_v[...] = (wide * scale).astype(jnp.bfloat16)
         normed_copy = pltpu.make_async_copy(normed_v, normed_out, w_sem.at[1])
         normed_copy.start()
-        q_copy(4).wait()
-        q_copy(5).wait()
-        keys = dot_nn(normed_v[...], wq_v[:, HQ : HQ + KV]).astype(jnp.bfloat16)
-        proj_v[:, HQ : HQ + KV] = keys
-        values = dot_nn(normed_v[...], wq_v[:, HQ + KV :])
-        proj_v[:, HQ + KV :] = values.astype(jnp.bfloat16)
-        values_t = values.T.astype(jnp.bfloat16)
-        for g in range(KVH):
-            key_s[g] = keys[:, g * HEAD : (g + 1) * HEAD]
-            vt_s[g] = values_t[g * HEAD : (g + 1) * HEAD, :]
+        both = dot_nn(normed_v[...], wq_v[:, HQ:]).astype(jnp.bfloat16)
+        proj_v[:, HQ:] = both
+        fill_keys(both[:, :KV], key_s, place[1])
+        fill_values(both[:, KV:], value_s, 1.0)
 
         def group(g, carry):
             c = cols(g * CHUNK, CHUNK)
-            q_copy(g).wait()
             queries = dot_nn(normed_v[...], wq_v[:, c]).astype(jnp.bfloat16)
             proj_v[:, c] = queries
-            pieces = []
-            for i in range(GROUP):
-                part = queries[:, i * HEAD : (i + 1) * HEAD]
-                weights = probs_t(key_s[g], part, bias_v[...]).astype(jnp.bfloat16)
-                pieces.append(dot_nn(vt_s[g], weights))
-            ctx_v[:, c] = jnp.concatenate(pieces, axis=0).T.astype(jnp.bfloat16)
+            left = jnp.concatenate([stack_pairs(queries), seen.astype(jnp.bfloat16)], axis=1)
+            raw = dot_nt(left, key_s[g])
+            top_low = jnp.max(raw[:, :ROWS], axis=1, keepdims=True)
+            top_high = jnp.max(raw[:, ROWS:], axis=1, keepdims=True)
+            weights = jnp.concatenate(
+                [jnp.exp2((raw[:, :ROWS] - top_low) * TO_EXP2), jnp.exp2((raw[:, ROWS:] - top_high) * TO_EXP2)], axis=1
+            ).astype(jnp.bfloat16)
+            mixed = dot_nn(weights, value_s[g])
+            total = mixed[:, 128:]
+            context = (mixed[:, :128] / total).astype(jnp.bfloat16)
+            ctx_v[:, c] = jnp.concatenate([context[:ROWS], context[ROWS:]], axis=1)
+            level = jnp.where(lane < HEAD, top_low, top_high) + jnp.log2(total) * (1.0 / TO_EXP2)
+            first = level.astype(jnp.bfloat16).astype(jnp.float32)
+            second = (level - first).astype(jnp.bfloat16).astype(jnp.float32)
+            third = level - first - second
+            marks = jnp.where(
+                spot == 0, first, jnp.where(spot == 1, second, jnp.where(spot == 2, third, seen))
+            ).astype(jnp.bfloat16)
+            marks_v[:, c] = jnp.concatenate([marks[:ROWS], marks[ROWS:]], axis=1)
             return carry
 
         lax.fori_loop(0, KVH, group, 0)
-        proj_copy = pltpu.make_async_copy(proj_v, proj_out, w_sem.at[2])
-        proj_copy.start()
-        ctx_copy = pltpu.make_async_copy(ctx_v, ctx_out, w_sem.at[3])
-        ctx_copy.start()
+        copies = [
+            pltpu.make_async_copy(proj_v, proj_out, w_sem.at[2]),
+            pltpu.make_async_copy(ctx_v, ctx_out, w_sem.at[3]),
+            pltpu.make_async_copy(marks_v, marks_out, w_sem.at[5]),
+        ]
+        for copy in copies:
+            copy.start()
 
         def finish(i, carry):
             c = cols(i * CHUNK, CHUNK)
-            o_copy(i).wait()
             out = h_v[:, c].astype(jnp.float32) + dot_nn(ctx_v[...], wo_v[:, c])
             out_v[:, c] = out.astype(jnp.bfloat16)
             return carry
@@ -132,8 +160,8 @@
             out_copy.wait()
         keep.wait()
         normed_copy.wait()
-        proj_copy.wait()
-        ctx_copy.wait()
+        for copy in copies:
+            copy.wait()
 
 
 def bf16(*shape):
@@ -148,93 +176,78 @@
     return pltpu.VMEM(shape, jnp.float32)
 
 
-def forward_layer(final, info, hidden, w_qkv, w_out, normed, proj, ctx, kept):
+def forward_layer(layer, place, hidden, w_qkv, w_out, normed, proj, ctx, kept, marks):
+    final = layer == 7
     return pl.pallas_call(
-        functools.partial(forward_kernel, final),
-        out_shape=(bf16(ROWS, D), bf16(ROWS, D), bf16(ROWS, WCOLS), bf16(ROWS, HQ), bf16(ROWS, D)),
-        in_specs=[SMEM] + [ANY] * 7,
-        out_specs=(ANY,) * 5,
-        input_output_aliases={4: 1, 5: 2, 6: 3, 7: 4},
+        functools.partial(forward_kernel, final, layer),
+        out_shape=(
+            bf16(ROWS, D), bf16(ROWS, D), bf16(ROWS, WCOLS), bf16(ROWS, HQ), bf16(ROWS, D), bf16(ROWS, HQ)
+        ),
+        in_specs=[SMEM, ANY, INSIDE, INSIDE] + [ANY] * 5,
+        out_specs=(ANY,) * 6,
+        input_output_aliases={4: 1, 5: 2, 6: 3, 7: 4, 8: 5},
         scratch_shapes=[
-            v16(ROWS, D), v16(ROWS, D), v16(D, WCOLS), v16(HQ, D), v16(ROWS, WCOLS), v16(ROWS, HQ), v16(ROWS, D),
-            v32(ROWS, ROWS), v16(KVH, ROWS, HEAD), v16(KVH, HEAD, ROWS),
-            pltpu.SemaphoreType.DMA, pltpu.SemaphoreType.DMA((6,)), pltpu.SemaphoreType.DMA((8,)),
-            pltpu.SemaphoreType.DMA((5,)),
+            v16(ROWS, D), v16(ROWS, D), v16(ROWS, WCOLS), v16(ROWS, HQ), v16(ROWS, D), v16(ROWS, HQ),
+            v16(KVH, 2 * ROWS, 256), v16(KVH, 2 * ROWS, 256),
+            pltpu.SemaphoreType.DMA, pltpu.SemaphoreType.DMA((6,)),
         ],
         compiler_params=pltpu.CompilerParams(vmem_limit_bytes=VMEM_LIMIT),
         cost_estimate=pl.CostEstimate(flops=3_000_000_000, bytes_accessed=14_000_000, transcendentals=2_000_000),
         name="forward_last" if final else "forward_layer",
-    )(info, hidden, w_qkv, w_out, normed, proj, ctx, kept)
+    )(place, hidden, w_qkv, w_out, normed, proj, ctx, kept, marks)
 
 
 def backward_kernel(
-    last, info, u_in, h_in, proj_in, wq_in, wo_in, a0, a1,
+    last, layer, place, u_in, h_in, proj_in, ctx_in, marks_in, wq_v, wo_v, a0, a1,
     up_out, dproj_out, keep_out,
-    u_v, h_v, proj_v, wq_v, wo_v, dproj_v, dn_v, bias_v, key_s, kt_s, value_s, dk_s, dv_s,
-    in_sem, q_sem, o_sem, w_sem,
+    u_v, h_v, proj_v, ctx_v, marks_v, dproj_v, dn_v, key_s, value_s, dkt_s, dvt_s, in_sem, w_sem,
 ):
     del a0, a1
 
-    @pl.when(info[0] == 1)
+    @pl.when(place[0] == layer)
     def _():
         u_copy = pltpu.make_async_copy(u_in, u_v, in_sem.at[0])
         u_copy.start()
         proj_copy = pltpu.make_async_copy(proj_in, proj_v, in_sem.at[1])
         h_copy = pltpu.make_async_copy(h_in, h_v, in_sem.at[2])
-
-        def o_copy(i):
-            r = cols(i * CHUNK, CHUNK)
-            return pltpu.make_async_copy(wo_in.at[r, :], wo_v.at[r, :], o_sem.at[i])
-
-        def q_copy(i):
-            r = cols(i * CHUNK, CHUNK)
-            return pltpu.make_async_copy(wq_in.at[r, :], wq_v.at[r, :], q_sem.at[i])
-
-        o_copy(0).start()
+        ctx_copy = pltpu.make_async_copy(ctx_in, ctx_v, in_sem.at[3])
+        marks_copy = pltpu.make_async_copy(marks_in, marks_v, in_sem.at[4])
         proj_copy.start()
-        for i in range(1, 4):
-            o_copy(i).start()
+        ctx_copy.start()
+        marks_copy.start()
         if not last:
             h_copy.start()
-            for i in range(8):
-                q_copy(i).start()
-        bias_v[...] = bias_matrix(info[1])
         proj_copy.wait()
-        keys_t = proj_v[:, HQ : HQ + KV].astype(jnp.float32).T.astype(jnp.bfloat16)
-        for g in range(KVH):
-            key_s[g] = proj_v[:, HQ + g * HEAD : HQ + (g + 1) * HEAD]
-            value_s[g] = proj_v[:, HQ + KV + g * HEAD : HQ + KV + (g + 1) * HEAD]
-            kt_s[g] = keys_t[g * HEAD : (g + 1) * HEAD, :]
+        fill_keys(proj_v[:, HQ : HQ + KV], key_s, place[1])
+        fill_values(proj_v[:, HQ + KV :], value_s, -1.0)
         u_copy.wait()
         keep = pltpu.make_async_copy(u_v, keep_out, w_sem.at[0])
         keep.start()
+        ctx_copy.wait()
+        marks_copy.wait()
 
         def group(g, carry):
             c = cols(g * CHUNK, CHUNK)
-            o_copy(g).wait()
             d_ctx = dot_nt(u_v[...], wo_v[c, :]).astype(jnp.bfloat16)
-            queries = proj_v[:, c]
-            pieces = []
-            d_key = jnp.zeros((ROWS, HEAD), jnp.float32)
-            d_value = jnp.zeros((ROWS, HEAD), jnp.float32)
-            for i in range(GROUP):
-                part = queries[:, i * HEAD : (i + 1) * HEAD]
-                d_part = d_ctx[:, i * HEAD : (i + 1) * HEAD]
-                weights = probs_t(key_s[g], part, bias_v[...])
-                d_weights = dot_nt(value_s[g], d_part)
-                inner = jnp.sum(d_weights * weights, axis=0, keepdims=True)
-                d_scores = (weights * (d_weights - inner) * SCALE).astype(jnp.bfloat16)
-                pieces.append(dot_nn(kt_s[g], d_scores))
-                d_key += dot_nn(d_scores, part)
-                d_value += dot_nn(weights.astype(jnp.bfloat16), d_part)
-            dproj_v[:, c] = jnp.concatenate(pieces, axis=0).T.astype(jnp.bfloat16)
-            dk_s[g] = d_key.astype(jnp.bfloat16)
-            dv_s[g] = d_value.astype(jnp.bfloat16)
+            queries = stack_pairs(proj_v[:, c])
+            d_pairs = stack_pairs(d_ctx)
+            left = jnp.concatenate([queries, stack_pairs(marks_v[:, c])], axis=1)
+            weights = jnp.exp2(dot_nt(left, key_s[g]) * TO_EXP2)
+            inner = d_pairs.astype(jnp.float32) * stack_pairs(ctx_v[:, c]).astype(jnp.float32)
+            d_left = jnp.concatenate([d_pairs, inner.astype(jnp.bfloat16)], axis=1)
+            d_scores = (weights * dot_nt(d_left, value_s[g])).astype(jnp.bfloat16)
+            d_query = (dot_nn(d_scores, key_s[g][:, :128]) * SCALE).astype(jnp.bfloat16)
+            dproj_v[:, c] = jnp.concatenate([d_query[:ROWS], d_query[ROWS:]], axis=1)
+            d_key = dot_nn(queries.T, d_scores)
+            d_value = dot_nn(d_pairs.T, weights.astype(jnp.bfloat16))
+            rows = pl.ds(pl.multiple_of(g * HEAD, HEAD), HEAD)
+            dkt_s[rows, :] = (d_key[:HEAD, :ROWS] + d_key[HEAD:, ROWS:]) * SCALE
+            dvt_s[rows, :] = d_value[:HEAD, :ROWS] + d_value[HEAD:, ROWS:]
             return carry
 
         lax.fori_loop(0, KVH, group, 0)
-        dproj_v[:, HQ : HQ + KV] = jnp.concatenate([dk_s[g] for g in range(KVH)], axis=1)
-        dproj_v[:, HQ + KV :] = jnp.concatenate([dv_s[g] for g in range(KVH)], axis=1)
+        dproj_v[:, HQ : HQ + KV] = dkt_s[...].T.astype(jnp.bfloat16)
+        dproj_v[:, HQ + KV :] = dvt_s[...].T.astype(jnp.bfloat16)
         dproj_copy = pltpu.make_async_copy(dproj_v, dproj_out, w_sem.at[1])
         dproj_copy.start()
         if not last:
@@ -242,7 +255,6 @@
 
             def widen(i, partial):
                 c = cols(i * CHUNK, CHUNK)
-                q_copy(i).wait()
                 d_normed = dot_nt(dproj_v[...], wq_v[c, :])
                 dn_v[:, c] = d_normed
                 product = d_normed * h_v[:, c].astype(jnp.float32)
@@ -268,24 +280,23 @@
         dproj_copy.wait()
 
 
-def backward_layer(last, info, upstream, kept, proj, w_qkv, w_out, dproj, ups):
+def backward_layer(layer, place, upstream, kept, proj, ctx, marks, w_qkv, w_out, dproj, ups):
+    last = layer == 0
     return pl.pallas_call(
-        functools.partial(backward_kernel, last),
+        functools.partial(backward_kernel, last, layer),
         out_shape=(bf16(ROWS, D), bf16(ROWS, WCOLS), bf16(ROWS, D)),
-        in_specs=[SMEM] + [ANY] * 7,
+        in_specs=[SMEM] + [ANY] * 5 + [INSIDE, INSIDE] + [ANY] * 2,
         out_specs=(ANY,) * 3,
-        input_output_aliases={6: 1, 7: 2},
+        input_output_aliases={8: 1, 9: 2},
         scratch_shapes=[
-            v16(ROWS, D), v16(ROWS, D), v16(ROWS, WCOLS), v16(D, WCOLS), v16(HQ, D), v16(ROWS, WCOLS), v32(ROWS, D),
-            v32(ROWS, ROWS), v16(KVH, ROWS, HEAD), v16(KVH, HEAD, ROWS), v16(KVH, ROWS, HEAD),
-            v16(KVH, ROWS, HEAD), v16(KVH, ROWS, HEAD),
-            pltpu.SemaphoreType.DMA((3,)), pltpu.SemaphoreType.DMA((8,)), pltpu.SemaphoreType.DMA((4,)),
-            pltpu.SemaphoreType.DMA((3,)),
+            v16(ROWS, D), v16(ROWS, D), v16(ROWS, WCOLS), v16(ROWS, HQ), v16(ROWS, HQ), v16(ROWS, WCOLS), v32(ROWS, D),
+            v16(KVH, 2 * ROWS, 256), v16(KVH, 2 * ROWS, 256), v32(KV, ROWS), v32(KV, ROWS),
+            pltpu.SemaphoreType.DMA((5,)), pltpu.SemaphoreType.DMA((3,)),
         ],
         compiler_params=pltpu.CompilerParams(vmem_limit_bytes=VMEM_LIMIT),
         cost_estimate=pl.CostEstimate(flops=4_000_000_000, bytes_accessed=15_000_000, transcendentals=2_000_000),
         name="backward_last" if last else "backward_layer",
-    )(info, upstream, kept, proj, w_qkv, w_out, dproj, ups)
+    )(place, upstream, kept, proj, ctx, marks, w_qkv, w_out, dproj, ups)
 
 
 LAYERS = 8
@@ -379,10 +390,11 @@
     out_parts = gather_ring(row, 8, send_z)
     return pl.pallas_call(
         assemble_kernel,
-        out_shape=(bf16(D, WCOLS), bf16(HQ, D)),
+        out_shape=(v16(D, WCOLS), v16(HQ, D)),
         in_specs=[SMEM] + [ANY] * 14,
-        out_specs=(ANY, ANY),
+        out_specs=(INSIDE, INSIDE),
         scratch_shapes=[pltpu.SemaphoreType.DMA((64,))],
+        compiler_params=pltpu.CompilerParams(vmem_limit_bytes=4 * 1024 * 1024),
         cost_estimate=pl.CostEstimate(flops=0, bytes_accessed=21_000_000, transcendentals=0),
         name="assemble",
     )(jnp.stack([x, z]), *qkv_parts, *out_parts)
@@ -416,25 +428,23 @@
     block = lax.dynamic_index_in_dim(cotangent, micro, 0, keepdims=False)
     upstream = jnp.concatenate([lax.ppermute(block, "core", [(0, 1)]), block])
 
-    def info(layer):
-        return jnp.stack([(stage == layer).astype(jnp.int32), flag])
-
+    place = jnp.stack([stage, flag])
     normed = jnp.zeros((ROWS, D), jnp.bfloat16)
     kept = jnp.zeros((ROWS, D), jnp.bfloat16)
     proj = jnp.zeros((ROWS, WCOLS), jnp.bfloat16)
     ctx = jnp.zeros((ROWS, HQ), jnp.bfloat16)
+    marks = jnp.zeros((ROWS, HQ), jnp.bfloat16)
     for layer in range(LAYERS):
-        final = layer == LAYERS - 1
-        result, normed, proj, ctx, kept = forward_layer(
-            final, info(layer), hidden, full_qkv, full_out, normed, proj, ctx, kept
+        result, normed, proj, ctx, kept, marks = forward_layer(
+            layer, place, hidden, full_qkv, full_out, normed, proj, ctx, kept, marks
         )
-        if not final:
+        if layer < LAYERS - 1:
             hidden = lax.ppermute(result, STAGE, [(layer, layer + 1)])
     dproj = jnp.zeros((ROWS, WCOLS), jnp.bfloat16)
     ups = jnp.zeros((ROWS, D), jnp.bfloat16)
     for layer in reversed(range(LAYERS)):
         result, dproj, ups = backward_layer(
-            layer == 0, info(layer), upstream, kept, proj, full_qkv, full_out, dproj, ups
+            layer, place, upstream, kept, proj, ctx, marks, full_qkv, full_out, dproj, ups
         )
         if layer:
             upstream = lax.ppermute(result, STAGE, [(layer, layer - 1)])

time: 941 us -> 571 us (0.61)
  Pallas kernels: 358 us -> 72 us
  waiting for transfers between devices: 380 us -> 314 us
  starting transfers between devices: 143 us -> 129 us
    pallas_call x17, Pallas kernels: 358 us -> 72 us  [the longest x8 34.1 us: forward_layer(): pl.pallas_call(functools.partial(forward_kernel, final, layer), out_shape...]
    ppermute x7, waiting for transfers between devices: 286 us -> 217 us  [on_device(): upstream = lax.ppermute(result, STAGE, [(layer, layer - 1)])]
  transfers between devices with their start and end apart: 68 -> 68, of which waited for: 36 -> 33; matrix products, arithmetic and copies ran while one was open for 4% -> 5% of each run, Pallas kernels for 0% -> 0%
where the time goes in v3:
time: 571 us; the launch traced here: 561 us
  waiting for transfers between devices  314 us (55%)
  starting transfers between devices  129 us (23%)
  Pallas kernels  72 us (13%)
  local copies, waits for them, and re-layouts  24.5 us (4%)
  other arithmetic  16.8 us (3%)
    ppermute x7, waiting for transfers between devices, on_device(): upstream = lax.ppermute(result, STAGE, [(layer, layer - 1)])  217 us
    ppermute x32, waiting for transfers between devices, send_z(): lax.ppermute(value, ('zlo', 'zhi'), [(z_index(i), z_index((i + step) % 8)...  76.9 us
    ppermute x32, starting transfers between devices, send_z(): lax.ppermute(value, ('zlo', 'zhi'), [(z_index(i), z_index((i + step) % 8)...  52.6 us
    pallas_call x8, Pallas kernels, forward_layer(): pl.pallas_call(functools.partial(forward_kernel, final, layer), out_shape...  34.1 us
    pallas_call x8, Pallas kernels, backward_layer(): pl.pallas_call(functools.partial(backward_kernel, last, layer), out_shape...  30.6 us
    ppermute x16, starting transfers between devices, send_x(): return lax.ppermute(value, 'x', [(i, (i + step) % 4) for i in range(4)])  28.1 us
    ppermute x1, starting transfers between devices, on_device(): upstream = jnp.concatenate([lax.ppermute(block, 'core', [(0, 1)]), block])  24.2 us
    unnamed x50, local copies, waits for them, and re-layouts  16.1 us
  transfers between devices with their start and end apart: 68, of which 33 were waited for; matrix products, arithmetic and copies ran while one was open for 5% of the time, Pallas kernels for 0%

profile of v3, /device:TPU:32, one launch (start us, length us, event | category | flops | bytes accessed | tf_op | source)
XLA Modules:
  0.0 561.0 jit_solution(2860403527499568723)
XLA Ops:
  0.6 4.8 collective-permute-start.14
  8.2 2.8 collective-permute-start.15
  18.0 3.3 collective-permute-start.18
  27.4 4.1 collective-permute-start.4
  32.6 6.2 %collective-permute-done.7 = bf16[64,1536]{1,0:T(8,128)(2,1)S(1)} collective-permute-done((bf16[64,1536]{1,0:T(8,128)(2,1)S(1)}, bf16[64,1536]{1,0:T(8,128)(2,1)S(1)}, u32[]{:S(2)}, u32[]{:S(2)}) %collective-permute-start.7) | collective-permute-done | bytes 196640 | tf_op jit(solution)/shard_map/ppermute | solution.py:327
  39.0 3.3 collective-permute-start.9
  52.5 2.8 collective-permute-start.19
  56.1 7.6 %collective-permute-done.22.refs_13_ = bf16[128,2048]{1,0:T(8,128)(2,1)S(1)} collective-permute-done((bf16[128,2048]{1,0:T(8,128)(2,1)S(1)}, bf16[128,2048]{1,0:T(8,128)(2,1)S(1)}, u32[]{:S(2)}, u32[]{:S(2)}) %collective-permute-start.22) | collective-permute-done | bytes 524320 | tf_op jit(solution)/shard_map/ppermute | solution.py:327
  68.0 8.9 %collective-permute-done.23.refs_12_ = bf16[128,2048]{1,0:T(8,128)(2,1)} collective-permute-done((bf16[128,2048]{1,0:T(8,128)(2,1)S(1)}, bf16[128,2048]{1,0:T(8,128)(2,1)}, u32[]{:S(2)}, u32[]{:S(2)}) %collective-permute-start.23) | collective-permute-done | bytes 524320 | tf_op jit(solution)/shard_map/ppermute | solution.py:327
  100.3 3.2 collective-permute-done.26.refs_10_
  103.5 7.3 %assemble.1 = (bf16[2048,1536]{1,0:T(8,128)(2,1)S(1)}, bf16[1024,2048]{1,0:T(8,128)(2,1)S(1)}) custom-call(s32[2]{0:T(128)S(1)} %pad_add_fusion.1.place, bf16[512,1536]{1,0:T(8,128)(2,1)} %constant_dynamic-update-slice_fusion.refs_0_, bf16[512,1536]{1,0:T(8,128)(2,1)} %collective-permute-done.10.refs_1_, bf16[256,1536]{1,0:T(8,128)(2,1)} %collective-permute-done.12.refs_2_, ...), custom_call_target="tpu_custom_call" | custom-call | bytes 21000000 | tf_op jit(solution)/shard_map/assemble/pallas_call | solution.py:391
  113.8 13.5 %forward_layer.7 = (bf16[256,2048]{1,0:T(8,128)(2,1)S(1)}, bf16[256,2048]{1,0:T(8,128)(2,1)S(1)}, bf16[256,1536]{1,0:T(8,128)(2,1)S(1)}, bf16[256,1024]{1,0:T(8,...) custom-call(s32[2]{0:T(128)S(1)} %pad_add_fusion.place, ...), custom_call_target="tpu_custom_call", output_to_operand_aliasing={{1}: (4, {}), {2}: (5, {}), {3}: (6, {}), {4}: (7, {}), {5}... | custom-call | flops 3000000000 | bytes 14000000 | tf_op jit(solution)/shard_map/forward_layer/pallas_call | solution.py:181
  130.9 3.0 forward_layer.8
  134.7 2.9 forward_layer.9
  138.3 2.9 forward_layer.10
  141.9 2.9 forward_layer.11
  145.6 3.1 forward_layer.12
  149.4 3.0 forward_layer.13
  153.2 24.2 %collective-permute-start.34 = (bf16[128,2048]{1,0:T(8,128)(2,1)S(1)}, bf16[128,2048]{1,0:T(8,128)(2,1)S(1)}, u32[]{:S(2)}, u32[]{:S(2)}) collective-permute-start(bf16[128,2048]{1,0:T(8,128)(2,1)S(1)} %dynamic-slice_bitcast_fusion.6), channel_id=1, source_target_pairs={{0,1},{2,3},{4,5},{6,7},{8,9},{10,11},{12,13},{14,15},{16,17},{18,... | collective-permute-start | bytes 1572872 | tf_op jit(solution)/shard_map/ppermute | solution.py:429
  179.0 2.9 forward_last.1
  182.0 3.1 backward_layer.7
  185.8 3.3 backward_layer.8
  189.9 2.9 backward_layer.9
  193.5 2.9 backward_layer.10
  197.1 2.9 backward_layer.11
  200.8 3.0 backward_layer.12
  204.6 2.9 backward_layer.13
  210.7 216.8 %collective-permute-done.41.u_in = bf16[256,2048]{1,0:T(8,128)(2,1)} collective-permute-done((bf16[256,2048]{1,0:T(8,128)(2,1)}, bf16[256,2048]{1,0:T(8,128)(2,1)}, u32[]{:S(2)}, u32[]{:S(2)}) %collective-permute-start.41) | collective-permute-done | bytes 1048608 | tf_op jit(solution)/shard_map/ppermute | solution.py:450
  432.1 9.7 %backward_last.1 = (bf16[256,2048]{1,0:T(8,128)(2,1)}, bf16[256,1536]{1,0:T(8,128)(2,1)S(1)}, bf16[256,2048]{1,0:T(8,128)(2,1)S(1)}) custom-call(s32[2]{0:T(128)S(1)} %pad_add_fusion.place, bf16[256,2048]{1,0:T(8,128)(2,1)} %collective-permute-done.41.u_in, ...), custom_call_target="tpu_custom_call", output_to_operand_aliasing={{1}: (8, {}), {2}: (9, {})} | custom-call | flops 4000000000 | bytes 15000000 | tf_op jit(solution)/shard_map/backward_last/pallas_call | solution.py:285
  447.6 4.8 collective-permute-done.55
  452.6 2.8 collective-permute-start.56
  456.8 3.2 collective-permute-start.44
  460.7 5.3 collective-permute-done.56
  472.2 5.8 %collective-permute-done.57 = bf16[4,32,2048]{2,1,0:T(8,128)(2,1)S(1)} collective-permute-done((bf16[4,32,2048]{2,1,0:T(8,128)(2,1)S(1)}, bf16[4,32,2048]{2,1,0:T(8,128)(2,1)S(1)}, u32[]{:S(2)}, u32[]{:S(2)}) %collective-permute-start.57) | collective-permute-done | bytes 524320 | tf_op jit(solution)/shard_map/ppermute | solution.py:327
  480.4 3.2 collective-permute-start.61
  485.1 3.2 collective-permute-start.45
  488.3 6.6 %collective-permute-done.61 = bf16[4,32,2048]{2,1,0:T(8,128)(2,1)S(1)} collective-permute-done((bf16[4,32,2048]{2,1,0:T(8,128)(2,1)S(1)}, bf16[4,32,2048]{2,1,0:T(8,128)(2,1)S(1)}, u32[]{:S(2)}, u32[]{:S(2)}) %collective-permute-start.61) | collective-permute-done | bytes 524320 | tf_op jit(solution)/shard_map/ppermute | solution.py:327
  498.4 7.0 %collective-permute-done.62 = bf16[4,32,2048]{2,1,0:T(8,128)(2,1)S(1)} collective-permute-done((bf16[4,32,2048]{2,1,0:T(8,128)(2,1)S(1)}, bf16[4,32,2048]{2,1,0:T(8,128)(2,1)S(1)}, u32[]{:S(2)}, u32[]{:S(2)}) %collective-permute-start.62) | collective-permute-done | bytes 524320 | tf_op jit(solution)/shard_map/ppermute | solution.py:327
  506.8 3.2 collective-permute-start.65
  513.0 2.9 fusion.1
  518.3 3.4 collective-permute-done.46
  524.4 3.5 collective-permute-done.47
  527.9 3.4 collective-permute-start.48
  531.4 3.5 collective-permute-done.48
  535.0 3.3 collective-permute-start.52
  538.3 5.7 %collective-permute-start.66 = (bf16[32,2048]{1,0:T(8,128)(2,1)S(1)}, bf16[32,2048]{1,0:T(8,128)(2,1)S(1)}, u32[]{:S(2)}, u32[]{:S(2)}) collective-permute-start(bf16[32,2048]{1,0:T(8,128)(2,1)S(1)} %pad_maximum_fusion.9), channel_id=1, source_target_pairs={{0,24},{8,0},{16,8},{24,16},{1,25},{9,1},{17,9},{25,17},{2,26},{10... | collective-permute-start | bytes 393224 | tf_op jit(solution)/shard_map/ppermute | solution.py:323
  551.8 4.0 collective-permute-done.67
  556.5 3.3 collective-permute-done.54
  (209 shorter events, 120.8 us)
Async XLA Ops:
  0.6 7.6 %collective-permute-start.14 = (bf16[32,2048]{1,0:T(8,128)(2,1)}, bf16[32,2048]{1,0:T(8,128)(2,1)S(1)}, u32[]{:S(2)}, u32[]{:S(2)}) collective-permute-start(bf16[32,2048]{1,0:T(8,128)(2,1)} %bitcast.172), channel_id=1, source_target_pairs={{0,0},{1,128},{2,2},{3,130},{4,4},{5,132},{6,6},{7,134},{8,8},{9,1... | collective-permute-start | bytes 393224 | tf_op jit(solution)/shard_map/ppermute | solution.py:424
  5.4 7.2 %collective-permute-start.1 = (bf16[64,1536]{1,0:T(8,128)(2,1)}, bf16[64,1536]{1,0:T(8,128)(2,1)S(1)}, u32[]{:S(2)}, u32[]{:S(2)}) collective-permute-start(bf16[64,1536]{1,0:T(8,128)(2,1)} %bitcast.171), channel_id=1, source_target_pairs={{0,0},{1,128},{2,2},{3,130},{4,4},{5,132},{6,6},{7,134},{8,8},{9,1... | collective-permute-start | bytes 589832 | tf_op jit(solution)/shard_map/ppermute | solution.py:423
  8.2 9.7 %collective-permute-start.15 = (bf16[32,2048]{1,0:T(8,128)(2,1)S(1)}, bf16[32,2048]{1,0:T(8,128)(2,1)S(1)}, u32[]{:S(2)}, u32[]{:S(2)}) collective-permute-start(bf16[32,2048]{1,0:T(8,128)(2,1)S(1)} %collective-permute-done.14), channel_id=1, source_target_pairs={{0,24},{8,0},{16,8},{24,16},{1,25},{9,1},{17,9},{25,17},{2,26},{10... | collective-permute-start | bytes 393224 | tf_op jit(solution)/shard_map/ppermute | solution.py:323
  11.0 6.9 %collective-permute-start.16 = (bf16[32,2048]{1,0:T(8,128)(2,1)S(1)}, bf16[32,2048]{1,0:T(8,128)(2,1)S(1)}, u32[]{:S(2)}, u32[]{:S(2)}) collective-permute-start(bf16[32,2048]{1,0:T(8,128)(2,1)S(1)} %collective-permute-done.14), channel_id=1, source_target_pairs={{0,8},{8,16},{16,24},{24,0},{1,9},{9,17},{17,25},{25,1},{2,10},{10... | collective-permute-start | bytes 393224 | tf_op jit(solution)/shard_map/ppermute | solution.py:323
  12.6 8.6 %collective-permute-start.2 = (bf16[64,1536]{1,0:T(8,128)(2,1)S(1)}, bf16[64,1536]{1,0:T(8,128)(2,1)S(1)}, u32[]{:S(2)}, u32[]{:S(2)}) collective-permute-start(bf16[64,1536]{1,0:T(8,128)(2,1)S(1)} %collective-permute-done.1), channel_id=1, source_target_pairs={{0,134},{128,0},{2,128},{130,2},{4,130},{132,4},{6,132},{134,6},{1... | collective-permute-start | bytes 589832 | tf_op jit(solution)/shard_map/ppermute | solution.py:327
  12.6 11.6 %collective-permute-start.5 = (bf16[64,1536]{1,0:T(8,128)(2,1)S(1)}, bf16[64,1536]{1,0:T(8,128)(2,1)S(1)}, u32[]{:S(2)}, u32[]{:S(2)}) collective-permute-start(bf16[64,1536]{1,0:T(8,128)(2,1)S(1)} %collective-permute-done.1), channel_id=1, source_target_pairs={{0,128},{128,2},{2,130},{130,4},{4,132},{132,6},{6,134},{134,0},{1... | collective-permute-start | bytes 589832 | tf_op jit(solution)/shard_map/ppermute | solution.py:327
  17.9 33.4 %collective-permute-start.17 = (bf16[16,2048]{1,0:T(8,128)(2,1)S(1)}, bf16[16,2048]{1,0:T(8,128)(2,1)S(1)}, u32[]{:S(2)}, u32[]{:S(2)}) collective-permute-start(bf16[16,2048]{1,0:T(8,128)(2,1)S(1)} %slice.60), channel_id=1, source_target_pairs={{0,8},{8,16},{16,24},{24,0},{1,9},{9,17},{17,25},{25,1},{2,10},{10... | collective-permute-start | bytes 196616 | tf_op jit(solution)/shard_map/ppermute | solution.py:323
  18.0 33.4 %collective-permute-start.18 = (bf16[16,2048]{1,0:T(8,128)(2,1)S(1)}, bf16[16,2048]{1,0:T(8,128)(2,1)S(1)}, u32[]{:S(2)}, u32[]{:S(2)}) collective-permute-start(bf16[16,2048]{1,0:T(8,128)(2,1)S(1)} %slice.61), channel_id=1, source_target_pairs={{0,24},{8,0},{16,8},{24,16},{1,25},{9,1},{17,9},{25,17},{2,26},{10... | collective-permute-start | bytes 196616 | tf_op jit(solution)/shard_map/ppermute | solution.py:323
  24.3 7.7 %collective-permute-start.6 = (bf16[64,1536]{1,0:T(8,128)(2,1)S(1)}, bf16[64,1536]{1,0:T(8,128)(2,1)S(1)}, u32[]{:S(2)}, u32[]{:S(2)}) collective-permute-start(bf16[64,1536]{1,0:T(8,128)(2,1)S(1)} %collective-permute-done.5), channel_id=1, source_target_pairs={{0,128},{128,2},{2,130},{130,4},{4,132},{132,6},{6,134},{134,0},{1... | collective-permute-start | bytes 589832 | tf_op jit(solution)/shard_map/ppermute | solution.py:327
  27.4 11.5 %collective-permute-start.4 = (bf16[64,1536]{1,0:T(8,128)(2,1)S(1)}, bf16[64,1536]{1,0:T(8,128)(2,1)S(1)}, u32[]{:S(2)}, u32[]{:S(2)}) collective-permute-start(bf16[64,1536]{1,0:T(8,128)(2,1)S(1)} %collective-permute-done.3), channel_id=1, source_target_pairs={{0,134},{128,0},{2,128},{130,2},{4,130},{132,4},{6,132},{134,6},{1... | collective-permute-start | bytes 589832 | tf_op jit(solution)/shard_map/ppermute | solution.py:327
  31.9 6.9 %collective-permute-start.7 = (bf16[64,1536]{1,0:T(8,128)(2,1)S(1)}, bf16[64,1536]{1,0:T(8,128)(2,1)S(1)}, u32[]{:S(2)}, u32[]{:S(2)}) collective-permute-start(bf16[64,1536]{1,0:T(8,128)(2,1)S(1)} %collective-permute-done.6), channel_id=1, source_target_pairs={{0,128},{128,2},{2,130},{130,4},{4,132},{132,6},{6,134},{134,0},{1... | collective-permute-start | bytes 589832 | tf_op jit(solution)/shard_map/ppermute | solution.py:327
  48.1 33.6 %collective-permute-start.11 = (bf16[512,1536]{1,0:T(8,128)(2,1)}, bf16[512,1536]{1,0:T(8,128)(2,1)S(1)}, u32[]{:S(2)}, u32[]{:S(2)}) collective-permute-start(bf16[512,1536]{1,0:T(8,128)(2,1)} %constant_dynamic-update-slice_fusion.refs_0_), channel_id=1, source_target_pairs={{0,8},{8,16},{16,24},{24,0},{1,9},{9,17},{17,25},{25,1},{2,10},{10... | collective-permute-start | bytes 4718600 | tf_op jit(solution)/shard_map/ppermute | solution.py:323
  49.1 34.5 %collective-permute-start.10 = (bf16[512,1536]{1,0:T(8,128)(2,1)}, bf16[512,1536]{1,0:T(8,128)(2,1)}, u32[]{:S(2)}, u32[]{:S(2)}) collective-permute-start(bf16[512,1536]{1,0:T(8,128)(2,1)} %constant_dynamic-update-slice_fusion.refs_0_), channel_id=1, source_target_pairs={{0,24},{8,0},{16,8},{24,16},{1,25},{9,1},{17,9},{25,17},{2,26},{10... | collective-permute-start | bytes 4718600 | tf_op jit(solution)/shard_map/ppermute | solution.py:323
  51.4 12.3 %collective-permute-start.22 = (bf16[128,2048]{1,0:T(8,128)(2,1)S(1)}, bf16[128,2048]{1,0:T(8,128)(2,1)S(1)}, u32[]{:S(2)}, u32[]{:S(2)}) collective-permute-start(bf16[128,2048]{1,0:T(8,128)(2,1)S(1)} %constant_dynamic-update-slice_fusion.9.refs_5_), channel_id=1, source_target_pairs={{0,128},{128,2},{2,130},{130,4},{4,132},{132,6},{6,134},{134,0},{1... | collective-permute-start | bytes 1572872 | tf_op jit(solution)/shard_map/ppermute | solution.py:327
  52.5 13.5 %collective-permute-start.19 = (bf16[128,2048]{1,0:T(8,128)(2,1)S(1)}, bf16[128,2048]{1,0:T(8,128)(2,1)}, u32[]{:S(2)}, u32[]{:S(2)}) collective-permute-start(bf16[128,2048]{1,0:T(8,128)(2,1)S(1)} %constant_dynamic-update-slice_fusion.9.refs_5_), channel_id=1, source_target_pairs={{0,134},{128,0},{2,128},{130,2},{4,130},{132,4},{6,132},{134,6},{1... | collective-permute-start | bytes 1572872 | tf_op jit(solution)/shard_map/ppermute | solution.py:327
  63.7 13.2 %collective-permute-start.23 = (bf16[128,2048]{1,0:T(8,128)(2,1)S(1)}, bf16[128,2048]{1,0:T(8,128)(2,1)}, u32[]{:S(2)}, u32[]{:S(2)}) collective-permute-start(bf16[128,2048]{1,0:T(8,128)(2,1)S(1)} %collective-permute-done.22.refs_13_), channel_id=1, source_target_pairs={{0,128},{128,2},{2,130},{130,4},{4,132},{132,6},{6,134},{134,0},{1... | collective-permute-start | bytes 1572872 | tf_op jit(solution)/shard_map/ppermute | solution.py:327
  66.0 12.7 %collective-permute-start.20 = (bf16[128,2048]{1,0:T(8,128)(2,1)}, bf16[128,2048]{1,0:T(8,128)(2,1)}, u32[]{:S(2)}, u32[]{:S(2)}) collective-permute-start(bf16[128,2048]{1,0:T(8,128)(2,1)} %collective-permute-done.19.refs_6_), channel_id=1, source_target_pairs={{0,134},{128,0},{2,128},{130,2},{4,130},{132,4},{6,132},{134,6},{1... | collective-permute-start | bytes 1572872 | tf_op jit(solution)/shard_map/ppermute | solution.py:327
  76.9 13.9 %collective-permute-start.24 = (bf16[128,2048]{1,0:T(8,128)(2,1)}, bf16[128,2048]{1,0:T(8,128)(2,1)S(1)}, u32[]{:S(2)}, u32[]{:S(2)}) collective-permute-start(bf16[128,2048]{1,0:T(8,128)(2,1)} %collective-permute-done.23.refs_12_), channel_id=1, source_target_pairs={{0,128},{128,2},{2,130},{130,4},{4,132},{132,6},{6,134},{134,0},{1... | collective-permute-start | bytes 1572872 | tf_op jit(solution)/shard_map/ppermute | solution.py:327
  78.8 14.5 %collective-permute-start.21 = (bf16[128,2048]{1,0:T(8,128)(2,1)}, bf16[128,2048]{1,0:T(8,128)(2,1)}, u32[]{:S(2)}, u32[]{:S(2)}) collective-permute-start(bf16[128,2048]{1,0:T(8,128)(2,1)} %collective-permute-done.20.refs_7_), channel_id=1, source_target_pairs={{0,134},{128,0},{2,128},{130,2},{4,130},{132,4},{6,132},{134,6},{1... | collective-permute-start | bytes 1572872 | tf_op jit(solution)/shard_map/ppermute | solution.py:327
  82.7 20.9 %collective-permute-start.12 = (bf16[256,1536]{1,0:T(8,128)(2,1)}, bf16[256,1536]{1,0:T(8,128)(2,1)}, u32[]{:S(2)}, u32[]{:S(2)}) collective-permute-start(bf16[256,1536]{1,0:T(8,128)(2,1)} %slice.58), channel_id=1, source_target_pairs={{0,8},{8,16},{16,24},{24,0},{1,9},{9,17},{17,25},{25,1},{2,10},{10... | collective-permute-start | bytes 2359304 | tf_op jit(solution)/shard_map/ppermute | solution.py:323
  85.6 17.9 %collective-permute-start.13 = (bf16[256,1536]{1,0:T(8,128)(2,1)}, bf16[256,1536]{1,0:T(8,128)(2,1)}, u32[]{:S(2)}, u32[]{:S(2)}) collective-permute-start(bf16[256,1536]{1,0:T(8,128)(2,1)} %slice.59), channel_id=1, source_target_pairs={{0,24},{8,0},{16,8},{24,16},{1,25},{9,1},{17,9},{25,17},{2,26},{10... | collective-permute-start | bytes 2359304 | tf_op jit(solution)/shard_map/ppermute | solution.py:323
  88.8 7.4 %collective-permute-start = (bf16[128,2048]{1,0:T(8,128)(2,1)}, bf16[128,2048]{1,0:T(8,128)(2,1)}, u32[]{:S(2)}, u32[]{:S(2)}) collective-permute-start(bf16[128,2048]{1,0:T(8,128)(2,1)} %dynamic-slice_bitcast_fusion.7), channel_id=1, source_target_pairs={{1,0},{3,2},{5,4},{7,6},{9,8},{11,10},{13,12},{15,14},{17,16},{19,... | collective-permute-start | bytes 1572872 | tf_op jit(solution)/shard_map/ppermute | solution.py:427
  90.8 9.4 %collective-permute-start.25 = (bf16[64,2048]{1,0:T(8,128)(2,1)S(1)}, bf16[64,2048]{1,0:T(8,128)(2,1)S(1)}, u32[]{:S(2)}, u32[]{:S(2)}) collective-permute-start(bf16[64,2048]{1,0:T(8,128)(2,1)S(1)} %slice.62), channel_id=1, source_target_pairs={{0,128},{128,2},{2,130},{130,4},{4,132},{132,6},{6,134},{134,0},{1... | collective-permute-start | bytes 786440 | tf_op jit(solution)/shard_map/ppermute | solution.py:327
  94.2 9.3 %collective-permute-start.26 = (bf16[64,2048]{1,0:T(8,128)(2,1)S(1)}, bf16[64,2048]{1,0:T(8,128)(2,1)S(1)}, u32[]{:S(2)}, u32[]{:S(2)}) collective-permute-start(bf16[64,2048]{1,0:T(8,128)(2,1)S(1)} %slice.63), channel_id=1, source_target_pairs={{0,134},{128,0},{2,128},{130,2},{4,130},{132,4},{6,132},{134,6},{1... | collective-permute-start | bytes 786440 | tf_op jit(solution)/shard_map/ppermute | solution.py:327
  152.4 26.6 %collective-permute-start.33 = (bf16[256,2048]{1,0:T(8,128)(2,1)S(1)}, bf16[256,2048]{1,0:T(8,128)(2,1)S(1)}, u32[]{:S(2)}, u32[]{:S(2)}) collective-permute-start(bf16[256,2048]{1,0:T(8,128)(2,1)S(1)} %get-tuple-element.112), channel_id=1, source_target_pairs={{96,97},{98,99},{100,101},{102,103},{104,105},{106,107},{108,109},... | collective-permute-start | bytes 3145736 | tf_op jit(solution)/shard_map/ppermute | solution.py:442
  153.2 25.7 %collective-permute-start.34 = (bf16[128,2048]{1,0:T(8,128)(2,1)S(1)}, bf16[128,2048]{1,0:T(8,128)(2,1)S(1)}, u32[]{:S(2)}, u32[]{:S(2)}) collective-permute-start(bf16[128,2048]{1,0:T(8,128)(2,1)S(1)} %dynamic-slice_bitcast_fusion.6), channel_id=1, source_target_pairs={{0,1},{2,3},{4,5},{6,7},{8,9},{10,11},{12,13},{14,15},{16,17},{18,... | collective-permute-start | bytes 1572872 | tf_op jit(solution)/shard_map/ppermute | solution.py:429
  209.4 218.2 %collective-permute-start.41 = (bf16[256,2048]{1,0:T(8,128)(2,1)}, bf16[256,2048]{1,0:T(8,128)(2,1)}, u32[]{:S(2)}, u32[]{:S(2)}) collective-permute-start(bf16[256,2048]{1,0:T(8,128)(2,1)} %get-tuple-element.141), channel_id=1, source_target_pairs={{1,0},{3,2},{5,4},{7,6},{9,8},{11,10},{13,12},{15,14},{17,16},{19,... | collective-permute-start | bytes 3145736 | tf_op jit(solution)/shard_map/ppermute | solution.py:450
  443.3 9.1 %collective-permute-start.55 = (bf16[2,32,2048]{2,1,0:T(8,128)(2,1)S(1)}, bf16[2,32,2048]{2,1,0:T(8,128)(2,1)S(1)}, u32[]{:S(2)}, u32[]{:S(2)}) collective-permute-start(bf16[2,32,2048]{2,1,0:T(8,128)(2,1)S(1)} %get-tuple-element.156), channel_id=1, source_target_pairs={{0,128},{128,2},{2,130},{130,4},{4,132},{132,6},{6,134},{134,0},{1... | collective-permute-start | bytes 786440 | tf_op jit(solution)/shard_map/ppermute | solution.py:327
  445.7 6.7 %collective-permute-start.59 = (bf16[2,32,2048]{2,1,0:T(8,128)(2,1)S(1)}, bf16[2,32,2048]{2,1,0:T(8,128)(2,1)S(1)}, u32[]{:S(2)}, u32[]{:S(2)}) collective-permute-start(bf16[2,32,2048]{2,1,0:T(8,128)(2,1)S(1)} %get-tuple-element.158), channel_id=1, source_target_pairs={{0,134},{128,0},{2,128},{130,2},{4,130},{132,4},{6,132},{134,6},{1... | collective-permute-start | bytes 786440 | tf_op jit(solution)/shard_map/ppermute | solution.py:327
  452.6 13.4 %collective-permute-start.56 = (bf16[4,32,2048]{2,1,0:T(8,128)(2,1)S(1)}, bf16[4,32,2048]{2,1,0:T(8,128)(2,1)}, u32[]{:S(2)}, u32[]{:S(2)}) collective-permute-start(bf16[4,32,2048]{2,1,0:T(8,128)(2,1)S(1)} %pad_maximum_fusion.4), channel_id=1, source_target_pairs={{0,128},{128,2},{2,130},{130,4},{4,132},{132,6},{6,134},{134,0},{1... | collective-permute-start | bytes 1572872 | tf_op jit(solution)/shard_map/ppermute | solution.py:327
  456.8 13.4 %collective-permute-start.42 = (bf16[256,1536]{1,0:T(8,128)(2,1)}, bf16[256,1536]{1,0:T(8,128)(2,1)S(1)}, u32[]{:S(2)}, u32[]{:S(2)}) collective-permute-start(bf16[256,1536]{1,0:T(8,128)(2,1)} %get-tuple-element.148), channel_id=1, source_target_pairs={{0,8},{8,16},{16,24},{24,0},{1,9},{9,17},{17,25},{25,1},{2,10},{10... | collective-permute-start | bytes 2359304 | tf_op jit(solution)/shard_map/ppermute | solution.py:323
  456.8 13.4 %collective-permute-start.44 = (bf16[256,1536]{1,0:T(8,128)(2,1)}, bf16[256,1536]{1,0:T(8,128)(2,1)}, u32[]{:S(2)}, u32[]{:S(2)}) collective-permute-start(bf16[256,1536]{1,0:T(8,128)(2,1)} %get-tuple-element.150), channel_id=1, source_target_pairs={{0,24},{8,0},{16,8},{24,16},{1,25},{9,1},{17,9},{25,17},{2,26},{10... | collective-permute-start | bytes 2359304 | tf_op jit(solution)/shard_map/ppermute | solution.py:323
  460.1 12.1 %collective-permute-start.60 = (bf16[4,32,2048]{2,1,0:T(8,128)(2,1)S(1)}, bf16[4,32,2048]{2,1,0:T(8,128)(2,1)S(1)}, u32[]{:S(2)}, u32[]{:S(2)}) collective-permute-start(bf16[4,32,2048]{2,1,0:T(8,128)(2,1)S(1)} %pad_maximum_fusion.5), channel_id=1, source_target_pairs={{0,134},{128,0},{2,128},{130,2},{4,130},{132,4},{6,132},{134,6},{1... | collective-permute-start | bytes 1572872 | tf_op jit(solution)/shard_map/ppermute | solution.py:327
  467.3 10.7 %collective-permute-start.57 = (bf16[4,32,2048]{2,1,0:T(8,128)(2,1)S(1)}, bf16[4,32,2048]{2,1,0:T(8,128)(2,1)S(1)}, u32[]{:S(2)}, u32[]{:S(2)}) collective-permute-start(bf16[4,32,2048]{2,1,0:T(8,128)(2,1)S(1)} %fusion.6), channel_id=1, source_target_pairs={{0,128},{128,2},{2,130},{130,4},{4,132},{132,6},{6,134},{134,0},{1... | collective-permute-start | bytes 1572872 | tf_op jit(solution)/shard_map/ppermute | solution.py:327
  480.4 14.5 %collective-permute-start.61 = (bf16[4,32,2048]{2,1,0:T(8,128)(2,1)S(1)}, bf16[4,32,2048]{2,1,0:T(8,128)(2,1)S(1)}, u32[]{:S(2)}, u32[]{:S(2)}) collective-permute-start(bf16[4,32,2048]{2,1,0:T(8,128)(2,1)S(1)} %get-tuple-element.153), channel_id=1, source_target_pairs={{0,134},{128,0},{2,128},{130,2},{4,130},{132,4},{6,132},{134,6},{1... | collective-permute-start | bytes 1572872 | tf_op jit(solution)/shard_map/ppermute | solution.py:327
  483.8 28.5 %collective-permute-start.43 = (bf16[512,1536]{1,0:T(8,128)(2,1)S(1)}, bf16[512,1536]{1,0:T(8,128)(2,1)}, u32[]{:S(2)}, u32[]{:S(2)}) collective-permute-start(bf16[512,1536]{1,0:T(8,128)(2,1)S(1)} %pad_maximum_fusion), channel_id=1, source_target_pairs={{0,8},{8,16},{16,24},{24,0},{1,9},{9,17},{17,25},{25,1},{2,10},{10... | collective-permute-start | bytes 4718600 | tf_op jit(solution)/shard_map/ppermute | solution.py:323
  485.1 27.9 %collective-permute-start.45 = (bf16[512,1536]{1,0:T(8,128)(2,1)}, bf16[512,1536]{1,0:T(8,128)(2,1)}, u32[]{:S(2)}, u32[]{:S(2)}) collective-permute-start(bf16[512,1536]{1,0:T(8,128)(2,1)} %pad_maximum_fusion.1), channel_id=1, source_target_pairs={{0,24},{8,0},{16,8},{24,16},{1,25},{9,1},{17,9},{25,17},{2,26},{10... | collective-permute-start | bytes 4718600 | tf_op jit(solution)/shard_map/ppermute | solution.py:323
  488.3 10.1 %collective-permute-start.58 = (bf16[4,32,2048]{2,1,0:T(8,128)(2,1)}, bf16[4,32,2048]{2,1,0:T(8,128)(2,1)S(1)}, u32[]{:S(2)}, u32[]{:S(2)}) collective-permute-start(bf16[4,32,2048]{2,1,0:T(8,128)(2,1)} %get-tuple-element.152), channel_id=1, source_target_pairs={{0,128},{128,2},{2,130},{130,4},{4,132},{132,6},{6,134},{134,0},{1... | collective-permute-start | bytes 1572872 | tf_op jit(solution)/shard_map/ppermute | solution.py:327
  496.1 9.3 %collective-permute-start.62 = (bf16[4,32,2048]{2,1,0:T(8,128)(2,1)S(1)}, bf16[4,32,2048]{2,1,0:T(8,128)(2,1)S(1)}, u32[]{:S(2)}, u32[]{:S(2)}) collective-permute-start(bf16[4,32,2048]{2,1,0:T(8,128)(2,1)S(1)} %fusion.5), channel_id=1, source_target_pairs={{0,134},{128,0},{2,128},{130,2},{4,130},{132,4},{6,132},{134,6},{1... | collective-permute-start | bytes 1572872 | tf_op jit(solution)/shard_map/ppermute | solution.py:327
  506.7 11.6 %collective-permute-start.63 = (bf16[16,2048]{1,0:T(8,128)(2,1)S(1)}, bf16[16,2048]{1,0:T(8,128)(2,1)S(1)}, u32[]{:S(2)}, u32[]{:S(2)}) collective-permute-start(bf16[16,2048]{1,0:T(8,128)(2,1)S(1)} %get-tuple-element.170), channel_id=1, source_target_pairs={{0,8},{8,16},{16,24},{24,0},{1,9},{9,17},{17,25},{25,1},{2,10},{10... | collective-permute-start | bytes 196616 | tf_op jit(solution)/shard_map/ppermute | solution.py:323
  506.8 11.5 %collective-permute-start.65 = (bf16[16,2048]{1,0:T(8,128)(2,1)S(1)}, bf16[16,2048]{1,0:T(8,128)(2,1)S(1)}, u32[]{:S(2)}, u32[]{:S(2)}) collective-permute-start(bf16[16,2048]{1,0:T(8,128)(2,1)S(1)} %get-tuple-element.172), channel_id=1, source_target_pairs={{0,24},{8,0},{16,8},{24,16},{1,25},{9,1},{17,9},{25,17},{2,26},{10... | collective-permute-start | bytes 196616 | tf_op jit(solution)/shard_map/ppermute | solution.py:323
  523.9 7.5 %collective-permute-start.51 = (bf16[64,1536]{1,0:T(8,128)(2,1)S(1)}, bf16[64,1536]{1,0:T(8,128)(2,1)S(1)}, u32[]{:S(2)}, u32[]{:S(2)}) collective-permute-start(bf16[64,1536]{1,0:T(8,128)(2,1)S(1)} %pad_maximum_fusion.7), channel_id=1, source_target_pairs={{0,134},{128,0},{2,128},{130,2},{4,130},{132,4},{6,132},{134,6},{1... | collective-permute-start | bytes 589832 | tf_op jit(solution)/shard_map/ppermute | solution.py:327
  527.9 7.0 %collective-permute-start.48 = (bf16[64,1536]{1,0:T(8,128)(2,1)S(1)}, bf16[64,1536]{1,0:T(8,128)(2,1)S(1)}, u32[]{:S(2)}, u32[]{:S(2)}) collective-permute-start(bf16[64,1536]{1,0:T(8,128)(2,1)S(1)} %fusion.14), channel_id=1, source_target_pairs={{0,128},{128,2},{2,130},{130,4},{4,132},{132,6},{6,134},{134,0},{1... | collective-permute-start | bytes 589832 | tf_op jit(solution)/shard_map/ppermute | solution.py:327
  531.3 14.8 %collective-permute-start.64 = (bf16[32,2048]{1,0:T(8,128)(2,1)S(1)}, bf16[32,2048]{1,0:T(8,128)(2,1)S(1)}, u32[]{:S(2)}, u32[]{:S(2)}) collective-permute-start(bf16[32,2048]{1,0:T(8,128)(2,1)S(1)} %pad_maximum_fusion.8), channel_id=1, source_target_pairs={{0,8},{8,16},{16,24},{24,0},{1,9},{9,17},{17,25},{25,1},{2,10},{10... | collective-permute-start | bytes 393224 | tf_op jit(solution)/shard_map/ppermute | solution.py:323
  535.0 9.0 %collective-permute-start.52 = (bf16[64,1536]{1,0:T(8,128)(2,1)S(1)}, bf16[64,1536]{1,0:T(8,128)(2,1)S(1)}, u32[]{:S(2)}, u32[]{:S(2)}) collective-permute-start(bf16[64,1536]{1,0:T(8,128)(2,1)S(1)} %get-tuple-element.161), channel_id=1, source_target_pairs={{0,134},{128,0},{2,128},{130,2},{4,130},{132,4},{6,132},{134,6},{1... | collective-permute-start | bytes 589832 | tf_op jit(solution)/shard_map/ppermute | solution.py:327
  538.3 8.2 %collective-permute-start.66 = (bf16[32,2048]{1,0:T(8,128)(2,1)S(1)}, bf16[32,2048]{1,0:T(8,128)(2,1)S(1)}, u32[]{:S(2)}, u32[]{:S(2)}) collective-permute-start(bf16[32,2048]{1,0:T(8,128)(2,1)S(1)} %pad_maximum_fusion.9), channel_id=1, source_target_pairs={{0,24},{8,0},{16,8},{24,16},{1,25},{9,1},{17,9},{25,17},{2,26},{10... | collective-permute-start | bytes 393224 | tf_op jit(solution)/shard_map/ppermute | solution.py:323
  546.5 9.3 %collective-permute-start.67 = (bf16[32,2048]{1,0:T(8,128)(2,1)S(1)}, bf16[32,2048]{1,0:T(8,128)(2,1)S(1)}, u32[]{:S(2)}, u32[]{:S(2)}) collective-permute-start(bf16[32,2048]{1,0:T(8,128)(2,1)S(1)} %fusion.19), channel_id=1, source_target_pairs={{0,0},{128,1},{2,2},{130,3},{4,4},{132,5},{6,6},{134,7},{8,8},{136... | collective-permute-start | bytes 393224 | tf_op jit(solution)/shard_map/ppermute | solution.py:456
  549.9 10.0 %collective-permute-start.54 = (bf16[64,1536]{1,0:T(8,128)(2,1)S(1)}, bf16[64,1536]{1,0:T(8,128)(2,1)S(1)}, u32[]{:S(2)}, u32[]{:S(2)}) collective-permute-start(bf16[64,1536]{1,0:T(8,128)(2,1)S(1)} %fusion.17), channel_id=1, source_target_pairs={{0,0},{128,1},{2,2},{130,3},{4,4},{132,5},{6,6},{134,7},{8,8},{136... | collective-permute-start | bytes 589832 | tf_op jit(solution)/shard_map/ppermute | solution.py:457
  (39 other events, 331.5 us)

commit v4 on v3

--- a/solution.py
+++ b/solution.py
@@ -24,7 +24,7 @@
 SCALE = 1.0 / math.sqrt(HEAD)
 TO_EXP2 = SCALE * math.log2(math.e)
 NT = (((1,), (1,)), ((), ()))
-VMEM_LIMIT = 40 * 1024 * 1024
+VMEM_LIMIT = 16 * 1024 * 1024
 ANY = pl.BlockSpec(memory_space=pl.ANY)
 SMEM = pl.BlockSpec(memory_space=pltpu.SMEM)
 INSIDE = pl.BlockSpec(memory_space=pltpu.VMEM)
@@ -86,28 +86,21 @@
 
 
 def forward_kernel(
-    final, layer, place, h_in, wq_v, wo_v, a0, a1, a2, a3, a4,
-    h_out, normed_out, proj_out, ctx_out, keep_out, marks_out,
-    h_v, normed_v, proj_v, ctx_v, out_v, marks_v, key_s, value_s, in_sem, w_sem,
+    final, layer, place, h_v, wq_v, wo_v, a0, a1, a2, a3, a4,
+    out_v, normed_v, proj_v, ctx_v, keep_v, marks_v, key_s, value_s,
 ):
     del a0, a1, a2, a3, a4
 
     @pl.when(place[0] == layer)
     def _():
-        h_copy = pltpu.make_async_copy(h_in, h_v, in_sem)
-        h_copy.start()
         block = (lax.broadcasted_iota(jnp.int32, (2 * ROWS, 128), 0) // HALF) % 2
         lane = lax.broadcasted_iota(jnp.int32, (2 * ROWS, 128), 1)
         spot = lane % HEAD
         seen = jnp.where(jnp.logical_or(jnp.logical_and(lane == 3, block == 0), jnp.logical_and(lane == 4, block == 1)), 1.0, 0.0)
-        h_copy.wait()
-        keep = pltpu.make_async_copy(h_v, keep_out, w_sem.at[0])
-        keep.start()
+        keep_v[...] = h_v[...]
         wide = h_v[...].astype(jnp.float32)
         scale = lax.rsqrt(jnp.mean(wide * wide, axis=-1, keepdims=True) + EPS)
         normed_v[...] = (wide * scale).astype(jnp.bfloat16)
-        normed_copy = pltpu.make_async_copy(normed_v, normed_out, w_sem.at[1])
-        normed_copy.start()
         both = dot_nn(normed_v[...], wq_v[:, HQ:]).astype(jnp.bfloat16)
         proj_v[:, HQ:] = both
         fill_keys(both[:, :KV], key_s, place[1])
@@ -139,14 +132,6 @@
             return carry
 
         lax.fori_loop(0, KVH, group, 0)
-        copies = [
-            pltpu.make_async_copy(proj_v, proj_out, w_sem.at[2]),
-            pltpu.make_async_copy(ctx_v, ctx_out, w_sem.at[3]),
-            pltpu.make_async_copy(marks_v, marks_out, w_sem.at[5]),
-        ]
-        for copy in copies:
-            copy.start()
-
         def finish(i, carry):
             c = cols(i * CHUNK, CHUNK)
             out = h_v[:, c].astype(jnp.float32) + dot_nn(ctx_v[...], wo_v[:, c])
@@ -155,17 +140,14 @@
 
         if not final:
             lax.fori_loop(0, 8, finish, 0)
-            out_copy = pltpu.make_async_copy(out_v, h_out, w_sem.at[4])
-            out_copy.start()
-            out_copy.wait()
-        keep.wait()
-        normed_copy.wait()
-        for copy in copies:
-            copy.wait()
 
 
 def bf16(*shape):
     return jax.ShapeDtypeStruct(shape, jnp.bfloat16)
+
+
+def inside(*arrays):
+    return [pltpu.with_memory_space_constraint(array, pltpu.VMEM) for array in arrays]
 
 
 def v16(*shape):
@@ -180,51 +162,28 @@
     final = layer == 7
     return pl.pallas_call(
         functools.partial(forward_kernel, final, layer),
-        out_shape=(
-            bf16(ROWS, D), bf16(ROWS, D), bf16(ROWS, WCOLS), bf16(ROWS, HQ), bf16(ROWS, D), bf16(ROWS, HQ)
-        ),
-        in_specs=[SMEM, ANY, INSIDE, INSIDE] + [ANY] * 5,
-        out_specs=(ANY,) * 6,
+        out_shape=(v16(ROWS, D), v16(ROWS, D), v16(ROWS, WCOLS), v16(ROWS, HQ), v16(ROWS, D), v16(ROWS, HQ)),
+        in_specs=[SMEM] + [INSIDE] * 8,
+        out_specs=(INSIDE,) * 6,
         input_output_aliases={4: 1, 5: 2, 6: 3, 7: 4, 8: 5},
-        scratch_shapes=[
-            v16(ROWS, D), v16(ROWS, D), v16(ROWS, WCOLS), v16(ROWS, HQ), v16(ROWS, D), v16(ROWS, HQ),
-            v16(KVH, 2 * ROWS, 256), v16(KVH, 2 * ROWS, 256),
-            pltpu.SemaphoreType.DMA, pltpu.SemaphoreType.DMA((6,)),
-        ],
+        scratch_shapes=[v16(KVH, 2 * ROWS, 256), v16(KVH, 2 * ROWS, 256)],
         compiler_params=pltpu.CompilerParams(vmem_limit_bytes=VMEM_LIMIT),
         cost_estimate=pl.CostEstimate(flops=3_000_000_000, bytes_accessed=14_000_000, transcendentals=2_000_000),
         name="forward_last" if final else "forward_layer",
-    )(place, hidden, w_qkv, w_out, normed, proj, ctx, kept, marks)
+    )(place, *inside(hidden, w_qkv, w_out, normed, proj, ctx, kept, marks))
 
 
 def backward_kernel(
-    last, layer, place, u_in, h_in, proj_in, ctx_in, marks_in, wq_v, wo_v, a0, a1,
-    up_out, dproj_out, keep_out,
-    u_v, h_v, proj_v, ctx_v, marks_v, dproj_v, dn_v, key_s, value_s, dkt_s, dvt_s, in_sem, w_sem,
+    last, layer, place, u_v, h_v, proj_v, ctx_v, marks_v, wq_v, wo_v, a0, a1,
+    up_v, dproj_v, keep_v, dn_v, key_s, value_s, dkt_s, dvt_s,
 ):
     del a0, a1
 
     @pl.when(place[0] == layer)
     def _():
-        u_copy = pltpu.make_async_copy(u_in, u_v, in_sem.at[0])
-        u_copy.start()
-        proj_copy = pltpu.make_async_copy(proj_in, proj_v, in_sem.at[1])
-        h_copy = pltpu.make_async_copy(h_in, h_v, in_sem.at[2])
-        ctx_copy = pltpu.make_async_copy(ctx_in, ctx_v, in_sem.at[3])
-        marks_copy = pltpu.make_async_copy(marks_in, marks_v, in_sem.at[4])
-        proj_copy.start()
-        ctx_copy.start()
-        marks_copy.start()
-        if not last:
-            h_copy.start()
-        proj_copy.wait()
+        keep_v[...] = u_v[...]
         fill_keys(proj_v[:, HQ : HQ + KV], key_s, place[1])
         fill_values(proj_v[:, HQ + KV :], value_s, -1.0)
-        u_copy.wait()
-        keep = pltpu.make_async_copy(u_v, keep_out, w_sem.at[0])
-        keep.start()
-        ctx_copy.wait()
-        marks_copy.wait()
 
         def group(g, carry):
             c = cols(g * CHUNK, CHUNK)
@@ -248,11 +207,7 @@
         lax.fori_loop(0, KVH, group, 0)
         dproj_v[:, HQ : HQ + KV] = dkt_s[...].T.astype(jnp.bfloat16)
         dproj_v[:, HQ + KV :] = dvt_s[...].T.astype(jnp.bfloat16)
-        dproj_copy = pltpu.make_async_copy(dproj_v, dproj_out, w_sem.at[1])
-        dproj_copy.start()
         if not last:
-            h_copy.wait()
-
             def widen(i, partial):
                 c = cols(i * CHUNK, CHUNK)
                 d_normed = dot_nt(dproj_v[...], wq_v[c, :])
@@ -269,34 +224,29 @@
             def previous(i, carry):
                 c = cols(i * CHUNK, CHUNK)
                 out = u_v[:, c].astype(jnp.float32) + (scale * dn_v[:, c] - h_v[:, c].astype(jnp.float32) * pull)
-                h_v[:, c] = out.astype(jnp.bfloat16)
+                up_v[:, c] = out.astype(jnp.bfloat16)
                 return carry
 
             lax.fori_loop(0, 8, previous, 0)
-            up_copy = pltpu.make_async_copy(h_v, up_out, w_sem.at[2])
-            up_copy.start()
-            up_copy.wait()
-        keep.wait()
-        dproj_copy.wait()
 
 
 def backward_layer(layer, place, upstream, kept, proj, ctx, marks, w_qkv, w_out, dproj, ups):
     last = layer == 0
+    spare = [place, place] if last else inside(kept, w_qkv)
+    where = SMEM if last else INSIDE
     return pl.pallas_call(
         functools.partial(backward_kernel, last, layer),
-        out_shape=(bf16(ROWS, D), bf16(ROWS, WCOLS), bf16(ROWS, D)),
-        in_specs=[SMEM] + [ANY] * 5 + [INSIDE, INSIDE] + [ANY] * 2,
-        out_specs=(ANY,) * 3,
+        out_shape=(v16(ROWS, D), v16(ROWS, WCOLS), v16(ROWS, D)),
+        in_specs=[SMEM, INSIDE, where, INSIDE, INSIDE, INSIDE, where, INSIDE, INSIDE, INSIDE],
+        out_specs=(INSIDE,) * 3,
         input_output_aliases={8: 1, 9: 2},
         scratch_shapes=[
-            v16(ROWS, D), v16(ROWS, D), v16(ROWS, WCOLS), v16(ROWS, HQ), v16(ROWS, HQ), v16(ROWS, WCOLS), v32(ROWS, D),
-            v16(KVH, 2 * ROWS, 256), v16(KVH, 2 * ROWS, 256), v32(KV, ROWS), v32(KV, ROWS),
-            pltpu.SemaphoreType.DMA((5,)), pltpu.SemaphoreType.DMA((3,)),
+            v32(ROWS, D), v16(KVH, 2 * ROWS, 256), v16(KVH, 2 * ROWS, 256), v32(KV, ROWS), v32(KV, ROWS)
         ],
         compiler_params=pltpu.CompilerParams(vmem_limit_bytes=VMEM_LIMIT),
         cost_estimate=pl.CostEstimate(flops=4_000_000_000, bytes_accessed=15_000_000, transcendentals=2_000_000),
         name="backward_last" if last else "backward_layer",
-    )(place, upstream, kept, proj, ctx, marks, w_qkv, w_out, dproj, ups)
+    )(place, *inside(upstream), spare[0], *inside(proj, ctx, marks), spare[1], *inside(w_out, dproj, ups))
 
 
 LAYERS = 8
@@ -400,17 +350,17 @@
     )(jnp.stack([x, z]), *qkv_parts, *out_parts)
 
 
-def scatter_qkv(part, x, z):
+def scatter_qkv(part, turns, spins):
     part = part.reshape(4, 512, WCOLS)
-    mine = scatter_ring(lambda d: lax.dynamic_index_in_dim(part, (x + d) % 4, 0, keepdims=False), 4, send_x, 0)
+    mine = scatter_ring(lambda d: lax.dynamic_index_in_dim(part, turns[d % 4], 0, keepdims=False, allow_negative_indices=False), 4, send_x, 0)
     mine = mine.reshape(8, 64, WCOLS)
-    return scatter_ring(lambda d: lax.dynamic_index_in_dim(mine, (z + d) % 8, 0, keepdims=False), 8, send_z, 0)
-
-
-def scatter_out(part, x, z):
+    return scatter_ring(lambda d: lax.dynamic_index_in_dim(mine, spins[d % 8], 0, keepdims=False, allow_negative_indices=False), 8, send_z, 0)
+
+
+def scatter_out(part, turns, spins):
     part = part.reshape(4, 8, 32, D)
-    mine = scatter_ring(lambda d: lax.dynamic_index_in_dim(part, (z + d) % 8, 1, keepdims=False), 8, send_z, 0)
-    return scatter_ring(lambda d: lax.dynamic_index_in_dim(mine, (x + d) % 4, 0, keepdims=False), 4, send_x, 0)
+    mine = scatter_ring(lambda d: lax.dynamic_index_in_dim(part, spins[d % 8], 1, keepdims=False, allow_negative_indices=False), 8, send_z, 0)
+    return scatter_ring(lambda d: lax.dynamic_index_in_dim(mine, turns[d % 4], 0, keepdims=False, allow_negative_indices=False), 4, send_x, 0)
 
 
 def on_device(inputs, cotangent, joined, w_qkv, w_out):
@@ -429,6 +379,9 @@
     upstream = jnp.concatenate([lax.ppermute(block, "core", [(0, 1)]), block])
 
     place = jnp.stack([stage, flag])
+    turns = [((x_index + d) % 4) for d in range(4)]
+    spins = [((z_place + d) % 8) for d in range(8)]
+    place, turns, spins = lax.optimization_barrier((place, turns, spins))
     normed = jnp.zeros((ROWS, D), jnp.bfloat16)
     kept = jnp.zeros((ROWS, D), jnp.bfloat16)
     proj = jnp.zeros((ROWS, WCOLS), jnp.bfloat16)
@@ -448,11 +401,12 @@
         )
         if layer:
             upstream = lax.ppermute(result, STAGE, [(layer, layer - 1)])
+    ups, dproj, turns, spins = lax.optimization_barrier((ups, dproj, turns, spins))
     contract = (((0,), (0,)), ((), ()))
     part_out = lax.dot_general(ctx, ups, contract, preferred_element_type=jnp.float32).astype(jnp.bfloat16)
     part_qkv = lax.dot_general(normed, dproj, contract, preferred_element_type=jnp.float32).astype(jnp.bfloat16)
-    grad_out = scatter_out(part_out, x_index, z_place)
-    grad_qkv = scatter_qkv(part_qkv, x_index, z_place)
+    grad_out = scatter_out(part_out, turns, spins)
+    grad_qkv = scatter_qkv(part_qkv, turns, spins)
     grad_out = lax.ppermute(grad_out, NAMES, regroup(True)).astype(jnp.float32)
     grad_qkv = lax.ppermute(grad_qkv, NAMES, regroup(True)).astype(jnp.float32)
     return (grad_qkv[None], grad_out[None])

time: 571 us -> 529 us (0.926)
  Pallas kernels: 72 us -> 35.7 us
    pallas_call x8, Pallas kernels: 34.1 us -> 14.8 us  [forward_layer(): pl.pallas_call(functools.partial(forward_kernel, final, layer), out_shape...]
    pallas_call x8, Pallas kernels: 30.6 us -> 13.6 us  [backward_layer(): pl.pallas_call(functools.partial(backward_kernel, last, layer), out_shape...]
    ppermute x7, waiting for transfers between devices: 217 us -> 210 us  [on_device(): upstream = lax.ppermute(result, STAGE, [(layer, layer - 1)])]
  transfers between devices with their start and end apart: 68 -> 68, of which waited for: 33 -> 34; matrix products, arithmetic and copies ran while one was open for 5% -> 5% of each run, Pallas kernels for 0% -> 0%
where the time goes in v4:
time: 529 us; the launch traced here: 518 us
  waiting for transfers between devices  313 us (59%)
  starting transfers between devices  127 us (24%)
  Pallas kernels  35.7 us (7%)
  local copies, waits for them, and re-layouts  24.6 us (5%)
  other arithmetic  11.8 us (2%)
    ppermute x7, waiting for transfers between devices, on_device(): upstream = lax.ppermute(result, STAGE, [(layer, layer - 1)])  210 us
    ppermute x32, waiting for transfers between devices, send_z(): lax.ppermute(value, ('zlo', 'zhi'), [(z_index(i), z_index((i + step) % 8)...  82.3 us
    ppermute x32, starting transfers between devices, send_z(): lax.ppermute(value, ('zlo', 'zhi'), [(z_index(i), z_index((i + step) % 8)...  50.2 us
    ppermute x16, starting transfers between devices, send_x(): return lax.ppermute(value, 'x', [(i, (i + step) % 4) for i in range(4)])  29.4 us
    ppermute x1, starting transfers between devices, on_device(): upstream = jnp.concatenate([lax.ppermute(block, 'core', [(0, 1)]), block])  21.2 us
    unnamed x50, local copies, waits for them, and re-layouts  17.5 us
    pallas_call x8, Pallas kernels, forward_layer(): pl.pallas_call(functools.partial(forward_kernel, final, layer), out_shape...  14.8 us
    pallas_call x8, Pallas kernels, backward_layer(): pl.pallas_call(functools.partial(backward_kernel, last, layer), out_shape...  13.6 us
  transfers between devices with their start and end apart: 68, of which 34 were waited for; matrix products, arithmetic and copies ran while one was open for 5% of the time, Pallas kernels for 0%

profile of v4, /device:TPU:32, one launch (start us, length us, event | category | flops | bytes accessed | tf_op | source)
XLA Modules:
  0.0 518.4 jit_solution(5870248095465461276)
XLA Ops:
  0.6 4.8 collective-permute-start.14
  5.4 2.4 collective-permute-start.1
  8.2 2.8 collective-permute-start.15
  15.4 2.6 collective-permute-done.16
  18.0 3.3 collective-permute-start.18
  21.3 2.5 collective-permute-start.3
  25.0 2.4 collective-permute-done.3
  27.4 4.1 collective-permute-start.4
  32.6 6.2 %collective-permute-done.7 = bf16[64,1536]{1,0:T(8,128)(2,1)S(1)} collective-permute-done((bf16[64,1536]{1,0:T(8,128)(2,1)S(1)}, bf16[64,1536]{1,0:T(8,128)(2,1)S(1)}, u32[]{:S(2)}, u32[]{:S(2)}) %collective-permute-start.7) | collective-permute-done | bytes 196640 | tf_op jit(solution)/shard_map/ppermute | solution.py:277
  39.0 3.3 collective-permute-start.9
  49.1 2.2 collective-permute-start.10
  52.5 2.5 collective-permute-start.19
  55.8 7.9 %collective-permute-done.22.refs_13_ = bf16[128,2048]{1,0:T(8,128)(2,1)S(1)} collective-permute-done((bf16[128,2048]{1,0:T(8,128)(2,1)S(1)}, bf16[128,2048]{1,0:T(8,128)(2,1)S(1)}, u32[]{:S(2)}, u32[]{:S(2)}) %collective-permute-start.22) | collective-permute-done | bytes 524320 | tf_op jit(solution)/shard_map/ppermute | solution.py:277
  68.0 8.9 %collective-permute-done.23.refs_12_ = bf16[128,2048]{1,0:T(8,128)(2,1)} collective-permute-done((bf16[128,2048]{1,0:T(8,128)(2,1)S(1)}, bf16[128,2048]{1,0:T(8,128)(2,1)}, u32[]{:S(2)}, u32[]{:S(2)}) %collective-permute-start.23) | collective-permute-done | bytes 524320 | tf_op jit(solution)/shard_map/ppermute | solution.py:277
  79.0 2.7 collective-permute-start.21
  85.6 2.4 collective-permute-start.13
  91.5 2.4 collective-permute-start.25
  97.7 3.5 collective-permute-done.25.refs_9_
  101.2 3.0 collective-permute-done.26.refs_10_
  106.2 7.3 %assemble.1 = (bf16[2048,1536]{1,0:T(8,128)(2,1)S(1)}, bf16[1024,2048]{1,0:T(8,128)(2,1)S(1)}) custom-call(s32[2]{0:T(128)S(1)} %pad_add_fusion.1.place, bf16[512,1536]{1,0:T(8,128)(2,1)} %constant_dynamic-update-slice_fusion.refs_0_, bf16[512,1536]{1,0:T(8,128)(2,1)} %collective-permute-done.10.refs_1_, bf16[256,1536]{1,0:T(8,128)(2,1)} %collective-permute-done.12.refs_2_, ...), custom_call_target="tpu_custom_call" | custom-call | bytes 21000000 | tf_op jit(solution)/shard_map/assemble/pallas_call | solution.py:341
  114.0 9.6 %forward_layer.7 = (bf16[256,2048]{1,0:T(8,128)(2,1)S(1)}, bf16[256,2048]{1,0:T(8,128)(2,1)S(1)}, bf16[256,1536]{1,0:T(8,128)(2,1)S(1)}, bf16[256,1024]{1,0:T(8,...) custom-call(s32[2]{0:T(128)S(1)} %pad_add_fusion.place.h_v.wq_v, ...), custom_call_target="tpu_custom_call", output_to_operand_aliasing={{1}: (4, {}), {2}: (5, {}), {3}: (6, {}), {4}: (7, {}), {5}... | custom-call | flops 3000000000 | bytes 14000000 | tf_op jit(solution)/shard_map/forward_layer/pallas_call | solution.py:163
  124.9 2.2 collective-permute-done.27.h_v
  133.3 3.3 collective-permute-start.32
  138.0 21.2 %collective-permute-start.34 = (bf16[128,2048]{1,0:T(8,128)(2,1)S(1)}, bf16[128,2048]{1,0:T(8,128)(2,1)S(1)}, u32[]{:S(2)}, u32[]{:S(2)}) collective-permute-start(bf16[128,2048]{1,0:T(8,128)(2,1)S(1)} %dynamic-slice_bitcast_fusion.6), channel_id=1, source_target_pairs={{0,1},{2,3},{4,5},{6,7},{8,9},{10,11},{12,13},{14,15},{16,17},{18,... | collective-permute-start | bytes 1572872 | tf_op jit(solution)/shard_map/ppermute | solution.py:379
  175.3 209.6 %collective-permute-done.41.u_v = bf16[256,2048]{1,0:T(8,128)(2,1)} collective-permute-done((bf16[256,2048]{1,0:T(8,128)(2,1)}, bf16[256,2048]{1,0:T(8,128)(2,1)}, u32[]{:S(2)}, u32[]{:S(2)}) %collective-permute-start.41) | collective-permute-done | bytes 1048608 | tf_op jit(solution)/shard_map/ppermute | solution.py:403
  389.5 8.5 %backward_last.1 = (bf16[256,2048]{1,0:T(8,128)(2,1)}, bf16[256,1536]{1,0:T(8,128)(2,1)S(1)}, bf16[256,2048]{1,0:T(8,128)(2,1)S(1)}) custom-call(s32[2]{0:T(128)S(1)} %pad_add_fusion.place.h_v.wq_v, bf16[256,2048]{1,0:T(8,128)(2,1)} %collective-permute-done.41.u_v, s32[2]{0:T(128)S(1)} %pad_add_fusion.place.h_v.wq_v, ...), custom_call_target="tpu_custom_call", output_to_operand_aliasing={{1}: (8, {}), {2}: (9, {})} | custom-call | flops 4000000000 | bytes 15000000 | tf_op jit(solution)/shard_map/backward_last/pallas_call | solution.py:237
  399.9 2.5 convolution_convert_fusion.1
  402.6 2.4 collective-permute-start.55
  406.8 4.4 collective-permute-done.55
  411.5 2.4 collective-permute-start.56
  414.2 3.2 collective-permute-start.44
  418.6 6.9 %collective-permute-done.56 = bf16[4,32,2048]{2,1,0:T(8,128)(2,1)S(1)} collective-permute-done((bf16[4,32,2048]{2,1,0:T(8,128)(2,1)S(1)}, bf16[4,32,2048]{2,1,0:T(8,128)(2,1)S(1)}, u32[]{:S(2)}, u32[]{:S(2)}) %collective-permute-start.56) | collective-permute-done | bytes 524320 | tf_op jit(solution)/shard_map/ppermute | solution.py:277
  427.8 8.5 %collective-permute-done.57 = bf16[4,32,2048]{2,1,0:T(8,128)(2,1)S(1)} collective-permute-done((bf16[4,32,2048]{2,1,0:T(8,128)(2,1)S(1)}, bf16[4,32,2048]{2,1,0:T(8,128)(2,1)S(1)}, u32[]{:S(2)}, u32[]{:S(2)}) %collective-permute-start.57) | collective-permute-done | bytes 524320 | tf_op jit(solution)/shard_map/ppermute | solution.py:277
  437.5 3.2 collective-permute-start.61
  442.2 3.2 collective-permute-start.45
  445.6 6.2 %collective-permute-done.61 = bf16[4,32,2048]{2,1,0:T(8,128)(2,1)S(1)} collective-permute-done((bf16[4,32,2048]{2,1,0:T(8,128)(2,1)S(1)}, bf16[4,32,2048]{2,1,0:T(8,128)(2,1)S(1)}, u32[]{:S(2)}, u32[]{:S(2)}) %collective-permute-start.61) | collective-permute-done | bytes 524320 | tf_op jit(solution)/shard_map/ppermute | solution.py:277
  452.0 2.3 collective-permute-start.62
  455.0 6.2 %collective-permute-done.62 = bf16[4,32,2048]{2,1,0:T(8,128)(2,1)S(1)} collective-permute-done((bf16[4,32,2048]{2,1,0:T(8,128)(2,1)S(1)}, bf16[4,32,2048]{2,1,0:T(8,128)(2,1)S(1)}, u32[]{:S(2)}, u32[]{:S(2)}) %collective-permute-start.62) | collective-permute-done | bytes 524320 | tf_op jit(solution)/shard_map/ppermute | solution.py:277
  462.7 3.2 collective-permute-start.65
  465.9 4.3 collective-permute-done.43
  470.9 2.9 fusion.1
  476.0 3.6 collective-permute-done.46
  482.1 3.5 collective-permute-done.47
  489.0 4.2 collective-permute-done.48
  493.3 2.7 collective-permute-start.52
  496.0 5.5 %collective-permute-start.66 = (bf16[32,2048]{1,0:T(8,128)(2,1)S(1)}, bf16[32,2048]{1,0:T(8,128)(2,1)S(1)}, u32[]{:S(2)}, u32[]{:S(2)}) collective-permute-start(bf16[32,2048]{1,0:T(8,128)(2,1)S(1)} %pad_maximum_fusion.9), channel_id=1, source_target_pairs={{0,24},{8,0},{16,8},{24,16},{1,25},{9,1},{17,9},{25,17},{2,26},{10... | collective-permute-start | bytes 393224 | tf_op jit(solution)/shard_map/ppermute | solution.py:273
  509.4 4.0 collective-permute-done.67
  514.1 3.3 collective-permute-done.54
  (209 shorter events, 96.4 us)
Async XLA Ops:
  0.6 7.6 %collective-permute-start.14 = (bf16[32,2048]{1,0:T(8,128)(2,1)}, bf16[32,2048]{1,0:T(8,128)(2,1)S(1)}, u32[]{:S(2)}, u32[]{:S(2)}) collective-permute-start(bf16[32,2048]{1,0:T(8,128)(2,1)} %bitcast.172), channel_id=1, source_target_pairs={{0,0},{1,128},{2,2},{3,130},{4,4},{5,132},{6,6},{7,134},{8,8},{9,1... | collective-permute-start | bytes 393224 | tf_op jit(solution)/shard_map/ppermute | solution.py:374
  5.4 7.2 %collective-permute-start.1 = (bf16[64,1536]{1,0:T(8,128)(2,1)}, bf16[64,1536]{1,0:T(8,128)(2,1)S(1)}, u32[]{:S(2)}, u32[]{:S(2)}) collective-permute-start(bf16[64,1536]{1,0:T(8,128)(2,1)} %bitcast.171), channel_id=1, source_target_pairs={{0,0},{1,128},{2,2},{3,130},{4,4},{5,132},{6,6},{7,134},{8,8},{9,1... | collective-permute-start | bytes 589832 | tf_op jit(solution)/shard_map/ppermute | solution.py:373
  8.2 9.7 %collective-permute-start.15 = (bf16[32,2048]{1,0:T(8,128)(2,1)S(1)}, bf16[32,2048]{1,0:T(8,128)(2,1)S(1)}, u32[]{:S(2)}, u32[]{:S(2)}) collective-permute-start(bf16[32,2048]{1,0:T(8,128)(2,1)S(1)} %collective-permute-done.14), channel_id=1, source_target_pairs={{0,24},{8,0},{16,8},{24,16},{1,25},{9,1},{17,9},{25,17},{2,26},{10... | collective-permute-start | bytes 393224 | tf_op jit(solution)/shard_map/ppermute | solution.py:273
  11.0 6.9 %collective-permute-start.16 = (bf16[32,2048]{1,0:T(8,128)(2,1)S(1)}, bf16[32,2048]{1,0:T(8,128)(2,1)S(1)}, u32[]{:S(2)}, u32[]{:S(2)}) collective-permute-start(bf16[32,2048]{1,0:T(8,128)(2,1)S(1)} %collective-permute-done.14), channel_id=1, source_target_pairs={{0,8},{8,16},{16,24},{24,0},{1,9},{9,17},{17,25},{25,1},{2,10},{10... | collective-permute-start | bytes 393224 | tf_op jit(solution)/shard_map/ppermute | solution.py:273
  12.6 8.6 %collective-permute-start.2 = (bf16[64,1536]{1,0:T(8,128)(2,1)S(1)}, bf16[64,1536]{1,0:T(8,128)(2,1)S(1)}, u32[]{:S(2)}, u32[]{:S(2)}) collective-permute-start(bf16[64,1536]{1,0:T(8,128)(2,1)S(1)} %collective-permute-done.1), channel_id=1, source_target_pairs={{0,134},{128,0},{2,128},{130,2},{4,130},{132,4},{6,132},{134,6},{1... | collective-permute-start | bytes 589832 | tf_op jit(solution)/shard_map/ppermute | solution.py:277
  12.6 11.6 %collective-permute-start.5 = (bf16[64,1536]{1,0:T(8,128)(2,1)S(1)}, bf16[64,1536]{1,0:T(8,128)(2,1)S(1)}, u32[]{:S(2)}, u32[]{:S(2)}) collective-permute-start(bf16[64,1536]{1,0:T(8,128)(2,1)S(1)} %collective-permute-done.1), channel_id=1, source_target_pairs={{0,128},{128,2},{2,130},{130,4},{4,132},{132,6},{6,134},{134,0},{1... | collective-permute-start | bytes 589832 | tf_op jit(solution)/shard_map/ppermute | solution.py:277
  17.9 33.4 %collective-permute-start.17 = (bf16[16,2048]{1,0:T(8,128)(2,1)S(1)}, bf16[16,2048]{1,0:T(8,128)(2,1)S(1)}, u32[]{:S(2)}, u32[]{:S(2)}) collective-permute-start(bf16[16,2048]{1,0:T(8,128)(2,1)S(1)} %slice.60), channel_id=1, source_target_pairs={{0,8},{8,16},{16,24},{24,0},{1,9},{9,17},{17,25},{25,1},{2,10},{10... | collective-permute-start | bytes 196616 | tf_op jit(solution)/shard_map/ppermute | solution.py:273
  18.0 33.4 %collective-permute-start.18 = (bf16[16,2048]{1,0:T(8,128)(2,1)S(1)}, bf16[16,2048]{1,0:T(8,128)(2,1)S(1)}, u32[]{:S(2)}, u32[]{:S(2)}) collective-permute-start(bf16[16,2048]{1,0:T(8,128)(2,1)S(1)} %slice.61), channel_id=1, source_target_pairs={{0,24},{8,0},{16,8},{24,16},{1,25},{9,1},{17,9},{25,17},{2,26},{10... | collective-permute-start | bytes 196616 | tf_op jit(solution)/shard_map/ppermute | solution.py:273
  24.3 7.7 %collective-permute-start.6 = (bf16[64,1536]{1,0:T(8,128)(2,1)S(1)}, bf16[64,1536]{1,0:T(8,128)(2,1)S(1)}, u32[]{:S(2)}, u32[]{:S(2)}) collective-permute-start(bf16[64,1536]{1,0:T(8,128)(2,1)S(1)} %collective-permute-done.5), channel_id=1, source_target_pairs={{0,128},{128,2},{2,130},{130,4},{4,132},{132,6},{6,134},{134,0},{1... | collective-permute-start | bytes 589832 | tf_op jit(solution)/shard_map/ppermute | solution.py:277
  27.4 11.5 %collective-permute-start.4 = (bf16[64,1536]{1,0:T(8,128)(2,1)S(1)}, bf16[64,1536]{1,0:T(8,128)(2,1)S(1)}, u32[]{:S(2)}, u32[]{:S(2)}) collective-permute-start(bf16[64,1536]{1,0:T(8,128)(2,1)S(1)} %collective-permute-done.3), channel_id=1, source_target_pairs={{0,134},{128,0},{2,128},{130,2},{4,130},{132,4},{6,132},{134,6},{1... | collective-permute-start | bytes 589832 | tf_op jit(solution)/shard_map/ppermute | solution.py:277
  31.9 6.9 %collective-permute-start.7 = (bf16[64,1536]{1,0:T(8,128)(2,1)S(1)}, bf16[64,1536]{1,0:T(8,128)(2,1)S(1)}, u32[]{:S(2)}, u32[]{:S(2)}) collective-permute-start(bf16[64,1536]{1,0:T(8,128)(2,1)S(1)} %collective-permute-done.6), channel_id=1, source_target_pairs={{0,128},{128,2},{2,130},{130,4},{4,132},{132,6},{6,134},{134,0},{1... | collective-permute-start | bytes 589832 | tf_op jit(solution)/shard_map/ppermute | solution.py:277
  39.0 6.4 %collective-permute-start.9 = (bf16[32,1536]{1,0:T(8,128)(2,1)S(1)}, bf16[32,1536]{1,0:T(8,128)(2,1)S(1)}, u32[]{:S(2)}, u32[]{:S(2)}) collective-permute-start(bf16[32,1536]{1,0:T(8,128)(2,1)S(1)} %slice.57), channel_id=1, source_target_pairs={{0,134},{128,0},{2,128},{130,2},{4,130},{132,4},{6,132},{134,6},{1... | collective-permute-start | bytes 294920 | tf_op jit(solution)/shard_map/ppermute | solution.py:277
  48.1 33.6 %collective-permute-start.11 = (bf16[512,1536]{1,0:T(8,128)(2,1)}, bf16[512,1536]{1,0:T(8,128)(2,1)S(1)}, u32[]{:S(2)}, u32[]{:S(2)}) collective-permute-start(bf16[512,1536]{1,0:T(8,128)(2,1)} %constant_dynamic-update-slice_fusion.refs_0_), channel_id=1, source_target_pairs={{0,8},{8,16},{16,24},{24,0},{1,9},{9,17},{17,25},{25,1},{2,10},{10... | collective-permute-start | bytes 4718600 | tf_op jit(solution)/shard_map/ppermute | solution.py:273
  49.1 34.5 %collective-permute-start.10 = (bf16[512,1536]{1,0:T(8,128)(2,1)}, bf16[512,1536]{1,0:T(8,128)(2,1)}, u32[]{:S(2)}, u32[]{:S(2)}) collective-permute-start(bf16[512,1536]{1,0:T(8,128)(2,1)} %constant_dynamic-update-slice_fusion.refs_0_), channel_id=1, source_target_pairs={{0,24},{8,0},{16,8},{24,16},{1,25},{9,1},{17,9},{25,17},{2,26},{10... | collective-permute-start | bytes 4718600 | tf_op jit(solution)/shard_map/ppermute | solution.py:273
  51.4 12.3 %collective-permute-start.22 = (bf16[128,2048]{1,0:T(8,128)(2,1)S(1)}, bf16[128,2048]{1,0:T(8,128)(2,1)S(1)}, u32[]{:S(2)}, u32[]{:S(2)}) collective-permute-start(bf16[128,2048]{1,0:T(8,128)(2,1)S(1)} %constant_dynamic-update-slice_fusion.9.refs_5_), channel_id=1, source_target_pairs={{0,128},{128,2},{2,130},{130,4},{4,132},{132,6},{6,134},{134,0},{1... | collective-permute-start | bytes 1572872 | tf_op jit(solution)/shard_map/ppermute | solution.py:277
  52.5 13.5 %collective-permute-start.19 = (bf16[128,2048]{1,0:T(8,128)(2,1)S(1)}, bf16[128,2048]{1,0:T(8,128)(2,1)}, u32[]{:S(2)}, u32[]{:S(2)}) collective-permute-start(bf16[128,2048]{1,0:T(8,128)(2,1)S(1)} %constant_dynamic-update-slice_fusion.9.refs_5_), channel_id=1, source_target_pairs={{0,134},{128,0},{2,128},{130,2},{4,130},{132,4},{6,132},{134,6},{1... | collective-permute-start | bytes 1572872 | tf_op jit(solution)/shard_map/ppermute | solution.py:277
  63.7 13.2 %collective-permute-start.23 = (bf16[128,2048]{1,0:T(8,128)(2,1)S(1)}, bf16[128,2048]{1,0:T(8,128)(2,1)}, u32[]{:S(2)}, u32[]{:S(2)}) collective-permute-start(bf16[128,2048]{1,0:T(8,128)(2,1)S(1)} %collective-permute-done.22.refs_13_), channel_id=1, source_target_pairs={{0,128},{128,2},{2,130},{130,4},{4,132},{132,6},{6,134},{134,0},{1... | collective-permute-start | bytes 1572872 | tf_op jit(solution)/shard_map/ppermute | solution.py:277
  66.0 13.0 %collective-permute-start.20 = (bf16[128,2048]{1,0:T(8,128)(2,1)}, bf16[128,2048]{1,0:T(8,128)(2,1)}, u32[]{:S(2)}, u32[]{:S(2)}) collective-permute-start(bf16[128,2048]{1,0:T(8,128)(2,1)} %collective-permute-done.19.refs_6_), channel_id=1, source_target_pairs={{0,134},{128,0},{2,128},{130,2},{4,130},{132,4},{6,132},{134,6},{1... | collective-permute-start | bytes 1572872 | tf_op jit(solution)/shard_map/ppermute | solution.py:277
  76.9 14.6 %collective-permute-start.24 = (bf16[128,2048]{1,0:T(8,128)(2,1)}, bf16[128,2048]{1,0:T(8,128)(2,1)S(1)}, u32[]{:S(2)}, u32[]{:S(2)}) collective-permute-start(bf16[128,2048]{1,0:T(8,128)(2,1)} %collective-permute-done.23.refs_12_), channel_id=1, source_target_pairs={{0,128},{128,2},{2,130},{130,4},{4,132},{132,6},{6,134},{134,0},{1... | collective-permute-start | bytes 1572872 | tf_op jit(solution)/shard_map/ppermute | solution.py:277
  79.0 14.9 %collective-permute-start.21 = (bf16[128,2048]{1,0:T(8,128)(2,1)}, bf16[128,2048]{1,0:T(8,128)(2,1)}, u32[]{:S(2)}, u32[]{:S(2)}) collective-permute-start(bf16[128,2048]{1,0:T(8,128)(2,1)} %collective-permute-done.20.refs_7_), channel_id=1, source_target_pairs={{0,134},{128,0},{2,128},{130,2},{4,130},{132,4},{6,132},{134,6},{1... | collective-permute-start | bytes 1572872 | tf_op jit(solution)/shard_map/ppermute | solution.py:277
  82.7 21.5 %collective-permute-start.12 = (bf16[256,1536]{1,0:T(8,128)(2,1)}, bf16[256,1536]{1,0:T(8,128)(2,1)}, u32[]{:S(2)}, u32[]{:S(2)}) collective-permute-start(bf16[256,1536]{1,0:T(8,128)(2,1)} %slice.58), channel_id=1, source_target_pairs={{0,8},{8,16},{16,24},{24,0},{1,9},{9,17},{17,25},{25,1},{2,10},{10... | collective-permute-start | bytes 2359304 | tf_op jit(solution)/shard_map/ppermute | solution.py:273
  85.6 18.5 %collective-permute-start.13 = (bf16[256,1536]{1,0:T(8,128)(2,1)}, bf16[256,1536]{1,0:T(8,128)(2,1)}, u32[]{:S(2)}, u32[]{:S(2)}) collective-permute-start(bf16[256,1536]{1,0:T(8,128)(2,1)} %slice.59), channel_id=1, source_target_pairs={{0,24},{8,0},{16,8},{24,16},{1,25},{9,1},{17,9},{25,17},{2,26},{10... | collective-permute-start | bytes 2359304 | tf_op jit(solution)/shard_map/ppermute | solution.py:273
  88.8 7.6 %collective-permute-start = (bf16[128,2048]{1,0:T(8,128)(2,1)}, bf16[128,2048]{1,0:T(8,128)(2,1)}, u32[]{:S(2)}, u32[]{:S(2)}) collective-permute-start(bf16[128,2048]{1,0:T(8,128)(2,1)} %dynamic-slice_bitcast_fusion.7), channel_id=1, source_target_pairs={{1,0},{3,2},{5,4},{7,6},{9,8},{11,10},{13,12},{15,14},{17,16},{19,... | collective-permute-start | bytes 1572872 | tf_op jit(solution)/shard_map/ppermute | solution.py:377
  91.5 9.7 %collective-permute-start.25 = (bf16[64,2048]{1,0:T(8,128)(2,1)S(1)}, bf16[64,2048]{1,0:T(8,128)(2,1)S(1)}, u32[]{:S(2)}, u32[]{:S(2)}) collective-permute-start(bf16[64,2048]{1,0:T(8,128)(2,1)S(1)} %slice.62), channel_id=1, source_target_pairs={{0,128},{128,2},{2,130},{130,4},{4,132},{132,6},{6,134},{134,0},{1... | collective-permute-start | bytes 786440 | tf_op jit(solution)/shard_map/ppermute | solution.py:277
  94.9 9.3 %collective-permute-start.26 = (bf16[64,2048]{1,0:T(8,128)(2,1)S(1)}, bf16[64,2048]{1,0:T(8,128)(2,1)S(1)}, u32[]{:S(2)}, u32[]{:S(2)}) collective-permute-start(bf16[64,2048]{1,0:T(8,128)(2,1)S(1)} %slice.63), channel_id=1, source_target_pairs={{0,134},{128,0},{2,128},{130,2},{4,130},{132,4},{6,132},{134,6},{1... | collective-permute-start | bytes 786440 | tf_op jit(solution)/shard_map/ppermute | solution.py:277
  137.2 23.6 %collective-permute-start.33 = (bf16[256,2048]{1,0:T(8,128)(2,1)S(1)}, bf16[256,2048]{1,0:T(8,128)(2,1)S(1)}, u32[]{:S(2)}, u32[]{:S(2)}) collective-permute-start(bf16[256,2048]{1,0:T(8,128)(2,1)S(1)} %get-tuple-element.140), channel_id=1, source_target_pairs={{96,97},{98,99},{100,101},{102,103},{104,105},{106,107},{108,109},... | collective-permute-start | bytes 3145736 | tf_op jit(solution)/shard_map/ppermute | solution.py:395
  138.0 22.7 %collective-permute-start.34 = (bf16[128,2048]{1,0:T(8,128)(2,1)S(1)}, bf16[128,2048]{1,0:T(8,128)(2,1)S(1)}, u32[]{:S(2)}, u32[]{:S(2)}) collective-permute-start(bf16[128,2048]{1,0:T(8,128)(2,1)S(1)} %dynamic-slice_bitcast_fusion.6), channel_id=1, source_target_pairs={{0,1},{2,3},{4,5},{6,7},{8,9},{10,11},{12,13},{14,15},{16,17},{18,... | collective-permute-start | bytes 1572872 | tf_op jit(solution)/shard_map/ppermute | solution.py:379
  174.1 210.9 %collective-permute-start.41 = (bf16[256,2048]{1,0:T(8,128)(2,1)}, bf16[256,2048]{1,0:T(8,128)(2,1)}, u32[]{:S(2)}, u32[]{:S(2)}) collective-permute-start(bf16[256,2048]{1,0:T(8,128)(2,1)} %get-tuple-element.169), channel_id=1, source_target_pairs={{1,0},{3,2},{5,4},{7,6},{9,8},{11,10},{13,12},{15,14},{17,16},{19,... | collective-permute-start | bytes 3145736 | tf_op jit(solution)/shard_map/ppermute | solution.py:403
  402.6 8.6 %collective-permute-start.55 = (bf16[2,32,2048]{2,1,0:T(8,128)(2,1)S(1)}, bf16[2,32,2048]{2,1,0:T(8,128)(2,1)S(1)}, u32[]{:S(2)}, u32[]{:S(2)}) collective-permute-start(bf16[2,32,2048]{2,1,0:T(8,128)(2,1)S(1)} %get-tuple-element.210), channel_id=1, source_target_pairs={{0,128},{128,2},{2,130},{130,4},{4,132},{132,6},{6,134},{134,0},{1... | collective-permute-start | bytes 786440 | tf_op jit(solution)/shard_map/ppermute | solution.py:277
  411.5 14.0 %collective-permute-start.56 = (bf16[4,32,2048]{2,1,0:T(8,128)(2,1)S(1)}, bf16[4,32,2048]{2,1,0:T(8,128)(2,1)S(1)}, u32[]{:S(2)}, u32[]{:S(2)}) collective-permute-start(bf16[4,32,2048]{2,1,0:T(8,128)(2,1)S(1)} %pad_maximum_fusion.4), channel_id=1, source_target_pairs={{0,128},{128,2},{2,130},{130,4},{4,132},{132,6},{6,134},{134,0},{1... | collective-permute-start | bytes 1572872 | tf_op jit(solution)/shard_map/ppermute | solution.py:277
  414.1 13.3 %collective-permute-start.42 = (bf16[256,1536]{1,0:T(8,128)(2,1)S(1)}, bf16[256,1536]{1,0:T(8,128)(2,1)S(1)}, u32[]{:S(2)}, u32[]{:S(2)}) collective-permute-start(bf16[256,1536]{1,0:T(8,128)(2,1)S(1)} %get-tuple-element.202), channel_id=1, source_target_pairs={{0,8},{8,16},{16,24},{24,0},{1,9},{9,17},{17,25},{25,1},{2,10},{10... | collective-permute-start | bytes 2359304 | tf_op jit(solution)/shard_map/ppermute | solution.py:273
  414.2 13.2 %collective-permute-start.44 = (bf16[256,1536]{1,0:T(8,128)(2,1)S(1)}, bf16[256,1536]{1,0:T(8,128)(2,1)S(1)}, u32[]{:S(2)}, u32[]{:S(2)}) collective-permute-start(bf16[256,1536]{1,0:T(8,128)(2,1)S(1)} %get-tuple-element.204), channel_id=1, source_target_pairs={{0,24},{8,0},{16,8},{24,16},{1,25},{9,1},{17,9},{25,17},{2,26},{10... | collective-permute-start | bytes 2359304 | tf_op jit(solution)/shard_map/ppermute | solution.py:273
  417.5 10.3 %collective-permute-start.60 = (bf16[4,32,2048]{2,1,0:T(8,128)(2,1)S(1)}, bf16[4,32,2048]{2,1,0:T(8,128)(2,1)S(1)}, u32[]{:S(2)}, u32[]{:S(2)}) collective-permute-start(bf16[4,32,2048]{2,1,0:T(8,128)(2,1)S(1)} %pad_maximum_fusion.5), channel_id=1, source_target_pairs={{0,134},{128,0},{2,128},{130,2},{4,130},{132,4},{6,132},{134,6},{1... | collective-permute-start | bytes 1572872 | tf_op jit(solution)/shard_map/ppermute | solution.py:277
  425.6 10.7 %collective-permute-start.57 = (bf16[4,32,2048]{2,1,0:T(8,128)(2,1)S(1)}, bf16[4,32,2048]{2,1,0:T(8,128)(2,1)S(1)}, u32[]{:S(2)}, u32[]{:S(2)}) collective-permute-start(bf16[4,32,2048]{2,1,0:T(8,128)(2,1)S(1)} %fusion.6), channel_id=1, source_target_pairs={{0,128},{128,2},{2,130},{130,4},{4,132},{132,6},{6,134},{134,0},{1... | collective-permute-start | bytes 1572872 | tf_op jit(solution)/shard_map/ppermute | solution.py:277
  437.5 14.3 %collective-permute-start.61 = (bf16[4,32,2048]{2,1,0:T(8,128)(2,1)S(1)}, bf16[4,32,2048]{2,1,0:T(8,128)(2,1)S(1)}, u32[]{:S(2)}, u32[]{:S(2)}) collective-permute-start(bf16[4,32,2048]{2,1,0:T(8,128)(2,1)S(1)} %get-tuple-element.207), channel_id=1, source_target_pairs={{0,134},{128,0},{2,128},{130,2},{4,130},{132,4},{6,132},{134,6},{1... | collective-permute-start | bytes 1572872 | tf_op jit(solution)/shard_map/ppermute | solution.py:277
  440.9 29.3 %collective-permute-start.43 = (bf16[512,1536]{1,0:T(8,128)(2,1)S(1)}, bf16[512,1536]{1,0:T(8,128)(2,1)}, u32[]{:S(2)}, u32[]{:S(2)}) collective-permute-start(bf16[512,1536]{1,0:T(8,128)(2,1)S(1)} %pad_maximum_fusion), channel_id=1, source_target_pairs={{0,8},{8,16},{16,24},{24,0},{1,9},{9,17},{17,25},{25,1},{2,10},{10... | collective-permute-start | bytes 4718600 | tf_op jit(solution)/shard_map/ppermute | solution.py:273
  442.2 28.7 %collective-permute-start.45 = (bf16[512,1536]{1,0:T(8,128)(2,1)}, bf16[512,1536]{1,0:T(8,128)(2,1)}, u32[]{:S(2)}, u32[]{:S(2)}) collective-permute-start(bf16[512,1536]{1,0:T(8,128)(2,1)} %pad_maximum_fusion.1), channel_id=1, source_target_pairs={{0,24},{8,0},{16,8},{24,16},{1,25},{9,1},{17,9},{25,17},{2,26},{10... | collective-permute-start | bytes 4718600 | tf_op jit(solution)/shard_map/ppermute | solution.py:273
  445.4 9.5 %collective-permute-start.58 = (bf16[4,32,2048]{2,1,0:T(8,128)(2,1)}, bf16[4,32,2048]{2,1,0:T(8,128)(2,1)S(1)}, u32[]{:S(2)}, u32[]{:S(2)}) collective-permute-start(bf16[4,32,2048]{2,1,0:T(8,128)(2,1)} %get-tuple-element.206), channel_id=1, source_target_pairs={{0,128},{128,2},{2,130},{130,4},{4,132},{132,6},{6,134},{134,0},{1... | collective-permute-start | bytes 1572872 | tf_op jit(solution)/shard_map/ppermute | solution.py:277
  452.0 9.3 %collective-permute-start.62 = (bf16[4,32,2048]{2,1,0:T(8,128)(2,1)S(1)}, bf16[4,32,2048]{2,1,0:T(8,128)(2,1)S(1)}, u32[]{:S(2)}, u32[]{:S(2)}) collective-permute-start(bf16[4,32,2048]{2,1,0:T(8,128)(2,1)S(1)} %fusion.5), channel_id=1, source_target_pairs={{0,134},{128,0},{2,128},{130,2},{4,130},{132,4},{6,132},{134,6},{1... | collective-permute-start | bytes 1572872 | tf_op jit(solution)/shard_map/ppermute | solution.py:277
  462.6 13.4 %collective-permute-start.63 = (bf16[16,2048]{1,0:T(8,128)(2,1)S(1)}, bf16[16,2048]{1,0:T(8,128)(2,1)S(1)}, u32[]{:S(2)}, u32[]{:S(2)}) collective-permute-start(bf16[16,2048]{1,0:T(8,128)(2,1)S(1)} %get-tuple-element.224), channel_id=1, source_target_pairs={{0,8},{8,16},{16,24},{24,0},{1,9},{9,17},{17,25},{25,1},{2,10},{10... | collective-permute-start | bytes 196616 | tf_op jit(solution)/shard_map/ppermute | solution.py:273
  462.7 13.3 %collective-permute-start.65 = (bf16[16,2048]{1,0:T(8,128)(2,1)S(1)}, bf16[16,2048]{1,0:T(8,128)(2,1)S(1)}, u32[]{:S(2)}, u32[]{:S(2)}) collective-permute-start(bf16[16,2048]{1,0:T(8,128)(2,1)S(1)} %get-tuple-element.226), channel_id=1, source_target_pairs={{0,24},{8,0},{16,8},{24,16},{1,25},{9,1},{17,9},{25,17},{2,26},{10... | collective-permute-start | bytes 196616 | tf_op jit(solution)/shard_map/ppermute | solution.py:273
  480.4 8.6 %collective-permute-start.51 = (bf16[64,1536]{1,0:T(8,128)(2,1)S(1)}, bf16[64,1536]{1,0:T(8,128)(2,1)S(1)}, u32[]{:S(2)}, u32[]{:S(2)}) collective-permute-start(bf16[64,1536]{1,0:T(8,128)(2,1)S(1)} %pad_maximum_fusion.7), channel_id=1, source_target_pairs={{0,134},{128,0},{2,128},{130,2},{4,130},{132,4},{6,132},{134,6},{1... | collective-permute-start | bytes 589832 | tf_op jit(solution)/shard_map/ppermute | solution.py:277
  485.7 7.5 %collective-permute-start.48 = (bf16[64,1536]{1,0:T(8,128)(2,1)S(1)}, bf16[64,1536]{1,0:T(8,128)(2,1)S(1)}, u32[]{:S(2)}, u32[]{:S(2)}) collective-permute-start(bf16[64,1536]{1,0:T(8,128)(2,1)S(1)} %fusion.14), channel_id=1, source_target_pairs={{0,128},{128,2},{2,130},{130,4},{4,132},{132,6},{6,134},{134,0},{1... | collective-permute-start | bytes 589832 | tf_op jit(solution)/shard_map/ppermute | solution.py:277
  487.5 16.2 %collective-permute-start.64 = (bf16[32,2048]{1,0:T(8,128)(2,1)S(1)}, bf16[32,2048]{1,0:T(8,128)(2,1)S(1)}, u32[]{:S(2)}, u32[]{:S(2)}) collective-permute-start(bf16[32,2048]{1,0:T(8,128)(2,1)S(1)} %pad_maximum_fusion.8), channel_id=1, source_target_pairs={{0,8},{8,16},{16,24},{24,0},{1,9},{9,17},{17,25},{25,1},{2,10},{10... | collective-permute-start | bytes 393224 | tf_op jit(solution)/shard_map/ppermute | solution.py:273
  493.3 8.3 %collective-permute-start.52 = (bf16[64,1536]{1,0:T(8,128)(2,1)S(1)}, bf16[64,1536]{1,0:T(8,128)(2,1)S(1)}, u32[]{:S(2)}, u32[]{:S(2)}) collective-permute-start(bf16[64,1536]{1,0:T(8,128)(2,1)S(1)} %get-tuple-element.215), channel_id=1, source_target_pairs={{0,134},{128,0},{2,128},{130,2},{4,130},{132,4},{6,132},{134,6},{1... | collective-permute-start | bytes 589832 | tf_op jit(solution)/shard_map/ppermute | solution.py:277
  496.0 8.0 %collective-permute-start.66 = (bf16[32,2048]{1,0:T(8,128)(2,1)S(1)}, bf16[32,2048]{1,0:T(8,128)(2,1)S(1)}, u32[]{:S(2)}, u32[]{:S(2)}) collective-permute-start(bf16[32,2048]{1,0:T(8,128)(2,1)S(1)} %pad_maximum_fusion.9), channel_id=1, source_target_pairs={{0,24},{8,0},{16,8},{24,16},{1,25},{9,1},{17,9},{25,17},{2,26},{10... | collective-permute-start | bytes 393224 | tf_op jit(solution)/shard_map/ppermute | solution.py:273
  504.1 9.3 %collective-permute-start.67 = (bf16[32,2048]{1,0:T(8,128)(2,1)S(1)}, bf16[32,2048]{1,0:T(8,128)(2,1)S(1)}, u32[]{:S(2)}, u32[]{:S(2)}) collective-permute-start(bf16[32,2048]{1,0:T(8,128)(2,1)S(1)} %fusion.19), channel_id=1, source_target_pairs={{0,0},{128,1},{2,2},{130,3},{4,4},{132,5},{6,6},{134,7},{8,8},{136... | collective-permute-start | bytes 393224 | tf_op jit(solution)/shard_map/ppermute | solution.py:410
  507.5 10.0 %collective-permute-start.54 = (bf16[64,1536]{1,0:T(8,128)(2,1)S(1)}, bf16[64,1536]{1,0:T(8,128)(2,1)S(1)}, u32[]{:S(2)}, u32[]{:S(2)}) collective-permute-start(bf16[64,1536]{1,0:T(8,128)(2,1)S(1)} %fusion.17), channel_id=1, source_target_pairs={{0,0},{128,1},{2,2},{130,3},{4,4},{132,5},{6,6},{134,7},{8,8},{136... | collective-permute-start | bytes 589832 | tf_op jit(solution)/shard_map/ppermute | solution.py:411
  (39 other events, 321.4 us)

commit v5 on v4

--- a/solution.py
+++ b/solution.py
@@ -86,12 +86,12 @@
 
 
 def forward_kernel(
-    final, layer, place, h_v, wq_v, wo_v, a0, a1, a2, a3, a4,
+    final, place, h_v, wq_v, wo_v, a0, a1, a2, a3, a4,
     out_v, normed_v, proj_v, ctx_v, keep_v, marks_v, key_s, value_s,
 ):
     del a0, a1, a2, a3, a4
 
-    @pl.when(place[0] == layer)
+    @pl.when(place[0] == 0)
     def _():
         block = (lax.broadcasted_iota(jnp.int32, (2 * ROWS, 128), 0) // HALF) % 2
         lane = lax.broadcasted_iota(jnp.int32, (2 * ROWS, 128), 1)
@@ -161,7 +161,7 @@
 def forward_layer(layer, place, hidden, w_qkv, w_out, normed, proj, ctx, kept, marks):
     final = layer == 7
     return pl.pallas_call(
-        functools.partial(forward_kernel, final, layer),
+        functools.partial(forward_kernel, final),
         out_shape=(v16(ROWS, D), v16(ROWS, D), v16(ROWS, WCOLS), v16(ROWS, HQ), v16(ROWS, D), v16(ROWS, HQ)),
         in_specs=[SMEM] + [INSIDE] * 8,
         out_specs=(INSIDE,) * 6,
@@ -174,12 +174,12 @@
 
 
 def backward_kernel(
-    last, layer, place, u_v, h_v, proj_v, ctx_v, marks_v, wq_v, wo_v, a0, a1,
+    last, place, u_v, h_v, proj_v, ctx_v, marks_v, wq_v, wo_v, a0, a1,
     up_v, dproj_v, keep_v, dn_v, key_s, value_s, dkt_s, dvt_s,
 ):
     del a0, a1
 
-    @pl.when(place[0] == layer)
+    @pl.when(place[0] == 0)
     def _():
         keep_v[...] = u_v[...]
         fill_keys(proj_v[:, HQ : HQ + KV], key_s, place[1])
@@ -235,7 +235,7 @@
     spare = [place, place] if last else inside(kept, w_qkv)
     where = SMEM if last else INSIDE
     return pl.pallas_call(
-        functools.partial(backward_kernel, last, layer),
+        functools.partial(backward_kernel, last),
         out_shape=(v16(ROWS, D), v16(ROWS, WCOLS), v16(ROWS, D)),
         in_specs=[SMEM, INSIDE, where, INSIDE, INSIDE, INSIDE, where, INSIDE, INSIDE, INSIDE],
         out_specs=(INSIDE,) * 3,
@@ -287,28 +287,48 @@
     return above + far + below[:0:-1]
 
 
-def scatter_ring(take, count, send, axis):
+def add(own, came):
+    return (own.astype(jnp.float32) + came.astype(jnp.float32)).astype(jnp.bfloat16)
+
+
+def scatter_ring(take, count, send):
     far = count // 2
-
-    def halves(value):
-        return jnp.split(value, 2, axis=axis)
-
-    def add(own, came):
-        return (own.astype(jnp.float32) + came.astype(jnp.float32)).astype(jnp.bfloat16)
-
-    low, high = halves(take(far))
-    up, down = send(low, 1), send(high, -1)
+    up, down = send(take(far, 0), 1), send(take(far, 1), -1)
     for step in range(far - 1, 0, -1):
         if step == far - 1:
-            low, high = halves(take(step))
-            next_up = jnp.concatenate([add(low, up), high], axis=axis)
-            low, high = halves(take(-step))
-            next_down = jnp.concatenate([low, add(high, down)], axis=axis)
+            next_up = jnp.concatenate([add(take(step, 0), up), take(step, 1)])
+            next_down = jnp.concatenate([take(-step, 0), add(take(-step, 1), down)])
         else:
             next_up, next_down = add(take(step), up), add(take(-step), down)
         up, down = send(next_up, 1), send(next_down, -1)
     total = take(0).astype(jnp.float32) + up.astype(jnp.float32) + down.astype(jnp.float32)
     return total.astype(jnp.bfloat16)
+
+
+def scatter_direct(take, send):
+    total = take(0).astype(jnp.float32)
+    for came in [send(take(step), step) for step in (2, 1, -1)]:
+        total = total + came.astype(jnp.float32)
+    return total.astype(jnp.bfloat16)
+
+
+def gather_direct(own, send):
+    far, above, below = send(own, 2), send(own, -1), send(own, 1)
+    return [own, above, far, below]
+
+
+def taker(value, spots, axis, split):
+    def take(d, half=None):
+        spot = spots[d % len(spots)]
+        start, size = [0] * value.ndim, list(value.shape)
+        start[axis], size[axis] = spot, 1
+        if half is not None:
+            size[split] //= 2
+            start[split] = half * size[split]
+        block = lax.dynamic_slice(value, start, size, allow_negative_indices=False)
+        return block.reshape([n for dim, n in enumerate(size) if dim != axis])
+
+    return take
 
 
 def assemble_kernel(place, *refs):
@@ -335,7 +355,7 @@
 
 def gather_weights(near, far, x, z):
     column = jnp.concatenate(gather_ring(near, 8, send_z))
-    row = jnp.concatenate(gather_ring(far, 4, send_x))
+    row = jnp.concatenate(gather_direct(far, send_x))
     qkv_parts = gather_ring(column, 4, send_x)
     out_parts = gather_ring(row, 8, send_z)
     return pl.pallas_call(
@@ -351,16 +371,13 @@
 
 
 def scatter_qkv(part, turns, spins):
-    part = part.reshape(4, 512, WCOLS)
-    mine = scatter_ring(lambda d: lax.dynamic_index_in_dim(part, turns[d % 4], 0, keepdims=False, allow_negative_indices=False), 4, send_x, 0)
-    mine = mine.reshape(8, 64, WCOLS)
-    return scatter_ring(lambda d: lax.dynamic_index_in_dim(mine, spins[d % 8], 0, keepdims=False, allow_negative_indices=False), 8, send_z, 0)
+    mine = scatter_ring(taker(part.reshape(4, 512, WCOLS), turns, 0, 1), 4, send_x)
+    return scatter_ring(taker(mine.reshape(8, 64, WCOLS), spins, 0, 1), 8, send_z)
 
 
 def scatter_out(part, turns, spins):
-    part = part.reshape(4, 8, 32, D)
-    mine = scatter_ring(lambda d: lax.dynamic_index_in_dim(part, spins[d % 8], 1, keepdims=False, allow_negative_indices=False), 8, send_z, 0)
-    return scatter_ring(lambda d: lax.dynamic_index_in_dim(mine, turns[d % 4], 0, keepdims=False, allow_negative_indices=False), 4, send_x, 0)
+    mine = scatter_ring(taker(part.reshape(4, 8, 32, D), spins, 1, 0), 8, send_z)
+    return scatter_direct(taker(mine, turns, 0, 1), send_x)
 
 
 def on_device(inputs, cotangent, joined, w_qkv, w_out):
@@ -378,10 +395,10 @@
     block = lax.dynamic_index_in_dim(cotangent, micro, 0, keepdims=False)
     upstream = jnp.concatenate([lax.ppermute(block, "core", [(0, 1)]), block])
 
-    place = jnp.stack([stage, flag])
+    places = [jnp.stack([stage - layer, flag]) for layer in range(LAYERS)]
     turns = [((x_index + d) % 4) for d in range(4)]
     spins = [((z_place + d) % 8) for d in range(8)]
-    place, turns, spins = lax.optimization_barrier((place, turns, spins))
+    places, turns, spins = lax.optimization_barrier((places, turns, spins))
     normed = jnp.zeros((ROWS, D), jnp.bfloat16)
     kept = jnp.zeros((ROWS, D), jnp.bfloat16)
     proj = jnp.zeros((ROWS, WCOLS), jnp.bfloat16)
@@ -389,21 +406,23 @@
     marks = jnp.zeros((ROWS, HQ), jnp.bfloat16)
     for layer in range(LAYERS):
         result, normed, proj, ctx, kept, marks = forward_layer(
-            layer, place, hidden, full_qkv, full_out, normed, proj, ctx, kept, marks
+            layer, places[layer], hidden, full_qkv, full_out, normed, proj, ctx, kept, marks
         )
         if layer < LAYERS - 1:
             hidden = lax.ppermute(result, STAGE, [(layer, layer + 1)])
     dproj = jnp.zeros((ROWS, WCOLS), jnp.bfloat16)
     ups = jnp.zeros((ROWS, D), jnp.bfloat16)
+    contract = (((0,), (0,)), ((), ()))
     for layer in reversed(range(LAYERS)):
+        if layer == 0:
+            arrived = jnp.where(stage == 0, upstream, ups)
+            part_out = lax.dot_general(ctx, arrived, contract, preferred_element_type=jnp.float32).astype(jnp.bfloat16)
+            part_out, upstream = lax.optimization_barrier((part_out, upstream))
         result, dproj, ups = backward_layer(
-            layer, place, upstream, kept, proj, ctx, marks, full_qkv, full_out, dproj, ups
+            layer, places[layer], upstream, kept, proj, ctx, marks, full_qkv, full_out, dproj, ups
         )
         if layer:
             upstream = lax.ppermute(result, STAGE, [(layer, layer - 1)])
-    ups, dproj, turns, spins = lax.optimization_barrier((ups, dproj, turns, spins))
-    contract = (((0,), (0,)), ((), ()))
-    part_out = lax.dot_general(ctx, ups, contract, preferred_element_type=jnp.float32).astype(jnp.bfloat16)
     part_qkv = lax.dot_general(normed, dproj, contract, preferred_element_type=jnp.float32).astype(jnp.bfloat16)
     grad_out = scatter_out(part_out, turns, spins)
     grad_qkv = scatter_qkv(part_qkv, turns, spins)

time: 529 us -> 513 us (0.970)
  waiting for transfers between devices: 313 us -> 307 us
    ppermute x32, waiting for transfers between devices: 82.3 us -> 61.5 us  [send_z(): lax.ppermute(value, ('zlo', 'zhi'), [(z_index(i), z_index((i + step) % 8)...]
    ppermute x16 -> x14, waiting for transfers between devices: 8.21 us -> 26.9 us  [send_x(): return lax.ppermute(value, 'x', [(i, (i + step) % 4) for i in range(4)])]
    ppermute x16 -> x14, starting transfers between devices: 29.4 us -> 22.6 us  [send_x(): return lax.ppermute(value, 'x', [(i, (i + step) % 4) for i in range(4)])]
    unnamed x50 -> x39, local copies, waits for them, and re-layouts: 17.5 us -> 11.1 us
  transfers between devices with their start and end apart: 68 -> 66, of which waited for: 34 -> 30; matrix products, arithmetic and copies ran while one was open for 5% -> 5% of each run, Pallas kernels for 0% -> 2%
where the time goes in v5:
time: 513 us; the launch traced here: 504 us
  waiting for transfers between devices  307 us (60%)
  starting transfers between devices  125 us (24%)
  Pallas kernels  36.5 us (7%)
  local copies, waits for them, and re-layouts  19.6 us (4%)
  other arithmetic  8.61 us (2%)
    ppermute x7, waiting for transfers between devices, on_device(): upstream = lax.ppermute(result, STAGE, [(layer, layer - 1)])  207 us
    ppermute x32, waiting for transfers between devices, send_z(): lax.ppermute(value, ('zlo', 'zhi'), [(z_index(i), z_index((i + step) % 8)...  61.5 us
    ppermute x32, starting transfers between devices, send_z(): lax.ppermute(value, ('zlo', 'zhi'), [(z_index(i), z_index((i + step) % 8)...  52.6 us
    ppermute x14, waiting for transfers between devices, send_x(): return lax.ppermute(value, 'x', [(i, (i + step) % 4) for i in range(4)])  26.9 us
    ppermute x1, starting transfers between devices, on_device(): upstream = jnp.concatenate([lax.ppermute(block, 'core', [(0, 1)]), block])  23.6 us
    ppermute x14, starting transfers between devices, send_x(): return lax.ppermute(value, 'x', [(i, (i + step) % 4) for i in range(4)])  22.6 us
    pallas_call x8, Pallas kernels, forward_layer(): pl.pallas_call(functools.partial(forward_kernel, final), out_shape=(v16(R...  14.6 us
    pallas_call x8, Pallas kernels, backward_layer(): pl.pallas_call(functools.partial(backward_kernel, last), out_shape=(v16(R...  13.4 us
  transfers between devices with their start and end apart: 66, of which 30 were waited for; matrix products, arithmetic and copies ran while one was open for 5% of the time, Pallas kernels for 2%

profile of v5, /device:TPU:32, one launch (start us, length us, event | category | flops | bytes accessed | tf_op | source)
XLA Modules:
  0.0 503.6 jit_solution(16582524246880890230)
XLA Ops:
  0.6 4.8 collective-permute-start.14
  5.4 2.4 collective-permute-start.1
  8.2 2.8 collective-permute-start.15
  12.8 2.0 collective-permute-start.5
  15.5 1.8 collective-permute-done.15
  17.4 3.0 collective-permute-done.2
  20.3 3.5 collective-permute-start.3
  25.0 2.6 collective-permute-done.3
  27.5 3.3 collective-permute-start.4
  31.9 6.2 %collective-permute-done.7 = bf16[64,1536]{1,0:T(8,128)(2,1)S(1)} collective-permute-done((bf16[64,1536]{1,0:T(8,128)(2,1)S(1)}, bf16[64,1536]{1,0:T(8,128)(2,1)S(1)}, u32[]{:S(2)}, u32[]{:S(2)}) %collective-permute-start.7) | collective-permute-done | bytes 196640 | tf_op jit(solution)/shard_map/ppermute | solution.py:277
  38.3 3.3 collective-permute-start.9
  52.3 1.8 collective-permute-start.18
  54.9 7.8 %collective-permute-done.21.refs_13_ = bf16[128,2048]{1,0:T(8,128)(2,1)S(1)} collective-permute-done((bf16[128,2048]{1,0:T(8,128)(2,1)S(1)}, bf16[128,2048]{1,0:T(8,128)(2,1)S(1)}, u32[]{:S(2)}, u32[]{:S(2)}) %collective-permute-start.21) | collective-permute-done | bytes 524320 | tf_op jit(solution)/shard_map/ppermute | solution.py:277
  62.7 2.4 collective-permute-start.22
  67.1 8.7 %collective-permute-done.22.refs_12_ = bf16[128,2048]{1,0:T(8,128)(2,1)} collective-permute-done((bf16[128,2048]{1,0:T(8,128)(2,1)S(1)}, bf16[128,2048]{1,0:T(8,128)(2,1)}, u32[]{:S(2)}, u32[]{:S(2)}) %collective-permute-start.22) | collective-permute-done | bytes 524320 | tf_op jit(solution)/shard_map/ppermute | solution.py:277
  78.4 2.4 collective-permute-start.20
  86.1 2.1 slice.27
  95.6 3.3 collective-permute-start.25
  100.2 3.7 collective-permute-done.24.refs_9_
  105.6 2.8 collective-permute-done.13.refs_3_
  110.4 8.5 %assemble.1 = (bf16[2048,1536]{1,0:T(8,128)(2,1)S(1)}, bf16[1024,2048]{1,0:T(8,128)(2,1)S(1)}) custom-call(s32[2]{0:T(128)S(1)} %pad_add_fusion.8.place, bf16[512,1536]{1,0:T(8,128)(2,1)} %constant_dynamic-update-slice_fusion.refs_0_, bf16[512,1536]{1,0:T(8,128)(2,1)} %collective-permute-done.10.refs_1_, ...), custom_call_target="tpu_custom_call" | custom-call | bytes 21000000 | tf_op jit(solution)/shard_map/assemble/pallas_call | solution.py:361
  119.3 9.6 %forward_layer.7 = (bf16[256,2048]{1,0:T(8,128)(2,1)S(1)}, bf16[256,2048]{1,0:T(8,128)(2,1)S(1)}, bf16[256,1536]{1,0:T(8,128)(2,1)S(1)}, bf16[256,1024]{1,0:T(8,...) custom-call(s32[2]{0:T(128)S(1)} %get-tuple-element.102.place.h_v.wq, ...), custom_call_target="tpu_custom_call", output_to_operand_aliasing={{1}: (4, {}), {2}: (5, {}), {3}: (6, {}), {4}: (7, {}), {5}... | custom-call | flops 3000000000 | bytes 14000000 | tf_op jit(solution)/shard_map/forward_layer/pallas_call | solution.py:163
  130.3 2.2 collective-permute-done.26.h_v
  139.8 3.4 collective-permute-start.32
  143.3 23.6 %collective-permute-start.33 = (bf16[128,2048]{1,0:T(8,128)(2,1)S(1)}, bf16[128,2048]{1,0:T(8,128)(2,1)S(1)}, u32[]{:S(2)}, u32[]{:S(2)}) collective-permute-start(bf16[128,2048]{1,0:T(8,128)(2,1)S(1)} %dynamic-slice_bitcast_fusion.4), channel_id=1, source_target_pairs={{0,1},{2,3},{4,5},{6,7},{8,9},{10,11},{12,13},{14,15},{16,17},{18,... | collective-permute-start | bytes 1572872 | tf_op jit(solution)/shard_map/ppermute | solution.py:396
  183.1 207.4 %collective-permute-done.40.u_v = bf16[256,2048]{1,0:T(8,128)(2,1)} collective-permute-done((bf16[256,2048]{1,0:T(8,128)(2,1)}, bf16[256,2048]{1,0:T(8,128)(2,1)}, u32[]{:S(2)}, u32[]{:S(2)}) %collective-permute-start.40) | collective-permute-done | bytes 1048608 | tf_op jit(solution)/shard_map/ppermute | solution.py:425
  390.4 2.7 convolution_convert_fusion.1
  393.4 3.7 collective-permute-start.58
  397.1 8.3 %backward_last.1 = (bf16[256,2048]{1,0:T(8,128)(2,1)}, bf16[256,1536]{1,0:T(8,128)(2,1)S(1)}, bf16[256,2048]{1,0:T(8,128)(2,1)S(1)}) custom-call(s32[2]{0:T(128)S(1)} %get-tuple-element.102.place.h_v.wq_v, bf16[256,2048]{1,0:T(8,128)(2,1)} %collective-permute-done.40.u_v, ...), custom_call_target="tpu_custom_call", output_to_operand_aliasing={{1}: (8, {}), {2}: (9, {})} | custom-call | flops 4000000000 | bytes 15000000 | tf_op jit(solution)/shard_map/backward_last/pallas_call | solution.py:237
  405.4 1.8 convolution_convert_fusion
  408.7 2.1 collective-permute-start.43
  411.1 13.6 %collective-permute-done.41 = bf16[256,1536]{1,0:T(8,128)(2,1)S(1)} collective-permute-done((bf16[256,1536]{1,0:T(8,128)(2,1)S(1)}, bf16[256,1536]{1,0:T(8,128)(2,1)S(1)}, u32[]{:S(2)}, u32[]{:S(2)}) %collective-permute-start.41) | collective-permute-done | bytes 786464 | tf_op jit(solution)/shard_map/ppermute | solution.py:273
  426.3 2.4 collective-permute-start.44
  428.8 3.2 collective-permute-start.59
  432.2 11.3 %collective-permute-done.59 = bf16[4,32,2048]{2,1,0:T(8,128)(2,1)S(1)} collective-permute-done((bf16[4,32,2048]{2,1,0:T(8,128)(2,1)S(1)}, bf16[4,32,2048]{2,1,0:T(8,128)(2,1)S(1)}, u32[]{:S(2)}, u32[]{:S(2)}) %collective-permute-start.59) | collective-permute-done | bytes 524320 | tf_op jit(solution)/shard_map/ppermute | solution.py:277
  443.5 1.9 collective-permute-done.56
  448.0 8.0 %collective-permute-done.42 = bf16[512,1536]{1,0:T(8,128)(2,1)S(1)} collective-permute-done((bf16[512,1536]{1,0:T(8,128)(2,1)S(1)}, bf16[512,1536]{1,0:T(8,128)(2,1)S(1)}, u32[]{:S(2)}, u32[]{:S(2)}) %collective-permute-start.42) | collective-permute-done | bytes 1572896 | tf_op jit(solution)/shard_map/ppermute | solution.py:273
  456.7 3.2 collective-permute-start.49
  460.0 3.2 collective-permute-start.61
  465.9 3.5 collective-permute-done.46
  471.9 2.9 collective-permute-done.50
  476.5 4.7 collective-permute-start.51
  483.9 2.3 collective-permute-start.64
  486.6 1.8 collective-permute-start.52
  489.3 1.9 collective-permute-start.65
  492.5 1.9 collective-permute-start.53
  494.4 4.2 collective-permute-done.65
  499.3 3.1 collective-permute-done.53
  (192 shorter events, 84.9 us)
Async XLA Ops:
  0.6 7.6 %collective-permute-start.14 = (bf16[32,2048]{1,0:T(8,128)(2,1)}, bf16[32,2048]{1,0:T(8,128)(2,1)S(1)}, u32[]{:S(2)}, u32[]{:S(2)}) collective-permute-start(bf16[32,2048]{1,0:T(8,128)(2,1)} %bitcast.143), channel_id=1, source_target_pairs={{0,0},{1,128},{2,2},{3,130},{4,4},{5,132},{6,6},{7,134},{8,8},{9,1... | collective-permute-start | bytes 393224 | tf_op jit(solution)/shard_map/ppermute | solution.py:391
  5.4 7.3 %collective-permute-start.1 = (bf16[64,1536]{1,0:T(8,128)(2,1)}, bf16[64,1536]{1,0:T(8,128)(2,1)S(1)}, u32[]{:S(2)}, u32[]{:S(2)}) collective-permute-start(bf16[64,1536]{1,0:T(8,128)(2,1)} %bitcast.142), channel_id=1, source_target_pairs={{0,0},{1,128},{2,2},{3,130},{4,4},{5,132},{6,6},{7,134},{8,8},{9,1... | collective-permute-start | bytes 589832 | tf_op jit(solution)/shard_map/ppermute | solution.py:390
  8.2 9.1 %collective-permute-start.15 = (bf16[32,2048]{1,0:T(8,128)(2,1)S(1)}, bf16[32,2048]{1,0:T(8,128)(2,1)S(1)}, u32[]{:S(2)}, u32[]{:S(2)}) collective-permute-start(bf16[32,2048]{1,0:T(8,128)(2,1)S(1)} %collective-permute-done.14), channel_id=1, source_target_pairs={{0,24},{8,0},{16,8},{24,16},{1,25},{9,1},{17,9},{25,17},{2,26},{10... | collective-permute-start | bytes 393224 | tf_op jit(solution)/shard_map/ppermute | solution.py:273
  11.0 39.7 %collective-permute-start.16 = (bf16[32,2048]{1,0:T(8,128)(2,1)S(1)}, bf16[32,2048]{1,0:T(8,128)(2,1)S(1)}, u32[]{:S(2)}, u32[]{:S(2)}) collective-permute-start(bf16[32,2048]{1,0:T(8,128)(2,1)S(1)} %collective-permute-done.14), channel_id=1, source_target_pairs={{0,16},{8,24},{16,0},{24,8},{1,17},{9,25},{17,1},{25,9},{2,18},{10... | collective-permute-start | bytes 393224 | tf_op jit(solution)/shard_map/ppermute | solution.py:273
  11.8 38.9 %collective-permute-start.17 = (bf16[32,2048]{1,0:T(8,128)(2,1)S(1)}, bf16[32,2048]{1,0:T(8,128)(2,1)S(1)}, u32[]{:S(2)}, u32[]{:S(2)}) collective-permute-start(bf16[32,2048]{1,0:T(8,128)(2,1)S(1)} %collective-permute-done.14), channel_id=1, source_target_pairs={{0,8},{8,16},{16,24},{24,0},{1,9},{9,17},{17,25},{25,1},{2,10},{10... | collective-permute-start | bytes 393224 | tf_op jit(solution)/shard_map/ppermute | solution.py:273
  12.7 7.6 %collective-permute-start.2 = (bf16[64,1536]{1,0:T(8,128)(2,1)S(1)}, bf16[64,1536]{1,0:T(8,128)(2,1)S(1)}, u32[]{:S(2)}, u32[]{:S(2)}) collective-permute-start(bf16[64,1536]{1,0:T(8,128)(2,1)S(1)} %collective-permute-done.1), channel_id=1, source_target_pairs={{0,134},{128,0},{2,128},{130,2},{4,130},{132,4},{6,132},{134,6},{1... | collective-permute-start | bytes 589832 | tf_op jit(solution)/shard_map/ppermute | solution.py:277
  12.8 11.5 %collective-permute-start.5 = (bf16[64,1536]{1,0:T(8,128)(2,1)S(1)}, bf16[64,1536]{1,0:T(8,128)(2,1)S(1)}, u32[]{:S(2)}, u32[]{:S(2)}) collective-permute-start(bf16[64,1536]{1,0:T(8,128)(2,1)S(1)} %collective-permute-done.1), channel_id=1, source_target_pairs={{0,128},{128,2},{2,130},{130,4},{4,132},{132,6},{6,134},{134,0},{1... | collective-permute-start | bytes 589832 | tf_op jit(solution)/shard_map/ppermute | solution.py:277
  20.3 7.2 %collective-permute-start.3 = (bf16[64,1536]{1,0:T(8,128)(2,1)S(1)}, bf16[64,1536]{1,0:T(8,128)(2,1)S(1)}, u32[]{:S(2)}, u32[]{:S(2)}) collective-permute-start(bf16[64,1536]{1,0:T(8,128)(2,1)S(1)} %collective-permute-done.2), channel_id=1, source_target_pairs={{0,134},{128,0},{2,128},{130,2},{4,130},{132,4},{6,132},{134,6},{1... | collective-permute-start | bytes 589832 | tf_op jit(solution)/shard_map/ppermute | solution.py:277
  24.3 7.0 %collective-permute-start.6 = (bf16[64,1536]{1,0:T(8,128)(2,1)S(1)}, bf16[64,1536]{1,0:T(8,128)(2,1)S(1)}, u32[]{:S(2)}, u32[]{:S(2)}) collective-permute-start(bf16[64,1536]{1,0:T(8,128)(2,1)S(1)} %collective-permute-done.5), channel_id=1, source_target_pairs={{0,128},{128,2},{2,130},{130,4},{4,132},{132,6},{6,134},{134,0},{1... | collective-permute-start | bytes 589832 | tf_op jit(solution)/shard_map/ppermute | solution.py:277
  27.5 10.7 %collective-permute-start.4 = (bf16[64,1536]{1,0:T(8,128)(2,1)S(1)}, bf16[64,1536]{1,0:T(8,128)(2,1)S(1)}, u32[]{:S(2)}, u32[]{:S(2)}) collective-permute-start(bf16[64,1536]{1,0:T(8,128)(2,1)S(1)} %collective-permute-done.3), channel_id=1, source_target_pairs={{0,134},{128,0},{2,128},{130,2},{4,130},{132,4},{6,132},{134,6},{1... | collective-permute-start | bytes 589832 | tf_op jit(solution)/shard_map/ppermute | solution.py:277
  31.3 6.9 %collective-permute-start.7 = (bf16[64,1536]{1,0:T(8,128)(2,1)S(1)}, bf16[64,1536]{1,0:T(8,128)(2,1)S(1)}, u32[]{:S(2)}, u32[]{:S(2)}) collective-permute-start(bf16[64,1536]{1,0:T(8,128)(2,1)S(1)} %collective-permute-done.6), channel_id=1, source_target_pairs={{0,128},{128,2},{2,130},{130,4},{4,132},{132,6},{6,134},{134,0},{1... | collective-permute-start | bytes 589832 | tf_op jit(solution)/shard_map/ppermute | solution.py:277
  38.3 6.4 %collective-permute-start.9 = (bf16[32,1536]{1,0:T(8,128)(2,1)S(1)}, bf16[32,1536]{1,0:T(8,128)(2,1)S(1)}, u32[]{:S(2)}, u32[]{:S(2)}) collective-permute-start(bf16[32,1536]{1,0:T(8,128)(2,1)S(1)} %slice.25), channel_id=1, source_target_pairs={{0,134},{128,0},{2,128},{130,2},{4,130},{132,4},{6,132},{134,6},{1... | collective-permute-start | bytes 294920 | tf_op jit(solution)/shard_map/ppermute | solution.py:277
  47.4 36.2 %collective-permute-start.11 = (bf16[512,1536]{1,0:T(8,128)(2,1)}, bf16[512,1536]{1,0:T(8,128)(2,1)S(1)}, u32[]{:S(2)}, u32[]{:S(2)}) collective-permute-start(bf16[512,1536]{1,0:T(8,128)(2,1)} %constant_dynamic-update-slice_fusion.refs_0_), channel_id=1, source_target_pairs={{0,8},{8,16},{16,24},{24,0},{1,9},{9,17},{17,25},{25,1},{2,10},{10... | collective-permute-start | bytes 4718600 | tf_op jit(solution)/shard_map/ppermute | solution.py:273
  49.0 37.1 %collective-permute-start.10 = (bf16[512,1536]{1,0:T(8,128)(2,1)}, bf16[512,1536]{1,0:T(8,128)(2,1)}, u32[]{:S(2)}, u32[]{:S(2)}) collective-permute-start(bf16[512,1536]{1,0:T(8,128)(2,1)} %constant_dynamic-update-slice_fusion.refs_0_), channel_id=1, source_target_pairs={{0,24},{8,0},{16,8},{24,16},{1,25},{9,1},{17,9},{25,17},{2,26},{10... | collective-permute-start | bytes 4718600 | tf_op jit(solution)/shard_map/ppermute | solution.py:273
  50.7 11.9 %collective-permute-start.21 = (bf16[128,2048]{1,0:T(8,128)(2,1)S(1)}, bf16[128,2048]{1,0:T(8,128)(2,1)S(1)}, u32[]{:S(2)}, u32[]{:S(2)}) collective-permute-start(bf16[128,2048]{1,0:T(8,128)(2,1)S(1)} %constant_dynamic-update-slice_fusion.9.refs_5_), channel_id=1, source_target_pairs={{0,128},{128,2},{2,130},{130,4},{4,132},{132,6},{6,134},{134,0},{1... | collective-permute-start | bytes 1572872 | tf_op jit(solution)/shard_map/ppermute | solution.py:277
  52.3 13.5 %collective-permute-start.18 = (bf16[128,2048]{1,0:T(8,128)(2,1)S(1)}, bf16[128,2048]{1,0:T(8,128)(2,1)}, u32[]{:S(2)}, u32[]{:S(2)}) collective-permute-start(bf16[128,2048]{1,0:T(8,128)(2,1)S(1)} %constant_dynamic-update-slice_fusion.9.refs_5_), channel_id=1, source_target_pairs={{0,134},{128,0},{2,128},{130,2},{4,130},{132,4},{6,132},{134,6},{1... | collective-permute-start | bytes 1572872 | tf_op jit(solution)/shard_map/ppermute | solution.py:277
  62.7 13.1 %collective-permute-start.22 = (bf16[128,2048]{1,0:T(8,128)(2,1)S(1)}, bf16[128,2048]{1,0:T(8,128)(2,1)}, u32[]{:S(2)}, u32[]{:S(2)}) collective-permute-start(bf16[128,2048]{1,0:T(8,128)(2,1)S(1)} %collective-permute-done.21.refs_13_), channel_id=1, source_target_pairs={{0,128},{128,2},{2,130},{130,4},{4,132},{132,6},{6,134},{134,0},{1... | collective-permute-start | bytes 1572872 | tf_op jit(solution)/shard_map/ppermute | solution.py:277
  65.8 12.6 %collective-permute-start.19 = (bf16[128,2048]{1,0:T(8,128)(2,1)}, bf16[128,2048]{1,0:T(8,128)(2,1)}, u32[]{:S(2)}, u32[]{:S(2)}) collective-permute-start(bf16[128,2048]{1,0:T(8,128)(2,1)} %collective-permute-done.18.refs_6_), channel_id=1, source_target_pairs={{0,134},{128,0},{2,128},{130,2},{4,130},{132,4},{6,132},{134,6},{1... | collective-permute-start | bytes 1572872 | tf_op jit(solution)/shard_map/ppermute | solution.py:277
  75.8 17.0 %collective-permute-start.23 = (bf16[128,2048]{1,0:T(8,128)(2,1)}, bf16[128,2048]{1,0:T(8,128)(2,1)S(1)}, u32[]{:S(2)}, u32[]{:S(2)}) collective-permute-start(bf16[128,2048]{1,0:T(8,128)(2,1)} %collective-permute-done.22.refs_12_), channel_id=1, source_target_pairs={{0,128},{128,2},{2,130},{130,4},{4,132},{132,6},{6,134},{134,0},{1... | collective-permute-start | bytes 1572872 | tf_op jit(solution)/shard_map/ppermute | solution.py:277
  78.4 15.5 %collective-permute-start.20 = (bf16[128,2048]{1,0:T(8,128)(2,1)}, bf16[128,2048]{1,0:T(8,128)(2,1)}, u32[]{:S(2)}, u32[]{:S(2)}) collective-permute-start(bf16[128,2048]{1,0:T(8,128)(2,1)} %collective-permute-done.19.refs_7_), channel_id=1, source_target_pairs={{0,134},{128,0},{2,128},{130,2},{4,130},{132,4},{6,132},{134,6},{1... | collective-permute-start | bytes 1572872 | tf_op jit(solution)/shard_map/ppermute | solution.py:277
  81.7 17.2 %collective-permute-start = (bf16[128,2048]{1,0:T(8,128)(2,1)}, bf16[128,2048]{1,0:T(8,128)(2,1)}, u32[]{:S(2)}, u32[]{:S(2)}) collective-permute-start(bf16[128,2048]{1,0:T(8,128)(2,1)} %dynamic-slice_bitcast_fusion.5), channel_id=1, source_target_pairs={{1,0},{3,2},{5,4},{7,6},{9,8},{11,10},{13,12},{15,14},{17,16},{19,... | collective-permute-start | bytes 1572872 | tf_op jit(solution)/shard_map/ppermute | solution.py:394
  84.6 21.0 %collective-permute-start.12 = (bf16[256,1536]{1,0:T(8,128)(2,1)}, bf16[256,1536]{1,0:T(8,128)(2,1)S(1)}, u32[]{:S(2)}, u32[]{:S(2)}) collective-permute-start(bf16[256,1536]{1,0:T(8,128)(2,1)} %slice.26), channel_id=1, source_target_pairs={{0,8},{8,16},{16,24},{24,0},{1,9},{9,17},{17,25},{25,1},{2,10},{10... | collective-permute-start | bytes 2359304 | tf_op jit(solution)/shard_map/ppermute | solution.py:273
  88.2 20.1 %collective-permute-start.13 = (bf16[256,1536]{1,0:T(8,128)(2,1)}, bf16[256,1536]{1,0:T(8,128)(2,1)}, u32[]{:S(2)}, u32[]{:S(2)}) collective-permute-start(bf16[256,1536]{1,0:T(8,128)(2,1)} %slice.27), channel_id=1, source_target_pairs={{0,24},{8,0},{16,8},{24,16},{1,25},{9,1},{17,9},{25,17},{2,26},{10... | collective-permute-start | bytes 2359304 | tf_op jit(solution)/shard_map/ppermute | solution.py:273
  93.5 10.4 %collective-permute-start.24 = (bf16[64,2048]{1,0:T(8,128)(2,1)}, bf16[64,2048]{1,0:T(8,128)(2,1)S(1)}, u32[]{:S(2)}, u32[]{:S(2)}) collective-permute-start(bf16[64,2048]{1,0:T(8,128)(2,1)} %slice.28), channel_id=1, source_target_pairs={{0,128},{128,2},{2,130},{130,4},{4,132},{132,6},{6,134},{134,0},{1... | collective-permute-start | bytes 786440 | tf_op jit(solution)/shard_map/ppermute | solution.py:277
  95.6 10.0 %collective-permute-start.25 = (bf16[64,2048]{1,0:T(8,128)(2,1)}, bf16[64,2048]{1,0:T(8,128)(2,1)S(1)}, u32[]{:S(2)}, u32[]{:S(2)}) collective-permute-start(bf16[64,2048]{1,0:T(8,128)(2,1)} %slice.29), channel_id=1, source_target_pairs={{0,134},{128,0},{2,128},{130,2},{4,130},{132,4},{6,132},{134,6},{1... | collective-permute-start | bytes 786440 | tf_op jit(solution)/shard_map/ppermute | solution.py:277
  139.8 28.7 %collective-permute-start.32 = (bf16[256,2048]{1,0:T(8,128)(2,1)S(1)}, bf16[256,2048]{1,0:T(8,128)(2,1)S(1)}, u32[]{:S(2)}, u32[]{:S(2)}) collective-permute-start(bf16[256,2048]{1,0:T(8,128)(2,1)S(1)} %get-tuple-element.141), channel_id=1, source_target_pairs={{96,97},{98,99},{100,101},{102,103},{104,105},{106,107},{108,109},... | collective-permute-start | bytes 3145736 | tf_op jit(solution)/shard_map/ppermute | solution.py:412
  143.3 25.1 %collective-permute-start.33 = (bf16[128,2048]{1,0:T(8,128)(2,1)S(1)}, bf16[128,2048]{1,0:T(8,128)(2,1)S(1)}, u32[]{:S(2)}, u32[]{:S(2)}) collective-permute-start(bf16[128,2048]{1,0:T(8,128)(2,1)S(1)} %dynamic-slice_bitcast_fusion.4), channel_id=1, source_target_pairs={{0,1},{2,3},{4,5},{6,7},{8,9},{10,11},{12,13},{14,15},{16,17},{18,... | collective-permute-start | bytes 1572872 | tf_op jit(solution)/shard_map/ppermute | solution.py:396
  181.8 208.7 %collective-permute-start.40 = (bf16[256,2048]{1,0:T(8,128)(2,1)}, bf16[256,2048]{1,0:T(8,128)(2,1)}, u32[]{:S(2)}, u32[]{:S(2)}) collective-permute-start(bf16[256,2048]{1,0:T(8,128)(2,1)} %get-tuple-element.170), channel_id=1, source_target_pairs={{1,0},{3,2},{5,4},{7,6},{9,8},{11,10},{13,12},{15,14},{17,16},{19,... | collective-permute-start | bytes 3145736 | tf_op jit(solution)/shard_map/ppermute | solution.py:425
  393.2 17.6 %collective-permute-start.54 = (bf16[2,32,2048]{2,1,0:T(8,128)(2,1)S(1)}, bf16[2,32,2048]{2,1,0:T(8,128)(2,1)S(1)}, u32[]{:S(2)}, u32[]{:S(2)}) collective-permute-start(bf16[2,32,2048]{2,1,0:T(8,128)(2,1)S(1)} %get-tuple-element.198), channel_id=1, source_target_pairs={{0,128},{128,2},{2,130},{130,4},{4,132},{132,6},{6,134},{134,0},{1... | collective-permute-start | bytes 786440 | tf_op jit(solution)/shard_map/ppermute | solution.py:277
  393.4 17.4 %collective-permute-start.58 = (bf16[2,32,2048]{2,1,0:T(8,128)(2,1)S(1)}, bf16[2,32,2048]{2,1,0:T(8,128)(2,1)S(1)}, u32[]{:S(2)}, u32[]{:S(2)}) collective-permute-start(bf16[2,32,2048]{2,1,0:T(8,128)(2,1)S(1)} %get-tuple-element.201), channel_id=1, source_target_pairs={{0,134},{128,0},{2,128},{130,2},{4,130},{132,4},{6,132},{134,6},{1... | collective-permute-start | bytes 786440 | tf_op jit(solution)/shard_map/ppermute | solution.py:277
  407.5 17.2 %collective-permute-start.41 = (bf16[256,1536]{1,0:T(8,128)(2,1)S(1)}, bf16[256,1536]{1,0:T(8,128)(2,1)S(1)}, u32[]{:S(2)}, u32[]{:S(2)}) collective-permute-start(bf16[256,1536]{1,0:T(8,128)(2,1)S(1)} %get-tuple-element.190), channel_id=1, source_target_pairs={{0,8},{8,16},{16,24},{24,0},{1,9},{9,17},{17,25},{25,1},{2,10},{10... | collective-permute-start | bytes 2359304 | tf_op jit(solution)/shard_map/ppermute | solution.py:273
  408.7 15.9 %collective-permute-start.43 = (bf16[256,1536]{1,0:T(8,128)(2,1)S(1)}, bf16[256,1536]{1,0:T(8,128)(2,1)S(1)}, u32[]{:S(2)}, u32[]{:S(2)}) collective-permute-start(bf16[256,1536]{1,0:T(8,128)(2,1)S(1)} %get-tuple-element.191), channel_id=1, source_target_pairs={{0,24},{8,0},{16,8},{24,16},{1,25},{9,1},{17,9},{25,17},{2,26},{10... | collective-permute-start | bytes 2359304 | tf_op jit(solution)/shard_map/ppermute | solution.py:273
  411.0 20.9 %collective-permute-start.55 = (bf16[4,32,2048]{2,1,0:T(8,128)(2,1)S(1)}, bf16[4,32,2048]{2,1,0:T(8,128)(2,1)S(1)}, u32[]{:S(2)}, u32[]{:S(2)}) collective-permute-start(bf16[4,32,2048]{2,1,0:T(8,128)(2,1)S(1)} %pad_maximum_fusion.4), channel_id=1, source_target_pairs={{0,128},{128,2},{2,130},{130,4},{4,132},{132,6},{6,134},{134,0},{1... | collective-permute-start | bytes 1572872 | tf_op jit(solution)/shard_map/ppermute | solution.py:277
  425.2 30.7 %collective-permute-start.42 = (bf16[512,1536]{1,0:T(8,128)(2,1)S(1)}, bf16[512,1536]{1,0:T(8,128)(2,1)S(1)}, u32[]{:S(2)}, u32[]{:S(2)}) collective-permute-start(bf16[512,1536]{1,0:T(8,128)(2,1)S(1)} %pad_maximum_fusion), channel_id=1, source_target_pairs={{0,8},{8,16},{16,24},{24,0},{1,9},{9,17},{17,25},{25,1},{2,10},{10... | collective-permute-start | bytes 4718600 | tf_op jit(solution)/shard_map/ppermute | solution.py:273
  426.3 29.6 %collective-permute-start.44 = (bf16[512,1536]{1,0:T(8,128)(2,1)S(1)}, bf16[512,1536]{1,0:T(8,128)(2,1)S(1)}, u32[]{:S(2)}, u32[]{:S(2)}) collective-permute-start(bf16[512,1536]{1,0:T(8,128)(2,1)S(1)} %pad_maximum_fusion.1), channel_id=1, source_target_pairs={{0,24},{8,0},{16,8},{24,16},{1,25},{9,1},{17,9},{25,17},{2,26},{10... | collective-permute-start | bytes 4718600 | tf_op jit(solution)/shard_map/ppermute | solution.py:273
  428.8 14.8 %collective-permute-start.59 = (bf16[4,32,2048]{2,1,0:T(8,128)(2,1)S(1)}, bf16[4,32,2048]{2,1,0:T(8,128)(2,1)S(1)}, u32[]{:S(2)}, u32[]{:S(2)}) collective-permute-start(bf16[4,32,2048]{2,1,0:T(8,128)(2,1)S(1)} %pad_maximum_fusion.5), channel_id=1, source_target_pairs={{0,134},{128,0},{2,128},{130,2},{4,130},{132,4},{6,132},{134,6},{1... | collective-permute-start | bytes 1572872 | tf_op jit(solution)/shard_map/ppermute | solution.py:277
  432.1 13.3 %collective-permute-start.56 = (bf16[4,32,2048]{2,1,0:T(8,128)(2,1)S(1)}, bf16[4,32,2048]{2,1,0:T(8,128)(2,1)S(1)}, u32[]{:S(2)}, u32[]{:S(2)}) collective-permute-start(bf16[4,32,2048]{2,1,0:T(8,128)(2,1)S(1)} %fusion.6), channel_id=1, source_target_pairs={{0,128},{128,2},{2,130},{130,4},{4,132},{132,6},{6,134},{134,0},{1... | collective-permute-start | bytes 1572872 | tf_op jit(solution)/shard_map/ppermute | solution.py:277
  445.9 14.0 %collective-permute-start.60 = (bf16[4,32,2048]{2,1,0:T(8,128)(2,1)S(1)}, bf16[4,32,2048]{2,1,0:T(8,128)(2,1)S(1)}, u32[]{:S(2)}, u32[]{:S(2)}) collective-permute-start(bf16[4,32,2048]{2,1,0:T(8,128)(2,1)S(1)} %get-tuple-element.195), channel_id=1, source_target_pairs={{0,134},{128,0},{2,128},{130,2},{4,130},{132,4},{6,132},{134,6},{1... | collective-permute-start | bytes 1572872 | tf_op jit(solution)/shard_map/ppermute | solution.py:277
  447.5 22.9 %collective-permute-start.57 = (bf16[4,32,2048]{2,1,0:T(8,128)(2,1)S(1)}, bf16[4,32,2048]{2,1,0:T(8,128)(2,1)S(1)}, u32[]{:S(2)}, u32[]{:S(2)}) collective-permute-start(bf16[4,32,2048]{2,1,0:T(8,128)(2,1)S(1)} %get-tuple-element.194), channel_id=1, source_target_pairs={{0,128},{128,2},{2,130},{130,4},{4,132},{132,6},{6,134},{134,0},{1... | collective-permute-start | bytes 1572872 | tf_op jit(solution)/shard_map/ppermute | solution.py:277
  456.6 6.6 %collective-permute-start.45 = (bf16[32,1536]{1,0:T(8,128)(2,1)S(1)}, bf16[32,1536]{1,0:T(8,128)(2,1)S(1)}, u32[]{:S(2)}, u32[]{:S(2)}) collective-permute-start(bf16[32,1536]{1,0:T(8,128)(2,1)S(1)} %get-tuple-element.206), channel_id=1, source_target_pairs={{0,128},{128,2},{2,130},{130,4},{4,132},{132,6},{6,134},{134,0},{1... | collective-permute-start | bytes 294920 | tf_op jit(solution)/shard_map/ppermute | solution.py:277
  456.7 6.6 %collective-permute-start.49 = (bf16[32,1536]{1,0:T(8,128)(2,1)S(1)}, bf16[32,1536]{1,0:T(8,128)(2,1)S(1)}, u32[]{:S(2)}, u32[]{:S(2)}) collective-permute-start(bf16[32,1536]{1,0:T(8,128)(2,1)S(1)} %get-tuple-element.207), channel_id=1, source_target_pairs={{0,134},{128,0},{2,128},{130,2},{4,130},{132,4},{6,132},{134,6},{1... | collective-permute-start | bytes 294920 | tf_op jit(solution)/shard_map/ppermute | solution.py:277
  460.0 11.6 %collective-permute-start.61 = (bf16[4,32,2048]{2,1,0:T(8,128)(2,1)S(1)}, bf16[4,32,2048]{2,1,0:T(8,128)(2,1)S(1)}, u32[]{:S(2)}, u32[]{:S(2)}) collective-permute-start(bf16[4,32,2048]{2,1,0:T(8,128)(2,1)S(1)} %fusion.5), channel_id=1, source_target_pairs={{0,134},{128,0},{2,128},{130,2},{4,130},{132,4},{6,132},{134,6},{1... | collective-permute-start | bytes 1572872 | tf_op jit(solution)/shard_map/ppermute | solution.py:277
  464.6 10.2 %collective-permute-start.50 = (bf16[64,1536]{1,0:T(8,128)(2,1)S(1)}, bf16[64,1536]{1,0:T(8,128)(2,1)S(1)}, u32[]{:S(2)}, u32[]{:S(2)}) collective-permute-start(bf16[64,1536]{1,0:T(8,128)(2,1)S(1)} %pad_maximum_fusion.7), channel_id=1, source_target_pairs={{0,134},{128,0},{2,128},{130,2},{4,130},{132,4},{6,132},{134,6},{1... | collective-permute-start | bytes 589832 | tf_op jit(solution)/shard_map/ppermute | solution.py:277
  469.5 7.0 %collective-permute-start.47 = (bf16[64,1536]{1,0:T(8,128)(2,1)S(1)}, bf16[64,1536]{1,0:T(8,128)(2,1)S(1)}, u32[]{:S(2)}, u32[]{:S(2)}) collective-permute-start(bf16[64,1536]{1,0:T(8,128)(2,1)S(1)} %fusion.16), channel_id=1, source_target_pairs={{0,128},{128,2},{2,130},{130,4},{4,132},{132,6},{6,134},{134,0},{1... | collective-permute-start | bytes 589832 | tf_op jit(solution)/shard_map/ppermute | solution.py:277
  476.5 10.1 %collective-permute-start.51 = (bf16[64,1536]{1,0:T(8,128)(2,1)S(1)}, bf16[64,1536]{1,0:T(8,128)(2,1)S(1)}, u32[]{:S(2)}, u32[]{:S(2)}) collective-permute-start(bf16[64,1536]{1,0:T(8,128)(2,1)S(1)} %get-tuple-element.203), channel_id=1, source_target_pairs={{0,134},{128,0},{2,128},{130,2},{4,130},{132,4},{6,132},{134,6},{1... | collective-permute-start | bytes 589832 | tf_op jit(solution)/shard_map/ppermute | solution.py:277
  481.3 7.2 %collective-permute-start.62 = (bf16[32,2048]{1,0:T(8,128)(2,1)S(1)}, bf16[32,2048]{1,0:T(8,128)(2,1)S(1)}, u32[]{:S(2)}, u32[]{:S(2)}) collective-permute-start(bf16[32,2048]{1,0:T(8,128)(2,1)S(1)} %get-tuple-element.210), channel_id=1, source_target_pairs={{0,16},{8,24},{16,0},{24,8},{1,17},{9,25},{17,1},{25,9},{2,18},{10... | collective-permute-start | bytes 393224 | tf_op jit(solution)/shard_map/ppermute | solution.py:273
  489.3 9.3 %collective-permute-start.65 = (bf16[32,2048]{1,0:T(8,128)(2,1)S(1)}, bf16[32,2048]{1,0:T(8,128)(2,1)S(1)}, u32[]{:S(2)}, u32[]{:S(2)}) collective-permute-start(bf16[32,2048]{1,0:T(8,128)(2,1)S(1)} %fusion.22), channel_id=1, source_target_pairs={{0,0},{128,1},{2,2},{130,3},{4,4},{132,5},{6,6},{134,7},{8,8},{136... | collective-permute-start | bytes 393224 | tf_op jit(solution)/shard_map/ppermute | solution.py:429
  492.5 10.0 %collective-permute-start.53 = (bf16[64,1536]{1,0:T(8,128)(2,1)S(1)}, bf16[64,1536]{1,0:T(8,128)(2,1)S(1)}, u32[]{:S(2)}, u32[]{:S(2)}) collective-permute-start(bf16[64,1536]{1,0:T(8,128)(2,1)S(1)} %fusion.19), channel_id=1, source_target_pairs={{0,0},{128,1},{2,2},{130,3},{4,4},{132,5},{6,6},{134,7},{8,8},{136... | collective-permute-start | bytes 589832 | tf_op jit(solution)/shard_map/ppermute | solution.py:430
  (32 other events, 273.1 us)

commit v6 on v5

--- a/solution.py
+++ b/solution.py
@@ -291,23 +291,9 @@
     return (own.astype(jnp.float32) + came.astype(jnp.float32)).astype(jnp.bfloat16)
 
 
-def scatter_ring(take, count, send):
-    far = count // 2
-    up, down = send(take(far, 0), 1), send(take(far, 1), -1)
-    for step in range(far - 1, 0, -1):
-        if step == far - 1:
-            next_up = jnp.concatenate([add(take(step, 0), up), take(step, 1)])
-            next_down = jnp.concatenate([take(-step, 0), add(take(-step, 1), down)])
-        else:
-            next_up, next_down = add(take(step), up), add(take(-step), down)
-        up, down = send(next_up, 1), send(next_down, -1)
-    total = take(0).astype(jnp.float32) + up.astype(jnp.float32) + down.astype(jnp.float32)
-    return total.astype(jnp.bfloat16)
-
-
-def scatter_direct(take, send):
+def scatter_direct(take, send, steps):
     total = take(0).astype(jnp.float32)
-    for came in [send(take(step), step) for step in (2, 1, -1)]:
+    for came in [send(take(step), step) for step in steps]:
         total = total + came.astype(jnp.float32)
     return total.astype(jnp.bfloat16)
 
@@ -370,14 +356,36 @@
     )(jnp.stack([x, z]), *qkv_parts, *out_parts)
 
 
-def scatter_qkv(part, turns, spins):
-    mine = scatter_ring(taker(part.reshape(4, 512, WCOLS), turns, 0, 1), 4, send_x)
-    return scatter_ring(taker(mine.reshape(8, 64, WCOLS), spins, 0, 1), 8, send_z)
-
-
-def scatter_out(part, turns, spins):
-    mine = scatter_ring(taker(part.reshape(4, 8, 32, D), spins, 1, 0), 8, send_z)
-    return scatter_direct(taker(mine, turns, 0, 1), send_x)
+def sum_of(*terms):
+    return sum(term.astype(jnp.float32) for term in terms).astype(jnp.bfloat16)
+
+
+def scatter_start(part_out, spins):
+    take = taker(part_out.reshape(4, 8, 32, D), spins, 1, 0)
+    return take, send_z(take(4, 0), 1), send_z(take(4, 1), -1)
+
+
+def scatter_both(part_qkv, started, turns, spins):
+    take_z, up_z, down_z = started
+    take_x = taker(part_qkv.reshape(4, 512, WCOLS), turns, 0, 1)
+    up_x, down_x = send_x(take_x(2, 0), 1), send_x(take_x(2, 1), -1)
+    out_up = jnp.concatenate([add(take_z(3, 0), up_z), take_z(3, 1)])
+    out_down = jnp.concatenate([take_z(-3, 0), add(take_z(-3, 1), down_z)])
+    up_z, down_z = send_z(out_up, 1), send_z(out_down, -1)
+    qkv_up = jnp.concatenate([add(take_x(1, 0), up_x), take_x(1, 1)])
+    qkv_down = jnp.concatenate([take_x(-1, 0), add(take_x(-1, 1), down_x)])
+    out_up, out_down = add(take_z(2), up_z), add(take_z(-2), down_z)
+    qkv_up, qkv_down, out_up, out_down = lax.optimization_barrier((qkv_up, qkv_down, out_up, out_down))
+    up_x, down_x = send_x(qkv_up, 1), send_x(qkv_down, -1)
+    up_z, down_z = send_z(out_up, 1), send_z(out_down, -1)
+    up_z, down_z = send_z(add(take_z(1), up_z), 1), send_z(add(take_z(-1), down_z), -1)
+    mine_out = sum_of(take_z(0), up_z, down_z)
+    mine_qkv = sum_of(take_x(0), up_x, down_x)
+    grad_out = scatter_direct(taker(mine_out, turns, 0, 1), send_x, (2, 1, -1))
+    grad_qkv = scatter_direct(
+        taker(mine_qkv.reshape(8, 64, WCOLS), spins, 0, 1), send_z, (4, 3, -3, 2, -2, 1, -1)
+    )
+    return grad_qkv, grad_out
 
 
 def on_device(inputs, cotangent, joined, w_qkv, w_out):
@@ -418,14 +426,14 @@
             arrived = jnp.where(stage == 0, upstream, ups)
             part_out = lax.dot_general(ctx, arrived, contract, preferred_element_type=jnp.float32).astype(jnp.bfloat16)
             part_out, upstream = lax.optimization_barrier((part_out, upstream))
+            started = scatter_start(part_out, spins)
         result, dproj, ups = backward_layer(
             layer, places[layer], upstream, kept, proj, ctx, marks, full_qkv, full_out, dproj, ups
         )
         if layer:
             upstream = lax.ppermute(result, STAGE, [(layer, layer - 1)])
     part_qkv = lax.dot_general(normed, dproj, contract, preferred_element_type=jnp.float32).astype(jnp.bfloat16)
-    grad_out = scatter_out(part_out, turns, spins)
-    grad_qkv = scatter_qkv(part_qkv, turns, spins)
+    grad_qkv, grad_out = scatter_both(part_qkv, started, turns, spins)
     grad_out = lax.ppermute(grad_out, NAMES, regroup(True)).astype(jnp.float32)
     grad_qkv = lax.ppermute(grad_qkv, NAMES, regroup(True)).astype(jnp.float32)
     return (grad_qkv[None], grad_out[None])

time: 513 us -> 514 us (level)
    ppermute x32 -> x31, starting transfers between devices: 52.6 us -> 56.7 us  [send_z(): lax.ppermute(value, ('zlo', 'zhi'), [(z_index(i), z_index((i + step) % 8)...]
    ppermute x32 -> x31, waiting for transfers between devices: 61.5 us -> 62.4 us  [send_z(): lax.ppermute(value, ('zlo', 'zhi'), [(z_index(i), z_index((i + step) % 8)...]
  transfers between devices with their start and end apart: 66 -> 65, of which waited for: 30 -> 32; matrix products, arithmetic and copies ran while one was open for 5% -> 4% of each run, Pallas kernels for 2% -> 2%
where the time goes in v6:
time: 514 us; the launch traced here: 504 us
  waiting for transfers between devices  303 us (59%)
  starting transfers between devices  130 us (25%)
  Pallas kernels  36.6 us (7%)
  local copies, waits for them, and re-layouts  19.7 us (4%)
  other arithmetic  8.58 us (2%)
    ppermute x7, waiting for transfers between devices, on_device(): upstream = lax.ppermute(result, STAGE, [(layer, layer - 1)])  207 us
    ppermute x31, waiting for transfers between devices, send_z(): lax.ppermute(value, ('zlo', 'zhi'), [(z_index(i), z_index((i + step) % 8)...  62.4 us
    ppermute x31, starting transfers between devices, send_z(): lax.ppermute(value, ('zlo', 'zhi'), [(z_index(i), z_index((i + step) % 8)...  56.7 us
    ppermute x1, starting transfers between devices, on_device(): upstream = jnp.concatenate([lax.ppermute(block, 'core', [(0, 1)]), block])  23.6 us
    ppermute x14, starting transfers between devices, send_x(): return lax.ppermute(value, 'x', [(i, (i + step) % 4) for i in range(4)])  23.3 us
    ppermute x14, waiting for transfers between devices, send_x(): return lax.ppermute(value, 'x', [(i, (i + step) % 4) for i in range(4)])  21.9 us
    pallas_call x8, Pallas kernels, forward_layer(): pl.pallas_call(functools.partial(forward_kernel, final), out_shape=(v16(R...  14.7 us
    pallas_call x8, Pallas kernels, backward_layer(): pl.pallas_call(functools.partial(backward_kernel, last), out_shape=(v16(R...  13.4 us
  transfers between devices with their start and end apart: 65, of which 32 were waited for; matrix products, arithmetic and copies ran while one was open for 4% of the time, Pallas kernels for 2%

profile of v6, /device:TPU:32, one launch (start us, length us, event | category | flops | bytes accessed | tf_op | source)
XLA Modules:
  0.0 504.3 jit_solution(10516923109806786867)
XLA Ops:
  0.6 4.8 collective-permute-start.14
  5.4 2.4 collective-permute-start.1
  8.2 2.8 collective-permute-start.15
  12.8 2.0 collective-permute-start.5
  17.4 3.0 collective-permute-done.2
  20.3 3.5 collective-permute-start.3
  25.0 2.6 collective-permute-done.3
  27.5 3.3 collective-permute-start.4
  32.0 6.2 %collective-permute-done.7 = bf16[64,1536]{1,0:T(8,128)(2,1)S(1)} collective-permute-done((bf16[64,1536]{1,0:T(8,128)(2,1)S(1)}, bf16[64,1536]{1,0:T(8,128)(2,1)S(1)}, u32[]{:S(2)}, u32[]{:S(2)}) %collective-permute-start.7) | collective-permute-done | bytes 196640 | tf_op jit(solution)/shard_map/ppermute | solution.py:277
  38.3 3.3 collective-permute-start.9
  54.9 7.7 %collective-permute-done.21.refs_13_ = bf16[128,2048]{1,0:T(8,128)(2,1)S(1)} collective-permute-done((bf16[128,2048]{1,0:T(8,128)(2,1)S(1)}, bf16[128,2048]{1,0:T(8,128)(2,1)S(1)}, u32[]{:S(2)}, u32[]{:S(2)}) %collective-permute-start.21) | collective-permute-done | bytes 524320 | tf_op jit(solution)/shard_map/ppermute | solution.py:277
  62.6 2.4 collective-permute-start.22
  67.1 8.7 %collective-permute-done.22.refs_12_ = bf16[128,2048]{1,0:T(8,128)(2,1)} collective-permute-done((bf16[128,2048]{1,0:T(8,128)(2,1)S(1)}, bf16[128,2048]{1,0:T(8,128)(2,1)}, u32[]{:S(2)}, u32[]{:S(2)}) %collective-permute-start.22) | collective-permute-done | bytes 524320 | tf_op jit(solution)/shard_map/ppermute | solution.py:277
  78.4 2.4 collective-permute-start.20
  86.1 2.1 slice.27
  95.6 3.2 collective-permute-start.25
  100.2 3.7 collective-permute-done.24.refs_9_
  105.6 2.7 collective-permute-done.13.refs_3_
  110.4 8.5 %assemble.1 = (bf16[2048,1536]{1,0:T(8,128)(2,1)S(1)}, bf16[1024,2048]{1,0:T(8,128)(2,1)S(1)}) custom-call(s32[2]{0:T(128)S(1)} %pad_add_fusion.8.place, bf16[512,1536]{1,0:T(8,128)(2,1)} %constant_dynamic-update-slice_fusion.refs_0_, bf16[512,1536]{1,0:T(8,128)(2,1)} %collective-permute-done.10.refs_1_, ...), custom_call_target="tpu_custom_call" | custom-call | bytes 21000000 | tf_op jit(solution)/shard_map/assemble/pallas_call | solution.py:347
  119.3 9.6 %forward_layer.7 = (bf16[256,2048]{1,0:T(8,128)(2,1)S(1)}, bf16[256,2048]{1,0:T(8,128)(2,1)S(1)}, bf16[256,1536]{1,0:T(8,128)(2,1)S(1)}, bf16[256,1024]{1,0:T(8,...) custom-call(s32[2]{0:T(128)S(1)} %get-tuple-element.106.place.h_v.wq, ...), custom_call_target="tpu_custom_call", output_to_operand_aliasing={{1}: (4, {}), {2}: (5, {}), {3}: (6, {}), {4}: (7, {}), {5}... | custom-call | flops 3000000000 | bytes 14000000 | tf_op jit(solution)/shard_map/forward_layer/pallas_call | solution.py:163
  130.3 2.2 collective-permute-done.26.h_v
  139.8 3.4 collective-permute-start.32
  143.3 23.6 %collective-permute-start.33 = (bf16[128,2048]{1,0:T(8,128)(2,1)S(1)}, bf16[128,2048]{1,0:T(8,128)(2,1)S(1)}, u32[]{:S(2)}, u32[]{:S(2)}) collective-permute-start(bf16[128,2048]{1,0:T(8,128)(2,1)S(1)} %dynamic-slice_bitcast_fusion.4), channel_id=1, source_target_pairs={{0,1},{2,3},{4,5},{6,7},{8,9},{10,11},{12,13},{14,15},{16,17},{18,... | collective-permute-start | bytes 1572872 | tf_op jit(solution)/shard_map/ppermute | solution.py:404
  183.1 207.3 %collective-permute-done.40.u_v = bf16[256,2048]{1,0:T(8,128)(2,1)} collective-permute-done((bf16[256,2048]{1,0:T(8,128)(2,1)}, bf16[256,2048]{1,0:T(8,128)(2,1)}, u32[]{:S(2)}, u32[]{:S(2)}) %collective-permute-start.40) | collective-permute-done | bytes 1048608 | tf_op jit(solution)/shard_map/ppermute | solution.py:434
  390.5 2.7 convolution_convert_fusion.1
  393.4 3.7 collective-permute-start.45
  397.1 8.3 %backward_last.1 = (bf16[256,2048]{1,0:T(8,128)(2,1)}, bf16[256,1536]{1,0:T(8,128)(2,1)S(1)}, bf16[256,2048]{1,0:T(8,128)(2,1)S(1)}) custom-call(s32[2]{0:T(128)S(1)} %get-tuple-element.106.place.h_v.wq_v, bf16[256,2048]{1,0:T(8,128)(2,1)} %collective-permute-done.40.u_v, ...), custom_call_target="tpu_custom_call", output_to_operand_aliasing={{1}: (8, {}), {2}: (9, {})} | custom-call | flops 4000000000 | bytes 15000000 | tf_op jit(solution)/shard_map/backward_last/pallas_call | solution.py:237
  408.8 2.1 collective-permute-start.42
  411.2 3.2 collective-permute-start.46
  414.4 7.8 %collective-permute-done.41 = bf16[256,1536]{1,0:T(8,128)(2,1)S(1)} collective-permute-done((bf16[256,1536]{1,0:T(8,128)(2,1)S(1)}, bf16[256,1536]{1,0:T(8,128)(2,1)S(1)}, u32[]{:S(2)}, u32[]{:S(2)}) %collective-permute-start.41) | collective-permute-done | bytes 786464 | tf_op jit(solution)/shard_map/ppermute | solution.py:273
  424.3 2.9 collective-permute-start.59
  427.4 3.0 collective-permute-start.48
  430.4 6.5 %collective-permute-done.57 = bf16[4,32,2048]{2,1,0:T(8,128)(2,1)S(1)} collective-permute-done((bf16[4,32,2048]{2,1,0:T(8,128)(2,1)S(1)}, bf16[4,32,2048]{2,1,0:T(8,128)(2,1)S(1)}, u32[]{:S(2)}, u32[]{:S(2)}) %collective-permute-start.57) | collective-permute-done | bytes 524320 | tf_op jit(solution)/shard_map/ppermute | solution.py:277
  438.1 2.4 collective-permute-start.58
  441.4 7.1 %collective-permute-done.58 = bf16[4,32,2048]{2,1,0:T(8,128)(2,1)S(1)} collective-permute-done((bf16[4,32,2048]{2,1,0:T(8,128)(2,1)S(1)}, bf16[4,32,2048]{2,1,0:T(8,128)(2,1)S(1)}, u32[]{:S(2)}, u32[]{:S(2)}) %collective-permute-start.58) | collective-permute-done | bytes 524320 | tf_op jit(solution)/shard_map/ppermute | solution.py:277
  450.0 6.4 %collective-permute-done.47 = bf16[512,1536]{1,0:T(8,128)(2,1)S(1)} collective-permute-done((bf16[512,1536]{1,0:T(8,128)(2,1)S(1)}, bf16[512,1536]{1,0:T(8,128)(2,1)S(1)}, u32[]{:S(2)}, u32[]{:S(2)}) %collective-permute-start.47) | collective-permute-done | bytes 1572896 | tf_op jit(solution)/shard_map/ppermute | solution.py:273
  457.1 2.9 collective-permute-start.49
  460.0 7.1 %collective-permute-start.50 = (bf16[64,1536]{1,0:T(8,128)(2,1)S(1)}, bf16[64,1536]{1,0:T(8,128)(2,1)S(1)}, u32[]{:S(2)}, u32[]{:S(2)}) collective-permute-start(bf16[64,1536]{1,0:T(8,128)(2,1)S(1)} %get-tuple-element.218), channel_id=1, source_target_pairs={{0,130},{128,4},{2,132},{130,6},{4,134},{132,0},{6,128},{134,2},{1... | collective-permute-start | bytes 589832 | tf_op jit(solution)/shard_map/ppermute | solution.py:277
  467.1 2.6 collective-permute-start.61
  471.1 1.9 collective-permute-start.63
  473.7 2.2 collective-permute-done.62
  476.1 4.0 collective-permute-start.53
  480.1 2.0 collective-permute-start.55
  482.2 6.0 %collective-permute-done.51 = bf16[64,1536]{1,0:T(8,128)(2,1)S(1)} collective-permute-done((bf16[64,1536]{1,0:T(8,128)(2,1)S(1)}, bf16[64,1536]{1,0:T(8,128)(2,1)S(1)}, u32[]{:S(2)}, u32[]{:S(2)}) %collective-permute-start.51) | collective-permute-done | bytes 196640 | tf_op jit(solution)/shard_map/ppermute | solution.py:277
  488.2 1.9 collective-permute-start.64
  493.1 1.9 collective-permute-start.56
  495.0 2.5 collective-permute-done.64
  498.3 4.8 collective-permute-done.56
  (183 shorter events, 85.2 us)
Async XLA Ops:
  0.6 7.6 %collective-permute-start.14 = (bf16[32,2048]{1,0:T(8,128)(2,1)}, bf16[32,2048]{1,0:T(8,128)(2,1)S(1)}, u32[]{:S(2)}, u32[]{:S(2)}) collective-permute-start(bf16[32,2048]{1,0:T(8,128)(2,1)} %bitcast.126), channel_id=1, source_target_pairs={{0,0},{1,128},{2,2},{3,130},{4,4},{5,132},{6,6},{7,134},{8,8},{9,1... | collective-permute-start | bytes 393224 | tf_op jit(solution)/shard_map/ppermute | solution.py:399
  5.4 7.3 %collective-permute-start.1 = (bf16[64,1536]{1,0:T(8,128)(2,1)}, bf16[64,1536]{1,0:T(8,128)(2,1)S(1)}, u32[]{:S(2)}, u32[]{:S(2)}) collective-permute-start(bf16[64,1536]{1,0:T(8,128)(2,1)} %bitcast.125), channel_id=1, source_target_pairs={{0,0},{1,128},{2,2},{3,130},{4,4},{5,132},{6,6},{7,134},{8,8},{9,1... | collective-permute-start | bytes 589832 | tf_op jit(solution)/shard_map/ppermute | solution.py:398
  8.2 9.1 %collective-permute-start.15 = (bf16[32,2048]{1,0:T(8,128)(2,1)S(1)}, bf16[32,2048]{1,0:T(8,128)(2,1)S(1)}, u32[]{:S(2)}, u32[]{:S(2)}) collective-permute-start(bf16[32,2048]{1,0:T(8,128)(2,1)S(1)} %collective-permute-done.14), channel_id=1, source_target_pairs={{0,24},{8,0},{16,8},{24,16},{1,25},{9,1},{17,9},{25,17},{2,26},{10... | collective-permute-start | bytes 393224 | tf_op jit(solution)/shard_map/ppermute | solution.py:273
  11.0 39.6 %collective-permute-start.16 = (bf16[32,2048]{1,0:T(8,128)(2,1)S(1)}, bf16[32,2048]{1,0:T(8,128)(2,1)S(1)}, u32[]{:S(2)}, u32[]{:S(2)}) collective-permute-start(bf16[32,2048]{1,0:T(8,128)(2,1)S(1)} %collective-permute-done.14), channel_id=1, source_target_pairs={{0,16},{8,24},{16,0},{24,8},{1,17},{9,25},{17,1},{25,9},{2,18},{10... | collective-permute-start | bytes 393224 | tf_op jit(solution)/shard_map/ppermute | solution.py:273
  11.8 38.8 %collective-permute-start.17 = (bf16[32,2048]{1,0:T(8,128)(2,1)S(1)}, bf16[32,2048]{1,0:T(8,128)(2,1)S(1)}, u32[]{:S(2)}, u32[]{:S(2)}) collective-permute-start(bf16[32,2048]{1,0:T(8,128)(2,1)S(1)} %collective-permute-done.14), channel_id=1, source_target_pairs={{0,8},{8,16},{16,24},{24,0},{1,9},{9,17},{17,25},{25,1},{2,10},{10... | collective-permute-start | bytes 393224 | tf_op jit(solution)/shard_map/ppermute | solution.py:273
  12.7 7.6 %collective-permute-start.2 = (bf16[64,1536]{1,0:T(8,128)(2,1)S(1)}, bf16[64,1536]{1,0:T(8,128)(2,1)S(1)}, u32[]{:S(2)}, u32[]{:S(2)}) collective-permute-start(bf16[64,1536]{1,0:T(8,128)(2,1)S(1)} %collective-permute-done.1), channel_id=1, source_target_pairs={{0,134},{128,0},{2,128},{130,2},{4,130},{132,4},{6,132},{134,6},{1... | collective-permute-start | bytes 589832 | tf_op jit(solution)/shard_map/ppermute | solution.py:277
  12.8 11.5 %collective-permute-start.5 = (bf16[64,1536]{1,0:T(8,128)(2,1)S(1)}, bf16[64,1536]{1,0:T(8,128)(2,1)S(1)}, u32[]{:S(2)}, u32[]{:S(2)}) collective-permute-start(bf16[64,1536]{1,0:T(8,128)(2,1)S(1)} %collective-permute-done.1), channel_id=1, source_target_pairs={{0,128},{128,2},{2,130},{130,4},{4,132},{132,6},{6,134},{134,0},{1... | collective-permute-start | bytes 589832 | tf_op jit(solution)/shard_map/ppermute | solution.py:277
  20.3 7.2 %collective-permute-start.3 = (bf16[64,1536]{1,0:T(8,128)(2,1)S(1)}, bf16[64,1536]{1,0:T(8,128)(2,1)S(1)}, u32[]{:S(2)}, u32[]{:S(2)}) collective-permute-start(bf16[64,1536]{1,0:T(8,128)(2,1)S(1)} %collective-permute-done.2), channel_id=1, source_target_pairs={{0,134},{128,0},{2,128},{130,2},{4,130},{132,4},{6,132},{134,6},{1... | collective-permute-start | bytes 589832 | tf_op jit(solution)/shard_map/ppermute | solution.py:277
  24.3 7.0 %collective-permute-start.6 = (bf16[64,1536]{1,0:T(8,128)(2,1)S(1)}, bf16[64,1536]{1,0:T(8,128)(2,1)S(1)}, u32[]{:S(2)}, u32[]{:S(2)}) collective-permute-start(bf16[64,1536]{1,0:T(8,128)(2,1)S(1)} %collective-permute-done.5), channel_id=1, source_target_pairs={{0,128},{128,2},{2,130},{130,4},{4,132},{132,6},{6,134},{134,0},{1... | collective-permute-start | bytes 589832 | tf_op jit(solution)/shard_map/ppermute | solution.py:277
  27.5 10.7 %collective-permute-start.4 = (bf16[64,1536]{1,0:T(8,128)(2,1)S(1)}, bf16[64,1536]{1,0:T(8,128)(2,1)S(1)}, u32[]{:S(2)}, u32[]{:S(2)}) collective-permute-start(bf16[64,1536]{1,0:T(8,128)(2,1)S(1)} %collective-permute-done.3), channel_id=1, source_target_pairs={{0,134},{128,0},{2,128},{130,2},{4,130},{132,4},{6,132},{134,6},{1... | collective-permute-start | bytes 589832 | tf_op jit(solution)/shard_map/ppermute | solution.py:277
  31.3 6.9 %collective-permute-start.7 = (bf16[64,1536]{1,0:T(8,128)(2,1)S(1)}, bf16[64,1536]{1,0:T(8,128)(2,1)S(1)}, u32[]{:S(2)}, u32[]{:S(2)}) collective-permute-start(bf16[64,1536]{1,0:T(8,128)(2,1)S(1)} %collective-permute-done.6), channel_id=1, source_target_pairs={{0,128},{128,2},{2,130},{130,4},{4,132},{132,6},{6,134},{134,0},{1... | collective-permute-start | bytes 589832 | tf_op jit(solution)/shard_map/ppermute | solution.py:277
  47.4 36.2 %collective-permute-start.11 = (bf16[512,1536]{1,0:T(8,128)(2,1)}, bf16[512,1536]{1,0:T(8,128)(2,1)S(1)}, u32[]{:S(2)}, u32[]{:S(2)}) collective-permute-start(bf16[512,1536]{1,0:T(8,128)(2,1)} %constant_dynamic-update-slice_fusion.refs_0_), channel_id=1, source_target_pairs={{0,8},{8,16},{16,24},{24,0},{1,9},{9,17},{17,25},{25,1},{2,10},{10... | collective-permute-start | bytes 4718600 | tf_op jit(solution)/shard_map/ppermute | solution.py:273
  49.0 37.1 %collective-permute-start.10 = (bf16[512,1536]{1,0:T(8,128)(2,1)}, bf16[512,1536]{1,0:T(8,128)(2,1)}, u32[]{:S(2)}, u32[]{:S(2)}) collective-permute-start(bf16[512,1536]{1,0:T(8,128)(2,1)} %constant_dynamic-update-slice_fusion.refs_0_), channel_id=1, source_target_pairs={{0,24},{8,0},{16,8},{24,16},{1,25},{9,1},{17,9},{25,17},{2,26},{10... | collective-permute-start | bytes 4718600 | tf_op jit(solution)/shard_map/ppermute | solution.py:273
  50.7 11.9 %collective-permute-start.21 = (bf16[128,2048]{1,0:T(8,128)(2,1)S(1)}, bf16[128,2048]{1,0:T(8,128)(2,1)S(1)}, u32[]{:S(2)}, u32[]{:S(2)}) collective-permute-start(bf16[128,2048]{1,0:T(8,128)(2,1)S(1)} %constant_dynamic-update-slice_fusion.9.refs_5_), channel_id=1, source_target_pairs={{0,128},{128,2},{2,130},{130,4},{4,132},{132,6},{6,134},{134,0},{1... | collective-permute-start | bytes 1572872 | tf_op jit(solution)/shard_map/ppermute | solution.py:277
  52.3 13.5 %collective-permute-start.18 = (bf16[128,2048]{1,0:T(8,128)(2,1)S(1)}, bf16[128,2048]{1,0:T(8,128)(2,1)}, u32[]{:S(2)}, u32[]{:S(2)}) collective-permute-start(bf16[128,2048]{1,0:T(8,128)(2,1)S(1)} %constant_dynamic-update-slice_fusion.9.refs_5_), channel_id=1, source_target_pairs={{0,134},{128,0},{2,128},{130,2},{4,130},{132,4},{6,132},{134,6},{1... | collective-permute-start | bytes 1572872 | tf_op jit(solution)/shard_map/ppermute | solution.py:277
  62.6 13.1 %collective-permute-start.22 = (bf16[128,2048]{1,0:T(8,128)(2,1)S(1)}, bf16[128,2048]{1,0:T(8,128)(2,1)}, u32[]{:S(2)}, u32[]{:S(2)}) collective-permute-start(bf16[128,2048]{1,0:T(8,128)(2,1)S(1)} %collective-permute-done.21.refs_13_), channel_id=1, source_target_pairs={{0,128},{128,2},{2,130},{130,4},{4,132},{132,6},{6,134},{134,0},{1... | collective-permute-start | bytes 1572872 | tf_op jit(solution)/shard_map/ppermute | solution.py:277
  65.8 12.6 %collective-permute-start.19 = (bf16[128,2048]{1,0:T(8,128)(2,1)}, bf16[128,2048]{1,0:T(8,128)(2,1)}, u32[]{:S(2)}, u32[]{:S(2)}) collective-permute-start(bf16[128,2048]{1,0:T(8,128)(2,1)} %collective-permute-done.18.refs_6_), channel_id=1, source_target_pairs={{0,134},{128,0},{2,128},{130,2},{4,130},{132,4},{6,132},{134,6},{1... | collective-permute-start | bytes 1572872 | tf_op jit(solution)/shard_map/ppermute | solution.py:277
  75.8 17.0 %collective-permute-start.23 = (bf16[128,2048]{1,0:T(8,128)(2,1)}, bf16[128,2048]{1,0:T(8,128)(2,1)S(1)}, u32[]{:S(2)}, u32[]{:S(2)}) collective-permute-start(bf16[128,2048]{1,0:T(8,128)(2,1)} %collective-permute-done.22.refs_12_), channel_id=1, source_target_pairs={{0,128},{128,2},{2,130},{130,4},{4,132},{132,6},{6,134},{134,0},{1... | collective-permute-start | bytes 1572872 | tf_op jit(solution)/shard_map/ppermute | solution.py:277
  78.4 15.5 %collective-permute-start.20 = (bf16[128,2048]{1,0:T(8,128)(2,1)}, bf16[128,2048]{1,0:T(8,128)(2,1)}, u32[]{:S(2)}, u32[]{:S(2)}) collective-permute-start(bf16[128,2048]{1,0:T(8,128)(2,1)} %collective-permute-done.19.refs_7_), channel_id=1, source_target_pairs={{0,134},{128,0},{2,128},{130,2},{4,130},{132,4},{6,132},{134,6},{1... | collective-permute-start | bytes 1572872 | tf_op jit(solution)/shard_map/ppermute | solution.py:277
  81.7 17.2 %collective-permute-start = (bf16[128,2048]{1,0:T(8,128)(2,1)}, bf16[128,2048]{1,0:T(8,128)(2,1)}, u32[]{:S(2)}, u32[]{:S(2)}) collective-permute-start(bf16[128,2048]{1,0:T(8,128)(2,1)} %dynamic-slice_bitcast_fusion.5), channel_id=1, source_target_pairs={{1,0},{3,2},{5,4},{7,6},{9,8},{11,10},{13,12},{15,14},{17,16},{19,... | collective-permute-start | bytes 1572872 | tf_op jit(solution)/shard_map/ppermute | solution.py:402
  84.5 21.0 %collective-permute-start.12 = (bf16[256,1536]{1,0:T(8,128)(2,1)}, bf16[256,1536]{1,0:T(8,128)(2,1)S(1)}, u32[]{:S(2)}, u32[]{:S(2)}) collective-permute-start(bf16[256,1536]{1,0:T(8,128)(2,1)} %slice.26), channel_id=1, source_target_pairs={{0,8},{8,16},{16,24},{24,0},{1,9},{9,17},{17,25},{25,1},{2,10},{10... | collective-permute-start | bytes 2359304 | tf_op jit(solution)/shard_map/ppermute | solution.py:273
  88.2 20.1 %collective-permute-start.13 = (bf16[256,1536]{1,0:T(8,128)(2,1)}, bf16[256,1536]{1,0:T(8,128)(2,1)}, u32[]{:S(2)}, u32[]{:S(2)}) collective-permute-start(bf16[256,1536]{1,0:T(8,128)(2,1)} %slice.27), channel_id=1, source_target_pairs={{0,24},{8,0},{16,8},{24,16},{1,25},{9,1},{17,9},{25,17},{2,26},{10... | collective-permute-start | bytes 2359304 | tf_op jit(solution)/shard_map/ppermute | solution.py:273
  93.5 10.5 %collective-permute-start.24 = (bf16[64,2048]{1,0:T(8,128)(2,1)}, bf16[64,2048]{1,0:T(8,128)(2,1)S(1)}, u32[]{:S(2)}, u32[]{:S(2)}) collective-permute-start(bf16[64,2048]{1,0:T(8,128)(2,1)} %slice.28), channel_id=1, source_target_pairs={{0,128},{128,2},{2,130},{130,4},{4,132},{132,6},{6,134},{134,0},{1... | collective-permute-start | bytes 786440 | tf_op jit(solution)/shard_map/ppermute | solution.py:277
  95.6 10.0 %collective-permute-start.25 = (bf16[64,2048]{1,0:T(8,128)(2,1)}, bf16[64,2048]{1,0:T(8,128)(2,1)S(1)}, u32[]{:S(2)}, u32[]{:S(2)}) collective-permute-start(bf16[64,2048]{1,0:T(8,128)(2,1)} %slice.29), channel_id=1, source_target_pairs={{0,134},{128,0},{2,128},{130,2},{4,130},{132,4},{6,132},{134,6},{1... | collective-permute-start | bytes 786440 | tf_op jit(solution)/shard_map/ppermute | solution.py:277
  139.8 28.7 %collective-permute-start.32 = (bf16[256,2048]{1,0:T(8,128)(2,1)S(1)}, bf16[256,2048]{1,0:T(8,128)(2,1)S(1)}, u32[]{:S(2)}, u32[]{:S(2)}) collective-permute-start(bf16[256,2048]{1,0:T(8,128)(2,1)S(1)} %get-tuple-element.145), channel_id=1, source_target_pairs={{96,97},{98,99},{100,101},{102,103},{104,105},{106,107},{108,109},... | collective-permute-start | bytes 3145736 | tf_op jit(solution)/shard_map/ppermute | solution.py:420
  143.3 25.1 %collective-permute-start.33 = (bf16[128,2048]{1,0:T(8,128)(2,1)S(1)}, bf16[128,2048]{1,0:T(8,128)(2,1)S(1)}, u32[]{:S(2)}, u32[]{:S(2)}) collective-permute-start(bf16[128,2048]{1,0:T(8,128)(2,1)S(1)} %dynamic-slice_bitcast_fusion.4), channel_id=1, source_target_pairs={{0,1},{2,3},{4,5},{6,7},{8,9},{10,11},{12,13},{14,15},{16,17},{18,... | collective-permute-start | bytes 1572872 | tf_op jit(solution)/shard_map/ppermute | solution.py:404
  181.8 208.6 %collective-permute-start.40 = (bf16[256,2048]{1,0:T(8,128)(2,1)}, bf16[256,2048]{1,0:T(8,128)(2,1)}, u32[]{:S(2)}, u32[]{:S(2)}) collective-permute-start(bf16[256,2048]{1,0:T(8,128)(2,1)} %get-tuple-element.174), channel_id=1, source_target_pairs={{1,0},{3,2},{5,4},{7,6},{9,8},{11,10},{13,12},{15,14},{17,16},{19,... | collective-permute-start | bytes 3145736 | tf_op jit(solution)/shard_map/ppermute | solution.py:434
  393.3 17.6 %collective-permute-start.43 = (bf16[2,32,2048]{2,1,0:T(8,128)(2,1)S(1)}, bf16[2,32,2048]{2,1,0:T(8,128)(2,1)S(1)}, u32[]{:S(2)}, u32[]{:S(2)}) collective-permute-start(bf16[2,32,2048]{2,1,0:T(8,128)(2,1)S(1)} %get-tuple-element.209), channel_id=1, source_target_pairs={{0,128},{128,2},{2,130},{130,4},{4,132},{132,6},{6,134},{134,0},{1... | collective-permute-start | bytes 786440 | tf_op jit(solution)/shard_map/ppermute | solution.py:277
  393.4 17.4 %collective-permute-start.45 = (bf16[2,32,2048]{2,1,0:T(8,128)(2,1)S(1)}, bf16[2,32,2048]{2,1,0:T(8,128)(2,1)S(1)}, u32[]{:S(2)}, u32[]{:S(2)}) collective-permute-start(bf16[2,32,2048]{2,1,0:T(8,128)(2,1)S(1)} %get-tuple-element.207), channel_id=1, source_target_pairs={{0,134},{128,0},{2,128},{130,2},{4,130},{132,4},{6,132},{134,6},{1... | collective-permute-start | bytes 786440 | tf_op jit(solution)/shard_map/ppermute | solution.py:277
  407.5 14.7 %collective-permute-start.41 = (bf16[256,1536]{1,0:T(8,128)(2,1)S(1)}, bf16[256,1536]{1,0:T(8,128)(2,1)S(1)}, u32[]{:S(2)}, u32[]{:S(2)}) collective-permute-start(bf16[256,1536]{1,0:T(8,128)(2,1)S(1)} %get-tuple-element.199), channel_id=1, source_target_pairs={{0,8},{8,16},{16,24},{24,0},{1,9},{9,17},{17,25},{25,1},{2,10},{10... | collective-permute-start | bytes 2359304 | tf_op jit(solution)/shard_map/ppermute | solution.py:273
  408.8 13.5 %collective-permute-start.42 = (bf16[256,1536]{1,0:T(8,128)(2,1)S(1)}, bf16[256,1536]{1,0:T(8,128)(2,1)S(1)}, u32[]{:S(2)}, u32[]{:S(2)}) collective-permute-start(bf16[256,1536]{1,0:T(8,128)(2,1)S(1)} %get-tuple-element.197), channel_id=1, source_target_pairs={{0,24},{8,0},{16,8},{24,16},{1,25},{9,1},{17,9},{25,17},{2,26},{10... | collective-permute-start | bytes 2359304 | tf_op jit(solution)/shard_map/ppermute | solution.py:273
  411.1 11.9 %collective-permute-start.44 = (bf16[4,32,2048]{2,1,0:T(8,128)(2,1)S(1)}, bf16[4,32,2048]{2,1,0:T(8,128)(2,1)S(1)}, u32[]{:S(2)}, u32[]{:S(2)}) collective-permute-start(bf16[4,32,2048]{2,1,0:T(8,128)(2,1)S(1)} %pad_maximum_fusion.4), channel_id=1, source_target_pairs={{0,128},{128,2},{2,130},{130,4},{4,132},{132,6},{6,134},{134,0},{1... | collective-permute-start | bytes 1572872 | tf_op jit(solution)/shard_map/ppermute | solution.py:277
  411.2 11.8 %collective-permute-start.46 = (bf16[4,32,2048]{2,1,0:T(8,128)(2,1)S(1)}, bf16[4,32,2048]{2,1,0:T(8,128)(2,1)S(1)}, u32[]{:S(2)}, u32[]{:S(2)}) collective-permute-start(bf16[4,32,2048]{2,1,0:T(8,128)(2,1)S(1)} %pad_maximum_fusion.5), channel_id=1, source_target_pairs={{0,134},{128,0},{2,128},{130,2},{4,130},{132,4},{6,132},{134,6},{1... | collective-permute-start | bytes 1572872 | tf_op jit(solution)/shard_map/ppermute | solution.py:277
  423.4 13.5 %collective-permute-start.57 = (bf16[4,32,2048]{2,1,0:T(8,128)(2,1)S(1)}, bf16[4,32,2048]{2,1,0:T(8,128)(2,1)S(1)}, u32[]{:S(2)}, u32[]{:S(2)}) collective-permute-start(bf16[4,32,2048]{2,1,0:T(8,128)(2,1)S(1)} %get-tuple-element.194), channel_id=1, source_target_pairs={{0,128},{128,2},{2,130},{130,4},{4,132},{132,6},{6,134},{134,0},{1... | collective-permute-start | bytes 1572872 | tf_op jit(solution)/shard_map/ppermute | solution.py:277
  424.3 13.5 %collective-permute-start.59 = (bf16[4,32,2048]{2,1,0:T(8,128)(2,1)S(1)}, bf16[4,32,2048]{2,1,0:T(8,128)(2,1)S(1)}, u32[]{:S(2)}, u32[]{:S(2)}) collective-permute-start(bf16[4,32,2048]{2,1,0:T(8,128)(2,1)S(1)} %get-tuple-element.195), channel_id=1, source_target_pairs={{0,134},{128,0},{2,128},{130,2},{4,130},{132,4},{6,132},{134,6},{1... | collective-permute-start | bytes 1572872 | tf_op jit(solution)/shard_map/ppermute | solution.py:277
  427.1 29.2 %collective-permute-start.47 = (bf16[512,1536]{1,0:T(8,128)(2,1)S(1)}, bf16[512,1536]{1,0:T(8,128)(2,1)S(1)}, u32[]{:S(2)}, u32[]{:S(2)}) collective-permute-start(bf16[512,1536]{1,0:T(8,128)(2,1)S(1)} %pad_maximum_fusion), channel_id=1, source_target_pairs={{0,8},{8,16},{16,24},{24,0},{1,9},{9,17},{17,25},{25,1},{2,10},{10... | collective-permute-start | bytes 4718600 | tf_op jit(solution)/shard_map/ppermute | solution.py:273
  427.4 28.9 %collective-permute-start.48 = (bf16[512,1536]{1,0:T(8,128)(2,1)S(1)}, bf16[512,1536]{1,0:T(8,128)(2,1)S(1)}, u32[]{:S(2)}, u32[]{:S(2)}) collective-permute-start(bf16[512,1536]{1,0:T(8,128)(2,1)S(1)} %pad_maximum_fusion.1), channel_id=1, source_target_pairs={{0,24},{8,0},{16,8},{24,16},{1,25},{9,1},{17,9},{25,17},{2,26},{10... | collective-permute-start | bytes 4718600 | tf_op jit(solution)/shard_map/ppermute | solution.py:273
  438.1 10.4 %collective-permute-start.58 = (bf16[4,32,2048]{2,1,0:T(8,128)(2,1)S(1)}, bf16[4,32,2048]{2,1,0:T(8,128)(2,1)S(1)}, u32[]{:S(2)}, u32[]{:S(2)}) collective-permute-start(bf16[4,32,2048]{2,1,0:T(8,128)(2,1)S(1)} %get-tuple-element.202), channel_id=1, source_target_pairs={{0,128},{128,2},{2,130},{130,4},{4,132},{132,6},{6,134},{134,0},{1... | collective-permute-start | bytes 1572872 | tf_op jit(solution)/shard_map/ppermute | solution.py:277
  440.5 9.2 %collective-permute-start.60 = (bf16[4,32,2048]{2,1,0:T(8,128)(2,1)S(1)}, bf16[4,32,2048]{2,1,0:T(8,128)(2,1)S(1)}, u32[]{:S(2)}, u32[]{:S(2)}) collective-permute-start(bf16[4,32,2048]{2,1,0:T(8,128)(2,1)S(1)} %get-tuple-element.203), channel_id=1, source_target_pairs={{0,134},{128,0},{2,128},{130,2},{4,130},{132,4},{6,132},{134,6},{1... | collective-permute-start | bytes 1572872 | tf_op jit(solution)/shard_map/ppermute | solution.py:277
  457.1 23.0 %collective-permute-start.49 = (bf16[64,1536]{1,0:T(8,128)(2,1)S(1)}, bf16[64,1536]{1,0:T(8,128)(2,1)S(1)}, u32[]{:S(2)}, u32[]{:S(2)}) collective-permute-start(bf16[64,1536]{1,0:T(8,128)(2,1)S(1)} %get-tuple-element.212), channel_id=1, source_target_pairs={{0,4},{128,132},{2,6},{130,134},{4,0},{132,128},{6,2},{134,130},{1... | collective-permute-start | bytes 589832 | tf_op jit(solution)/shard_map/ppermute | solution.py:277
  460.0 20.1 %collective-permute-start.50 = (bf16[64,1536]{1,0:T(8,128)(2,1)S(1)}, bf16[64,1536]{1,0:T(8,128)(2,1)S(1)}, u32[]{:S(2)}, u32[]{:S(2)}) collective-permute-start(bf16[64,1536]{1,0:T(8,128)(2,1)S(1)} %get-tuple-element.218), channel_id=1, source_target_pairs={{0,130},{128,4},{2,132},{130,6},{4,134},{132,0},{6,128},{134,2},{1... | collective-permute-start | bytes 589832 | tf_op jit(solution)/shard_map/ppermute | solution.py:277
  473.7 14.5 %collective-permute-start.51 = (bf16[64,1536]{1,0:T(8,128)(2,1)S(1)}, bf16[64,1536]{1,0:T(8,128)(2,1)S(1)}, u32[]{:S(2)}, u32[]{:S(2)}) collective-permute-start(bf16[64,1536]{1,0:T(8,128)(2,1)S(1)} %get-tuple-element.217), channel_id=1, source_target_pairs={{0,132},{128,6},{2,134},{130,0},{4,128},{132,2},{6,130},{134,4},{1... | collective-permute-start | bytes 589832 | tf_op jit(solution)/shard_map/ppermute | solution.py:277
  475.9 14.2 %collective-permute-start.52 = (bf16[64,1536]{1,0:T(8,128)(2,1)S(1)}, bf16[64,1536]{1,0:T(8,128)(2,1)S(1)}, u32[]{:S(2)}, u32[]{:S(2)}) collective-permute-start(bf16[64,1536]{1,0:T(8,128)(2,1)S(1)} %get-tuple-element.216), channel_id=1, source_target_pairs={{0,2},{128,130},{2,4},{130,132},{4,6},{132,134},{6,0},{134,128},{1... | collective-permute-start | bytes 589832 | tf_op jit(solution)/shard_map/ppermute | solution.py:277
  476.1 15.5 %collective-permute-start.53 = (bf16[64,1536]{1,0:T(8,128)(2,1)S(1)}, bf16[64,1536]{1,0:T(8,128)(2,1)S(1)}, u32[]{:S(2)}, u32[]{:S(2)}) collective-permute-start(bf16[64,1536]{1,0:T(8,128)(2,1)S(1)} %get-tuple-element.215), channel_id=1, source_target_pairs={{0,6},{128,134},{2,0},{130,128},{4,2},{132,130},{6,4},{134,132},{1... | collective-permute-start | bytes 589832 | tf_op jit(solution)/shard_map/ppermute | solution.py:277
  480.1 11.5 %collective-permute-start.54 = (bf16[64,1536]{1,0:T(8,128)(2,1)S(1)}, bf16[64,1536]{1,0:T(8,128)(2,1)S(1)}, u32[]{:S(2)}, u32[]{:S(2)}) collective-permute-start(bf16[64,1536]{1,0:T(8,128)(2,1)S(1)} %get-tuple-element.214), channel_id=1, source_target_pairs={{0,128},{128,2},{2,130},{130,4},{4,132},{132,6},{6,134},{134,0},{1... | collective-permute-start | bytes 589832 | tf_op jit(solution)/shard_map/ppermute | solution.py:277
  480.1 12.8 %collective-permute-start.55 = (bf16[64,1536]{1,0:T(8,128)(2,1)S(1)}, bf16[64,1536]{1,0:T(8,128)(2,1)S(1)}, u32[]{:S(2)}, u32[]{:S(2)}) collective-permute-start(bf16[64,1536]{1,0:T(8,128)(2,1)S(1)} %get-tuple-element.213), channel_id=1, source_target_pairs={{0,134},{128,0},{2,128},{130,2},{4,130},{132,4},{6,132},{134,6},{1... | collective-permute-start | bytes 589832 | tf_op jit(solution)/shard_map/ppermute | solution.py:277
  488.2 9.4 %collective-permute-start.64 = (bf16[32,2048]{1,0:T(8,128)(2,1)S(1)}, bf16[32,2048]{1,0:T(8,128)(2,1)S(1)}, u32[]{:S(2)}, u32[]{:S(2)}) collective-permute-start(bf16[32,2048]{1,0:T(8,128)(2,1)S(1)} %fusion.23), channel_id=1, source_target_pairs={{0,0},{128,1},{2,2},{130,3},{4,4},{132,5},{6,6},{134,7},{8,8},{136... | collective-permute-start | bytes 393224 | tf_op jit(solution)/shard_map/ppermute | solution.py:437
  493.1 10.0 %collective-permute-start.56 = (bf16[64,1536]{1,0:T(8,128)(2,1)S(1)}, bf16[64,1536]{1,0:T(8,128)(2,1)S(1)}, u32[]{:S(2)}, u32[]{:S(2)}) collective-permute-start(bf16[64,1536]{1,0:T(8,128)(2,1)S(1)} %fusion.20), channel_id=1, source_target_pairs={{0,0},{128,1},{2,2},{130,3},{4,4},{132,5},{6,6},{134,7},{8,8},{136... | collective-permute-start | bytes 589832 | tf_op jit(solution)/shard_map/ppermute | solution.py:438
  (31 other events, 270.1 us)

commit v7 on v6

--- a/solution.py
+++ b/solution.py
@@ -131,7 +131,7 @@
             marks_v[:, c] = jnp.concatenate([marks[:ROWS], marks[ROWS:]], axis=1)
             return carry
 
-        lax.fori_loop(0, KVH, group, 0)
+        lax.fori_loop(0, KVH, group, 0, unroll=2)
         def finish(i, carry):
             c = cols(i * CHUNK, CHUNK)
             out = h_v[:, c].astype(jnp.float32) + dot_nn(ctx_v[...], wo_v[:, c])
@@ -139,7 +139,7 @@
             return carry
 
         if not final:
-            lax.fori_loop(0, 8, finish, 0)
+            lax.fori_loop(0, 8, finish, 0, unroll=True)
 
 
 def bf16(*shape):
@@ -204,7 +204,7 @@
             dvt_s[rows, :] = d_value[:HEAD, :ROWS] + d_value[HEAD:, ROWS:]
             return carry
 
-        lax.fori_loop(0, KVH, group, 0)
+        lax.fori_loop(0, KVH, group, 0, unroll=2)
         dproj_v[:, HQ : HQ + KV] = dkt_s[...].T.astype(jnp.bfloat16)
         dproj_v[:, HQ + KV :] = dvt_s[...].T.astype(jnp.bfloat16)
         if not last:
@@ -215,7 +215,7 @@
                 product = d_normed * h_v[:, c].astype(jnp.float32)
                 return partial + product[:, :HALF] + product[:, HALF:]
 
-            partial = lax.fori_loop(0, 8, widen, jnp.zeros((ROWS, HALF), jnp.float32))
+            partial = lax.fori_loop(0, 8, widen, jnp.zeros((ROWS, HALF), jnp.float32), unroll=True)
             mean = jnp.sum(partial, axis=-1, keepdims=True) * (1.0 / D)
             wide = h_v[...].astype(jnp.float32)
             scale = lax.rsqrt(jnp.mean(wide * wide, axis=-1, keepdims=True) + EPS)
@@ -227,7 +227,7 @@
                 up_v[:, c] = out.astype(jnp.bfloat16)
                 return carry
 
-            lax.fori_loop(0, 8, previous, 0)
+            lax.fori_loop(0, 8, previous, 0, unroll=True)
 
 
 def backward_layer(layer, place, upstream, kept, proj, ctx, marks, w_qkv, w_out, dproj, ups):
@@ -317,18 +317,17 @@
     return take
 
 
-def assemble_kernel(place, *refs):
-    qkv_parts, out_parts, (full_qkv, full_out, sems) = refs[:5], refs[5:14], refs[14:]
+def assemble_kernel(qkv_plan, out_plan, place, *refs):
+    count = len(qkv_plan) + len(out_plan)
+    parts, (full_qkv, full_out, sems) = refs[:count], refs[-3:]
     x, z = place[0], place[1]
     copies = []
-    for ref, dx, first, pieces in zip(qkv_parts, (0, 1, 2, 2, 3), (0, 0, 0, 4, 0), (8, 8, 4, 4, 8)):
+    for ref, (dx, first, pieces) in zip(parts, qkv_plan):
         for i in range(pieces):
             row = (lax.rem(x + dx, 4) * 8 + lax.rem(z + first + i, 8)) * 64
             target = full_qkv.at[pl.ds(pl.multiple_of(row, 64), 64), :]
             copies.append(pltpu.make_async_copy(ref.at[pl.ds(i * 64, 64), :], target, sems.at[len(copies)]))
-    for ref, dz, first, pieces in zip(
-        out_parts, (0, 1, 2, 3, 4, 4, 5, 6, 7), (0, 0, 0, 0, 0, 2, 0, 0, 0), (4, 4, 4, 4, 2, 2, 4, 4, 4)
-    ):
+    for ref, (dz, first, pieces) in zip(parts[len(qkv_plan) :], out_plan):
         for i in range(pieces):
             row = (lax.rem(x + first + i, 4) * 8 + lax.rem(z + dz, 8)) * 32
             target = full_out.at[pl.ds(pl.multiple_of(row, 32), 32), :]
@@ -339,21 +338,33 @@
         copy.wait()
 
 
+def assemble(place, qkv, out, before):
+    qkv_plan, out_plan = [plan for plan, part in qkv], [plan for plan, part in out]
+    count = len(qkv) + len(out)
+    return pl.pallas_call(
+        functools.partial(assemble_kernel, qkv_plan, out_plan),
+        out_shape=(v16(D, WCOLS), v16(HQ, D)),
+        in_specs=[SMEM] + [ANY] * count + [INSIDE] * len(before),
+        out_specs=(INSIDE, INSIDE),
+        input_output_aliases={count + 1: 0, count + 2: 1} if before else {},
+        scratch_shapes=[pltpu.SemaphoreType.DMA((64,))],
+        compiler_params=pltpu.CompilerParams(vmem_limit_bytes=4 * 1024 * 1024),
+        cost_estimate=pl.CostEstimate(flops=0, bytes_accessed=6_000_000 if before else 18_000_000, transcendentals=0),
+        name="assemble_rest" if before else "assemble",
+    )(place, *[part for plan, part in qkv], *[part for plan, part in out], *inside(*before))
+
+
 def gather_weights(near, far, x, z):
     column = jnp.concatenate(gather_ring(near, 8, send_z))
     row = jnp.concatenate(gather_direct(far, send_x))
     qkv_parts = gather_ring(column, 4, send_x)
     out_parts = gather_ring(row, 8, send_z)
-    return pl.pallas_call(
-        assemble_kernel,
-        out_shape=(v16(D, WCOLS), v16(HQ, D)),
-        in_specs=[SMEM] + [ANY] * 14,
-        out_specs=(INSIDE, INSIDE),
-        scratch_shapes=[pltpu.SemaphoreType.DMA((64,))],
-        compiler_params=pltpu.CompilerParams(vmem_limit_bytes=4 * 1024 * 1024),
-        cost_estimate=pl.CostEstimate(flops=0, bytes_accessed=21_000_000, transcendentals=0),
-        name="assemble",
-    )(jnp.stack([x, z]), *qkv_parts, *out_parts)
+    qkv = list(zip([(0, 0, 8), (1, 0, 8), (2, 0, 4), (2, 4, 4), (3, 0, 8)], qkv_parts))
+    spots = [(0, 0, 4), (1, 0, 4), (2, 0, 4), (3, 0, 4), (4, 0, 2), (4, 2, 2), (5, 0, 4), (6, 0, 4), (7, 0, 4)]
+    out = list(zip(spots, out_parts))
+    place = jnp.stack([x, z])
+    early = assemble(place, [qkv[0], qkv[1], qkv[4]], out[:3] + out[7:], ())
+    return assemble(place, qkv[2:4], out[3:7], early)
 
 
 def sum_of(*terms):

time: 514 us -> 469 us (0.912)
  waiting for transfers between devices: 303 us -> 258 us
  Pallas kernels: 36.6 us -> 50.2 us
  starting transfers between devices: 130 us -> 118 us
    ppermute x7, waiting for transfers between devices: 207 us -> 164 us  [on_device(): upstream = lax.ppermute(result, STAGE, [(layer, layer - 1)])]
    pallas_call x8, Pallas kernels: 13.4 us -> 24.7 us  [backward_layer(): pl.pallas_call(functools.partial(backward_kernel, last), out_shape=(v16(R...]
    ppermute x1, starting transfers between devices: 23.6 us -> 16.7 us  [on_device(): upstream = jnp.concatenate([lax.ppermute(block, 'core', [(0, 1)]), block])]
  transfers between devices with their start and end apart: 65 -> 65, of which waited for: 32 -> 28; matrix products, arithmetic and copies ran while one was open for 4% -> 5% of each run, Pallas kernels for 2% -> 3%
where the time goes in v7:
time: 469 us; the launch traced here: 459 us
  waiting for transfers between devices  258 us (55%)
  starting transfers between devices  118 us (25%)
  Pallas kernels  50.2 us (11%)
  local copies, waits for them, and re-layouts  18.7 us (4%)
  other arithmetic  8.43 us (2%)
    ppermute x7, waiting for transfers between devices, on_device(): upstream = lax.ppermute(result, STAGE, [(layer, layer - 1)])  164 us
    ppermute x31, waiting for transfers between devices, send_z(): lax.ppermute(value, ('zlo', 'zhi'), [(z_index(i), z_index((i + step) % 8)...  57.2 us
    ppermute x31, starting transfers between devices, send_z(): lax.ppermute(value, ('zlo', 'zhi'), [(z_index(i), z_index((i + step) % 8)...  52.9 us
    ppermute x14, waiting for transfers between devices, send_x(): return lax.ppermute(value, 'x', [(i, (i + step) % 4) for i in range(4)])  24.8 us
    pallas_call x8, Pallas kernels, backward_layer(): pl.pallas_call(functools.partial(backward_kernel, last), out_shape=(v16(R...  24.7 us
    ppermute x14, starting transfers between devices, send_x(): return lax.ppermute(value, 'x', [(i, (i + step) % 4) for i in range(4)])  24.4 us
    ppermute x1, starting transfers between devices, on_device(): upstream = jnp.concatenate([lax.ppermute(block, 'core', [(0, 1)]), block])  16.7 us
    pallas_call x8, Pallas kernels, forward_layer(): pl.pallas_call(functools.partial(forward_kernel, final), out_shape=(v16(R...  16.7 us
  transfers between devices with their start and end apart: 65, of which 28 were waited for; matrix products, arithmetic and copies ran while one was open for 5% of the time, Pallas kernels for 3%

profile of v7, /device:TPU:32, one launch (start us, length us, event | category | flops | bytes accessed | tf_op | source)
XLA Modules:
  0.0 459.4 jit_solution(9557193669105067049)
XLA Ops:
  0.6 4.8 %collective-permute-start.14 = (bf16[32,2048]{1,0:T(8,128)(2,1)}, bf16[32,2048]{1,0:T(8,128)(2,1)S(1)}, u32[]{:S(2)}, u32[]{:S(2)}) collective-permute-start(bf16[32,2048]{1,0:T(8,128)(2,1)} %bitcast.126), channel_id=1, source_target_pairs={{0,0},{1,128},{2,2},{3,130},{4,4},{5,132},{6,6},{7,134},{8,8},{9,1... | collective-permute-start | bytes 393224 | tf_op jit(solution)/shard_map/ppermute | solution.py:410
  5.4 2.4 collective-permute-start.1
  8.2 2.8 collective-permute-start.15
  12.8 2.0 collective-permute-start.5
  17.4 3.0 collective-permute-done.2
  20.3 3.5 collective-permute-start.3
  25.0 2.6 collective-permute-done.3
  27.5 3.3 collective-permute-start.4
  31.9 6.2 %collective-permute-done.7 = bf16[64,1536]{1,0:T(8,128)(2,1)S(1)} collective-permute-done((bf16[64,1536]{1,0:T(8,128)(2,1)S(1)}, bf16[64,1536]{1,0:T(8,128)(2,1)S(1)}, u32[]{:S(2)}, u32[]{:S(2)}) %collective-permute-start.7) | collective-permute-done | bytes 196640 | tf_op jit(solution)/shard_map/ppermute | solution.py:277
  38.3 3.3 collective-permute-start.9
  54.9 7.7 %collective-permute-done.21.refs_7_ = bf16[128,2048]{1,0:T(8,128)(2,1)S(1)} collective-permute-done((bf16[128,2048]{1,0:T(8,128)(2,1)S(1)}, bf16[128,2048]{1,0:T(8,128)(2,1)S(1)}, u32[]{:S(2)}, u32[]{:S(2)}) %collective-permute-start.21) | collective-permute-done | bytes 524320 | tf_op jit(solution)/shard_map/ppermute | solution.py:277
  62.7 2.4 collective-permute-start.22
  67.2 8.6 %collective-permute-done.22.refs_6_ = bf16[128,2048]{1,0:T(8,128)(2,1)} collective-permute-done((bf16[128,2048]{1,0:T(8,128)(2,1)S(1)}, bf16[128,2048]{1,0:T(8,128)(2,1)}, u32[]{:S(2)}, u32[]{:S(2)}) %collective-permute-start.22) | collective-permute-done | bytes 524320 | tf_op jit(solution)/shard_map/ppermute | solution.py:277
  78.5 2.4 collective-permute-start.20
  86.2 2.1 slice.27
  95.6 3.3 collective-permute-start.25
  101.2 5.9 %assemble.1 = (bf16[2048,1536]{1,0:T(8,128)(2,1)S(1)}, bf16[1024,2048]{1,0:T(8,128)(2,1)S(1)}) custom-call(s32[2]{0:T(128)S(1)} %pad_add_fusion.8.place, bf16[512,1536]{1,0:T(8,128)(2,1)} %constant_dynamic-update-slice_fusion.refs_0_, bf16[512,1536]{1,0:T(8,128)(2,1)} %collective-permute-done.12.refs_1_, ...), custom_call_target="tpu_custom_call" | custom-call | bytes 18000000 | tf_op jit(solution)/shard_map/assemble/pallas_call | solution.py:344
  108.9 2.9 assemble_rest.1
  112.2 6.8 %forward_layer.7 = (bf16[256,2048]{1,0:T(8,128)(2,1)S(1)}, bf16[256,2048]{1,0:T(8,128)(2,1)S(1)}, bf16[256,1536]{1,0:T(8,128)(2,1)S(1)}, bf16[256,1024]{1,0:T(8,...) custom-call(s32[2]{0:T(128)S(1)} %get-tuple-element.108.place.h_v.wq, ...), custom_call_target="tpu_custom_call", output_to_operand_aliasing={{1}: (4, {}), {2}: (5, {}), {3}: (6, {}), {4}: (7, {}), {5}... | custom-call | flops 3000000000 | bytes 14000000 | tf_op jit(solution)/shard_map/forward_layer/pallas_call | solution.py:163
  120.4 2.2 collective-permute-done.26.h_v
  126.7 5.1 %forward_layer.11 = (bf16[256,2048]{1,0:T(8,128)(2,1)S(1)}, bf16[256,2048]{1,0:T(8,128)(2,1)S(1)}, bf16[256,1536]{1,0:T(8,128)(2,1)S(1)}, bf16[256,1024]{1,0:T(8...) custom-call(s32[2]{0:T(128)S(1)} %get-tuple-element.104.place, ...), custom_call_target="tpu_custom_call", output_to_operand_aliasing={{1}: (4, {}), {2}: (5, {}), {3}: (6, {}), {4}: (7, {}), {5}... | custom-call | flops 3000000000 | bytes 14000000 | tf_op jit(solution)/shard_map/forward_layer/pallas_call | solution.py:163
  135.3 16.7 %collective-permute-start.33 = (bf16[128,2048]{1,0:T(8,128)(2,1)S(1)}, bf16[128,2048]{1,0:T(8,128)(2,1)S(1)}, u32[]{:S(2)}, u32[]{:S(2)}) collective-permute-start(bf16[128,2048]{1,0:T(8,128)(2,1)S(1)} %dynamic-slice_bitcast_fusion.4), channel_id=1, source_target_pairs={{0,1},{2,3},{4,5},{6,7},{8,9},{10,11},{12,13},{14,15},{16,17},{18,... | collective-permute-start | bytes 1572872 | tf_op jit(solution)/shard_map/ppermute | solution.py:415
  158.1 2.8 backward_layer.9
  162.9 4.7 %backward_layer.11 = (bf16[256,2048]{1,0:T(8,128)(2,1)S(1)}, bf16[256,1536]{1,0:T(8,128)(2,1)S(1)}, bf16[256,2048]{1,0:T(8,128)(2,1)S(1)}) custom-call(s32[2]{0:T(128)S(1)} %get-tuple-element.105.place, bf16[256,2048]{1,0:T(8,128)(2,1)S(1)} %collective-permute-done.37.u_v, ...), custom_call_target="tpu_custom_call", output_to_operand_aliasing={{1}: (8, {}), {2}: (9, {})} | custom-call | flops 4000000000 | bytes 15000000 | tf_op jit(solution)/shard_map/backward_layer/pallas_call | solution.py:237
  169.7 7.7 %backward_layer.13 = (bf16[256,2048]{1,0:T(8,128)(2,1)}, bf16[256,1536]{1,0:T(8,128)(2,1)S(1)}, bf16[256,2048]{1,0:T(8,128)(2,1)S(1)}) custom-call(s32[2]{0:T(128)S(1)} %get-tuple-element.107.place, bf16[256,2048]{1,0:T(8,128)(2,1)S(1)} %collective-permute-done.39.u_v, ...), custom_call_target="tpu_custom_call", output_to_operand_aliasing={{1}: (8, {}), {2}: (9, {})} | custom-call | flops 4000000000 | bytes 15000000 | tf_op jit(solution)/shard_map/backward_layer/pallas_call | solution.py:237
  180.6 164.5 %collective-permute-done.40.u_v = bf16[256,2048]{1,0:T(8,128)(2,1)} collective-permute-done((bf16[256,2048]{1,0:T(8,128)(2,1)}, bf16[256,2048]{1,0:T(8,128)(2,1)}, u32[]{:S(2)}, u32[]{:S(2)}) %collective-permute-start.40) | collective-permute-done | bytes 1048608 | tf_op jit(solution)/shard_map/ppermute | solution.py:445
  345.0 2.7 convolution_convert_fusion.1
  347.9 3.8 collective-permute-start.45
  351.7 7.4 %backward_last.1 = (bf16[256,2048]{1,0:T(8,128)(2,1)}, bf16[256,1536]{1,0:T(8,128)(2,1)S(1)}, bf16[256,2048]{1,0:T(8,128)(2,1)S(1)}) custom-call(s32[2]{0:T(128)S(1)} %get-tuple-element.108.place.h_v.wq_v, bf16[256,2048]{1,0:T(8,128)(2,1)} %collective-permute-done.40.u_v, ...), custom_call_target="tpu_custom_call", output_to_operand_aliasing={{1}: (8, {}), {2}: (9, {})} | custom-call | flops 4000000000 | bytes 15000000 | tf_op jit(solution)/shard_map/backward_last/pallas_call | solution.py:237
  362.6 2.1 collective-permute-start.42
  365.1 3.2 collective-permute-start.46
  368.3 8.5 %collective-permute-done.41 = bf16[256,1536]{1,0:T(8,128)(2,1)S(1)} collective-permute-done((bf16[256,1536]{1,0:T(8,128)(2,1)S(1)}, bf16[256,1536]{1,0:T(8,128)(2,1)S(1)}, u32[]{:S(2)}, u32[]{:S(2)}) %collective-permute-start.41) | collective-permute-done | bytes 786464 | tf_op jit(solution)/shard_map/ppermute | solution.py:273
  378.0 2.9 collective-permute-start.59
  382.0 2.2 collective-permute-start.48
  384.1 6.4 %collective-permute-done.57 = bf16[4,32,2048]{2,1,0:T(8,128)(2,1)S(1)} collective-permute-done((bf16[4,32,2048]{2,1,0:T(8,128)(2,1)S(1)}, bf16[4,32,2048]{2,1,0:T(8,128)(2,1)S(1)}, u32[]{:S(2)}, u32[]{:S(2)}) %collective-permute-start.57) | collective-permute-done | bytes 524320 | tf_op jit(solution)/shard_map/ppermute | solution.py:277
  392.0 2.2 collective-permute-start.60
  394.2 7.1 %collective-permute-done.58 = bf16[4,32,2048]{2,1,0:T(8,128)(2,1)S(1)} collective-permute-done((bf16[4,32,2048]{2,1,0:T(8,128)(2,1)S(1)}, bf16[4,32,2048]{2,1,0:T(8,128)(2,1)S(1)}, u32[]{:S(2)}, u32[]{:S(2)}) %collective-permute-start.58) | collective-permute-done | bytes 524320 | tf_op jit(solution)/shard_map/ppermute | solution.py:277
  402.0 9.6 %collective-permute-done.47 = bf16[512,1536]{1,0:T(8,128)(2,1)S(1)} collective-permute-done((bf16[512,1536]{1,0:T(8,128)(2,1)S(1)}, bf16[512,1536]{1,0:T(8,128)(2,1)S(1)}, u32[]{:S(2)}, u32[]{:S(2)}) %collective-permute-start.47) | collective-permute-done | bytes 1572896 | tf_op jit(solution)/shard_map/ppermute | solution.py:273
  414.1 6.4 %collective-permute-start.50 = (bf16[64,1536]{1,0:T(8,128)(2,1)S(1)}, bf16[64,1536]{1,0:T(8,128)(2,1)S(1)}, u32[]{:S(2)}, u32[]{:S(2)}) collective-permute-start(bf16[64,1536]{1,0:T(8,128)(2,1)S(1)} %get-tuple-element.222), channel_id=1, source_target_pairs={{0,130},{128,4},{2,132},{130,6},{4,134},{132,0},{6,128},{134,2},{1... | collective-permute-start | bytes 589832 | tf_op jit(solution)/shard_map/ppermute | solution.py:277
  420.5 3.3 collective-permute-start.61
  425.1 2.1 collective-permute-start.63
  427.3 2.7 collective-permute-done.62
  430.3 3.8 collective-permute-start.53
  436.2 4.8 %collective-permute-done.51 = bf16[64,1536]{1,0:T(8,128)(2,1)S(1)} collective-permute-done((bf16[64,1536]{1,0:T(8,128)(2,1)S(1)}, bf16[64,1536]{1,0:T(8,128)(2,1)S(1)}, u32[]{:S(2)}, u32[]{:S(2)}) %collective-permute-start.51) | collective-permute-done | bytes 196640 | tf_op jit(solution)/shard_map/ppermute | solution.py:277
  441.0 1.9 collective-permute-start.64
  443.0 4.0 collective-permute-done.53
  448.2 1.9 collective-permute-start.56
  451.0 7.2 %collective-permute-done.56 = bf16[64,1536]{1,0:T(8,128)(2,1)S(1)} collective-permute-done((bf16[64,1536]{1,0:T(8,128)(2,1)S(1)}, bf16[64,1536]{1,0:T(8,128)(2,1)S(1)}, u32[]{:S(2)}, u32[]{:S(2)}) %collective-permute-start.56) | collective-permute-done | bytes 196640 | tf_op jit(solution)/shard_map/ppermute | solution.py:449
  (184 shorter events, 81.7 us)
Async XLA Ops:
  0.6 7.6 %collective-permute-start.14 = (bf16[32,2048]{1,0:T(8,128)(2,1)}, bf16[32,2048]{1,0:T(8,128)(2,1)S(1)}, u32[]{:S(2)}, u32[]{:S(2)}) collective-permute-start(bf16[32,2048]{1,0:T(8,128)(2,1)} %bitcast.126), channel_id=1, source_target_pairs={{0,0},{1,128},{2,2},{3,130},{4,4},{5,132},{6,6},{7,134},{8,8},{9,1... | collective-permute-start | bytes 393224 | tf_op jit(solution)/shard_map/ppermute | solution.py:410
  5.4 7.3 %collective-permute-start.1 = (bf16[64,1536]{1,0:T(8,128)(2,1)}, bf16[64,1536]{1,0:T(8,128)(2,1)S(1)}, u32[]{:S(2)}, u32[]{:S(2)}) collective-permute-start(bf16[64,1536]{1,0:T(8,128)(2,1)} %bitcast.125), channel_id=1, source_target_pairs={{0,0},{1,128},{2,2},{3,130},{4,4},{5,132},{6,6},{7,134},{8,8},{9,1... | collective-permute-start | bytes 589832 | tf_op jit(solution)/shard_map/ppermute | solution.py:409
  8.2 9.1 %collective-permute-start.15 = (bf16[32,2048]{1,0:T(8,128)(2,1)S(1)}, bf16[32,2048]{1,0:T(8,128)(2,1)S(1)}, u32[]{:S(2)}, u32[]{:S(2)}) collective-permute-start(bf16[32,2048]{1,0:T(8,128)(2,1)S(1)} %collective-permute-done.14), channel_id=1, source_target_pairs={{0,24},{8,0},{16,8},{24,16},{1,25},{9,1},{17,9},{25,17},{2,26},{10... | collective-permute-start | bytes 393224 | tf_op jit(solution)/shard_map/ppermute | solution.py:273
  11.0 39.7 %collective-permute-start.16 = (bf16[32,2048]{1,0:T(8,128)(2,1)S(1)}, bf16[32,2048]{1,0:T(8,128)(2,1)S(1)}, u32[]{:S(2)}, u32[]{:S(2)}) collective-permute-start(bf16[32,2048]{1,0:T(8,128)(2,1)S(1)} %collective-permute-done.14), channel_id=1, source_target_pairs={{0,16},{8,24},{16,0},{24,8},{1,17},{9,25},{17,1},{25,9},{2,18},{10... | collective-permute-start | bytes 393224 | tf_op jit(solution)/shard_map/ppermute | solution.py:273
  11.8 38.9 %collective-permute-start.17 = (bf16[32,2048]{1,0:T(8,128)(2,1)S(1)}, bf16[32,2048]{1,0:T(8,128)(2,1)S(1)}, u32[]{:S(2)}, u32[]{:S(2)}) collective-permute-start(bf16[32,2048]{1,0:T(8,128)(2,1)S(1)} %collective-permute-done.14), channel_id=1, source_target_pairs={{0,8},{8,16},{16,24},{24,0},{1,9},{9,17},{17,25},{25,1},{2,10},{10... | collective-permute-start | bytes 393224 | tf_op jit(solution)/shard_map/ppermute | solution.py:273
  12.7 7.6 %collective-permute-start.2 = (bf16[64,1536]{1,0:T(8,128)(2,1)S(1)}, bf16[64,1536]{1,0:T(8,128)(2,1)S(1)}, u32[]{:S(2)}, u32[]{:S(2)}) collective-permute-start(bf16[64,1536]{1,0:T(8,128)(2,1)S(1)} %collective-permute-done.1), channel_id=1, source_target_pairs={{0,134},{128,0},{2,128},{130,2},{4,130},{132,4},{6,132},{134,6},{1... | collective-permute-start | bytes 589832 | tf_op jit(solution)/shard_map/ppermute | solution.py:277
  12.8 11.5 %collective-permute-start.5 = (bf16[64,1536]{1,0:T(8,128)(2,1)S(1)}, bf16[64,1536]{1,0:T(8,128)(2,1)S(1)}, u32[]{:S(2)}, u32[]{:S(2)}) collective-permute-start(bf16[64,1536]{1,0:T(8,128)(2,1)S(1)} %collective-permute-done.1), channel_id=1, source_target_pairs={{0,128},{128,2},{2,130},{130,4},{4,132},{132,6},{6,134},{134,0},{1... | collective-permute-start | bytes 589832 | tf_op jit(solution)/shard_map/ppermute | solution.py:277
  20.3 7.2 %collective-permute-start.3 = (bf16[64,1536]{1,0:T(8,128)(2,1)S(1)}, bf16[64,1536]{1,0:T(8,128)(2,1)S(1)}, u32[]{:S(2)}, u32[]{:S(2)}) collective-permute-start(bf16[64,1536]{1,0:T(8,128)(2,1)S(1)} %collective-permute-done.2), channel_id=1, source_target_pairs={{0,134},{128,0},{2,128},{130,2},{4,130},{132,4},{6,132},{134,6},{1... | collective-permute-start | bytes 589832 | tf_op jit(solution)/shard_map/ppermute | solution.py:277
  24.3 7.0 %collective-permute-start.6 = (bf16[64,1536]{1,0:T(8,128)(2,1)S(1)}, bf16[64,1536]{1,0:T(8,128)(2,1)S(1)}, u32[]{:S(2)}, u32[]{:S(2)}) collective-permute-start(bf16[64,1536]{1,0:T(8,128)(2,1)S(1)} %collective-permute-done.5), channel_id=1, source_target_pairs={{0,128},{128,2},{2,130},{130,4},{4,132},{132,6},{6,134},{134,0},{1... | collective-permute-start | bytes 589832 | tf_op jit(solution)/shard_map/ppermute | solution.py:277
  27.5 10.7 %collective-permute-start.4 = (bf16[64,1536]{1,0:T(8,128)(2,1)S(1)}, bf16[64,1536]{1,0:T(8,128)(2,1)S(1)}, u32[]{:S(2)}, u32[]{:S(2)}) collective-permute-start(bf16[64,1536]{1,0:T(8,128)(2,1)S(1)} %collective-permute-done.3), channel_id=1, source_target_pairs={{0,134},{128,0},{2,128},{130,2},{4,130},{132,4},{6,132},{134,6},{1... | collective-permute-start | bytes 589832 | tf_op jit(solution)/shard_map/ppermute | solution.py:277
  31.3 6.9 %collective-permute-start.7 = (bf16[64,1536]{1,0:T(8,128)(2,1)S(1)}, bf16[64,1536]{1,0:T(8,128)(2,1)S(1)}, u32[]{:S(2)}, u32[]{:S(2)}) collective-permute-start(bf16[64,1536]{1,0:T(8,128)(2,1)S(1)} %collective-permute-done.6), channel_id=1, source_target_pairs={{0,128},{128,2},{2,130},{130,4},{4,132},{132,6},{6,134},{134,0},{1... | collective-permute-start | bytes 589832 | tf_op jit(solution)/shard_map/ppermute | solution.py:277
  47.4 36.2 %collective-permute-start.10 = (bf16[512,1536]{1,0:T(8,128)(2,1)}, bf16[512,1536]{1,0:T(8,128)(2,1)S(1)}, u32[]{:S(2)}, u32[]{:S(2)}) collective-permute-start(bf16[512,1536]{1,0:T(8,128)(2,1)} %constant_dynamic-update-slice_fusion.refs_0_), channel_id=1, source_target_pairs={{0,8},{8,16},{16,24},{24,0},{1,9},{9,17},{17,25},{25,1},{2,10},{10... | collective-permute-start | bytes 4718600 | tf_op jit(solution)/shard_map/ppermute | solution.py:273
  49.1 37.1 %collective-permute-start.12 = (bf16[512,1536]{1,0:T(8,128)(2,1)}, bf16[512,1536]{1,0:T(8,128)(2,1)}, u32[]{:S(2)}, u32[]{:S(2)}) collective-permute-start(bf16[512,1536]{1,0:T(8,128)(2,1)} %constant_dynamic-update-slice_fusion.refs_0_), channel_id=1, source_target_pairs={{0,24},{8,0},{16,8},{24,16},{1,25},{9,1},{17,9},{25,17},{2,26},{10... | collective-permute-start | bytes 4718600 | tf_op jit(solution)/shard_map/ppermute | solution.py:273
  50.7 11.9 %collective-permute-start.21 = (bf16[128,2048]{1,0:T(8,128)(2,1)S(1)}, bf16[128,2048]{1,0:T(8,128)(2,1)S(1)}, u32[]{:S(2)}, u32[]{:S(2)}) collective-permute-start(bf16[128,2048]{1,0:T(8,128)(2,1)S(1)} %constant_dynamic-update-slice_fusion.9.refs_3_), channel_id=1, source_target_pairs={{0,128},{128,2},{2,130},{130,4},{4,132},{132,6},{6,134},{134,0},{1... | collective-permute-start | bytes 1572872 | tf_op jit(solution)/shard_map/ppermute | solution.py:277
  52.3 13.5 %collective-permute-start.18 = (bf16[128,2048]{1,0:T(8,128)(2,1)S(1)}, bf16[128,2048]{1,0:T(8,128)(2,1)}, u32[]{:S(2)}, u32[]{:S(2)}) collective-permute-start(bf16[128,2048]{1,0:T(8,128)(2,1)S(1)} %constant_dynamic-update-slice_fusion.9.refs_3_), channel_id=1, source_target_pairs={{0,134},{128,0},{2,128},{130,2},{4,130},{132,4},{6,132},{134,6},{1... | collective-permute-start | bytes 1572872 | tf_op jit(solution)/shard_map/ppermute | solution.py:277
  62.7 13.1 %collective-permute-start.22 = (bf16[128,2048]{1,0:T(8,128)(2,1)S(1)}, bf16[128,2048]{1,0:T(8,128)(2,1)}, u32[]{:S(2)}, u32[]{:S(2)}) collective-permute-start(bf16[128,2048]{1,0:T(8,128)(2,1)S(1)} %collective-permute-done.21.refs_7_), channel_id=1, source_target_pairs={{0,128},{128,2},{2,130},{130,4},{4,132},{132,6},{6,134},{134,0},{1... | collective-permute-start | bytes 1572872 | tf_op jit(solution)/shard_map/ppermute | solution.py:277
  65.8 12.6 %collective-permute-start.19 = (bf16[128,2048]{1,0:T(8,128)(2,1)}, bf16[128,2048]{1,0:T(8,128)(2,1)}, u32[]{:S(2)}, u32[]{:S(2)}) collective-permute-start(bf16[128,2048]{1,0:T(8,128)(2,1)} %collective-permute-done.18.refs_4_), channel_id=1, source_target_pairs={{0,134},{128,0},{2,128},{130,2},{4,130},{132,4},{6,132},{134,6},{1... | collective-permute-start | bytes 1572872 | tf_op jit(solution)/shard_map/ppermute | solution.py:277
  75.8 17.0 %collective-permute-start.23 = (bf16[128,2048]{1,0:T(8,128)(2,1)}, bf16[128,2048]{1,0:T(8,128)(2,1)S(1)}, u32[]{:S(2)}, u32[]{:S(2)}) collective-permute-start(bf16[128,2048]{1,0:T(8,128)(2,1)} %collective-permute-done.22.refs_6_), channel_id=1, source_target_pairs={{0,128},{128,2},{2,130},{130,4},{4,132},{132,6},{6,134},{134,0},{1... | collective-permute-start | bytes 1572872 | tf_op jit(solution)/shard_map/ppermute | solution.py:277
  78.5 15.5 %collective-permute-start.20 = (bf16[128,2048]{1,0:T(8,128)(2,1)}, bf16[128,2048]{1,0:T(8,128)(2,1)}, u32[]{:S(2)}, u32[]{:S(2)}) collective-permute-start(bf16[128,2048]{1,0:T(8,128)(2,1)} %collective-permute-done.19.refs_5_), channel_id=1, source_target_pairs={{0,134},{128,0},{2,128},{130,2},{4,130},{132,4},{6,132},{134,6},{1... | collective-permute-start | bytes 1572872 | tf_op jit(solution)/shard_map/ppermute | solution.py:277
  81.7 17.3 %collective-permute-start = (bf16[128,2048]{1,0:T(8,128)(2,1)}, bf16[128,2048]{1,0:T(8,128)(2,1)S(1)}, u32[]{:S(2)}, u32[]{:S(2)}) collective-permute-start(bf16[128,2048]{1,0:T(8,128)(2,1)} %dynamic-slice_bitcast_fusion.5), channel_id=1, source_target_pairs={{1,0},{3,2},{5,4},{7,6},{9,8},{11,10},{13,12},{15,14},{17,16},{19,... | collective-permute-start | bytes 1572872 | tf_op jit(solution)/shard_map/ppermute | solution.py:413
  84.6 22.6 %collective-permute-start.11 = (bf16[256,1536]{1,0:T(8,128)(2,1)}, bf16[256,1536]{1,0:T(8,128)(2,1)}, u32[]{:S(2)}, u32[]{:S(2)}) collective-permute-start(bf16[256,1536]{1,0:T(8,128)(2,1)} %slice.26), channel_id=1, source_target_pairs={{0,8},{8,16},{16,24},{24,0},{1,9},{9,17},{17,25},{25,1},{2,10},{10... | collective-permute-start | bytes 2359304 | tf_op jit(solution)/shard_map/ppermute | solution.py:273
  88.2 20.6 %collective-permute-start.13 = (bf16[256,1536]{1,0:T(8,128)(2,1)}, bf16[256,1536]{1,0:T(8,128)(2,1)}, u32[]{:S(2)}, u32[]{:S(2)}) collective-permute-start(bf16[256,1536]{1,0:T(8,128)(2,1)} %slice.27), channel_id=1, source_target_pairs={{0,24},{8,0},{16,8},{24,16},{1,25},{9,1},{17,9},{25,17},{2,26},{10... | collective-permute-start | bytes 2359304 | tf_op jit(solution)/shard_map/ppermute | solution.py:273
  93.5 13.6 %collective-permute-start.24 = (bf16[64,2048]{1,0:T(8,128)(2,1)}, bf16[64,2048]{1,0:T(8,128)(2,1)S(1)}, u32[]{:S(2)}, u32[]{:S(2)}) collective-permute-start(bf16[64,2048]{1,0:T(8,128)(2,1)} %slice.28), channel_id=1, source_target_pairs={{0,128},{128,2},{2,130},{130,4},{4,132},{132,6},{6,134},{134,0},{1... | collective-permute-start | bytes 786440 | tf_op jit(solution)/shard_map/ppermute | solution.py:277
  95.6 11.5 %collective-permute-start.25 = (bf16[64,2048]{1,0:T(8,128)(2,1)}, bf16[64,2048]{1,0:T(8,128)(2,1)}, u32[]{:S(2)}, u32[]{:S(2)}) collective-permute-start(bf16[64,2048]{1,0:T(8,128)(2,1)} %slice.29), channel_id=1, source_target_pairs={{0,134},{128,0},{2,128},{130,2},{4,130},{132,4},{6,132},{134,6},{1... | collective-permute-start | bytes 786440 | tf_op jit(solution)/shard_map/ppermute | solution.py:277
  134.5 19.0 %collective-permute-start.32 = (bf16[256,2048]{1,0:T(8,128)(2,1)S(1)}, bf16[256,2048]{1,0:T(8,128)(2,1)S(1)}, u32[]{:S(2)}, u32[]{:S(2)}) collective-permute-start(bf16[256,2048]{1,0:T(8,128)(2,1)S(1)} %get-tuple-element.149), channel_id=1, source_target_pairs={{96,97},{98,99},{100,101},{102,103},{104,105},{106,107},{108,109},... | collective-permute-start | bytes 3145736 | tf_op jit(solution)/shard_map/ppermute | solution.py:431
  135.3 18.2 %collective-permute-start.33 = (bf16[128,2048]{1,0:T(8,128)(2,1)S(1)}, bf16[128,2048]{1,0:T(8,128)(2,1)S(1)}, u32[]{:S(2)}, u32[]{:S(2)}) collective-permute-start(bf16[128,2048]{1,0:T(8,128)(2,1)S(1)} %dynamic-slice_bitcast_fusion.4), channel_id=1, source_target_pairs={{0,1},{2,3},{4,5},{6,7},{8,9},{10,11},{12,13},{14,15},{16,17},{18,... | collective-permute-start | bytes 1572872 | tf_op jit(solution)/shard_map/ppermute | solution.py:415
  179.3 165.8 %collective-permute-start.40 = (bf16[256,2048]{1,0:T(8,128)(2,1)}, bf16[256,2048]{1,0:T(8,128)(2,1)}, u32[]{:S(2)}, u32[]{:S(2)}) collective-permute-start(bf16[256,2048]{1,0:T(8,128)(2,1)} %get-tuple-element.178), channel_id=1, source_target_pairs={{1,0},{3,2},{5,4},{7,6},{9,8},{11,10},{13,12},{15,14},{17,16},{19,... | collective-permute-start | bytes 3145736 | tf_op jit(solution)/shard_map/ppermute | solution.py:445
  347.8 16.9 %collective-permute-start.43 = (bf16[2,32,2048]{2,1,0:T(8,128)(2,1)S(1)}, bf16[2,32,2048]{2,1,0:T(8,128)(2,1)S(1)}, u32[]{:S(2)}, u32[]{:S(2)}) collective-permute-start(bf16[2,32,2048]{2,1,0:T(8,128)(2,1)S(1)} %get-tuple-element.213), channel_id=1, source_target_pairs={{0,128},{128,2},{2,130},{130,4},{4,132},{132,6},{6,134},{134,0},{1... | collective-permute-start | bytes 786440 | tf_op jit(solution)/shard_map/ppermute | solution.py:277
  347.9 16.8 %collective-permute-start.45 = (bf16[2,32,2048]{2,1,0:T(8,128)(2,1)S(1)}, bf16[2,32,2048]{2,1,0:T(8,128)(2,1)S(1)}, u32[]{:S(2)}, u32[]{:S(2)}) collective-permute-start(bf16[2,32,2048]{2,1,0:T(8,128)(2,1)S(1)} %get-tuple-element.211), channel_id=1, source_target_pairs={{0,134},{128,0},{2,128},{130,2},{4,130},{132,4},{6,132},{134,6},{1... | collective-permute-start | bytes 786440 | tf_op jit(solution)/shard_map/ppermute | solution.py:277
  361.2 15.6 %collective-permute-start.41 = (bf16[256,1536]{1,0:T(8,128)(2,1)S(1)}, bf16[256,1536]{1,0:T(8,128)(2,1)S(1)}, u32[]{:S(2)}, u32[]{:S(2)}) collective-permute-start(bf16[256,1536]{1,0:T(8,128)(2,1)S(1)} %get-tuple-element.203), channel_id=1, source_target_pairs={{0,8},{8,16},{16,24},{24,0},{1,9},{9,17},{17,25},{25,1},{2,10},{10... | collective-permute-start | bytes 2359304 | tf_op jit(solution)/shard_map/ppermute | solution.py:273
  362.6 14.2 %collective-permute-start.42 = (bf16[256,1536]{1,0:T(8,128)(2,1)S(1)}, bf16[256,1536]{1,0:T(8,128)(2,1)S(1)}, u32[]{:S(2)}, u32[]{:S(2)}) collective-permute-start(bf16[256,1536]{1,0:T(8,128)(2,1)S(1)} %get-tuple-element.201), channel_id=1, source_target_pairs={{0,24},{8,0},{16,8},{24,16},{1,25},{9,1},{17,9},{25,17},{2,26},{10... | collective-permute-start | bytes 2359304 | tf_op jit(solution)/shard_map/ppermute | solution.py:273
  365.0 12.5 %collective-permute-start.44 = (bf16[4,32,2048]{2,1,0:T(8,128)(2,1)S(1)}, bf16[4,32,2048]{2,1,0:T(8,128)(2,1)S(1)}, u32[]{:S(2)}, u32[]{:S(2)}) collective-permute-start(bf16[4,32,2048]{2,1,0:T(8,128)(2,1)S(1)} %pad_maximum_fusion.4), channel_id=1, source_target_pairs={{0,128},{128,2},{2,130},{130,4},{4,132},{132,6},{6,134},{134,0},{1... | collective-permute-start | bytes 1572872 | tf_op jit(solution)/shard_map/ppermute | solution.py:277
  365.1 12.4 %collective-permute-start.46 = (bf16[4,32,2048]{2,1,0:T(8,128)(2,1)S(1)}, bf16[4,32,2048]{2,1,0:T(8,128)(2,1)S(1)}, u32[]{:S(2)}, u32[]{:S(2)}) collective-permute-start(bf16[4,32,2048]{2,1,0:T(8,128)(2,1)S(1)} %pad_maximum_fusion.5), channel_id=1, source_target_pairs={{0,134},{128,0},{2,128},{130,2},{4,130},{132,4},{6,132},{134,6},{1... | collective-permute-start | bytes 1572872 | tf_op jit(solution)/shard_map/ppermute | solution.py:277
  377.9 12.7 %collective-permute-start.57 = (bf16[4,32,2048]{2,1,0:T(8,128)(2,1)S(1)}, bf16[4,32,2048]{2,1,0:T(8,128)(2,1)S(1)}, u32[]{:S(2)}, u32[]{:S(2)}) collective-permute-start(bf16[4,32,2048]{2,1,0:T(8,128)(2,1)S(1)} %get-tuple-element.198), channel_id=1, source_target_pairs={{0,128},{128,2},{2,130},{130,4},{4,132},{132,6},{6,134},{134,0},{1... | collective-permute-start | bytes 1572872 | tf_op jit(solution)/shard_map/ppermute | solution.py:277
  378.0 12.6 %collective-permute-start.59 = (bf16[4,32,2048]{2,1,0:T(8,128)(2,1)S(1)}, bf16[4,32,2048]{2,1,0:T(8,128)(2,1)S(1)}, u32[]{:S(2)}, u32[]{:S(2)}) collective-permute-start(bf16[4,32,2048]{2,1,0:T(8,128)(2,1)S(1)} %get-tuple-element.199), channel_id=1, source_target_pairs={{0,134},{128,0},{2,128},{130,2},{4,130},{132,4},{6,132},{134,6},{1... | collective-permute-start | bytes 1572872 | tf_op jit(solution)/shard_map/ppermute | solution.py:277
  380.9 30.7 %collective-permute-start.47 = (bf16[512,1536]{1,0:T(8,128)(2,1)S(1)}, bf16[512,1536]{1,0:T(8,128)(2,1)S(1)}, u32[]{:S(2)}, u32[]{:S(2)}) collective-permute-start(bf16[512,1536]{1,0:T(8,128)(2,1)S(1)} %pad_maximum_fusion), channel_id=1, source_target_pairs={{0,8},{8,16},{16,24},{24,0},{1,9},{9,17},{17,25},{25,1},{2,10},{10... | collective-permute-start | bytes 4718600 | tf_op jit(solution)/shard_map/ppermute | solution.py:273
  382.0 29.7 %collective-permute-start.48 = (bf16[512,1536]{1,0:T(8,128)(2,1)S(1)}, bf16[512,1536]{1,0:T(8,128)(2,1)S(1)}, u32[]{:S(2)}, u32[]{:S(2)}) collective-permute-start(bf16[512,1536]{1,0:T(8,128)(2,1)S(1)} %pad_maximum_fusion.1), channel_id=1, source_target_pairs={{0,24},{8,0},{16,8},{24,16},{1,25},{9,1},{17,9},{25,17},{2,26},{10... | collective-permute-start | bytes 4718600 | tf_op jit(solution)/shard_map/ppermute | solution.py:273
  390.9 10.3 %collective-permute-start.58 = (bf16[4,32,2048]{2,1,0:T(8,128)(2,1)S(1)}, bf16[4,32,2048]{2,1,0:T(8,128)(2,1)S(1)}, u32[]{:S(2)}, u32[]{:S(2)}) collective-permute-start(bf16[4,32,2048]{2,1,0:T(8,128)(2,1)S(1)} %get-tuple-element.206), channel_id=1, source_target_pairs={{0,128},{128,2},{2,130},{130,4},{4,132},{132,6},{6,134},{134,0},{1... | collective-permute-start | bytes 1572872 | tf_op jit(solution)/shard_map/ppermute | solution.py:277
  392.0 9.7 %collective-permute-start.60 = (bf16[4,32,2048]{2,1,0:T(8,128)(2,1)S(1)}, bf16[4,32,2048]{2,1,0:T(8,128)(2,1)S(1)}, u32[]{:S(2)}, u32[]{:S(2)}) collective-permute-start(bf16[4,32,2048]{2,1,0:T(8,128)(2,1)S(1)} %get-tuple-element.207), channel_id=1, source_target_pairs={{0,134},{128,0},{2,128},{130,2},{4,130},{132,4},{6,132},{134,6},{1... | collective-permute-start | bytes 1572872 | tf_op jit(solution)/shard_map/ppermute | solution.py:277
  412.4 21.7 %collective-permute-start.49 = (bf16[64,1536]{1,0:T(8,128)(2,1)S(1)}, bf16[64,1536]{1,0:T(8,128)(2,1)S(1)}, u32[]{:S(2)}, u32[]{:S(2)}) collective-permute-start(bf16[64,1536]{1,0:T(8,128)(2,1)S(1)} %get-tuple-element.216), channel_id=1, source_target_pairs={{0,4},{128,132},{2,6},{130,134},{4,0},{132,128},{6,2},{134,130},{1... | collective-permute-start | bytes 589832 | tf_op jit(solution)/shard_map/ppermute | solution.py:277
  414.1 21.0 %collective-permute-start.50 = (bf16[64,1536]{1,0:T(8,128)(2,1)S(1)}, bf16[64,1536]{1,0:T(8,128)(2,1)S(1)}, u32[]{:S(2)}, u32[]{:S(2)}) collective-permute-start(bf16[64,1536]{1,0:T(8,128)(2,1)S(1)} %get-tuple-element.222), channel_id=1, source_target_pairs={{0,130},{128,4},{2,132},{130,6},{4,134},{132,0},{6,128},{134,2},{1... | collective-permute-start | bytes 589832 | tf_op jit(solution)/shard_map/ppermute | solution.py:277
  427.3 13.8 %collective-permute-start.51 = (bf16[64,1536]{1,0:T(8,128)(2,1)S(1)}, bf16[64,1536]{1,0:T(8,128)(2,1)S(1)}, u32[]{:S(2)}, u32[]{:S(2)}) collective-permute-start(bf16[64,1536]{1,0:T(8,128)(2,1)S(1)} %get-tuple-element.221), channel_id=1, source_target_pairs={{0,132},{128,6},{2,134},{130,0},{4,128},{132,2},{6,130},{134,4},{1... | collective-permute-start | bytes 589832 | tf_op jit(solution)/shard_map/ppermute | solution.py:277
  430.0 13.0 %collective-permute-start.52 = (bf16[64,1536]{1,0:T(8,128)(2,1)S(1)}, bf16[64,1536]{1,0:T(8,128)(2,1)S(1)}, u32[]{:S(2)}, u32[]{:S(2)}) collective-permute-start(bf16[64,1536]{1,0:T(8,128)(2,1)S(1)} %get-tuple-element.220), channel_id=1, source_target_pairs={{0,2},{128,130},{2,4},{130,132},{4,6},{132,134},{6,0},{134,128},{1... | collective-permute-start | bytes 589832 | tf_op jit(solution)/shard_map/ppermute | solution.py:277
  430.3 16.7 %collective-permute-start.53 = (bf16[64,1536]{1,0:T(8,128)(2,1)S(1)}, bf16[64,1536]{1,0:T(8,128)(2,1)S(1)}, u32[]{:S(2)}, u32[]{:S(2)}) collective-permute-start(bf16[64,1536]{1,0:T(8,128)(2,1)S(1)} %get-tuple-element.219), channel_id=1, source_target_pairs={{0,6},{128,134},{2,0},{130,128},{4,2},{132,130},{6,4},{134,132},{1... | collective-permute-start | bytes 589832 | tf_op jit(solution)/shard_map/ppermute | solution.py:277
  434.1 12.9 %collective-permute-start.54 = (bf16[64,1536]{1,0:T(8,128)(2,1)S(1)}, bf16[64,1536]{1,0:T(8,128)(2,1)S(1)}, u32[]{:S(2)}, u32[]{:S(2)}) collective-permute-start(bf16[64,1536]{1,0:T(8,128)(2,1)S(1)} %get-tuple-element.218), channel_id=1, source_target_pairs={{0,128},{128,2},{2,130},{130,4},{4,132},{132,6},{6,134},{134,0},{1... | collective-permute-start | bytes 589832 | tf_op jit(solution)/shard_map/ppermute | solution.py:277
  435.1 12.9 %collective-permute-start.55 = (bf16[64,1536]{1,0:T(8,128)(2,1)S(1)}, bf16[64,1536]{1,0:T(8,128)(2,1)S(1)}, u32[]{:S(2)}, u32[]{:S(2)}) collective-permute-start(bf16[64,1536]{1,0:T(8,128)(2,1)S(1)} %get-tuple-element.217), channel_id=1, source_target_pairs={{0,134},{128,0},{2,128},{130,2},{4,130},{132,4},{6,132},{134,6},{1... | collective-permute-start | bytes 589832 | tf_op jit(solution)/shard_map/ppermute | solution.py:277
  441.0 9.3 %collective-permute-start.64 = (bf16[32,2048]{1,0:T(8,128)(2,1)S(1)}, bf16[32,2048]{1,0:T(8,128)(2,1)S(1)}, u32[]{:S(2)}, u32[]{:S(2)}) collective-permute-start(bf16[32,2048]{1,0:T(8,128)(2,1)S(1)} %fusion.23), channel_id=1, source_target_pairs={{0,0},{128,1},{2,2},{130,3},{4,4},{132,5},{6,6},{134,7},{8,8},{136... | collective-permute-start | bytes 393224 | tf_op jit(solution)/shard_map/ppermute | solution.py:448
  448.2 10.0 %collective-permute-start.56 = (bf16[64,1536]{1,0:T(8,128)(2,1)S(1)}, bf16[64,1536]{1,0:T(8,128)(2,1)S(1)}, u32[]{:S(2)}, u32[]{:S(2)}) collective-permute-start(bf16[64,1536]{1,0:T(8,128)(2,1)S(1)} %fusion.20), channel_id=1, source_target_pairs={{0,0},{128,1},{2,2},{130,3},{4,4},{132,5},{6,6},{134,7},{8,8},{136... | collective-permute-start | bytes 589832 | tf_op jit(solution)/shard_map/ppermute | solution.py:449
  (31 other events, 272.1 us)

commit v8 on v7

--- a/solution.py
+++ b/solution.py
@@ -131,7 +131,7 @@
             marks_v[:, c] = jnp.concatenate([marks[:ROWS], marks[ROWS:]], axis=1)
             return carry
 
-        lax.fori_loop(0, KVH, group, 0, unroll=2)
+        lax.fori_loop(0, KVH, group, 0, unroll=True)
         def finish(i, carry):
             c = cols(i * CHUNK, CHUNK)
             out = h_v[:, c].astype(jnp.float32) + dot_nn(ctx_v[...], wo_v[:, c])
@@ -204,7 +204,7 @@
             dvt_s[rows, :] = d_value[:HEAD, :ROWS] + d_value[HEAD:, ROWS:]
             return carry
 
-        lax.fori_loop(0, KVH, group, 0, unroll=2)
+        lax.fori_loop(0, KVH, group, 0, unroll=True)
         dproj_v[:, HQ : HQ + KV] = dkt_s[...].T.astype(jnp.bfloat16)
         dproj_v[:, HQ + KV :] = dvt_s[...].T.astype(jnp.bfloat16)
         if not last:
@@ -407,7 +407,8 @@
     bin_index = 4 * x_index + lax.axis_index("zhi")
     flag = joined[micro, bin_index]
     near = lax.ppermute(w_qkv[0], NAMES, regroup(False))
-    far = lax.ppermute(w_out[0], NAMES, regroup(False))
+    near, later = lax.optimization_barrier((near, w_out[0]))
+    far = lax.ppermute(later, NAMES, regroup(False))
     full_qkv, full_out = gather_weights(near, far, x_index, z_place)
     block = lax.dynamic_index_in_dim(inputs, micro, 0, keepdims=False)
     hidden = jnp.concatenate([block, lax.ppermute(block, "core", [(1, 0)])])

time: 469 us -> 469 us (level)
  waiting for transfers between devices: 258 us -> 238 us
  Pallas kernels: 50.2 us -> 63.2 us
  starting transfers between devices: 118 us -> 125 us
    ppermute x7, waiting for transfers between devices: 164 us -> 143 us  [on_device(): upstream = lax.ppermute(result, STAGE, [(layer, layer - 1)])]
    pallas_call x8, Pallas kernels: 24.7 us -> 34 us  [backward_layer(): pl.pallas_call(functools.partial(backward_kernel, last), out_shape=(v16(R...]
  transfers between devices with their start and end apart: 65 -> 65, of which waited for: 28 -> 23; matrix products, arithmetic and copies ran while one was open for 5% -> 5% of each run, Pallas kernels for 3% -> 3%
where the time goes in v8:
time: 469 us; the launch traced here: 460 us
  waiting for transfers between devices  238 us (51%)
  starting transfers between devices  125 us (27%)
  Pallas kernels  63.2 us (13%)
  local copies, waits for them, and re-layouts  18.7 us (4%)
  other arithmetic  8.43 us (2%)
    ppermute x7, waiting for transfers between devices, on_device(): upstream = lax.ppermute(result, STAGE, [(layer, layer - 1)])  143 us
    ppermute x31, starting transfers between devices, send_z(): lax.ppermute(value, ('zlo', 'zhi'), [(z_index(i), z_index((i + step) % 8)...  54.2 us
    ppermute x31, waiting for transfers between devices, send_z(): lax.ppermute(value, ('zlo', 'zhi'), [(z_index(i), z_index((i + step) % 8)...  52.7 us
    pallas_call x8, Pallas kernels, backward_layer(): pl.pallas_call(functools.partial(backward_kernel, last), out_shape=(v16(R...  34 us
    ppermute x14, waiting for transfers between devices, send_x(): return lax.ppermute(value, 'x', [(i, (i + step) % 4) for i in range(4)])  26 us
    ppermute x14, starting transfers between devices, send_x(): return lax.ppermute(value, 'x', [(i, (i + step) % 4) for i in range(4)])  25 us
    pallas_call x8, Pallas kernels, forward_layer(): pl.pallas_call(functools.partial(forward_kernel, final), out_shape=(v16(R...  20.4 us
    ppermute x1, starting transfers between devices, on_device(): upstream = jnp.concatenate([lax.ppermute(block, 'core', [(0, 1)]), block])  15.6 us
  transfers between devices with their start and end apart: 65, of which 23 were waited for; matrix products, arithmetic and copies ran while one was open for 5% of the time, Pallas kernels for 3%

profile of v8, /device:TPU:32, one launch (start us, length us, event | category | flops | bytes accessed | tf_op | source)
XLA Modules:
  0.0 459.8 jit_solution(15721658820533544688)
XLA Ops:
  0.6 4.8 %collective-permute-start.1 = (bf16[64,1536]{1,0:T(8,128)(2,1)}, bf16[64,1536]{1,0:T(8,128)(2,1)S(1)}, u32[]{:S(2)}, u32[]{:S(2)}) collective-permute-start(bf16[64,1536]{1,0:T(8,128)(2,1)} %bitcast.125), channel_id=1, source_target_pairs={{0,0},{1,128},{2,2},{3,130},{4,4},{5,132},{6,6},{7,134},{8,8},{9,1... | collective-permute-start | bytes 589832 | tf_op jit(solution)/shard_map/ppermute | solution.py:409
  5.4 3.5 collective-permute-done.1
  10.9 9.1 %collective-permute-start.14 = (bf16[32,2048]{1,0:T(8,128)(2,1)}, bf16[32,2048]{1,0:T(8,128)(2,1)S(1)}, u32[]{:S(2)}, u32[]{:S(2)}) collective-permute-start(bf16[32,2048]{1,0:T(8,128)(2,1)} %bitcast.126), channel_id=1, source_target_pairs={{0,0},{1,128},{2,2},{3,130},{4,4},{5,132},{6,6},{7,134},{8,8},{9,1... | collective-permute-start | bytes 393224 | tf_op jit(solution)/shard_map/ppermute | solution.py:411
  22.8 2.8 collective-permute-start.15
  30.1 2.2 collective-permute-done.15
  37.0 6.0 %collective-permute-done.7 = bf16[64,1536]{1,0:T(8,128)(2,1)S(1)} collective-permute-done((bf16[64,1536]{1,0:T(8,128)(2,1)S(1)}, bf16[64,1536]{1,0:T(8,128)(2,1)S(1)}, u32[]{:S(2)}, u32[]{:S(2)}) %collective-permute-start.7) | collective-permute-done | bytes 196640 | tf_op jit(solution)/shard_map/ppermute | solution.py:277
  43.2 3.6 collective-permute-start.9
  57.1 2.3 collective-permute-start.18
  60.1 8.6 %collective-permute-done.21.refs_7_ = bf16[128,2048]{1,0:T(8,128)(2,1)S(1)} collective-permute-done((bf16[128,2048]{1,0:T(8,128)(2,1)S(1)}, bf16[128,2048]{1,0:T(8,128)(2,1)S(1)}, u32[]{:S(2)}, u32[]{:S(2)}) %collective-permute-start.21) | collective-permute-done | bytes 524320 | tf_op jit(solution)/shard_map/ppermute | solution.py:277
  70.6 3.1 collective-permute-start.19
  73.7 10.0 %collective-permute-done.22.refs_6_ = bf16[128,2048]{1,0:T(8,128)(2,1)} collective-permute-done((bf16[128,2048]{1,0:T(8,128)(2,1)S(1)}, bf16[128,2048]{1,0:T(8,128)(2,1)}, u32[]{:S(2)}, u32[]{:S(2)}) %collective-permute-start.22) | collective-permute-done | bytes 524320 | tf_op jit(solution)/shard_map/ppermute | solution.py:277
  85.6 4.6 %collective-permute-start.20 = (bf16[128,2048]{1,0:T(8,128)(2,1)}, bf16[128,2048]{1,0:T(8,128)(2,1)}, u32[]{:S(2)}, u32[]{:S(2)}) collective-permute-start(bf16[128,2048]{1,0:T(8,128)(2,1)} %collective-permute-done.19.refs_5_), channel_id=1, source_target_pairs={{0,134},{128,0},{2,128},{130,2},{4,130},{132,4},{6,132},{134,6},{1... | collective-permute-start | bytes 1572872 | tf_op jit(solution)/shard_map/ppermute | solution.py:277
  96.5 2.7 collective-permute-start.13
  104.6 3.7 collective-permute-start.25
  110.6 5.9 %assemble.1 = (bf16[2048,1536]{1,0:T(8,128)(2,1)S(1)}, bf16[1024,2048]{1,0:T(8,128)(2,1)S(1)}) custom-call(s32[2]{0:T(128)S(1)} %pad_add_fusion.8.place, bf16[512,1536]{1,0:T(8,128)(2,1)} %constant_dynamic-update-slice_fusion.refs_0_, bf16[512,1536]{1,0:T(8,128)(2,1)} %collective-permute-done.12.refs_1_, ...), custom_call_target="tpu_custom_call" | custom-call | bytes 18000000 | tf_op jit(solution)/shard_map/assemble/pallas_call | solution.py:344
  117.4 2.9 assemble_rest.1
  120.8 5.8 %forward_layer.7 = (bf16[256,2048]{1,0:T(8,128)(2,1)S(1)}, bf16[256,2048]{1,0:T(8,128)(2,1)S(1)}, bf16[256,1536]{1,0:T(8,128)(2,1)S(1)}, bf16[256,1024]{1,0:T(8,...) custom-call(s32[2]{0:T(128)S(1)} %get-tuple-element.110.place.h_v.wq, ...), custom_call_target="tpu_custom_call", output_to_operand_aliasing={{1}: (4, {}), {2}: (5, {}), {3}: (6, {}), {4}: (7, {}), {5}... | custom-call | flops 3000000000 | bytes 14000000 | tf_op jit(solution)/shard_map/forward_layer/pallas_call | solution.py:163
  128.0 2.2 collective-permute-done.26.h_v
  133.0 5.2 %forward_layer.10 = (bf16[256,2048]{1,0:T(8,128)(2,1)S(1)}, bf16[256,2048]{1,0:T(8,128)(2,1)S(1)}, bf16[256,1536]{1,0:T(8,128)(2,1)S(1)}, bf16[256,1024]{1,0:T(8...) custom-call(s32[2]{0:T(128)S(1)} %get-tuple-element.107.place, ...), custom_call_target="tpu_custom_call", output_to_operand_aliasing={{1}: (4, {}), {2}: (5, {}), {3}: (6, {}), {4}: (7, {}), {5}... | custom-call | flops 3000000000 | bytes 14000000 | tf_op jit(solution)/shard_map/forward_layer/pallas_call | solution.py:163
  140.3 5.1 %forward_layer.12 = (bf16[256,2048]{1,0:T(8,128)(2,1)S(1)}, bf16[256,2048]{1,0:T(8,128)(2,1)S(1)}, bf16[256,1536]{1,0:T(8,128)(2,1)S(1)}, bf16[256,1024]{1,0:T(8...) custom-call(s32[2]{0:T(128)S(1)} %get-tuple-element.105.place, ...), custom_call_target="tpu_custom_call", output_to_operand_aliasing={{1}: (4, {}), {2}: (5, {}), {3}: (6, {}), {4}: (7, {}), {5}... | custom-call | flops 3000000000 | bytes 14000000 | tf_op jit(solution)/shard_map/forward_layer/pallas_call | solution.py:163
  147.5 15.6 %collective-permute-start.33 = (bf16[128,2048]{1,0:T(8,128)(2,1)S(1)}, bf16[128,2048]{1,0:T(8,128)(2,1)S(1)}, u32[]{:S(2)}, u32[]{:S(2)}) collective-permute-start(bf16[128,2048]{1,0:T(8,128)(2,1)S(1)} %dynamic-slice_bitcast_fusion.4), channel_id=1, source_target_pairs={{0,1},{2,3},{4,5},{6,7},{8,9},{10,11},{12,13},{14,15},{16,17},{18,... | collective-permute-start | bytes 1572872 | tf_op jit(solution)/shard_map/ppermute | solution.py:416
  168.0 2.4 backward_layer.8
  171.2 4.4 backward_layer.9
  176.3 4.1 backward_layer.10
  181.1 4.1 backward_layer.11
  186.0 4.2 backward_layer.12
  190.9 7.2 %backward_layer.13 = (bf16[256,2048]{1,0:T(8,128)(2,1)}, bf16[256,1536]{1,0:T(8,128)(2,1)S(1)}, bf16[256,2048]{1,0:T(8,128)(2,1)S(1)}) custom-call(s32[2]{0:T(128)S(1)} %get-tuple-element.109.place, bf16[256,2048]{1,0:T(8,128)(2,1)S(1)} %collective-permute-done.39.u_v, ...), custom_call_target="tpu_custom_call", output_to_operand_aliasing={{1}: (8, {}), {2}: (9, {})} | custom-call | flops 4000000000 | bytes 15000000 | tf_op jit(solution)/shard_map/backward_layer/pallas_call | solution.py:237
  201.3 142.8 %collective-permute-done.40.u_v = bf16[256,2048]{1,0:T(8,128)(2,1)} collective-permute-done((bf16[256,2048]{1,0:T(8,128)(2,1)}, bf16[256,2048]{1,0:T(8,128)(2,1)}, u32[]{:S(2)}, u32[]{:S(2)}) %collective-permute-start.40) | collective-permute-done | bytes 1048608 | tf_op jit(solution)/shard_map/ppermute | solution.py:446
  344.1 2.7 convolution_convert_fusion.1
  347.0 3.8 collective-permute-start.45
  350.7 7.1 %backward_last.1 = (bf16[256,2048]{1,0:T(8,128)(2,1)}, bf16[256,1536]{1,0:T(8,128)(2,1)S(1)}, bf16[256,2048]{1,0:T(8,128)(2,1)S(1)}) custom-call(s32[2]{0:T(128)S(1)} %get-tuple-element.110.place.h_v.wq_v, bf16[256,2048]{1,0:T(8,128)(2,1)} %collective-permute-done.40.u_v, ...), custom_call_target="tpu_custom_call", output_to_operand_aliasing={{1}: (8, {}), {2}: (9, {})} | custom-call | flops 4000000000 | bytes 15000000 | tf_op jit(solution)/shard_map/backward_last/pallas_call | solution.py:237
  360.1 3.8 collective-permute-start.42
  364.2 3.2 collective-permute-start.46
  367.4 9.1 %collective-permute-done.41 = bf16[256,1536]{1,0:T(8,128)(2,1)S(1)} collective-permute-done((bf16[256,1536]{1,0:T(8,128)(2,1)S(1)}, bf16[256,1536]{1,0:T(8,128)(2,1)S(1)}, u32[]{:S(2)}, u32[]{:S(2)}) %collective-permute-start.41) | collective-permute-done | bytes 786464 | tf_op jit(solution)/shard_map/ppermute | solution.py:273
  377.7 2.9 collective-permute-start.59
  384.0 6.0 %collective-permute-done.57 = bf16[4,32,2048]{2,1,0:T(8,128)(2,1)S(1)} collective-permute-done((bf16[4,32,2048]{2,1,0:T(8,128)(2,1)S(1)}, bf16[4,32,2048]{2,1,0:T(8,128)(2,1)S(1)}, u32[]{:S(2)}, u32[]{:S(2)}) %collective-permute-start.57) | collective-permute-done | bytes 524320 | tf_op jit(solution)/shard_map/ppermute | solution.py:277
  390.5 3.6 collective-permute-start.60
  394.1 7.1 %collective-permute-done.58 = bf16[4,32,2048]{2,1,0:T(8,128)(2,1)S(1)} collective-permute-done((bf16[4,32,2048]{2,1,0:T(8,128)(2,1)S(1)}, bf16[4,32,2048]{2,1,0:T(8,128)(2,1)S(1)}, u32[]{:S(2)}, u32[]{:S(2)}) %collective-permute-start.58) | collective-permute-done | bytes 524320 | tf_op jit(solution)/shard_map/ppermute | solution.py:277
  401.4 10.8 %collective-permute-done.47 = bf16[512,1536]{1,0:T(8,128)(2,1)S(1)} collective-permute-done((bf16[512,1536]{1,0:T(8,128)(2,1)S(1)}, bf16[512,1536]{1,0:T(8,128)(2,1)S(1)}, u32[]{:S(2)}, u32[]{:S(2)}) %collective-permute-start.47) | collective-permute-done | bytes 1572896 | tf_op jit(solution)/shard_map/ppermute | solution.py:273
  413.9 6.5 %collective-permute-start.50 = (bf16[64,1536]{1,0:T(8,128)(2,1)S(1)}, bf16[64,1536]{1,0:T(8,128)(2,1)S(1)}, u32[]{:S(2)}, u32[]{:S(2)}) collective-permute-start(bf16[64,1536]{1,0:T(8,128)(2,1)S(1)} %get-tuple-element.226), channel_id=1, source_target_pairs={{0,130},{128,4},{2,132},{130,6},{4,134},{132,0},{6,128},{134,2},{1... | collective-permute-start | bytes 589832 | tf_op jit(solution)/shard_map/ppermute | solution.py:277
  420.4 3.5 collective-permute-start.61
  424.3 2.8 collective-permute-start.63
  427.2 2.9 collective-permute-done.62
  430.1 4.1 collective-permute-start.53
  434.3 3.6 collective-permute-start.55
  437.9 3.3 collective-permute-done.51
  443.1 3.9 collective-permute-done.53
  451.5 7.3 %collective-permute-done.56 = bf16[64,1536]{1,0:T(8,128)(2,1)S(1)} collective-permute-done((bf16[64,1536]{1,0:T(8,128)(2,1)S(1)}, bf16[64,1536]{1,0:T(8,128)(2,1)S(1)}, u32[]{:S(2)}, u32[]{:S(2)}) %collective-permute-start.56) | collective-permute-done | bytes 196640 | tf_op jit(solution)/shard_map/ppermute | solution.py:450
  (184 shorter events, 81.1 us)
Async XLA Ops:
  0.6 8.3 %collective-permute-start.1 = (bf16[64,1536]{1,0:T(8,128)(2,1)}, bf16[64,1536]{1,0:T(8,128)(2,1)S(1)}, u32[]{:S(2)}, u32[]{:S(2)}) collective-permute-start(bf16[64,1536]{1,0:T(8,128)(2,1)} %bitcast.125), channel_id=1, source_target_pairs={{0,0},{1,128},{2,2},{3,130},{4,4},{5,132},{6,6},{7,134},{8,8},{9,1... | collective-permute-start | bytes 589832 | tf_op jit(solution)/shard_map/ppermute | solution.py:409
  8.9 18.4 %collective-permute-start.2 = (bf16[64,1536]{1,0:T(8,128)(2,1)S(1)}, bf16[64,1536]{1,0:T(8,128)(2,1)S(1)}, u32[]{:S(2)}, u32[]{:S(2)}) collective-permute-start(bf16[64,1536]{1,0:T(8,128)(2,1)S(1)} %collective-permute-done.1), channel_id=1, source_target_pairs={{0,134},{128,0},{2,128},{130,2},{4,130},{132,4},{6,132},{134,6},{1... | collective-permute-start | bytes 589832 | tf_op jit(solution)/shard_map/ppermute | solution.py:277
  8.9 18.5 %collective-permute-start.5 = (bf16[64,1536]{1,0:T(8,128)(2,1)S(1)}, bf16[64,1536]{1,0:T(8,128)(2,1)S(1)}, u32[]{:S(2)}, u32[]{:S(2)}) collective-permute-start(bf16[64,1536]{1,0:T(8,128)(2,1)S(1)} %collective-permute-done.1), channel_id=1, source_target_pairs={{0,128},{128,2},{2,130},{130,4},{4,132},{132,6},{6,134},{134,0},{1... | collective-permute-start | bytes 589832 | tf_op jit(solution)/shard_map/ppermute | solution.py:277
  10.9 11.9 %collective-permute-start.14 = (bf16[32,2048]{1,0:T(8,128)(2,1)}, bf16[32,2048]{1,0:T(8,128)(2,1)S(1)}, u32[]{:S(2)}, u32[]{:S(2)}) collective-permute-start(bf16[32,2048]{1,0:T(8,128)(2,1)} %bitcast.126), channel_id=1, source_target_pairs={{0,0},{1,128},{2,2},{3,130},{4,4},{5,132},{6,6},{7,134},{8,8},{9,1... | collective-permute-start | bytes 393224 | tf_op jit(solution)/shard_map/ppermute | solution.py:411
  22.8 9.5 %collective-permute-start.15 = (bf16[32,2048]{1,0:T(8,128)(2,1)S(1)}, bf16[32,2048]{1,0:T(8,128)(2,1)S(1)}, u32[]{:S(2)}, u32[]{:S(2)}) collective-permute-start(bf16[32,2048]{1,0:T(8,128)(2,1)S(1)} %collective-permute-done.14), channel_id=1, source_target_pairs={{0,24},{8,0},{16,8},{24,16},{1,25},{9,1},{17,9},{25,17},{2,26},{10... | collective-permute-start | bytes 393224 | tf_op jit(solution)/shard_map/ppermute | solution.py:273
  25.6 30.3 %collective-permute-start.16 = (bf16[32,2048]{1,0:T(8,128)(2,1)S(1)}, bf16[32,2048]{1,0:T(8,128)(2,1)S(1)}, u32[]{:S(2)}, u32[]{:S(2)}) collective-permute-start(bf16[32,2048]{1,0:T(8,128)(2,1)S(1)} %collective-permute-done.14), channel_id=1, source_target_pairs={{0,16},{8,24},{16,0},{24,8},{1,17},{9,25},{17,1},{25,9},{2,18},{10... | collective-permute-start | bytes 393224 | tf_op jit(solution)/shard_map/ppermute | solution.py:273
  26.4 29.5 %collective-permute-start.17 = (bf16[32,2048]{1,0:T(8,128)(2,1)S(1)}, bf16[32,2048]{1,0:T(8,128)(2,1)S(1)}, u32[]{:S(2)}, u32[]{:S(2)}) collective-permute-start(bf16[32,2048]{1,0:T(8,128)(2,1)S(1)} %collective-permute-done.14), channel_id=1, source_target_pairs={{0,8},{8,16},{16,24},{24,0},{1,9},{9,17},{17,25},{25,1},{2,10},{10... | collective-permute-start | bytes 393224 | tf_op jit(solution)/shard_map/ppermute | solution.py:273
  27.3 7.0 %collective-permute-start.3 = (bf16[64,1536]{1,0:T(8,128)(2,1)S(1)}, bf16[64,1536]{1,0:T(8,128)(2,1)S(1)}, u32[]{:S(2)}, u32[]{:S(2)}) collective-permute-start(bf16[64,1536]{1,0:T(8,128)(2,1)S(1)} %collective-permute-done.2), channel_id=1, source_target_pairs={{0,134},{128,0},{2,128},{130,2},{4,130},{132,4},{6,132},{134,6},{1... | collective-permute-start | bytes 589832 | tf_op jit(solution)/shard_map/ppermute | solution.py:277
  27.4 8.4 %collective-permute-start.6 = (bf16[64,1536]{1,0:T(8,128)(2,1)S(1)}, bf16[64,1536]{1,0:T(8,128)(2,1)S(1)}, u32[]{:S(2)}, u32[]{:S(2)}) collective-permute-start(bf16[64,1536]{1,0:T(8,128)(2,1)S(1)} %collective-permute-done.5), channel_id=1, source_target_pairs={{0,128},{128,2},{2,130},{130,4},{4,132},{132,6},{6,134},{134,0},{1... | collective-permute-start | bytes 589832 | tf_op jit(solution)/shard_map/ppermute | solution.py:277
  34.3 8.9 %collective-permute-start.4 = (bf16[64,1536]{1,0:T(8,128)(2,1)S(1)}, bf16[64,1536]{1,0:T(8,128)(2,1)S(1)}, u32[]{:S(2)}, u32[]{:S(2)}) collective-permute-start(bf16[64,1536]{1,0:T(8,128)(2,1)S(1)} %collective-permute-done.3), channel_id=1, source_target_pairs={{0,134},{128,0},{2,128},{130,2},{4,130},{132,4},{6,132},{134,6},{1... | collective-permute-start | bytes 589832 | tf_op jit(solution)/shard_map/ppermute | solution.py:277
  35.8 7.2 %collective-permute-start.7 = (bf16[64,1536]{1,0:T(8,128)(2,1)S(1)}, bf16[64,1536]{1,0:T(8,128)(2,1)S(1)}, u32[]{:S(2)}, u32[]{:S(2)}) collective-permute-start(bf16[64,1536]{1,0:T(8,128)(2,1)S(1)} %collective-permute-done.6), channel_id=1, source_target_pairs={{0,128},{128,2},{2,130},{130,4},{4,132},{132,6},{6,134},{134,0},{1... | collective-permute-start | bytes 589832 | tf_op jit(solution)/shard_map/ppermute | solution.py:277
  52.6 40.4 %collective-permute-start.10 = (bf16[512,1536]{1,0:T(8,128)(2,1)}, bf16[512,1536]{1,0:T(8,128)(2,1)S(1)}, u32[]{:S(2)}, u32[]{:S(2)}) collective-permute-start(bf16[512,1536]{1,0:T(8,128)(2,1)} %constant_dynamic-update-slice_fusion.refs_0_), channel_id=1, source_target_pairs={{0,8},{8,16},{16,24},{24,0},{1,9},{9,17},{17,25},{25,1},{2,10},{10... | collective-permute-start | bytes 4718600 | tf_op jit(solution)/shard_map/ppermute | solution.py:273
  54.8 39.7 %collective-permute-start.12 = (bf16[512,1536]{1,0:T(8,128)(2,1)}, bf16[512,1536]{1,0:T(8,128)(2,1)}, u32[]{:S(2)}, u32[]{:S(2)}) collective-permute-start(bf16[512,1536]{1,0:T(8,128)(2,1)} %constant_dynamic-update-slice_fusion.refs_0_), channel_id=1, source_target_pairs={{0,24},{8,0},{16,8},{24,16},{1,25},{9,1},{17,9},{25,17},{2,26},{10... | collective-permute-start | bytes 4718600 | tf_op jit(solution)/shard_map/ppermute | solution.py:273
  55.9 12.8 %collective-permute-start.21 = (bf16[128,2048]{1,0:T(8,128)(2,1)S(1)}, bf16[128,2048]{1,0:T(8,128)(2,1)S(1)}, u32[]{:S(2)}, u32[]{:S(2)}) collective-permute-start(bf16[128,2048]{1,0:T(8,128)(2,1)S(1)} %constant_dynamic-update-slice_fusion.9.refs_3_), channel_id=1, source_target_pairs={{0,128},{128,2},{2,130},{130,4},{4,132},{132,6},{6,134},{134,0},{1... | collective-permute-start | bytes 1572872 | tf_op jit(solution)/shard_map/ppermute | solution.py:277
  57.1 13.5 %collective-permute-start.18 = (bf16[128,2048]{1,0:T(8,128)(2,1)S(1)}, bf16[128,2048]{1,0:T(8,128)(2,1)}, u32[]{:S(2)}, u32[]{:S(2)}) collective-permute-start(bf16[128,2048]{1,0:T(8,128)(2,1)S(1)} %constant_dynamic-update-slice_fusion.9.refs_3_), channel_id=1, source_target_pairs={{0,134},{128,0},{2,128},{130,2},{4,130},{132,4},{6,132},{134,6},{1... | collective-permute-start | bytes 1572872 | tf_op jit(solution)/shard_map/ppermute | solution.py:277
  68.8 14.9 %collective-permute-start.22 = (bf16[128,2048]{1,0:T(8,128)(2,1)S(1)}, bf16[128,2048]{1,0:T(8,128)(2,1)}, u32[]{:S(2)}, u32[]{:S(2)}) collective-permute-start(bf16[128,2048]{1,0:T(8,128)(2,1)S(1)} %collective-permute-done.21.refs_7_), channel_id=1, source_target_pairs={{0,128},{128,2},{2,130},{130,4},{4,132},{132,6},{6,134},{134,0},{1... | collective-permute-start | bytes 1572872 | tf_op jit(solution)/shard_map/ppermute | solution.py:277
  70.6 15.0 %collective-permute-start.19 = (bf16[128,2048]{1,0:T(8,128)(2,1)}, bf16[128,2048]{1,0:T(8,128)(2,1)}, u32[]{:S(2)}, u32[]{:S(2)}) collective-permute-start(bf16[128,2048]{1,0:T(8,128)(2,1)} %collective-permute-done.18.refs_4_), channel_id=1, source_target_pairs={{0,134},{128,0},{2,128},{130,2},{4,130},{132,4},{6,132},{134,6},{1... | collective-permute-start | bytes 1572872 | tf_op jit(solution)/shard_map/ppermute | solution.py:277
  83.6 18.5 %collective-permute-start.23 = (bf16[128,2048]{1,0:T(8,128)(2,1)}, bf16[128,2048]{1,0:T(8,128)(2,1)S(1)}, u32[]{:S(2)}, u32[]{:S(2)}) collective-permute-start(bf16[128,2048]{1,0:T(8,128)(2,1)} %collective-permute-done.22.refs_6_), channel_id=1, source_target_pairs={{0,128},{128,2},{2,130},{130,4},{4,132},{132,6},{6,134},{134,0},{1... | collective-permute-start | bytes 1572872 | tf_op jit(solution)/shard_map/ppermute | solution.py:277
  85.6 17.3 %collective-permute-start.20 = (bf16[128,2048]{1,0:T(8,128)(2,1)}, bf16[128,2048]{1,0:T(8,128)(2,1)}, u32[]{:S(2)}, u32[]{:S(2)}) collective-permute-start(bf16[128,2048]{1,0:T(8,128)(2,1)} %collective-permute-done.19.refs_5_), channel_id=1, source_target_pairs={{0,134},{128,0},{2,128},{130,2},{4,130},{132,4},{6,132},{134,6},{1... | collective-permute-start | bytes 1572872 | tf_op jit(solution)/shard_map/ppermute | solution.py:277
  91.1 17.3 %collective-permute-start = (bf16[128,2048]{1,0:T(8,128)(2,1)}, bf16[128,2048]{1,0:T(8,128)(2,1)S(1)}, u32[]{:S(2)}, u32[]{:S(2)}) collective-permute-start(bf16[128,2048]{1,0:T(8,128)(2,1)} %dynamic-slice_bitcast_fusion.5), channel_id=1, source_target_pairs={{1,0},{3,2},{5,4},{7,6},{9,8},{11,10},{13,12},{15,14},{17,16},{19,... | collective-permute-start | bytes 1572872 | tf_op jit(solution)/shard_map/ppermute | solution.py:414
  94.0 22.6 %collective-permute-start.11 = (bf16[256,1536]{1,0:T(8,128)(2,1)}, bf16[256,1536]{1,0:T(8,128)(2,1)}, u32[]{:S(2)}, u32[]{:S(2)}) collective-permute-start(bf16[256,1536]{1,0:T(8,128)(2,1)} %slice.26), channel_id=1, source_target_pairs={{0,8},{8,16},{16,24},{24,0},{1,9},{9,17},{17,25},{25,1},{2,10},{10... | collective-permute-start | bytes 2359304 | tf_op jit(solution)/shard_map/ppermute | solution.py:273
  96.5 20.9 %collective-permute-start.13 = (bf16[256,1536]{1,0:T(8,128)(2,1)}, bf16[256,1536]{1,0:T(8,128)(2,1)}, u32[]{:S(2)}, u32[]{:S(2)}) collective-permute-start(bf16[256,1536]{1,0:T(8,128)(2,1)} %slice.27), channel_id=1, source_target_pairs={{0,24},{8,0},{16,8},{24,16},{1,25},{9,1},{17,9},{25,17},{2,26},{10... | collective-permute-start | bytes 2359304 | tf_op jit(solution)/shard_map/ppermute | solution.py:273
  102.9 13.6 %collective-permute-start.24 = (bf16[64,2048]{1,0:T(8,128)(2,1)}, bf16[64,2048]{1,0:T(8,128)(2,1)S(1)}, u32[]{:S(2)}, u32[]{:S(2)}) collective-permute-start(bf16[64,2048]{1,0:T(8,128)(2,1)} %slice.28), channel_id=1, source_target_pairs={{0,128},{128,2},{2,130},{130,4},{4,132},{132,6},{6,134},{134,0},{1... | collective-permute-start | bytes 786440 | tf_op jit(solution)/shard_map/ppermute | solution.py:277
  104.6 11.9 %collective-permute-start.25 = (bf16[64,2048]{1,0:T(8,128)(2,1)}, bf16[64,2048]{1,0:T(8,128)(2,1)}, u32[]{:S(2)}, u32[]{:S(2)}) collective-permute-start(bf16[64,2048]{1,0:T(8,128)(2,1)} %slice.29), channel_id=1, source_target_pairs={{0,134},{128,0},{2,128},{130,2},{4,130},{132,4},{6,132},{134,6},{1... | collective-permute-start | bytes 786440 | tf_op jit(solution)/shard_map/ppermute | solution.py:277
  146.7 18.0 %collective-permute-start.32 = (bf16[256,2048]{1,0:T(8,128)(2,1)S(1)}, bf16[256,2048]{1,0:T(8,128)(2,1)S(1)}, u32[]{:S(2)}, u32[]{:S(2)}) collective-permute-start(bf16[256,2048]{1,0:T(8,128)(2,1)S(1)} %get-tuple-element.153), channel_id=1, source_target_pairs={{96,97},{98,99},{100,101},{102,103},{104,105},{106,107},{108,109},... | collective-permute-start | bytes 3145736 | tf_op jit(solution)/shard_map/ppermute | solution.py:432
  147.5 17.1 %collective-permute-start.33 = (bf16[128,2048]{1,0:T(8,128)(2,1)S(1)}, bf16[128,2048]{1,0:T(8,128)(2,1)S(1)}, u32[]{:S(2)}, u32[]{:S(2)}) collective-permute-start(bf16[128,2048]{1,0:T(8,128)(2,1)S(1)} %dynamic-slice_bitcast_fusion.4), channel_id=1, source_target_pairs={{0,1},{2,3},{4,5},{6,7},{8,9},{10,11},{12,13},{14,15},{16,17},{18,... | collective-permute-start | bytes 1572872 | tf_op jit(solution)/shard_map/ppermute | solution.py:416
  200.0 144.1 %collective-permute-start.40 = (bf16[256,2048]{1,0:T(8,128)(2,1)}, bf16[256,2048]{1,0:T(8,128)(2,1)}, u32[]{:S(2)}, u32[]{:S(2)}) collective-permute-start(bf16[256,2048]{1,0:T(8,128)(2,1)} %get-tuple-element.182), channel_id=1, source_target_pairs={{1,0},{3,2},{5,4},{7,6},{9,8},{11,10},{13,12},{15,14},{17,16},{19,... | collective-permute-start | bytes 3145736 | tf_op jit(solution)/shard_map/ppermute | solution.py:446
  346.9 17.0 %collective-permute-start.43 = (bf16[2,32,2048]{2,1,0:T(8,128)(2,1)S(1)}, bf16[2,32,2048]{2,1,0:T(8,128)(2,1)S(1)}, u32[]{:S(2)}, u32[]{:S(2)}) collective-permute-start(bf16[2,32,2048]{2,1,0:T(8,128)(2,1)S(1)} %get-tuple-element.217), channel_id=1, source_target_pairs={{0,128},{128,2},{2,130},{130,4},{4,132},{132,6},{6,134},{134,0},{1... | collective-permute-start | bytes 786440 | tf_op jit(solution)/shard_map/ppermute | solution.py:277
  347.0 16.9 %collective-permute-start.45 = (bf16[2,32,2048]{2,1,0:T(8,128)(2,1)S(1)}, bf16[2,32,2048]{2,1,0:T(8,128)(2,1)S(1)}, u32[]{:S(2)}, u32[]{:S(2)}) collective-permute-start(bf16[2,32,2048]{2,1,0:T(8,128)(2,1)S(1)} %get-tuple-element.215), channel_id=1, source_target_pairs={{0,134},{128,0},{2,128},{130,2},{4,130},{132,4},{6,132},{134,6},{1... | collective-permute-start | bytes 786440 | tf_op jit(solution)/shard_map/ppermute | solution.py:277
  360.0 16.6 %collective-permute-start.41 = (bf16[256,1536]{1,0:T(8,128)(2,1)S(1)}, bf16[256,1536]{1,0:T(8,128)(2,1)S(1)}, u32[]{:S(2)}, u32[]{:S(2)}) collective-permute-start(bf16[256,1536]{1,0:T(8,128)(2,1)S(1)} %get-tuple-element.207), channel_id=1, source_target_pairs={{0,8},{8,16},{16,24},{24,0},{1,9},{9,17},{17,25},{25,1},{2,10},{10... | collective-permute-start | bytes 2359304 | tf_op jit(solution)/shard_map/ppermute | solution.py:273
  360.1 16.5 %collective-permute-start.42 = (bf16[256,1536]{1,0:T(8,128)(2,1)S(1)}, bf16[256,1536]{1,0:T(8,128)(2,1)S(1)}, u32[]{:S(2)}, u32[]{:S(2)}) collective-permute-start(bf16[256,1536]{1,0:T(8,128)(2,1)S(1)} %get-tuple-element.205), channel_id=1, source_target_pairs={{0,24},{8,0},{16,8},{24,16},{1,25},{9,1},{17,9},{25,17},{2,26},{10... | collective-permute-start | bytes 2359304 | tf_op jit(solution)/shard_map/ppermute | solution.py:273
  364.1 13.1 %collective-permute-start.44 = (bf16[4,32,2048]{2,1,0:T(8,128)(2,1)S(1)}, bf16[4,32,2048]{2,1,0:T(8,128)(2,1)S(1)}, u32[]{:S(2)}, u32[]{:S(2)}) collective-permute-start(bf16[4,32,2048]{2,1,0:T(8,128)(2,1)S(1)} %pad_maximum_fusion.4), channel_id=1, source_target_pairs={{0,128},{128,2},{2,130},{130,4},{4,132},{132,6},{6,134},{134,0},{1... | collective-permute-start | bytes 1572872 | tf_op jit(solution)/shard_map/ppermute | solution.py:277
  364.2 13.0 %collective-permute-start.46 = (bf16[4,32,2048]{2,1,0:T(8,128)(2,1)S(1)}, bf16[4,32,2048]{2,1,0:T(8,128)(2,1)S(1)}, u32[]{:S(2)}, u32[]{:S(2)}) collective-permute-start(bf16[4,32,2048]{2,1,0:T(8,128)(2,1)S(1)} %pad_maximum_fusion.5), channel_id=1, source_target_pairs={{0,134},{128,0},{2,128},{130,2},{4,130},{132,4},{6,132},{134,6},{1... | collective-permute-start | bytes 1572872 | tf_op jit(solution)/shard_map/ppermute | solution.py:277
  377.6 12.4 %collective-permute-start.57 = (bf16[4,32,2048]{2,1,0:T(8,128)(2,1)S(1)}, bf16[4,32,2048]{2,1,0:T(8,128)(2,1)S(1)}, u32[]{:S(2)}, u32[]{:S(2)}) collective-permute-start(bf16[4,32,2048]{2,1,0:T(8,128)(2,1)S(1)} %get-tuple-element.202), channel_id=1, source_target_pairs={{0,128},{128,2},{2,130},{130,4},{4,132},{132,6},{6,134},{134,0},{1... | collective-permute-start | bytes 1572872 | tf_op jit(solution)/shard_map/ppermute | solution.py:277
  377.7 12.3 %collective-permute-start.59 = (bf16[4,32,2048]{2,1,0:T(8,128)(2,1)S(1)}, bf16[4,32,2048]{2,1,0:T(8,128)(2,1)S(1)}, u32[]{:S(2)}, u32[]{:S(2)}) collective-permute-start(bf16[4,32,2048]{2,1,0:T(8,128)(2,1)S(1)} %get-tuple-element.203), channel_id=1, source_target_pairs={{0,134},{128,0},{2,128},{130,2},{4,130},{132,4},{6,132},{134,6},{1... | collective-permute-start | bytes 1572872 | tf_op jit(solution)/shard_map/ppermute | solution.py:277
  380.6 31.6 %collective-permute-start.47 = (bf16[512,1536]{1,0:T(8,128)(2,1)S(1)}, bf16[512,1536]{1,0:T(8,128)(2,1)S(1)}, u32[]{:S(2)}, u32[]{:S(2)}) collective-permute-start(bf16[512,1536]{1,0:T(8,128)(2,1)S(1)} %pad_maximum_fusion), channel_id=1, source_target_pairs={{0,8},{8,16},{16,24},{24,0},{1,9},{9,17},{17,25},{25,1},{2,10},{10... | collective-permute-start | bytes 4718600 | tf_op jit(solution)/shard_map/ppermute | solution.py:273
  381.9 30.3 %collective-permute-start.48 = (bf16[512,1536]{1,0:T(8,128)(2,1)S(1)}, bf16[512,1536]{1,0:T(8,128)(2,1)S(1)}, u32[]{:S(2)}, u32[]{:S(2)}) collective-permute-start(bf16[512,1536]{1,0:T(8,128)(2,1)S(1)} %pad_maximum_fusion.1), channel_id=1, source_target_pairs={{0,24},{8,0},{16,8},{24,16},{1,25},{9,1},{17,9},{25,17},{2,26},{10... | collective-permute-start | bytes 4718600 | tf_op jit(solution)/shard_map/ppermute | solution.py:273
  390.4 10.7 %collective-permute-start.58 = (bf16[4,32,2048]{2,1,0:T(8,128)(2,1)S(1)}, bf16[4,32,2048]{2,1,0:T(8,128)(2,1)S(1)}, u32[]{:S(2)}, u32[]{:S(2)}) collective-permute-start(bf16[4,32,2048]{2,1,0:T(8,128)(2,1)S(1)} %get-tuple-element.210), channel_id=1, source_target_pairs={{0,128},{128,2},{2,130},{130,4},{4,132},{132,6},{6,134},{134,0},{1... | collective-permute-start | bytes 1572872 | tf_op jit(solution)/shard_map/ppermute | solution.py:277
  390.5 10.7 %collective-permute-start.60 = (bf16[4,32,2048]{2,1,0:T(8,128)(2,1)S(1)}, bf16[4,32,2048]{2,1,0:T(8,128)(2,1)S(1)}, u32[]{:S(2)}, u32[]{:S(2)}) collective-permute-start(bf16[4,32,2048]{2,1,0:T(8,128)(2,1)S(1)} %get-tuple-element.211), channel_id=1, source_target_pairs={{0,134},{128,0},{2,128},{130,2},{4,130},{132,4},{6,132},{134,6},{1... | collective-permute-start | bytes 1572872 | tf_op jit(solution)/shard_map/ppermute | solution.py:277
  413.0 21.3 %collective-permute-start.49 = (bf16[64,1536]{1,0:T(8,128)(2,1)S(1)}, bf16[64,1536]{1,0:T(8,128)(2,1)S(1)}, u32[]{:S(2)}, u32[]{:S(2)}) collective-permute-start(bf16[64,1536]{1,0:T(8,128)(2,1)S(1)} %get-tuple-element.220), channel_id=1, source_target_pairs={{0,4},{128,132},{2,6},{130,134},{4,0},{132,128},{6,2},{134,130},{1... | collective-permute-start | bytes 589832 | tf_op jit(solution)/shard_map/ppermute | solution.py:277
  413.9 20.3 %collective-permute-start.50 = (bf16[64,1536]{1,0:T(8,128)(2,1)S(1)}, bf16[64,1536]{1,0:T(8,128)(2,1)S(1)}, u32[]{:S(2)}, u32[]{:S(2)}) collective-permute-start(bf16[64,1536]{1,0:T(8,128)(2,1)S(1)} %get-tuple-element.226), channel_id=1, source_target_pairs={{0,130},{128,4},{2,132},{130,6},{4,134},{132,0},{6,128},{134,2},{1... | collective-permute-start | bytes 589832 | tf_op jit(solution)/shard_map/ppermute | solution.py:277
  427.2 14.0 %collective-permute-start.51 = (bf16[64,1536]{1,0:T(8,128)(2,1)S(1)}, bf16[64,1536]{1,0:T(8,128)(2,1)S(1)}, u32[]{:S(2)}, u32[]{:S(2)}) collective-permute-start(bf16[64,1536]{1,0:T(8,128)(2,1)S(1)} %get-tuple-element.225), channel_id=1, source_target_pairs={{0,132},{128,6},{2,134},{130,0},{4,128},{132,2},{6,130},{134,4},{1... | collective-permute-start | bytes 589832 | tf_op jit(solution)/shard_map/ppermute | solution.py:277
  430.1 13.0 %collective-permute-start.52 = (bf16[64,1536]{1,0:T(8,128)(2,1)S(1)}, bf16[64,1536]{1,0:T(8,128)(2,1)S(1)}, u32[]{:S(2)}, u32[]{:S(2)}) collective-permute-start(bf16[64,1536]{1,0:T(8,128)(2,1)S(1)} %get-tuple-element.224), channel_id=1, source_target_pairs={{0,2},{128,130},{2,4},{130,132},{4,6},{132,134},{6,0},{134,128},{1... | collective-permute-start | bytes 589832 | tf_op jit(solution)/shard_map/ppermute | solution.py:277
  430.1 17.0 %collective-permute-start.53 = (bf16[64,1536]{1,0:T(8,128)(2,1)S(1)}, bf16[64,1536]{1,0:T(8,128)(2,1)S(1)}, u32[]{:S(2)}, u32[]{:S(2)}) collective-permute-start(bf16[64,1536]{1,0:T(8,128)(2,1)S(1)} %get-tuple-element.223), channel_id=1, source_target_pairs={{0,6},{128,134},{2,0},{130,128},{4,2},{132,130},{6,4},{134,132},{1... | collective-permute-start | bytes 589832 | tf_op jit(solution)/shard_map/ppermute | solution.py:277
  434.3 12.8 %collective-permute-start.54 = (bf16[64,1536]{1,0:T(8,128)(2,1)S(1)}, bf16[64,1536]{1,0:T(8,128)(2,1)S(1)}, u32[]{:S(2)}, u32[]{:S(2)}) collective-permute-start(bf16[64,1536]{1,0:T(8,128)(2,1)S(1)} %get-tuple-element.222), channel_id=1, source_target_pairs={{0,128},{128,2},{2,130},{130,4},{4,132},{132,6},{6,134},{134,0},{1... | collective-permute-start | bytes 589832 | tf_op jit(solution)/shard_map/ppermute | solution.py:277
  434.3 14.4 %collective-permute-start.55 = (bf16[64,1536]{1,0:T(8,128)(2,1)S(1)}, bf16[64,1536]{1,0:T(8,128)(2,1)S(1)}, u32[]{:S(2)}, u32[]{:S(2)}) collective-permute-start(bf16[64,1536]{1,0:T(8,128)(2,1)S(1)} %get-tuple-element.221), channel_id=1, source_target_pairs={{0,134},{128,0},{2,128},{130,2},{4,130},{132,4},{6,132},{134,6},{1... | collective-permute-start | bytes 589832 | tf_op jit(solution)/shard_map/ppermute | solution.py:277
  441.2 9.6 %collective-permute-start.64 = (bf16[32,2048]{1,0:T(8,128)(2,1)S(1)}, bf16[32,2048]{1,0:T(8,128)(2,1)S(1)}, u32[]{:S(2)}, u32[]{:S(2)}) collective-permute-start(bf16[32,2048]{1,0:T(8,128)(2,1)S(1)} %fusion.23), channel_id=1, source_target_pairs={{0,0},{128,1},{2,2},{130,3},{4,4},{132,5},{6,6},{134,7},{8,8},{136... | collective-permute-start | bytes 393224 | tf_op jit(solution)/shard_map/ppermute | solution.py:449
  448.8 10.0 %collective-permute-start.56 = (bf16[64,1536]{1,0:T(8,128)(2,1)S(1)}, bf16[64,1536]{1,0:T(8,128)(2,1)S(1)}, u32[]{:S(2)}, u32[]{:S(2)}) collective-permute-start(bf16[64,1536]{1,0:T(8,128)(2,1)S(1)} %fusion.20), channel_id=1, source_target_pairs={{0,0},{128,1},{2,2},{130,3},{4,4},{132,5},{6,6},{134,7},{8,8},{136... | collective-permute-start | bytes 589832 | tf_op jit(solution)/shard_map/ppermute | solution.py:450
  (31 other events, 300.9 us)

commit v9 on v8

--- a/solution.py
+++ b/solution.py
@@ -407,8 +407,7 @@
     bin_index = 4 * x_index + lax.axis_index("zhi")
     flag = joined[micro, bin_index]
     near = lax.ppermute(w_qkv[0], NAMES, regroup(False))
-    near, later = lax.optimization_barrier((near, w_out[0]))
-    far = lax.ppermute(later, NAMES, regroup(False))
+    far = lax.ppermute(w_out[0], NAMES, regroup(False))
     full_qkv, full_out = gather_weights(near, far, x_index, z_place)
     block = lax.dynamic_index_in_dim(inputs, micro, 0, keepdims=False)
     hidden = jnp.concatenate([block, lax.ppermute(block, "core", [(1, 0)])])

time: 469 us -> 460 us (0.981)
  starting transfers between devices: 125 us -> 119 us
  transfers between devices with their start and end apart: 65 -> 65, of which waited for: 23 -> 25; matrix products, arithmetic and copies ran while one was open for 5% -> 5% of each run, Pallas kernels for 3% -> 3%
where the time goes in v9:
time: 460 us; the launch traced here: 451 us
  waiting for transfers between devices  235 us (51%)
  starting transfers between devices  119 us (26%)
  Pallas kernels  63.2 us (14%)
  local copies, waits for them, and re-layouts  18.7 us (4%)
  other arithmetic  8.43 us (2%)
    ppermute x7, waiting for transfers between devices, on_device(): upstream = lax.ppermute(result, STAGE, [(layer, layer - 1)])  143 us
    ppermute x31, waiting for transfers between devices, send_z(): lax.ppermute(value, ('zlo', 'zhi'), [(z_index(i), z_index((i + step) % 8)...  55.7 us
    ppermute x31, starting transfers between devices, send_z(): lax.ppermute(value, ('zlo', 'zhi'), [(z_index(i), z_index((i + step) % 8)...  55.3 us
    pallas_call x8, Pallas kernels, backward_layer(): pl.pallas_call(functools.partial(backward_kernel, last), out_shape=(v16(R...  34 us
    ppermute x14, waiting for transfers between devices, send_x(): return lax.ppermute(value, 'x', [(i, (i + step) % 4) for i in range(4)])  25.2 us
    ppermute x14, starting transfers between devices, send_x(): return lax.ppermute(value, 'x', [(i, (i + step) % 4) for i in range(4)])  24.4 us
    pallas_call x8, Pallas kernels, forward_layer(): pl.pallas_call(functools.partial(forward_kernel, final), out_shape=(v16(R...  20.4 us
    ppermute x1, starting transfers between devices, on_device(): upstream = jnp.concatenate([lax.ppermute(block, 'core', [(0, 1)]), block])  15.6 us
  transfers between devices with their start and end apart: 65, of which 25 were waited for; matrix products, arithmetic and copies ran while one was open for 5% of the time, Pallas kernels for 3%

profile of v9, /device:TPU:32, one launch (start us, length us, event | category | flops | bytes accessed | tf_op | source)
XLA Modules:
  0.0 450.7 jit_solution(7493545952465692195)
XLA Ops:
  0.6 4.8 %collective-permute-start.14 = (bf16[32,2048]{1,0:T(8,128)(2,1)}, bf16[32,2048]{1,0:T(8,128)(2,1)S(1)}, u32[]{:S(2)}, u32[]{:S(2)}) collective-permute-start(bf16[32,2048]{1,0:T(8,128)(2,1)} %bitcast.126), channel_id=1, source_target_pairs={{0,0},{1,128},{2,2},{3,130},{4,4},{5,132},{6,6},{7,134},{8,8},{9,1... | collective-permute-start | bytes 393224 | tf_op jit(solution)/shard_map/ppermute | solution.py:410
  5.4 2.4 collective-permute-start.1
  8.2 2.8 collective-permute-start.15
  17.4 3.0 collective-permute-done.2
  20.3 3.5 collective-permute-start.3
  25.0 2.6 collective-permute-done.3
  27.5 3.3 collective-permute-start.4
  31.9 6.2 %collective-permute-done.7 = bf16[64,1536]{1,0:T(8,128)(2,1)S(1)} collective-permute-done((bf16[64,1536]{1,0:T(8,128)(2,1)S(1)}, bf16[64,1536]{1,0:T(8,128)(2,1)S(1)}, u32[]{:S(2)}, u32[]{:S(2)}) %collective-permute-start.7) | collective-permute-done | bytes 196640 | tf_op jit(solution)/shard_map/ppermute | solution.py:277
  38.3 3.3 collective-permute-start.9
  54.9 7.7 %collective-permute-done.21.refs_7_ = bf16[128,2048]{1,0:T(8,128)(2,1)S(1)} collective-permute-done((bf16[128,2048]{1,0:T(8,128)(2,1)S(1)}, bf16[128,2048]{1,0:T(8,128)(2,1)S(1)}, u32[]{:S(2)}, u32[]{:S(2)}) %collective-permute-start.21) | collective-permute-done | bytes 524320 | tf_op jit(solution)/shard_map/ppermute | solution.py:277
  62.7 2.4 collective-permute-start.22
  67.2 8.6 %collective-permute-done.22.refs_6_ = bf16[128,2048]{1,0:T(8,128)(2,1)} collective-permute-done((bf16[128,2048]{1,0:T(8,128)(2,1)S(1)}, bf16[128,2048]{1,0:T(8,128)(2,1)}, u32[]{:S(2)}, u32[]{:S(2)}) %collective-permute-start.22) | collective-permute-done | bytes 524320 | tf_op jit(solution)/shard_map/ppermute | solution.py:277
  78.5 2.4 collective-permute-start.20
  95.6 3.3 collective-permute-start.25
  101.2 5.9 %assemble.1 = (bf16[2048,1536]{1,0:T(8,128)(2,1)S(1)}, bf16[1024,2048]{1,0:T(8,128)(2,1)S(1)}) custom-call(s32[2]{0:T(128)S(1)} %pad_add_fusion.8.place, bf16[512,1536]{1,0:T(8,128)(2,1)} %constant_dynamic-update-slice_fusion.refs_0_, bf16[512,1536]{1,0:T(8,128)(2,1)} %collective-permute-done.12.refs_1_, ...), custom_call_target="tpu_custom_call" | custom-call | bytes 18000000 | tf_op jit(solution)/shard_map/assemble/pallas_call | solution.py:344
  108.9 2.9 assemble_rest.1
  112.2 5.8 %forward_layer.7 = (bf16[256,2048]{1,0:T(8,128)(2,1)S(1)}, bf16[256,2048]{1,0:T(8,128)(2,1)S(1)}, bf16[256,1536]{1,0:T(8,128)(2,1)S(1)}, bf16[256,1024]{1,0:T(8,...) custom-call(s32[2]{0:T(128)S(1)} %get-tuple-element.108.place.h_v.wq, ...), custom_call_target="tpu_custom_call", output_to_operand_aliasing={{1}: (4, {}), {2}: (5, {}), {3}: (6, {}), {4}: (7, {}), {5}... | custom-call | flops 3000000000 | bytes 14000000 | tf_op jit(solution)/shard_map/forward_layer/pallas_call | solution.py:163
  119.4 2.2 collective-permute-done.26.h_v
  124.4 5.2 %forward_layer.10 = (bf16[256,2048]{1,0:T(8,128)(2,1)S(1)}, bf16[256,2048]{1,0:T(8,128)(2,1)S(1)}, bf16[256,1536]{1,0:T(8,128)(2,1)S(1)}, bf16[256,1024]{1,0:T(8...) custom-call(s32[2]{0:T(128)S(1)} %get-tuple-element.105.place, ...), custom_call_target="tpu_custom_call", output_to_operand_aliasing={{1}: (4, {}), {2}: (5, {}), {3}: (6, {}), {4}: (7, {}), {5}... | custom-call | flops 3000000000 | bytes 14000000 | tf_op jit(solution)/shard_map/forward_layer/pallas_call | solution.py:163
  131.7 5.1 %forward_layer.12 = (bf16[256,2048]{1,0:T(8,128)(2,1)S(1)}, bf16[256,2048]{1,0:T(8,128)(2,1)S(1)}, bf16[256,1536]{1,0:T(8,128)(2,1)S(1)}, bf16[256,1024]{1,0:T(8...) custom-call(s32[2]{0:T(128)S(1)} %get-tuple-element.103.place, ...), custom_call_target="tpu_custom_call", output_to_operand_aliasing={{1}: (4, {}), {2}: (5, {}), {3}: (6, {}), {4}: (7, {}), {5}... | custom-call | flops 3000000000 | bytes 14000000 | tf_op jit(solution)/shard_map/forward_layer/pallas_call | solution.py:163
  139.0 15.6 %collective-permute-start.33 = (bf16[128,2048]{1,0:T(8,128)(2,1)S(1)}, bf16[128,2048]{1,0:T(8,128)(2,1)S(1)}, u32[]{:S(2)}, u32[]{:S(2)}) collective-permute-start(bf16[128,2048]{1,0:T(8,128)(2,1)S(1)} %dynamic-slice_bitcast_fusion.4), channel_id=1, source_target_pairs={{0,1},{2,3},{4,5},{6,7},{8,9},{10,11},{12,13},{14,15},{16,17},{18,... | collective-permute-start | bytes 1572872 | tf_op jit(solution)/shard_map/ppermute | solution.py:415
  159.4 2.4 backward_layer.8
  162.6 4.4 backward_layer.9
  167.7 4.1 backward_layer.10
  172.5 4.1 backward_layer.11
  177.4 4.2 backward_layer.12
  182.3 7.2 %backward_layer.13 = (bf16[256,2048]{1,0:T(8,128)(2,1)}, bf16[256,1536]{1,0:T(8,128)(2,1)S(1)}, bf16[256,2048]{1,0:T(8,128)(2,1)S(1)}) custom-call(s32[2]{0:T(128)S(1)} %get-tuple-element.107.place, bf16[256,2048]{1,0:T(8,128)(2,1)S(1)} %collective-permute-done.39.u_v, ...), custom_call_target="tpu_custom_call", output_to_operand_aliasing={{1}: (8, {}), {2}: (9, {})} | custom-call | flops 4000000000 | bytes 15000000 | tf_op jit(solution)/shard_map/backward_layer/pallas_call | solution.py:237
  192.7 142.8 %collective-permute-done.40.u_v = bf16[256,2048]{1,0:T(8,128)(2,1)} collective-permute-done((bf16[256,2048]{1,0:T(8,128)(2,1)}, bf16[256,2048]{1,0:T(8,128)(2,1)}, u32[]{:S(2)}, u32[]{:S(2)}) %collective-permute-start.40) | collective-permute-done | bytes 1048608 | tf_op jit(solution)/shard_map/ppermute | solution.py:445
  335.5 2.7 convolution_convert_fusion.1
  338.4 3.8 collective-permute-start.45
  342.2 7.1 %backward_last.1 = (bf16[256,2048]{1,0:T(8,128)(2,1)}, bf16[256,1536]{1,0:T(8,128)(2,1)S(1)}, bf16[256,2048]{1,0:T(8,128)(2,1)S(1)}) custom-call(s32[2]{0:T(128)S(1)} %get-tuple-element.108.place.h_v.wq_v, bf16[256,2048]{1,0:T(8,128)(2,1)} %collective-permute-done.40.u_v, ...), custom_call_target="tpu_custom_call", output_to_operand_aliasing={{1}: (8, {}), {2}: (9, {})} | custom-call | flops 4000000000 | bytes 15000000 | tf_op jit(solution)/shard_map/backward_last/pallas_call | solution.py:237
  355.1 3.2 collective-permute-start.46
  358.3 8.9 %collective-permute-done.41 = bf16[256,1536]{1,0:T(8,128)(2,1)S(1)} collective-permute-done((bf16[256,1536]{1,0:T(8,128)(2,1)S(1)}, bf16[256,1536]{1,0:T(8,128)(2,1)S(1)}, u32[]{:S(2)}, u32[]{:S(2)}) %collective-permute-start.41) | collective-permute-done | bytes 786464 | tf_op jit(solution)/shard_map/ppermute | solution.py:273
  368.4 2.9 collective-permute-start.59
  372.6 2.2 collective-permute-start.48
  374.7 6.2 %collective-permute-done.57 = bf16[4,32,2048]{2,1,0:T(8,128)(2,1)S(1)} collective-permute-done((bf16[4,32,2048]{2,1,0:T(8,128)(2,1)S(1)}, bf16[4,32,2048]{2,1,0:T(8,128)(2,1)S(1)}, u32[]{:S(2)}, u32[]{:S(2)}) %collective-permute-start.57) | collective-permute-done | bytes 524320 | tf_op jit(solution)/shard_map/ppermute | solution.py:277
  381.5 3.6 collective-permute-start.60
  385.0 7.1 %collective-permute-done.58 = bf16[4,32,2048]{2,1,0:T(8,128)(2,1)S(1)} collective-permute-done((bf16[4,32,2048]{2,1,0:T(8,128)(2,1)S(1)}, bf16[4,32,2048]{2,1,0:T(8,128)(2,1)S(1)}, u32[]{:S(2)}, u32[]{:S(2)}) %collective-permute-start.58) | collective-permute-done | bytes 524320 | tf_op jit(solution)/shard_map/ppermute | solution.py:277
  392.8 9.8 %collective-permute-done.47 = bf16[512,1536]{1,0:T(8,128)(2,1)S(1)} collective-permute-done((bf16[512,1536]{1,0:T(8,128)(2,1)S(1)}, bf16[512,1536]{1,0:T(8,128)(2,1)S(1)}, u32[]{:S(2)}, u32[]{:S(2)}) %collective-permute-start.47) | collective-permute-done | bytes 1572896 | tf_op jit(solution)/shard_map/ppermute | solution.py:273
  405.1 5.7 %collective-permute-start.50 = (bf16[64,1536]{1,0:T(8,128)(2,1)S(1)}, bf16[64,1536]{1,0:T(8,128)(2,1)S(1)}, u32[]{:S(2)}, u32[]{:S(2)}) collective-permute-start(bf16[64,1536]{1,0:T(8,128)(2,1)S(1)} %get-tuple-element.222), channel_id=1, source_target_pairs={{0,130},{128,4},{2,132},{130,6},{4,134},{132,0},{6,128},{134,2},{1... | collective-permute-start | bytes 589832 | tf_op jit(solution)/shard_map/ppermute | solution.py:277
  410.8 3.5 collective-permute-start.61
  414.7 2.8 collective-permute-start.63
  417.6 2.9 collective-permute-done.62
  420.5 4.1 collective-permute-start.53
  424.7 3.4 collective-permute-start.55
  428.2 3.8 collective-permute-done.51
  433.9 3.7 collective-permute-done.53
  442.4 7.3 %collective-permute-done.56 = bf16[64,1536]{1,0:T(8,128)(2,1)S(1)} collective-permute-done((bf16[64,1536]{1,0:T(8,128)(2,1)S(1)}, bf16[64,1536]{1,0:T(8,128)(2,1)S(1)}, u32[]{:S(2)}, u32[]{:S(2)}) %collective-permute-start.56) | collective-permute-done | bytes 196640 | tf_op jit(solution)/shard_map/ppermute | solution.py:449
  (184 shorter events, 86.2 us)
Async XLA Ops:
  0.6 7.6 %collective-permute-start.14 = (bf16[32,2048]{1,0:T(8,128)(2,1)}, bf16[32,2048]{1,0:T(8,128)(2,1)S(1)}, u32[]{:S(2)}, u32[]{:S(2)}) collective-permute-start(bf16[32,2048]{1,0:T(8,128)(2,1)} %bitcast.126), channel_id=1, source_target_pairs={{0,0},{1,128},{2,2},{3,130},{4,4},{5,132},{6,6},{7,134},{8,8},{9,1... | collective-permute-start | bytes 393224 | tf_op jit(solution)/shard_map/ppermute | solution.py:410
  5.4 7.3 %collective-permute-start.1 = (bf16[64,1536]{1,0:T(8,128)(2,1)}, bf16[64,1536]{1,0:T(8,128)(2,1)S(1)}, u32[]{:S(2)}, u32[]{:S(2)}) collective-permute-start(bf16[64,1536]{1,0:T(8,128)(2,1)} %bitcast.125), channel_id=1, source_target_pairs={{0,0},{1,128},{2,2},{3,130},{4,4},{5,132},{6,6},{7,134},{8,8},{9,1... | collective-permute-start | bytes 589832 | tf_op jit(solution)/shard_map/ppermute | solution.py:409
  8.2 9.1 %collective-permute-start.15 = (bf16[32,2048]{1,0:T(8,128)(2,1)S(1)}, bf16[32,2048]{1,0:T(8,128)(2,1)S(1)}, u32[]{:S(2)}, u32[]{:S(2)}) collective-permute-start(bf16[32,2048]{1,0:T(8,128)(2,1)S(1)} %collective-permute-done.14), channel_id=1, source_target_pairs={{0,24},{8,0},{16,8},{24,16},{1,25},{9,1},{17,9},{25,17},{2,26},{10... | collective-permute-start | bytes 393224 | tf_op jit(solution)/shard_map/ppermute | solution.py:273
  11.0 39.7 %collective-permute-start.16 = (bf16[32,2048]{1,0:T(8,128)(2,1)S(1)}, bf16[32,2048]{1,0:T(8,128)(2,1)S(1)}, u32[]{:S(2)}, u32[]{:S(2)}) collective-permute-start(bf16[32,2048]{1,0:T(8,128)(2,1)S(1)} %collective-permute-done.14), channel_id=1, source_target_pairs={{0,16},{8,24},{16,0},{24,8},{1,17},{9,25},{17,1},{25,9},{2,18},{10... | collective-permute-start | bytes 393224 | tf_op jit(solution)/shard_map/ppermute | solution.py:273
  11.8 38.9 %collective-permute-start.17 = (bf16[32,2048]{1,0:T(8,128)(2,1)S(1)}, bf16[32,2048]{1,0:T(8,128)(2,1)S(1)}, u32[]{:S(2)}, u32[]{:S(2)}) collective-permute-start(bf16[32,2048]{1,0:T(8,128)(2,1)S(1)} %collective-permute-done.14), channel_id=1, source_target_pairs={{0,8},{8,16},{16,24},{24,0},{1,9},{9,17},{17,25},{25,1},{2,10},{10... | collective-permute-start | bytes 393224 | tf_op jit(solution)/shard_map/ppermute | solution.py:273
  12.7 7.6 %collective-permute-start.2 = (bf16[64,1536]{1,0:T(8,128)(2,1)S(1)}, bf16[64,1536]{1,0:T(8,128)(2,1)S(1)}, u32[]{:S(2)}, u32[]{:S(2)}) collective-permute-start(bf16[64,1536]{1,0:T(8,128)(2,1)S(1)} %collective-permute-done.1), channel_id=1, source_target_pairs={{0,134},{128,0},{2,128},{130,2},{4,130},{132,4},{6,132},{134,6},{1... | collective-permute-start | bytes 589832 | tf_op jit(solution)/shard_map/ppermute | solution.py:277
  12.8 11.5 %collective-permute-start.5 = (bf16[64,1536]{1,0:T(8,128)(2,1)S(1)}, bf16[64,1536]{1,0:T(8,128)(2,1)S(1)}, u32[]{:S(2)}, u32[]{:S(2)}) collective-permute-start(bf16[64,1536]{1,0:T(8,128)(2,1)S(1)} %collective-permute-done.1), channel_id=1, source_target_pairs={{0,128},{128,2},{2,130},{130,4},{4,132},{132,6},{6,134},{134,0},{1... | collective-permute-start | bytes 589832 | tf_op jit(solution)/shard_map/ppermute | solution.py:277
  20.3 7.2 %collective-permute-start.3 = (bf16[64,1536]{1,0:T(8,128)(2,1)S(1)}, bf16[64,1536]{1,0:T(8,128)(2,1)S(1)}, u32[]{:S(2)}, u32[]{:S(2)}) collective-permute-start(bf16[64,1536]{1,0:T(8,128)(2,1)S(1)} %collective-permute-done.2), channel_id=1, source_target_pairs={{0,134},{128,0},{2,128},{130,2},{4,130},{132,4},{6,132},{134,6},{1... | collective-permute-start | bytes 589832 | tf_op jit(solution)/shard_map/ppermute | solution.py:277
  24.3 7.0 %collective-permute-start.6 = (bf16[64,1536]{1,0:T(8,128)(2,1)S(1)}, bf16[64,1536]{1,0:T(8,128)(2,1)S(1)}, u32[]{:S(2)}, u32[]{:S(2)}) collective-permute-start(bf16[64,1536]{1,0:T(8,128)(2,1)S(1)} %collective-permute-done.5), channel_id=1, source_target_pairs={{0,128},{128,2},{2,130},{130,4},{4,132},{132,6},{6,134},{134,0},{1... | collective-permute-start | bytes 589832 | tf_op jit(solution)/shard_map/ppermute | solution.py:277
  27.5 10.7 %collective-permute-start.4 = (bf16[64,1536]{1,0:T(8,128)(2,1)S(1)}, bf16[64,1536]{1,0:T(8,128)(2,1)S(1)}, u32[]{:S(2)}, u32[]{:S(2)}) collective-permute-start(bf16[64,1536]{1,0:T(8,128)(2,1)S(1)} %collective-permute-done.3), channel_id=1, source_target_pairs={{0,134},{128,0},{2,128},{130,2},{4,130},{132,4},{6,132},{134,6},{1... | collective-permute-start | bytes 589832 | tf_op jit(solution)/shard_map/ppermute | solution.py:277
  31.3 6.9 %collective-permute-start.7 = (bf16[64,1536]{1,0:T(8,128)(2,1)S(1)}, bf16[64,1536]{1,0:T(8,128)(2,1)S(1)}, u32[]{:S(2)}, u32[]{:S(2)}) collective-permute-start(bf16[64,1536]{1,0:T(8,128)(2,1)S(1)} %collective-permute-done.6), channel_id=1, source_target_pairs={{0,128},{128,2},{2,130},{130,4},{4,132},{132,6},{6,134},{134,0},{1... | collective-permute-start | bytes 589832 | tf_op jit(solution)/shard_map/ppermute | solution.py:277
  47.4 36.2 %collective-permute-start.10 = (bf16[512,1536]{1,0:T(8,128)(2,1)}, bf16[512,1536]{1,0:T(8,128)(2,1)S(1)}, u32[]{:S(2)}, u32[]{:S(2)}) collective-permute-start(bf16[512,1536]{1,0:T(8,128)(2,1)} %constant_dynamic-update-slice_fusion.refs_0_), channel_id=1, source_target_pairs={{0,8},{8,16},{16,24},{24,0},{1,9},{9,17},{17,25},{25,1},{2,10},{10... | collective-permute-start | bytes 4718600 | tf_op jit(solution)/shard_map/ppermute | solution.py:273
  49.1 37.1 %collective-permute-start.12 = (bf16[512,1536]{1,0:T(8,128)(2,1)}, bf16[512,1536]{1,0:T(8,128)(2,1)}, u32[]{:S(2)}, u32[]{:S(2)}) collective-permute-start(bf16[512,1536]{1,0:T(8,128)(2,1)} %constant_dynamic-update-slice_fusion.refs_0_), channel_id=1, source_target_pairs={{0,24},{8,0},{16,8},{24,16},{1,25},{9,1},{17,9},{25,17},{2,26},{10... | collective-permute-start | bytes 4718600 | tf_op jit(solution)/shard_map/ppermute | solution.py:273
  50.7 11.9 %collective-permute-start.21 = (bf16[128,2048]{1,0:T(8,128)(2,1)S(1)}, bf16[128,2048]{1,0:T(8,128)(2,1)S(1)}, u32[]{:S(2)}, u32[]{:S(2)}) collective-permute-start(bf16[128,2048]{1,0:T(8,128)(2,1)S(1)} %constant_dynamic-update-slice_fusion.9.refs_3_), channel_id=1, source_target_pairs={{0,128},{128,2},{2,130},{130,4},{4,132},{132,6},{6,134},{134,0},{1... | collective-permute-start | bytes 1572872 | tf_op jit(solution)/shard_map/ppermute | solution.py:277
  52.3 13.5 %collective-permute-start.18 = (bf16[128,2048]{1,0:T(8,128)(2,1)S(1)}, bf16[128,2048]{1,0:T(8,128)(2,1)}, u32[]{:S(2)}, u32[]{:S(2)}) collective-permute-start(bf16[128,2048]{1,0:T(8,128)(2,1)S(1)} %constant_dynamic-update-slice_fusion.9.refs_3_), channel_id=1, source_target_pairs={{0,134},{128,0},{2,128},{130,2},{4,130},{132,4},{6,132},{134,6},{1... | collective-permute-start | bytes 1572872 | tf_op jit(solution)/shard_map/ppermute | solution.py:277
  62.7 13.1 %collective-permute-start.22 = (bf16[128,2048]{1,0:T(8,128)(2,1)S(1)}, bf16[128,2048]{1,0:T(8,128)(2,1)}, u32[]{:S(2)}, u32[]{:S(2)}) collective-permute-start(bf16[128,2048]{1,0:T(8,128)(2,1)S(1)} %collective-permute-done.21.refs_7_), channel_id=1, source_target_pairs={{0,128},{128,2},{2,130},{130,4},{4,132},{132,6},{6,134},{134,0},{1... | collective-permute-start | bytes 1572872 | tf_op jit(solution)/shard_map/ppermute | solution.py:277
  65.8 12.6 %collective-permute-start.19 = (bf16[128,2048]{1,0:T(8,128)(2,1)}, bf16[128,2048]{1,0:T(8,128)(2,1)}, u32[]{:S(2)}, u32[]{:S(2)}) collective-permute-start(bf16[128,2048]{1,0:T(8,128)(2,1)} %collective-permute-done.18.refs_4_), channel_id=1, source_target_pairs={{0,134},{128,0},{2,128},{130,2},{4,130},{132,4},{6,132},{134,6},{1... | collective-permute-start | bytes 1572872 | tf_op jit(solution)/shard_map/ppermute | solution.py:277
  75.8 17.0 %collective-permute-start.23 = (bf16[128,2048]{1,0:T(8,128)(2,1)}, bf16[128,2048]{1,0:T(8,128)(2,1)S(1)}, u32[]{:S(2)}, u32[]{:S(2)}) collective-permute-start(bf16[128,2048]{1,0:T(8,128)(2,1)} %collective-permute-done.22.refs_6_), channel_id=1, source_target_pairs={{0,128},{128,2},{2,130},{130,4},{4,132},{132,6},{6,134},{134,0},{1... | collective-permute-start | bytes 1572872 | tf_op jit(solution)/shard_map/ppermute | solution.py:277
  78.5 15.5 %collective-permute-start.20 = (bf16[128,2048]{1,0:T(8,128)(2,1)}, bf16[128,2048]{1,0:T(8,128)(2,1)}, u32[]{:S(2)}, u32[]{:S(2)}) collective-permute-start(bf16[128,2048]{1,0:T(8,128)(2,1)} %collective-permute-done.19.refs_5_), channel_id=1, source_target_pairs={{0,134},{128,0},{2,128},{130,2},{4,130},{132,4},{6,132},{134,6},{1... | collective-permute-start | bytes 1572872 | tf_op jit(solution)/shard_map/ppermute | solution.py:277
  81.7 17.3 %collective-permute-start = (bf16[128,2048]{1,0:T(8,128)(2,1)}, bf16[128,2048]{1,0:T(8,128)(2,1)S(1)}, u32[]{:S(2)}, u32[]{:S(2)}) collective-permute-start(bf16[128,2048]{1,0:T(8,128)(2,1)} %dynamic-slice_bitcast_fusion.5), channel_id=1, source_target_pairs={{1,0},{3,2},{5,4},{7,6},{9,8},{11,10},{13,12},{15,14},{17,16},{19,... | collective-permute-start | bytes 1572872 | tf_op jit(solution)/shard_map/ppermute | solution.py:413
  84.6 22.6 %collective-permute-start.11 = (bf16[256,1536]{1,0:T(8,128)(2,1)}, bf16[256,1536]{1,0:T(8,128)(2,1)}, u32[]{:S(2)}, u32[]{:S(2)}) collective-permute-start(bf16[256,1536]{1,0:T(8,128)(2,1)} %slice.26), channel_id=1, source_target_pairs={{0,8},{8,16},{16,24},{24,0},{1,9},{9,17},{17,25},{25,1},{2,10},{10... | collective-permute-start | bytes 2359304 | tf_op jit(solution)/shard_map/ppermute | solution.py:273
  88.2 20.6 %collective-permute-start.13 = (bf16[256,1536]{1,0:T(8,128)(2,1)}, bf16[256,1536]{1,0:T(8,128)(2,1)}, u32[]{:S(2)}, u32[]{:S(2)}) collective-permute-start(bf16[256,1536]{1,0:T(8,128)(2,1)} %slice.27), channel_id=1, source_target_pairs={{0,24},{8,0},{16,8},{24,16},{1,25},{9,1},{17,9},{25,17},{2,26},{10... | collective-permute-start | bytes 2359304 | tf_op jit(solution)/shard_map/ppermute | solution.py:273
  93.5 13.6 %collective-permute-start.24 = (bf16[64,2048]{1,0:T(8,128)(2,1)}, bf16[64,2048]{1,0:T(8,128)(2,1)S(1)}, u32[]{:S(2)}, u32[]{:S(2)}) collective-permute-start(bf16[64,2048]{1,0:T(8,128)(2,1)} %slice.28), channel_id=1, source_target_pairs={{0,128},{128,2},{2,130},{130,4},{4,132},{132,6},{6,134},{134,0},{1... | collective-permute-start | bytes 786440 | tf_op jit(solution)/shard_map/ppermute | solution.py:277
  95.6 11.5 %collective-permute-start.25 = (bf16[64,2048]{1,0:T(8,128)(2,1)}, bf16[64,2048]{1,0:T(8,128)(2,1)}, u32[]{:S(2)}, u32[]{:S(2)}) collective-permute-start(bf16[64,2048]{1,0:T(8,128)(2,1)} %slice.29), channel_id=1, source_target_pairs={{0,134},{128,0},{2,128},{130,2},{4,130},{132,4},{6,132},{134,6},{1... | collective-permute-start | bytes 786440 | tf_op jit(solution)/shard_map/ppermute | solution.py:277
  138.2 18.0 %collective-permute-start.32 = (bf16[256,2048]{1,0:T(8,128)(2,1)S(1)}, bf16[256,2048]{1,0:T(8,128)(2,1)S(1)}, u32[]{:S(2)}, u32[]{:S(2)}) collective-permute-start(bf16[256,2048]{1,0:T(8,128)(2,1)S(1)} %get-tuple-element.149), channel_id=1, source_target_pairs={{96,97},{98,99},{100,101},{102,103},{104,105},{106,107},{108,109},... | collective-permute-start | bytes 3145736 | tf_op jit(solution)/shard_map/ppermute | solution.py:431
  139.0 17.1 %collective-permute-start.33 = (bf16[128,2048]{1,0:T(8,128)(2,1)S(1)}, bf16[128,2048]{1,0:T(8,128)(2,1)S(1)}, u32[]{:S(2)}, u32[]{:S(2)}) collective-permute-start(bf16[128,2048]{1,0:T(8,128)(2,1)S(1)} %dynamic-slice_bitcast_fusion.4), channel_id=1, source_target_pairs={{0,1},{2,3},{4,5},{6,7},{8,9},{10,11},{12,13},{14,15},{16,17},{18,... | collective-permute-start | bytes 1572872 | tf_op jit(solution)/shard_map/ppermute | solution.py:415
  191.4 144.1 %collective-permute-start.40 = (bf16[256,2048]{1,0:T(8,128)(2,1)}, bf16[256,2048]{1,0:T(8,128)(2,1)}, u32[]{:S(2)}, u32[]{:S(2)}) collective-permute-start(bf16[256,2048]{1,0:T(8,128)(2,1)} %get-tuple-element.178), channel_id=1, source_target_pairs={{1,0},{3,2},{5,4},{7,6},{9,8},{11,10},{13,12},{15,14},{17,16},{19,... | collective-permute-start | bytes 3145736 | tf_op jit(solution)/shard_map/ppermute | solution.py:445
  338.3 16.4 %collective-permute-start.43 = (bf16[2,32,2048]{2,1,0:T(8,128)(2,1)S(1)}, bf16[2,32,2048]{2,1,0:T(8,128)(2,1)S(1)}, u32[]{:S(2)}, u32[]{:S(2)}) collective-permute-start(bf16[2,32,2048]{2,1,0:T(8,128)(2,1)S(1)} %get-tuple-element.213), channel_id=1, source_target_pairs={{0,128},{128,2},{2,130},{130,4},{4,132},{132,6},{6,134},{134,0},{1... | collective-permute-start | bytes 786440 | tf_op jit(solution)/shard_map/ppermute | solution.py:277
  338.4 16.3 %collective-permute-start.45 = (bf16[2,32,2048]{2,1,0:T(8,128)(2,1)S(1)}, bf16[2,32,2048]{2,1,0:T(8,128)(2,1)S(1)}, u32[]{:S(2)}, u32[]{:S(2)}) collective-permute-start(bf16[2,32,2048]{2,1,0:T(8,128)(2,1)S(1)} %get-tuple-element.211), channel_id=1, source_target_pairs={{0,134},{128,0},{2,128},{130,2},{4,130},{132,4},{6,132},{134,6},{1... | collective-permute-start | bytes 786440 | tf_op jit(solution)/shard_map/ppermute | solution.py:277
  351.4 15.8 %collective-permute-start.41 = (bf16[256,1536]{1,0:T(8,128)(2,1)S(1)}, bf16[256,1536]{1,0:T(8,128)(2,1)S(1)}, u32[]{:S(2)}, u32[]{:S(2)}) collective-permute-start(bf16[256,1536]{1,0:T(8,128)(2,1)S(1)} %get-tuple-element.203), channel_id=1, source_target_pairs={{0,8},{8,16},{16,24},{24,0},{1,9},{9,17},{17,25},{25,1},{2,10},{10... | collective-permute-start | bytes 2359304 | tf_op jit(solution)/shard_map/ppermute | solution.py:273
  352.6 14.6 %collective-permute-start.42 = (bf16[256,1536]{1,0:T(8,128)(2,1)S(1)}, bf16[256,1536]{1,0:T(8,128)(2,1)S(1)}, u32[]{:S(2)}, u32[]{:S(2)}) collective-permute-start(bf16[256,1536]{1,0:T(8,128)(2,1)S(1)} %get-tuple-element.201), channel_id=1, source_target_pairs={{0,24},{8,0},{16,8},{24,16},{1,25},{9,1},{17,9},{25,17},{2,26},{10... | collective-permute-start | bytes 2359304 | tf_op jit(solution)/shard_map/ppermute | solution.py:273
  354.9 12.9 %collective-permute-start.44 = (bf16[4,32,2048]{2,1,0:T(8,128)(2,1)S(1)}, bf16[4,32,2048]{2,1,0:T(8,128)(2,1)S(1)}, u32[]{:S(2)}, u32[]{:S(2)}) collective-permute-start(bf16[4,32,2048]{2,1,0:T(8,128)(2,1)S(1)} %pad_maximum_fusion.4), channel_id=1, source_target_pairs={{0,128},{128,2},{2,130},{130,4},{4,132},{132,6},{6,134},{134,0},{1... | collective-permute-start | bytes 1572872 | tf_op jit(solution)/shard_map/ppermute | solution.py:277
  355.1 12.8 %collective-permute-start.46 = (bf16[4,32,2048]{2,1,0:T(8,128)(2,1)S(1)}, bf16[4,32,2048]{2,1,0:T(8,128)(2,1)S(1)}, u32[]{:S(2)}, u32[]{:S(2)}) collective-permute-start(bf16[4,32,2048]{2,1,0:T(8,128)(2,1)S(1)} %pad_maximum_fusion.5), channel_id=1, source_target_pairs={{0,134},{128,0},{2,128},{130,2},{4,130},{132,4},{6,132},{134,6},{1... | collective-permute-start | bytes 1572872 | tf_op jit(solution)/shard_map/ppermute | solution.py:277
  368.3 12.7 %collective-permute-start.57 = (bf16[4,32,2048]{2,1,0:T(8,128)(2,1)S(1)}, bf16[4,32,2048]{2,1,0:T(8,128)(2,1)S(1)}, u32[]{:S(2)}, u32[]{:S(2)}) collective-permute-start(bf16[4,32,2048]{2,1,0:T(8,128)(2,1)S(1)} %get-tuple-element.198), channel_id=1, source_target_pairs={{0,128},{128,2},{2,130},{130,4},{4,132},{132,6},{6,134},{134,0},{1... | collective-permute-start | bytes 1572872 | tf_op jit(solution)/shard_map/ppermute | solution.py:277
  368.4 12.6 %collective-permute-start.59 = (bf16[4,32,2048]{2,1,0:T(8,128)(2,1)S(1)}, bf16[4,32,2048]{2,1,0:T(8,128)(2,1)S(1)}, u32[]{:S(2)}, u32[]{:S(2)}) collective-permute-start(bf16[4,32,2048]{2,1,0:T(8,128)(2,1)S(1)} %get-tuple-element.199), channel_id=1, source_target_pairs={{0,134},{128,0},{2,128},{130,2},{4,130},{132,4},{6,132},{134,6},{1... | collective-permute-start | bytes 1572872 | tf_op jit(solution)/shard_map/ppermute | solution.py:277
  371.3 31.3 %collective-permute-start.47 = (bf16[512,1536]{1,0:T(8,128)(2,1)S(1)}, bf16[512,1536]{1,0:T(8,128)(2,1)S(1)}, u32[]{:S(2)}, u32[]{:S(2)}) collective-permute-start(bf16[512,1536]{1,0:T(8,128)(2,1)S(1)} %pad_maximum_fusion), channel_id=1, source_target_pairs={{0,8},{8,16},{16,24},{24,0},{1,9},{9,17},{17,25},{25,1},{2,10},{10... | collective-permute-start | bytes 4718600 | tf_op jit(solution)/shard_map/ppermute | solution.py:273
  372.6 30.1 %collective-permute-start.48 = (bf16[512,1536]{1,0:T(8,128)(2,1)S(1)}, bf16[512,1536]{1,0:T(8,128)(2,1)S(1)}, u32[]{:S(2)}, u32[]{:S(2)}) collective-permute-start(bf16[512,1536]{1,0:T(8,128)(2,1)S(1)} %pad_maximum_fusion.1), channel_id=1, source_target_pairs={{0,24},{8,0},{16,8},{24,16},{1,25},{9,1},{17,9},{25,17},{2,26},{10... | collective-permute-start | bytes 4718600 | tf_op jit(solution)/shard_map/ppermute | solution.py:273
  381.4 10.7 %collective-permute-start.58 = (bf16[4,32,2048]{2,1,0:T(8,128)(2,1)S(1)}, bf16[4,32,2048]{2,1,0:T(8,128)(2,1)S(1)}, u32[]{:S(2)}, u32[]{:S(2)}) collective-permute-start(bf16[4,32,2048]{2,1,0:T(8,128)(2,1)S(1)} %get-tuple-element.206), channel_id=1, source_target_pairs={{0,128},{128,2},{2,130},{130,4},{4,132},{132,6},{6,134},{134,0},{1... | collective-permute-start | bytes 1572872 | tf_op jit(solution)/shard_map/ppermute | solution.py:277
  381.5 11.1 %collective-permute-start.60 = (bf16[4,32,2048]{2,1,0:T(8,128)(2,1)S(1)}, bf16[4,32,2048]{2,1,0:T(8,128)(2,1)S(1)}, u32[]{:S(2)}, u32[]{:S(2)}) collective-permute-start(bf16[4,32,2048]{2,1,0:T(8,128)(2,1)S(1)} %get-tuple-element.207), channel_id=1, source_target_pairs={{0,134},{128,0},{2,128},{130,2},{4,130},{132,4},{6,132},{134,6},{1... | collective-permute-start | bytes 1572872 | tf_op jit(solution)/shard_map/ppermute | solution.py:277
  403.4 21.3 %collective-permute-start.49 = (bf16[64,1536]{1,0:T(8,128)(2,1)S(1)}, bf16[64,1536]{1,0:T(8,128)(2,1)S(1)}, u32[]{:S(2)}, u32[]{:S(2)}) collective-permute-start(bf16[64,1536]{1,0:T(8,128)(2,1)S(1)} %get-tuple-element.216), channel_id=1, source_target_pairs={{0,4},{128,132},{2,6},{130,134},{4,0},{132,128},{6,2},{134,130},{1... | collective-permute-start | bytes 589832 | tf_op jit(solution)/shard_map/ppermute | solution.py:277
  405.1 19.5 %collective-permute-start.50 = (bf16[64,1536]{1,0:T(8,128)(2,1)S(1)}, bf16[64,1536]{1,0:T(8,128)(2,1)S(1)}, u32[]{:S(2)}, u32[]{:S(2)}) collective-permute-start(bf16[64,1536]{1,0:T(8,128)(2,1)S(1)} %get-tuple-element.222), channel_id=1, source_target_pairs={{0,130},{128,4},{2,132},{130,6},{4,134},{132,0},{6,128},{134,2},{1... | collective-permute-start | bytes 589832 | tf_op jit(solution)/shard_map/ppermute | solution.py:277
  417.6 14.4 %collective-permute-start.51 = (bf16[64,1536]{1,0:T(8,128)(2,1)S(1)}, bf16[64,1536]{1,0:T(8,128)(2,1)S(1)}, u32[]{:S(2)}, u32[]{:S(2)}) collective-permute-start(bf16[64,1536]{1,0:T(8,128)(2,1)S(1)} %get-tuple-element.221), channel_id=1, source_target_pairs={{0,132},{128,6},{2,134},{130,0},{4,128},{132,2},{6,130},{134,4},{1... | collective-permute-start | bytes 589832 | tf_op jit(solution)/shard_map/ppermute | solution.py:277
  420.5 13.3 %collective-permute-start.52 = (bf16[64,1536]{1,0:T(8,128)(2,1)S(1)}, bf16[64,1536]{1,0:T(8,128)(2,1)S(1)}, u32[]{:S(2)}, u32[]{:S(2)}) collective-permute-start(bf16[64,1536]{1,0:T(8,128)(2,1)S(1)} %get-tuple-element.220), channel_id=1, source_target_pairs={{0,2},{128,130},{2,4},{130,132},{4,6},{132,134},{6,0},{134,128},{1... | collective-permute-start | bytes 589832 | tf_op jit(solution)/shard_map/ppermute | solution.py:277
  420.5 17.0 %collective-permute-start.53 = (bf16[64,1536]{1,0:T(8,128)(2,1)S(1)}, bf16[64,1536]{1,0:T(8,128)(2,1)S(1)}, u32[]{:S(2)}, u32[]{:S(2)}) collective-permute-start(bf16[64,1536]{1,0:T(8,128)(2,1)S(1)} %get-tuple-element.219), channel_id=1, source_target_pairs={{0,6},{128,134},{2,0},{130,128},{4,2},{132,130},{6,4},{134,132},{1... | collective-permute-start | bytes 589832 | tf_op jit(solution)/shard_map/ppermute | solution.py:277
  424.6 12.9 %collective-permute-start.54 = (bf16[64,1536]{1,0:T(8,128)(2,1)S(1)}, bf16[64,1536]{1,0:T(8,128)(2,1)S(1)}, u32[]{:S(2)}, u32[]{:S(2)}) collective-permute-start(bf16[64,1536]{1,0:T(8,128)(2,1)S(1)} %get-tuple-element.218), channel_id=1, source_target_pairs={{0,128},{128,2},{2,130},{130,4},{4,132},{132,6},{6,134},{134,0},{1... | collective-permute-start | bytes 589832 | tf_op jit(solution)/shard_map/ppermute | solution.py:277
  424.7 14.9 %collective-permute-start.55 = (bf16[64,1536]{1,0:T(8,128)(2,1)S(1)}, bf16[64,1536]{1,0:T(8,128)(2,1)S(1)}, u32[]{:S(2)}, u32[]{:S(2)}) collective-permute-start(bf16[64,1536]{1,0:T(8,128)(2,1)S(1)} %get-tuple-element.217), channel_id=1, source_target_pairs={{0,134},{128,0},{2,128},{130,2},{4,130},{132,4},{6,132},{134,6},{1... | collective-permute-start | bytes 589832 | tf_op jit(solution)/shard_map/ppermute | solution.py:277
  431.9 9.8 %collective-permute-start.64 = (bf16[32,2048]{1,0:T(8,128)(2,1)S(1)}, bf16[32,2048]{1,0:T(8,128)(2,1)S(1)}, u32[]{:S(2)}, u32[]{:S(2)}) collective-permute-start(bf16[32,2048]{1,0:T(8,128)(2,1)S(1)} %fusion.23), channel_id=1, source_target_pairs={{0,0},{128,1},{2,2},{130,3},{4,4},{132,5},{6,6},{134,7},{8,8},{136... | collective-permute-start | bytes 393224 | tf_op jit(solution)/shard_map/ppermute | solution.py:448
  439.8 10.0 %collective-permute-start.56 = (bf16[64,1536]{1,0:T(8,128)(2,1)S(1)}, bf16[64,1536]{1,0:T(8,128)(2,1)S(1)}, u32[]{:S(2)}, u32[]{:S(2)}) collective-permute-start(bf16[64,1536]{1,0:T(8,128)(2,1)S(1)} %fusion.20), channel_id=1, source_target_pairs={{0,0},{128,1},{2,2},{130,3},{4,4},{132,5},{6,6},{134,7},{8,8},{136... | collective-permute-start | bytes 589832 | tf_op jit(solution)/shard_map/ppermute | solution.py:449
  (31 other events, 287.3 us)
